TPU v7x, 256 devices: a whole 4x4x8 slice. The times are simulated.
256 devices in a mesh: blk: 64 (over y, x, z_hi, core), grp: 4 (over z_lo).
Axes of the slice: x: 4, y: 4, z: 8 (z_hi: 2, z_lo: 4; z = z_hi * 4 + z_lo), core: 2. Of those that a mesh axis runs over, the one named last changes fastest.
Arguments:
- amplitudes: float32 [2048, 4, 65536], P('grp', None, 'blk'), may hold values from -6 to 6
- integrals: float32 [4, 65536, 256], P('grp', 'blk'), may hold values from -0.0234375 to 0.0234375
- irrep_sizes: int32 [4], replicated, may hold values from 86 to 256, as said below
- owner_map: int32 [4], replicated, may hold values from 0 to 3, each once
Outputs:
- ladder: float32 [2048, 4, 256], P('grp', None, 'blk')
Inputs may be any that keep to these rules, and one draw needn't show every extreme that they name: `irrep_sizes`: one irrep fills its block and one has the smallest size.
All inputs are finite; a program needn't handle non-finite values.
Results may differ from a plain program's by a relative error of at most 0.0001.
Values sent between devices are 32-bit elements; how exact they have to be, the bound alone decides.
No kernel may reach another device: no remote copies, remote signals or barrier semaphores. Data moves between devices by JAX's collectives and lax.ppermute only.
A program may use at most 128 MiB of HBM per device.

v0:
```python
import jax
import jax.numpy as jnp
from jax import lax
from jax.sharding import PartitionSpec as P

BLOCK = 256
IRREPS = 4


def from_root(shard, axis, root):
    mine = lax.axis_index(axis) == root
    return lax.psum(jnp.where(mine, shard, jnp.zeros_like(shard)), axis)


def slot_valid(irrep_sizes, offset, width):
    slot = offset + jnp.arange(width, dtype=jnp.int32)
    sizes = irrep_sizes[:, None]
    return ((slot[None, :] // BLOCK < sizes) & (slot[None, :] % BLOCK < sizes)).astype(jnp.float32)


def local(amplitudes, integrals, irrep_sizes, owner_map):
    slot_width = amplitudes.shape[2]
    column_width = integrals.shape[2] // lax.axis_size("blk")
    position = lax.axis_index("blk")
    row_valid = slot_valid(irrep_sizes, position * slot_width, slot_width)
    column_valid = slot_valid(irrep_sizes, position * column_width, column_width)
    masked = amplitudes * row_valid[None, :, :]
    blocks = []
    for irrep in range(IRREPS):
        slab_rows = from_root(integrals, "grp", owner_map[irrep])[0]
        blocks.append(
            jnp.dot(
                masked[:, irrep, :],
                slab_rows,
                precision=lax.Precision.HIGHEST,
                preferred_element_type=jnp.float32,
            )
        )
    partial_value = jnp.stack(blocks, axis=1)
    result = lax.psum_scatter(partial_value, "blk", scatter_dimension=2, tiled=True)
    return result * column_valid[None, :, :]


def solution(mesh):
    in_specs = (P("grp", None, "blk"), P("grp", "blk", None), P(), P())
    out_specs = P("grp", None, "blk")
    return jax.shard_map(local, mesh=mesh, in_specs=in_specs, out_specs=out_specs, check_vma=False)
```

profile of v0, /device:TPU:1, one launch (start us, length us, event | category | flops | bytes accessed | tf_op | source)
XLA Modules:
  0.0 1000.0 jit_solution(15541328283892642709)
XLA Ops:
  6.5 0.0 all-reduce.7.cloned.1.call-start
  6.5 1.4 fusion.13
  10.5 3.3 select_bitcast_fusion.3
  13.7 0.0 copy-start.3
  13.7 0.0 all-reduce.7.cloned.1.call-update
  13.7 0.0 all-reduce.5.cloned.1.call-start
  13.8 0.6 copy-done.3
  14.4 0.1 and_convert_fusion
  14.4 11.5 %copy_multiply_fusion = f32[512,4,1024]{2,0,1:T(8,128)} fusion(f32[512,4,1024]{2,1,0:T(4,128)} %param.4, f32[4,1024]{1,0:T(4,128)S(1)} %and_convert_fusion), kind=kLoop, calls=%fused_computation | loop fusion | flops 2097152 | bytes 16793600 | tf_op jit(solution)/shard_map/mul | solution.py:27
  25.9 156.1 %all-reduce.7.cloned.1.call-done = (f32[1024,256]{1,0:T(8,128)}, f32[1024,256]{1,0:T(8,128)}, f32[1024,256]{1,0:T(8,128)}, f32[1024,256]{1,0:T(8,128)}) async-done(((f32[1024,256]{1,0:T(8,128)}, f32[1024,256]{1,0:T(8,128)}, f32[1024,256]{1,0:T(8,128)}, f32[1024,256]{1,0:T(8,128)}), (f32[1024,256]{1,0:T(8,128)}, f32[1024,256]{1,0:T(8,128)}, f32[1024,256]{1,0:T(8,128)}, ...) | async-done | bytes 4194320 | tf_op jit(solution)/shard_map/psum | solution.py:12
  182.0 0.0 copy-start.2
  182.0 3.7 fusion.4
  185.7 0.0 copy-start.1
  185.7 0.0 copy-done.2
  185.8 3.5 fusion.5
  189.2 0.0 copy-start
  189.3 0.0 copy-done.1
  189.3 3.5 fusion.6
  192.8 0.0 copy-done
  192.8 3.4 fusion.7
  196.2 0.1 pad_maximum_fusion
  196.3 2.0 copy.9
  198.3 0.0 copy-start.4
  198.3 0.0 all-reduce.5.cloned.1.call-update
  198.4 0.6 copy-done.4
  199.0 0.6 dynamic-slice
  200.3 0.1 and_convert_fusion.1
  200.3 791.4 %all-reduce.5.cloned.1.call-done = f32[512,4,256]{0,1,2:T(4,128)} async-done(((f32[512,4,256]{0,1,2:T(4,128)}), f32[512,4,256]{0,1,2:T(4,128)}) %all-reduce.5.cloned.1.call-update) | async-done | bytes 2097168
  991.7 0.8 dynamic-slice_multiply_fusion
  992.6 0.6 copy.10
  (2 shorter events, 0.0 us)
Async XLA Ops:
  6.5 175.5 %all-reduce.7.cloned.1.call-start = ((), (), s32[]{:S(2)}) async-start(), calls=%async_computation.1 | async-start | bytes 8388608 | tf_op jit(solution)/shard_map/psum | solution.py:12
  13.7 0.7 copy-start.3
  13.7 978.0 %all-reduce.5.cloned.1.call-start = ((), (), s32[]{:S(2)}) async-start(), calls=%async_computation | async-start | bytes 4194304
  182.0 3.8 copy-start.2
  185.7 3.5 copy-start.1
  189.2 3.5 copy-start
  198.3 0.7 copy-start.4
Sparse Core Ops, SparseCore 0:
  13.9 168.0 all-reduce.6
  198.5 793.2 all-reduce.4
where the time goes:
time: 1000 us
  waiting for transfers between devices  948 us (95%)
  between operations  16.6 us (2%)
  other arithmetic  15.9 us (2%)
  matrix products  14.1 us (1%)
    unnamed x3, waiting for transfers between devices  791 us
    psum x1, waiting for transfers between devices, from_root(): return lax.psum(jnp.where(mine, shard, jnp.zeros_like(shard)), axis)  156 us
  transfers between devices with their start and end apart: 2, of which 2 were waited for; matrix products, arithmetic and copies ran while one was open for 1% of the time, Pallas kernels for 0%

commit v1 on v0

v1 whole, which is shorter than its diff:
```python
import jax
import jax.numpy as jnp
from jax import lax
from jax.sharding import PartitionSpec as P

BLOCK = 256
IRREPS = 4
NY, NX, NZ, NC, NG = 4, 4, 2, 2, 4
AXES = ("blk", "grp")


def blk_index(y, x, z, c):
    return ((y * NX + x) * NZ + z) * NC + c


def every_device():
    for y in range(NY):
        for x in range(NX):
            for z in range(NZ):
                for c in range(NC):
                    for g in range(NG):
                        yield y, x, z, c, g


def permute(value, target):
    pairs = []
    for place in every_device():
        there = target(*place)
        pairs.append((blk_index(*place[:4]) * NG + place[4], blk_index(*there[:4]) * NG + there[4]))
    return lax.ppermute(value, AXES, pairs)


def plane_groups():
    return [[blk_index(y, x, z, c) for y in range(NY) for x in range(NX)] for z in range(NZ) for c in range(NC)]


RELAY = {1: 0, 0: 2, 2: 3, 3: 1}


def slot_valid(irrep_sizes, offset, width):
    slot = offset + jnp.arange(width, dtype=jnp.int32)
    sizes = irrep_sizes[:, None]
    return ((slot[None, :] // BLOCK < sizes) & (slot[None, :] % BLOCK < sizes)).astype(jnp.float32)


def local(amplitudes, integrals, irrep_sizes, owner_map):
    pairs, _, slot_width = amplitudes.shape
    columns = integrals.shape[2]
    column_width = columns // lax.axis_size("blk")
    half = pairs // 2
    position = lax.axis_index("blk")
    group = lax.axis_index("grp")
    core = position % NC
    z_part = (position // NC) % NZ

    own = integrals[0]
    one = permute(own, lambda y, x, z, c, g: (y, x, z, c, g ^ 1))
    two = permute(own, lambda y, x, z, c, g: (y, x, z, c, g ^ 2))
    relayed = jnp.where((group == 0) | (group == 3), one, two)
    three = permute(relayed, lambda y, x, z, c, g: (y, x, z, c, RELAY[g]))

    row_valid = slot_valid(irrep_sizes, position * slot_width, slot_width)
    irrep_of = jnp.argsort(owner_map)

    def reduced(slot, slab):
        irrep = irrep_of[group ^ slot]
        chosen = lax.dynamic_index_in_dim(amplitudes, irrep, 1, keepdims=False)
        chosen = chosen * lax.dynamic_index_in_dim(row_valid, irrep, 0, keepdims=True)
        mine = lax.dynamic_slice_in_dim(chosen, core * half, half, 0)
        other = lax.dynamic_slice_in_dim(chosen, (1 - core) * half, half, 0)

        def product(rows):
            return lax.dot_general(
                slab, rows, (((0,), (1,)), ((), ())), precision=lax.Precision.HIGH, preferred_element_type=jnp.float32
            )

        sent = permute(product(other), lambda y, x, z, c, g: (y, x, z, 1 - c, g))
        chip = product(mine) + sent
        chip = chip.reshape(NY * NX, columns // (NY * NX), half)
        spread = lax.all_to_all(chip, "blk", 0, 0, tiled=True, axis_index_groups=plane_groups())
        return jnp.sum(spread, axis=0)

    parts = jnp.stack([reduced(slot, slab) for slot, slab in enumerate((own, one, two, three))])
    parts = parts.reshape(IRREPS, NZ, NC * column_width, half)
    kept = lax.dynamic_index_in_dim(parts, z_part, 1, keepdims=False)
    sent = lax.dynamic_index_in_dim(parts, 1 - z_part, 1, keepdims=False)
    parts = kept + permute(sent, lambda y, x, z, c, g: (y, x, 1 - z, c, g))
    parts = parts.reshape(IRREPS, NC, column_width, half)
    kept = lax.dynamic_index_in_dim(parts, core, 1, keepdims=False)
    sent = lax.dynamic_index_in_dim(parts, 1 - core, 1, keepdims=False)
    got = permute(sent, lambda y, x, z, c, g: (y, x, z, 1 - c, g))
    first = core == 0
    whole = jnp.concatenate([jnp.where(first, kept, got), jnp.where(first, got, kept)], axis=2)
    result = whole[owner_map ^ group]
    column_valid = slot_valid(irrep_sizes, position * column_width, column_width)
    return jnp.transpose(result * column_valid[:, :, None], (2, 0, 1))


def solution(mesh):
    in_specs = (P("grp", None, "blk"), P("grp", "blk", None), P(), P())
    out_specs = P("grp", None, "blk")
    return jax.shard_map(local, mesh=mesh, in_specs=in_specs, out_specs=out_specs, check_vma=False)
```

time: 1000 us -> 131 us (0.13)
  waiting for transfers between devices: 948 us -> 20.6 us
  starting transfers between devices: 0.04 us -> 45.6 us
  local copies, waits for them, and re-layouts: 5.88 us -> 21.2 us
    unnamed x3 -> x0, waiting for transfers between devices: 791 us -> none
    psum x1 -> x0, waiting for transfers between devices: 156 us -> none  [from_root(): return lax.psum(jnp.where(mine, shard, jnp.zeros_like(shard)), axis)]
    ppermute x0 -> x9, starting transfers between devices: none -> 25 us  [permute(): return lax.ppermute(value, AXES, pairs)]
    all_to_all x0 -> x4, starting transfers between devices: none -> 20.6 us  [reduced(): lax.all_to_all(chip, 'blk', 0, 0, tiled=True, axis_index_groups=plane_gro...]
    dynamic_slice x0 -> x5, local copies, waits for them, and re-layouts: none -> 20.5 us  [the longest x1 19.9 us: reduced(): chosen = lax.dynamic_index_in_dim(amplitudes, irrep, 1, keepdims=False)]
    all_to_all x0 -> x4, waiting for transfers between devices: none -> 17 us  [reduced(): lax.all_to_all(chip, 'blk', 0, 0, tiled=True, axis_index_groups=plane_gro...]
    dot_general x4 -> x8, matrix products: 14.1 us -> 21.7 us  [product(): lax.dot_general(slab, rows, (((0,), (1,)), ((), ())), precision=lax.Preci...]
  transfers between devices with their start and end apart: 2 -> 13, of which waited for: 2 -> 6; matrix products, arithmetic and copies ran while one was open for 1% -> 42% of each run, Pallas kernels for 0% -> 0%
where the time goes in v1:
time: 131 us; the launch traced here: 130 us
  starting transfers between devices  45.6 us (35%)
  matrix products  21.7 us (17%)
  local copies, waits for them, and re-layouts  21.2 us (16%)
  waiting for transfers between devices  20.6 us (16%)
  other arithmetic  13.2 us (10%)
  between operations  7.66 us (6%)
    ppermute x9, starting transfers between devices, permute(): return lax.ppermute(value, AXES, pairs)  25 us
    dot_general x8, matrix products, product(): lax.dot_general(slab, rows, (((0,), (1,)), ((), ())), precision=lax.Preci...  21.7 us
    all_to_all x4, starting transfers between devices, reduced(): lax.all_to_all(chip, 'blk', 0, 0, tiled=True, axis_index_groups=plane_gro...  20.6 us
    dynamic_slice x1, local copies, waits for them, and re-layouts, reduced(): chosen = lax.dynamic_index_in_dim(amplitudes, irrep, 1, keepdims=False)  19.9 us
    all_to_all x4, waiting for transfers between devices, reduced(): lax.all_to_all(chip, 'blk', 0, 0, tiled=True, axis_index_groups=plane_gro...  17 us
    mul x4, other arithmetic, reduced(): chosen * lax.dynamic_index_in_dim(row_valid, irrep, 0, keepdims=True)  9.01 us
    ppermute x9, waiting for transfers between devices, permute(): return lax.ppermute(value, AXES, pairs)  3.61 us
  transfers between devices with their start and end apart: 13, of which 6 were waited for; matrix products, arithmetic and copies ran while one was open for 42% of the time, Pallas kernels for 0%

profile of v1, /device:TPU:1, one launch (start us, length us, event | category | flops | bytes accessed | tf_op | source)
XLA Modules:
  0.0 130.0 jit_solution(9091898977383814548)
XLA Ops:
  0.0 2.5 %collective-permute-start.1 = (f32[1024,256]{1,0:T(8,128)}, f32[1024,256]{1,0:T(8,128)S(1)}, u32[]{:S(2)}, u32[]{:S(2)}) collective-permute-start(f32[1024,256]{1,0:T(8,128)} %bitcast.70), channel_id=1, source_target_pairs={{0,1},{1,0},{2,3},{3,2},{4,5},{5,4},{6,7},{7,6},{8,9},{9,8},{10,11... | collective-permute-start | bytes 3145736 | tf_op jit(solution)/shard_map/ppermute | solution.py:30
  2.5 3.0 %collective-permute-start.3 = (f32[1024,256]{1,0:T(8,128)}, f32[1024,256]{1,0:T(8,128)S(1)}, u32[]{:S(2)}, u32[]{:S(2)}) collective-permute-start(f32[1024,256]{1,0:T(8,128)} %bitcast.71), channel_id=1, source_target_pairs={{0,2},{1,3},{2,0},{3,1},{4,6},{5,7},{6,4},{7,5},{8,10},{9,11},{10,... | collective-permute-start | bytes 3145736 | tf_op jit(solution)/shard_map/ppermute | solution.py:30
  5.5 1.4 %sort.17 = (s32[4]{0:T(128)}, s32[4]{0:T(128)S(1)}) sort(s32[4]{0:T(128)} %param.7, s32[4]{0:T(128)S(1)} %iota.18), dimensions={0}, to_apply=%region_0.1 | sort | flops 8 | bytes 64 | tf_op jit(solution)/shard_map/jit(argsort)/sort | solution.py:63
  6.8 0.6 fusion.31
  14.9 0.7 and_convert_fusion
  15.7 19.9 %constant_dynamic-slice_fusion.9 = (f32[512,1,1024]{2,1,0:T(1,128)S(1)}, f32[512,1,1024]{2,1,0:T(1,128)}, f32[512,1,1024]{2,1,0:T(1,128)}, f32[512,1,1024]{2,1,0:T(1,128)}) fusion(f32[512,4,1024]{2,1,0:T(4,128)} %param.4, s32[]{:T(128)S(6)} %select_n.139, s32[]{:T(128)S(6)} %select_n.147, s32[]{:T(128)S(6)} %select_n.145, s32[]{:T(128)S(6)} %select_n.151), kind=kLoop, calls=%fused_computation.60 | loop fusion | bytes 16777232 | tf_op jit(solution)/shard_map/jit(dynamic_index_in_dim)/dynamic_slice | solution.py:67
  35.5 0.0 copy-start.4
  35.5 1.8 %fusion.3 = f32[512,1024]{1,0:T(8,128)} fusion(f32[512,1,1024]{2,1,0:T(1,128)S(1)} %get-tuple-element.7, f32[1024]{0:T(1024)S(1)} %bitcast.76), kind=kLoop, calls=%fused_computation.8 | loop fusion | flops 524288 | bytes 4198400 | tf_op jit(solution)/shard_map/mul | solution.py:68
  37.4 0.0 copy-done.4
  37.4 2.2 %convolution_bitcast_fusion.4 = f32[256,256]{1,0:T(8,128)S(1)} fusion(f32[512,1024]{1,0:T(8,128)} %fusion.3, s32[]{:T(128)S(6)} %select_n.143, f32[1,1024,256]{2,1,0:T(8,128)S(1)} %copy-done.4), kind=kOutput, calls=%fused_computation.16 | convolution fusion | flops 402653184 | bytes 2359300 | tf_op jit(solution)/shard_map/dot_general | solution.py:73
  39.6 1.3 %collective-permute-start = (f32[256,256]{1,0:T(8,128)S(1)}, f32[256,256]{1,0:T(8,128)}, u32[]{:S(2)}, u32[]{:S(2)}) collective-permute-start(f32[256,256]{1,0:T(8,128)S(1)} %convolution_bitcast_fusion.4), channel_id=1, source_target_pairs={{0,4},{1,5},{2,6},{3,7},{4,0},{5,1},{6,2},{7,3},{8,12},{9,13},{10,... | collective-permute-start | bytes 786440 | tf_op jit(solution)/shard_map/ppermute | solution.py:30
  40.9 0.0 copy-start.1
  40.9 3.6 %fusion.2 = f32[512,1024]{1,0:T(8,128)} fusion(f32[512,1,1024]{2,1,0:T(1,128)} %get-tuple-element.9, f32[1024]{0:T(1024)S(1)} %bitcast.75), kind=kLoop, calls=%fused_computation.6 | loop fusion | flops 524288 | bytes 4198400 | tf_op jit(solution)/shard_map/mul | solution.py:68
  44.5 0.0 copy-done.1
  44.5 1.8 %fusion.1 = f32[512,1024]{1,0:T(8,128)} fusion(f32[512,1,1024]{2,1,0:T(1,128)S(1)} %copy-done.1, f32[1024]{0:T(1024)S(1)} %bitcast.74), kind=kLoop, calls=%fused_computation.4 | loop fusion | flops 524288 | bytes 4198400 | tf_op jit(solution)/shard_map/mul | solution.py:68
  46.3 0.0 copy-start
  46.3 0.0 collective-permute-done.1
  46.3 0.8 collective-permute-done.3
  47.1 1.1 broadcast_select_fusion
  48.2 3.0 %collective-permute-start.5 = (f32[1024,256]{1,0:T(8,128)}, f32[1024,256]{1,0:T(8,128)}, u32[]{:S(2)}, u32[]{:S(2)}) collective-permute-start(f32[1024,256]{1,0:T(8,128)} %broadcast_select_fusion), channel_id=1, source_target_pairs={{0,2},{1,0},{2,3},{3,1},{4,6},{5,4},{6,7},{7,5},{8,10},{9,8},{10,1... | collective-permute-start | bytes 3145736 | tf_op jit(solution)/shard_map/ppermute | solution.py:30
  51.2 0.0 copy-done
  51.2 1.8 %fusion = f32[512,1024]{1,0:T(8,128)} fusion(f32[512,1,1024]{2,1,0:T(1,128)S(1)} %copy-done, f32[1024]{0:T(1024)S(1)} %bitcast.73), kind=kLoop, calls=%fused_computation.2 | loop fusion | flops 524288 | bytes 4198400 | tf_op jit(solution)/shard_map/mul | solution.py:68
  53.0 0.0 copy-start.3
  53.0 3.1 %convolution_bitcast_fusion.2 = f32[256,256]{1,0:T(8,128)} fusion(f32[1024,256]{1,0:T(8,128)S(1)} %collective-permute-done.1, f32[512,1024]{1,0:T(8,128)} %fusion.2, s32[]{:T(128)S(6)} %select_n.143), kind=kOutput, calls=%fused_computation.13 | convolution fusion | flops 402653184 | bytes 2359300 | tf_op jit(solution)/shard_map/dot_general | solution.py:73
  56.1 2.2 %collective-permute-start.2 = (f32[256,256]{1,0:T(8,128)}, f32[256,256]{1,0:T(8,128)}, u32[]{:S(2)}, u32[]{:S(2)}) collective-permute-start(f32[256,256]{1,0:T(8,128)} %convolution_bitcast_fusion.2), channel_id=1, source_target_pairs={{0,4},{1,5},{2,6},{3,7},{4,0},{5,1},{6,2},{7,3},{8,12},{9,13},{10,... | collective-permute-start | bytes 786440 | tf_op jit(solution)/shard_map/ppermute | solution.py:30
  58.3 0.0 collective-permute-done
  58.3 0.0 copy-done.3
  58.3 2.6 %fusion.6 = f32[256,256]{1,0:T(8,128)} fusion(f32[256,256]{1,0:T(8,128)} %collective-permute-done, f32[512,1024]{1,0:T(8,128)S(1)} %copy-done.3, s32[]{:T(128)S(6)} %select_n.142, f32[1,1024,256]{2,1,0:T(8,128)S(1)} %copy-done.4), kind=kOutput, calls=%fused_computation.18 | convolution fusion | flops 402718720 | bytes 2621444 | tf_op jit(solution)/shard_map/dot_general | solution.py:73
  61.0 6.8 %all-to-all-start = ((f32[16,16,256]{2,1,0:T(8,128)}), f32[16,16,256]{2,1,0:T(8,128)S(1)}, u32[]{:S(2)}, u32[]{:S(2)}) async-start(f32[16,16,256]{2,1,0:T(8,128)} %bitcast.6), calls=%async_computation | async-start | bytes 524288 | tf_op jit(solution)/shard_map/all_to_all | solution.py:80
  67.7 0.0 copy-start.2
  67.7 2.4 %convolution_bitcast_fusion = f32[256,256]{1,0:T(8,128)S(1)} fusion(f32[1024,256]{1,0:T(8,128)S(1)} %collective-permute-done.3, f32[512,1024]{1,0:T(8,128)} %fusion.1, s32[]{:T(128)S(6)} %select_n.143), kind=kOutput, calls=%fused_computation.10 | convolution fusion | flops 402653184 | bytes 2359300 | tf_op jit(solution)/shard_map/dot_general | solution.py:73
  70.1 0.4 collective-permute-start.4
  70.5 0.0 collective-permute-done.2
  70.5 3.0 %fusion.5 = f32[256,256]{1,0:T(8,128)} fusion(f32[256,256]{1,0:T(8,128)} %collective-permute-done.2, f32[1024,256]{1,0:T(8,128)S(1)} %collective-permute-done.1, f32[512,1024]{1,0:T(8,128)} %fusion.2, s32[]{:T(128)S(6)} %select_n.142), kind=kOutput, calls=%fused_computation.15 | convolution fusion | flops 402718720 | bytes 2621444 | tf_op jit(solution)/shard_map/dot_general | solution.py:73
  73.5 0.0 collective-permute-done.5
  73.5 0.0 copy-done.2
  73.5 2.2 %fusion.7 = f32[256,256]{1,0:T(8,128)S(1)} fusion(f32[1024,256]{1,0:T(8,128)} %collective-permute-done.5, f32[512,1024]{1,0:T(8,128)S(1)} %copy-done.2, s32[]{:T(128)S(6)} %select_n.143), kind=kOutput, calls=%fused_computation.19 | convolution fusion | flops 402653184 | bytes 2359300 | tf_op jit(solution)/shard_map/dot_general | solution.py:73
  75.7 3.0 %collective-permute-start.6 = (f32[256,256]{1,0:T(8,128)S(1)}, f32[256,256]{1,0:T(8,128)S(1)}, u32[]{:S(2)}, u32[]{:S(2)}) collective-permute-start(f32[256,256]{1,0:T(8,128)S(1)} %fusion.7), channel_id=1, source_target_pairs={{0,4},{1,5},{2,6},{3,7},{4,0},{5,1},{6,2},{7,3},{8,12},{9,13},{10,... | collective-permute-start | bytes 786440 | tf_op jit(solution)/shard_map/ppermute | solution.py:30
  78.8 0.0 all-to-all-done
  78.8 6.8 %all-to-all-start.1 = ((f32[16,16,256]{2,1,0:T(8,128)}), f32[16,16,256]{2,1,0:T(8,128)S(1)}, u32[]{:S(2)}, u32[]{:S(2)}) async-start(f32[16,16,256]{2,1,0:T(8,128)} %bitcast.12), calls=%async_computation.1 | async-start | bytes 524288 | tf_op jit(solution)/shard_map/all_to_all | solution.py:80
  85.5 0.0 collective-permute-done.4
  85.5 2.9 %fusion.4 = f32[256,256]{1,0:T(8,128)} fusion(f32[256,256]{1,0:T(8,128)S(1)} %collective-permute-done.4, f32[1024,256]{1,0:T(8,128)S(1)} %collective-permute-done.3, f32[512,1024]{1,0:T(8,128)} %fusion.1, s32[]{:T(128)S(6)} %select_n.142), kind=kOutput, calls=%fused_computation.12 | convolution fusion | flops 402718720 | bytes 2621444 | tf_op jit(solution)/shard_map/dot_general | solution.py:73
  88.5 0.0 copy-start.5
  88.5 5.5 %all-to-all-done.1 = f32[16,16,256]{2,1,0:T(8,128)S(1)} async-done(((f32[16,16,256]{2,1,0:T(8,128)}), f32[16,16,256]{2,1,0:T(8,128)S(1)}, u32[]{:S(2)}, u32[]{:S(2)}) %all-to-all-start.1) | async-done | bytes 262176 | tf_op jit(solution)/shard_map/all_to_all | solution.py:80
  94.0 3.5 %all-to-all-start.2 = ((f32[16,16,256]{2,1,0:T(8,128)}), f32[16,16,256]{2,1,0:T(8,128)S(1)}, u32[]{:S(2)}, u32[]{:S(2)}) async-start(f32[16,16,256]{2,1,0:T(8,128)} %bitcast.18), calls=%async_computation.2 | async-start | bytes 524288 | tf_op jit(solution)/shard_map/all_to_all | solution.py:80
  97.5 0.0 copy-start.6
  97.5 0.0 collective-permute-done.6
  97.5 3.2 %convolution_add_fusion = f32[256,256]{1,0:T(8,128)} fusion(f32[256,256]{1,0:T(8,128)S(1)} %collective-permute-done.6, f32[1024,256]{1,0:T(8,128)} %collective-permute-done.5, f32[512,1024]{1,0:T(8,128)} %fusion, s32[]{:T(128)S(6)} %select_n.142), kind=kOutput, calls=%fused_computation.9 | convolution fusion | flops 402718720 | bytes 2621444 | tf_op jit(solution)/shard_map/dot_general | solution.py:73
  100.8 4.3 %all-to-all-done.2 = f32[16,16,256]{2,1,0:T(8,128)S(1)} async-done(((f32[16,16,256]{2,1,0:T(8,128)}), f32[16,16,256]{2,1,0:T(8,128)S(1)}, u32[]{:S(2)}, u32[]{:S(2)}) %all-to-all-start.2) | async-done | bytes 262176 | tf_op jit(solution)/shard_map/all_to_all | solution.py:80
  105.1 3.5 %all-to-all-start.3 = ((f32[16,16,256]{2,1,0:T(8,128)}), f32[16,16,256]{2,1,0:T(8,128)S(1)}, u32[]{:S(2)}, u32[]{:S(2)}) async-start(f32[16,16,256]{2,1,0:T(8,128)} %bitcast.22), calls=%async_computation.3 | async-start | bytes 524288 | tf_op jit(solution)/shard_map/all_to_all | solution.py:80
  108.7 0.0 copy-done.5
  108.7 0.1 and_convert_fusion.1
  108.9 7.2 %all-to-all-done.3 = f32[16,16,256]{2,1,0:T(8,128)S(1)} async-done(((f32[16,16,256]{2,1,0:T(8,128)}), f32[16,16,256]{2,1,0:T(8,128)S(1)}, u32[]{:S(2)}, u32[]{:S(2)}) %all-to-all-start.3) | async-done | bytes 262176 | tf_op jit(solution)/shard_map/all_to_all | solution.py:80
  116.2 0.1 pad_maximum_fusion
  116.3 4.9 %collective-permute-start.7 = (f32[4,8,256]{2,0,1:T(4,128)S(1)}, f32[4,8,256]{2,0,1:T(4,128)S(1)}, u32[]{:S(2)}, u32[]{:S(2)}) collective-permute-start(f32[4,8,256]{2,0,1:T(4,128)S(1)} %dynamic-slice_bitcast_fusion), channel_id=1, source_target_pairs={{0,8},{1,9},{2,10},{3,11},{4,12},{5,13},{6,14},{7,15},{8,0},{9,1},... | collective-permute-start | bytes 98312 | tf_op jit(solution)/shard_map/ppermute | solution.py:30
  121.1 0.0 copy-done.6
  121.1 1.9 %collective-permute-done.7 = f32[4,8,256]{2,0,1:T(4,128)S(1)} collective-permute-done((f32[4,8,256]{2,0,1:T(4,128)S(1)}, f32[4,8,256]{2,0,1:T(4,128)S(1)}, u32[]{:S(2)}, u32[]{:S(2)}) %collective-permute-start.7) | collective-permute-done | bytes 32800 | tf_op jit(solution)/shard_map/ppermute | solution.py:30
  123.1 4.8 %collective-permute-start.8 = (f32[4,4,256]{2,1,0:T(4,128)S(1)}, f32[4,4,256]{2,1,0:T(4,128)S(1)}, u32[]{:S(2)}, u32[]{:S(2)}) collective-permute-start(f32[4,4,256]{2,1,0:T(4,128)S(1)} %bitcast.77), channel_id=1, source_target_pairs={{0,4},{1,5},{2,6},{3,7},{4,0},{5,1},{6,2},{7,3},{8,12},{9,13},{10,... | collective-permute-start | bytes 49160 | tf_op jit(solution)/shard_map/ppermute | solution.py:30
  127.8 0.8 collective-permute-done.8
  128.7 0.6 gather_fusion
  129.3 0.7 multiply_bitcast_fusion
  (20 shorter events, 0.3 us)
Async XLA Ops:
  0.0 46.3 %collective-permute-start.1 = (f32[1024,256]{1,0:T(8,128)}, f32[1024,256]{1,0:T(8,128)S(1)}, u32[]{:S(2)}, u32[]{:S(2)}) collective-permute-start(f32[1024,256]{1,0:T(8,128)} %bitcast.70), channel_id=1, source_target_pairs={{0,1},{1,0},{2,3},{3,2},{4,5},{5,4},{6,7},{7,6},{8,9},{9,8},{10,11... | collective-permute-start | bytes 3145736 | tf_op jit(solution)/shard_map/ppermute | solution.py:30
  2.5 44.7 %collective-permute-start.3 = (f32[1024,256]{1,0:T(8,128)}, f32[1024,256]{1,0:T(8,128)S(1)}, u32[]{:S(2)}, u32[]{:S(2)}) collective-permute-start(f32[1024,256]{1,0:T(8,128)} %bitcast.71), channel_id=1, source_target_pairs={{0,2},{1,3},{2,0},{3,1},{4,6},{5,7},{6,4},{7,5},{8,10},{9,11},{10,... | collective-permute-start | bytes 3145736 | tf_op jit(solution)/shard_map/ppermute | solution.py:30
  35.5 1.9 %copy-start.4 = (f32[1,1024,256]{2,1,0:T(8,128)S(1)}, f32[1,1024,256]{2,1,0:T(8,128)}, u32[]{:S(2)}) copy-start(f32[1,1024,256]{2,1,0:T(8,128)} %param.5) | copy-start | bytes 3145732
  39.6 18.7 %collective-permute-start = (f32[256,256]{1,0:T(8,128)S(1)}, f32[256,256]{1,0:T(8,128)}, u32[]{:S(2)}, u32[]{:S(2)}) collective-permute-start(f32[256,256]{1,0:T(8,128)S(1)} %convolution_bitcast_fusion.4), channel_id=1, source_target_pairs={{0,4},{1,5},{2,6},{3,7},{4,0},{5,1},{6,2},{7,3},{8,12},{9,13},{10,... | collective-permute-start | bytes 786440 | tf_op jit(solution)/shard_map/ppermute | solution.py:30
  40.9 3.6 %copy-start.1 = (f32[512,1,1024]{2,1,0:T(1,128)S(1)}, f32[512,1,1024]{2,1,0:T(1,128)}, u32[]{:S(2)}) copy-start(f32[512,1,1024]{2,1,0:T(1,128)} %get-tuple-element.8) | copy-start | bytes 6291460
  46.3 4.9 %copy-start = (f32[512,1,1024]{2,1,0:T(1,128)S(1)}, f32[512,1,1024]{2,1,0:T(1,128)}, u32[]{:S(2)}) copy-start(f32[512,1,1024]{2,1,0:T(1,128)} %get-tuple-element.10) | copy-start | bytes 6291460
  48.2 25.3 %collective-permute-start.5 = (f32[1024,256]{1,0:T(8,128)}, f32[1024,256]{1,0:T(8,128)}, u32[]{:S(2)}, u32[]{:S(2)}) collective-permute-start(f32[1024,256]{1,0:T(8,128)} %broadcast_select_fusion), channel_id=1, source_target_pairs={{0,2},{1,0},{2,3},{3,1},{4,6},{5,4},{6,7},{7,5},{8,10},{9,8},{10,1... | collective-permute-start | bytes 3145736 | tf_op jit(solution)/shard_map/ppermute | solution.py:30
  53.0 5.3 %copy-start.3 = (f32[512,1024]{1,0:T(8,128)S(1)}, f32[512,1024]{1,0:T(8,128)}, u32[]{:S(2)}) copy-start(f32[512,1024]{1,0:T(8,128)} %fusion.3) | copy-start | bytes 6291460
  56.1 14.4 %collective-permute-start.2 = (f32[256,256]{1,0:T(8,128)}, f32[256,256]{1,0:T(8,128)}, u32[]{:S(2)}, u32[]{:S(2)}) collective-permute-start(f32[256,256]{1,0:T(8,128)} %convolution_bitcast_fusion.2), channel_id=1, source_target_pairs={{0,4},{1,5},{2,6},{3,7},{4,0},{5,1},{6,2},{7,3},{8,12},{9,13},{10,... | collective-permute-start | bytes 786440 | tf_op jit(solution)/shard_map/ppermute | solution.py:30
  61.0 17.8 %all-to-all-start = ((f32[16,16,256]{2,1,0:T(8,128)}), f32[16,16,256]{2,1,0:T(8,128)S(1)}, u32[]{:S(2)}, u32[]{:S(2)}) async-start(f32[16,16,256]{2,1,0:T(8,128)} %bitcast.6), calls=%async_computation | async-start | bytes 524288 | tf_op jit(solution)/shard_map/all_to_all | solution.py:80
  67.7 5.8 %copy-start.2 = (f32[512,1024]{1,0:T(8,128)S(1)}, f32[512,1024]{1,0:T(8,128)}, u32[]{:S(2)}) copy-start(f32[512,1024]{1,0:T(8,128)} %fusion) | copy-start | bytes 6291460
  70.1 15.4 %collective-permute-start.4 = (f32[256,256]{1,0:T(8,128)S(1)}, f32[256,256]{1,0:T(8,128)S(1)}, u32[]{:S(2)}, u32[]{:S(2)}) collective-permute-start(f32[256,256]{1,0:T(8,128)S(1)} %convolution_bitcast_fusion), channel_id=1, source_target_pairs={{0,4},{1,5},{2,6},{3,7},{4,0},{5,1},{6,2},{7,3},{8,12},{9,13},{10,... | collective-permute-start | bytes 786440 | tf_op jit(solution)/shard_map/ppermute | solution.py:30
  75.7 21.8 %collective-permute-start.6 = (f32[256,256]{1,0:T(8,128)S(1)}, f32[256,256]{1,0:T(8,128)S(1)}, u32[]{:S(2)}, u32[]{:S(2)}) collective-permute-start(f32[256,256]{1,0:T(8,128)S(1)} %fusion.7), channel_id=1, source_target_pairs={{0,4},{1,5},{2,6},{3,7},{4,0},{5,1},{6,2},{7,3},{8,12},{9,13},{10,... | collective-permute-start | bytes 786440 | tf_op jit(solution)/shard_map/ppermute | solution.py:30
  78.8 15.2 %all-to-all-start.1 = ((f32[16,16,256]{2,1,0:T(8,128)}), f32[16,16,256]{2,1,0:T(8,128)S(1)}, u32[]{:S(2)}, u32[]{:S(2)}) async-start(f32[16,16,256]{2,1,0:T(8,128)} %bitcast.12), calls=%async_computation.1 | async-start | bytes 524288 | tf_op jit(solution)/shard_map/all_to_all | solution.py:80
  88.5 20.2 %copy-start.5 = (s32[4]{0:T(128)S(1)}, s32[4]{0:T(128)}, u32[]{:S(2)}) copy-start(s32[4]{0:T(128)} %param.6) | copy-start | bytes 52
  94.0 11.1 %all-to-all-start.2 = ((f32[16,16,256]{2,1,0:T(8,128)}), f32[16,16,256]{2,1,0:T(8,128)S(1)}, u32[]{:S(2)}, u32[]{:S(2)}) async-start(f32[16,16,256]{2,1,0:T(8,128)} %bitcast.18), calls=%async_computation.2 | async-start | bytes 524288 | tf_op jit(solution)/shard_map/all_to_all | solution.py:80
  97.5 23.6 %copy-start.6 = (s32[4]{0:T(128)S(1)}, s32[4]{0:T(128)}, u32[]{:S(2)}) copy-start(s32[4]{0:T(128)} %param.7) | copy-start | bytes 52
  105.1 11.0 %all-to-all-start.3 = ((f32[16,16,256]{2,1,0:T(8,128)}), f32[16,16,256]{2,1,0:T(8,128)S(1)}, u32[]{:S(2)}, u32[]{:S(2)}) async-start(f32[16,16,256]{2,1,0:T(8,128)} %bitcast.22), calls=%async_computation.3 | async-start | bytes 524288 | tf_op jit(solution)/shard_map/all_to_all | solution.py:80
  116.3 6.8 %collective-permute-start.7 = (f32[4,8,256]{2,0,1:T(4,128)S(1)}, f32[4,8,256]{2,0,1:T(4,128)S(1)}, u32[]{:S(2)}, u32[]{:S(2)}) collective-permute-start(f32[4,8,256]{2,0,1:T(4,128)S(1)} %dynamic-slice_bitcast_fusion), channel_id=1, source_target_pairs={{0,8},{1,9},{2,10},{3,11},{4,12},{5,13},{6,14},{7,15},{8,0},{9,1},... | collective-permute-start | bytes 98312 | tf_op jit(solution)/shard_map/ppermute | solution.py:30
  123.1 5.6 %collective-permute-start.8 = (f32[4,4,256]{2,1,0:T(4,128)S(1)}, f32[4,4,256]{2,1,0:T(4,128)S(1)}, u32[]{:S(2)}, u32[]{:S(2)}) collective-permute-start(f32[4,4,256]{2,1,0:T(4,128)S(1)} %bitcast.77), channel_id=1, source_target_pairs={{0,4},{1,5},{2,6},{3,7},{4,0},{5,1},{6,2},{7,3},{8,12},{9,13},{10,... | collective-permute-start | bytes 49160 | tf_op jit(solution)/shard_map/ppermute | solution.py:30

commit v2 on v1

--- a/solution.py
+++ b/solution.py
@@ -1,10 +1,15 @@
+import functools
+
 import jax
 import jax.numpy as jnp
 from jax import lax
+from jax.experimental import pallas as pl
+from jax.experimental.pallas import tpu as pltpu
 from jax.sharding import PartitionSpec as P
 
 BLOCK = 256
 IRREPS = 4
+LANES = 128
 NY, NX, NZ, NC, NG = 4, 4, 2, 2, 4
 AXES = ("blk", "grp")
 
@@ -43,11 +48,82 @@
     return ((slot[None, :] // BLOCK < sizes) & (slot[None, :] % BLOCK < sizes)).astype(jnp.float32)
 
 
+def split_kernel(rows, slot_width, scalars, source, *outputs):
+    tiles = slot_width // LANES
+    group, position = scalars[2 * IRREPS], scalars[2 * IRREPS + 1]
+    lane = lax.broadcasted_iota(jnp.int32, (rows, LANES), 1)
+    for slot in range(IRREPS):
+        irrep = jnp.int32(0)
+        for h in range(IRREPS):
+            irrep = jnp.where(scalars[h] == (group ^ slot), h, irrep)
+        size = scalars[IRREPS + irrep]
+        high, low = outputs[2 * slot], outputs[2 * slot + 1]
+        for tile in range(tiles):
+            first = position * slot_width + tile * LANES
+            limit = jnp.where(first // BLOCK < size, size - first % BLOCK, 0)
+            value = source[pl.ds(tile * IRREPS + irrep, rows, stride=tiles * IRREPS), :]
+            value = jnp.where(lane < limit, value, 0.0)
+            rounded = value.astype(jnp.bfloat16)
+            place = slice(tile * LANES, (tile + 1) * LANES)
+            high[0, :, place] = rounded
+            low[0, :, place] = (value - rounded.astype(jnp.float32)).astype(jnp.bfloat16)
+
+
+def split_rows(amplitudes, scalars):
+    pairs, _, slot_width = amplitudes.shape
+    half = pairs // 2
+    rows = 64
+    steps = half // rows
+    view = amplitudes.reshape(pairs, IRREPS, slot_width // LANES, LANES).transpose(0, 2, 1, 3).reshape(-1, LANES)
+
+    def out_index(i, scalars):
+        return ((i // steps) ^ scalars[2 * IRREPS + 2] ^ 1, i % steps, 0)
+
+    return pl.pallas_call(
+        functools.partial(split_kernel, rows, slot_width),
+        out_shape=[jax.ShapeDtypeStruct((2, half, slot_width), jnp.bfloat16)] * (2 * IRREPS),
+        grid_spec=pltpu.PrefetchScalarGridSpec(
+            num_scalar_prefetch=1,
+            grid=(2 * steps,),
+            in_specs=[pl.BlockSpec((rows * IRREPS * slot_width // LANES, LANES), lambda i, scalars: (i, 0))],
+            out_specs=[pl.BlockSpec((1, rows, slot_width), out_index)] * (2 * IRREPS),
+        ),
+        compiler_params=pltpu.CompilerParams(vmem_limit_bytes=16 << 20),
+        cost_estimate=pl.CostEstimate(flops=0, bytes_accessed=8 * pairs * IRREPS * slot_width, transcendentals=0),
+        name="split_rows",
+    )(scalars, view)
+
+
+def product_kernel(part, slab, high, low, out):
+    value = slab[...]
+    rounded = value.astype(jnp.bfloat16)
+    rest = (value - rounded.astype(jnp.float32)).astype(jnp.bfloat16)
+    dot = functools.partial(jnp.dot, preferred_element_type=jnp.float32)
+    total = dot(high[part], rounded) + (dot(high[part], rest) + dot(low[part], rounded))
+    out[...] = total.T
+
+
+def product(slab, high, low, part):
+    slots, columns = slab.shape
+    half = high.shape[1]
+    return pl.pallas_call(
+        functools.partial(product_kernel, part),
+        out_shape=jax.ShapeDtypeStruct((columns, half), jnp.float32),
+        in_specs=[pl.BlockSpec(memory_space=pltpu.VMEM)] * 3,
+        out_specs=pl.BlockSpec(memory_space=pltpu.VMEM),
+        compiler_params=pltpu.CompilerParams(vmem_limit_bytes=16 << 20),
+        cost_estimate=pl.CostEstimate(
+            flops=6 * slots * columns * half, bytes_accessed=4 * slots * (columns + half), transcendentals=0
+        ),
+        name="product",
+    )(slab, high, low)
+
+
 def local(amplitudes, integrals, irrep_sizes, owner_map):
-    pairs, _, slot_width = amplitudes.shape
+    slot_width = amplitudes.shape[2]
     columns = integrals.shape[2]
     column_width = columns // lax.axis_size("blk")
-    half = pairs // 2
+    half = amplitudes.shape[0] // 2
     position = lax.axis_index("blk")
     group = lax.axis_index("grp")
     core = position % NC
@@ -56,31 +132,28 @@
     own = integrals[0]
     one = permute(own, lambda y, x, z, c, g: (y, x, z, c, g ^ 1))
     two = permute(own, lambda y, x, z, c, g: (y, x, z, c, g ^ 2))
-    relayed = jnp.where((group == 0) | (group == 3), one, two)
-    three = permute(relayed, lambda y, x, z, c, g: (y, x, z, c, RELAY[g]))
 
-    row_valid = slot_valid(irrep_sizes, position * slot_width, slot_width)
-    irrep_of = jnp.argsort(owner_map)
+    scalars = jnp.concatenate([owner_map, irrep_sizes, jnp.stack([group, position, core])])
+    split = split_rows(amplitudes, scalars)
 
-    def reduced(slot, slab):
-        irrep = irrep_of[group ^ slot]
-        chosen = lax.dynamic_index_in_dim(amplitudes, irrep, 1, keepdims=False)
-        chosen = chosen * lax.dynamic_index_in_dim(row_valid, irrep, 0, keepdims=True)
-        mine = lax.dynamic_slice_in_dim(chosen, core * half, half, 0)
-        other = lax.dynamic_slice_in_dim(chosen, (1 - core) * half, half, 0)
+    def on_chip(slot, slab):
+        high, low = split[2 * slot], split[2 * slot + 1]
+        sent = permute(product(slab, high, low, 0), lambda y, x, z, c, g: (y, x, z, 1 - c, g))
+        chip = product(slab, high, low, 1) + sent
+        return chip.reshape(NY * NX, columns // (NY * NX), half)
 
-        def product(rows):
-            return lax.dot_general(
-                slab, rows, (((0,), (1,)), ((), ())), precision=lax.Precision.HIGH, preferred_element_type=jnp.float32
-            )
-
-        sent = permute(product(other), lambda y, x, z, c, g: (y, x, z, 1 - c, g))
-        chip = product(mine) + sent
-        chip = chip.reshape(NY * NX, columns // (NY * NX), half)
+    def over_plane(chip):
         spread = lax.all_to_all(chip, "blk", 0, 0, tiled=True, axis_index_groups=plane_groups())
         return jnp.sum(spread, axis=0)
 
-    parts = jnp.stack([reduced(slot, slab) for slot, slab in enumerate((own, one, two, three))])
+    part_own = over_plane(on_chip(0, own))
+    one, two, part_own = lax.optimization_barrier((one, two, part_own))
+    relayed = jnp.where((group == 0) | (group == 3), one, two)
+    three = permute(relayed, lambda y, x, z, c, g: (y, x, z, c, RELAY[g]))
+    part_pair = over_plane(jnp.concatenate([on_chip(1, one), on_chip(2, two)], axis=1))
+    part_three = over_plane(on_chip(3, three))
+
+    parts = jnp.concatenate([part_own, part_pair, part_three], axis=0)
     parts = parts.reshape(IRREPS, NZ, NC * column_width, half)
     kept = lax.dynamic_index_in_dim(parts, z_part, 1, keepdims=False)
     sent = lax.dynamic_index_in_dim(parts, 1 - z_part, 1, keepdims=False)

time: 131 us -> 111 us (0.85)
  matrix products: 21.7 us -> 0 us
  Pallas kernels: 0 us -> 15 us
  waiting for transfers between devices: 20.6 us -> 33.6 us
  other arithmetic: 13.2 us -> 4.42 us
  local copies, waits for them, and re-layouts: 21.2 us -> 13.4 us
  between operations: 7.66 us -> 0.4 us
  starting transfers between devices: 45.6 us -> 43.5 us
    dot_general x8 -> x0, matrix products: 21.7 us -> none  [product(): lax.dot_general(slab, rows, (((0,), (1,)), ((), ())), precision=lax.Preci...]
    dynamic_slice x3 -> x0, local copies, waits for them, and re-layouts: 20.5 us -> none  [the longest x1 19.9 us: reduced(): chosen = lax.dynamic_index_in_dim(amplitudes, irrep, 1, keepdims=False)]
    pallas_call x0 -> x9, Pallas kernels: none -> 15 us  [the longest x8 7.62 us: product(): pl.pallas_call(functools.partial(product_kernel, part), out_shape=jax.Sha...]
    ppermute x9, waiting for transfers between devices: 3.61 us -> 17.1 us  [permute(): return lax.ppermute(value, AXES, pairs)]
    unnamed x14 -> x42, local copies, waits for them, and re-layouts: 0.03 us -> 12 us
    mul x4 -> x0, other arithmetic: 9.01 us -> none  [reduced(): chosen * lax.dynamic_index_in_dim(row_valid, irrep, 0, keepdims=True)]
    ppermute x9, starting transfers between devices: 25 us -> 23.3 us  [permute(): return lax.ppermute(value, AXES, pairs)]
    add x0 -> x4, other arithmetic: none -> 1.55 us  [on_chip(): chip = product(slab, high, low, 1) + sent]
  transfers between devices with their start and end apart: 13 -> 12, of which waited for: 6 -> 8; matrix products, arithmetic and copies ran while one was open for 42% -> 3% of each run, Pallas kernels for 0% -> 14%
where the time goes in v2:
time: 111 us; the launch traced here: 110 us
  starting transfers between devices  43.5 us (39%)
  waiting for transfers between devices  33.6 us (30%)
  Pallas kernels  15 us (14%)
  local copies, waits for them, and re-layouts  13.4 us (12%)
  other arithmetic  4.42 us (4%)
    ppermute x9, starting transfers between devices, permute(): return lax.ppermute(value, AXES, pairs)  23.3 us
    all_to_all x3, starting transfers between devices, over_plane(): lax.all_to_all(chip, 'blk', 0, 0, tiled=True, axis_index_groups=plane_gro...  20.3 us
    ppermute x9, waiting for transfers between devices, permute(): return lax.ppermute(value, AXES, pairs)  17.1 us
    all_to_all x3, waiting for transfers between devices, over_plane(): lax.all_to_all(chip, 'blk', 0, 0, tiled=True, axis_index_groups=plane_gro...  16.4 us
    unnamed x42, local copies, waits for them, and re-layouts  12 us
    pallas_call x8, Pallas kernels, product(): pl.pallas_call(functools.partial(product_kernel, part), out_shape=jax.Sha...  7.62 us
    pallas_call x1, Pallas kernels, split_rows(): pl.pallas_call(functools.partial(split_kernel, rows, slot_width), out_sha...  7.34 us
  transfers between devices with their start and end apart: 12, of which 8 were waited for; matrix products, arithmetic and copies ran while one was open for 3% of the time, Pallas kernels for 14%

profile of v2, /device:TPU:1, one launch (start us, length us, event | category | flops | bytes accessed | tf_op | source)
XLA Modules:
  0.0 110.3 jit_solution(2711821267102175220)
XLA Ops:
  0.0 2.5 %collective-permute-start = (f32[1024,256]{1,0:T(8,128)}, f32[1024,256]{1,0:T(8,128)S(1)}, u32[]{:S(2)}, u32[]{:S(2)}) collective-permute-start(f32[1024,256]{1,0:T(8,128)} %bitcast.28), channel_id=1, source_target_pairs={{0,1},{1,0},{2,3},{3,2},{4,5},{5,4},{6,7},{7,6},{8,9},{9,8},{10,11... | collective-permute-start | bytes 3145736 | tf_op jit(solution)/shard_map/ppermute | solution.py:35
  2.5 3.0 %collective-permute-start.1 = (f32[1024,256]{1,0:T(8,128)}, f32[1024,256]{1,0:T(8,128)S(1)}, u32[]{:S(2)}, u32[]{:S(2)}) collective-permute-start(f32[1024,256]{1,0:T(8,128)} %bitcast.29), channel_id=1, source_target_pairs={{0,2},{1,3},{2,0},{3,1},{4,6},{5,7},{6,4},{7,5},{8,10},{9,11},{10,... | collective-permute-start | bytes 3145736 | tf_op jit(solution)/shard_map/ppermute | solution.py:35
  5.4 0.7 concatenate.12.scalars
  6.2 3.4 %copy-done = f32[512,4,1024]{2,1,0:T(4,128)S(1)} copy-done((f32[512,4,1024]{2,1,0:T(4,128)S(1)}, f32[512,4,1024]{2,1,0:T(4,128)}, u32[]{:S(2)}) %copy-start) | copy-done | bytes 8388632
  9.6 7.3 %split_rows.1 = (bf16[2,256,1024]{2,1,0:T(8,128)(2,1)S(1)}, bf16[2,256,1024]{2,1,0:T(8,128)(2,1)S(1)}, bf16[2,256,1024]{2,1,0:T(8,128)(2,1)S(1)}, bf16[2,256,102...) custom-call(s32[11]{0:T(128)S(1)} %concatenate.12.scalars, ...), custom_call_target="tpu_custom_call" | custom-call | bytes 16777216 | tf_op jit(solution)/shard_map/split_rows/pallas_call | solution.py:82
  16.9 0.0 copy-start.2
  16.9 0.0 copy-start.4
  16.9 0.0 copy-start.7
  17.0 0.0 copy-start.10
  17.0 0.0 copy-start.13
  17.0 0.0 copy-start.16
  17.0 0.0 copy-done.1
  17.0 0.7 product.9
  17.7 1.3 %collective-permute-start.2 = (f32[256,256]{1,0:T(8,128)S(1)}, f32[256,256]{1,0:T(8,128)S(1)}, u32[]{:S(2)}, u32[]{:S(2)}) collective-permute-start(f32[256,256]{1,0:T(8,128)S(1)} %product.9), channel_id=1, source_target_pairs={{0,4},{1,5},{2,6},{3,7},{4,0},{5,1},{6,2},{7,3},{8,12},{9,13},{10,... | collective-permute-start | bytes 786440 | tf_op jit(solution)/shard_map/ppermute | solution.py:35
  19.0 0.7 product.8
  19.7 0.0 copy-done.2
  19.7 0.5 collective-permute-done.2
  20.2 0.0 copy-done.4
  20.2 0.7 add.73
  20.9 0.0 copy-done.13
  20.9 6.8 %all-to-all-start = ((f32[16,16,256]{2,1,0:T(8,128)}), f32[16,16,256]{2,1,0:T(8,128)S(1)}, u32[]{:S(2)}, u32[]{:S(2)}) async-start(f32[16,16,256]{2,1,0:T(8,128)} %bitcast.7), calls=%async_computation | async-start | bytes 524288 | tf_op jit(solution)/shard_map/all_to_all | solution.py:146
  27.7 8.1 %all-to-all-done = f32[16,16,256]{2,1,0:T(8,128)S(1)} async-done(((f32[16,16,256]{2,1,0:T(8,128)}), f32[16,16,256]{2,1,0:T(8,128)S(1)}, u32[]{:S(2)}, u32[]{:S(2)}) %all-to-all-start) | async-done | bytes 262176 | tf_op jit(solution)/shard_map/all_to_all | solution.py:146
  35.8 0.0 copy-start.15
  35.8 0.0 copy-start.9
  35.9 0.0 copy-start.12
  35.9 10.1 %collective-permute-done.slab = f32[1024,256]{1,0:T(8,128)S(1)} collective-permute-done((f32[1024,256]{1,0:T(8,128)}, f32[1024,256]{1,0:T(8,128)S(1)}, u32[]{:S(2)}, u32[]{:S(2)}) %collective-permute-start) | collective-permute-done | bytes 1048608 | tf_op jit(solution)/shard_map/ppermute | solution.py:35
  45.9 1.2 %collective-permute-done.1.slab = f32[1024,256]{1,0:T(8,128)S(1)} collective-permute-done((f32[1024,256]{1,0:T(8,128)}, f32[1024,256]{1,0:T(8,128)S(1)}, u32[]{:S(2)}, u32[]{:S(2)}) %collective-permute-start.1) | collective-permute-done | bytes 1048608 | tf_op jit(solution)/shard_map/ppermute | solution.py:35
  47.1 1.1 %broadcast_select_fusion = f32[1024,256]{1,0:T(8,128)} fusion(f32[1024,256]{1,0:T(8,128)S(1)} %collective-permute-done.slab, f32[1024,256]{1,0:T(8,128)S(1)} %collective-permute-done.1.slab, pred[]{:T(512)S(6)} %or.3), kind=kLoop, calls=%fused_computation.2 | loop fusion | flops 262144 | bytes 3145729 | tf_op jit(solution)/shard_map/jit(_where)/select_n | solution.py:151
  48.3 3.0 %collective-permute-start.5 = (f32[1024,256]{1,0:T(8,128)}, f32[1024,256]{1,0:T(8,128)}, u32[]{:S(2)}, u32[]{:S(2)}) collective-permute-start(f32[1024,256]{1,0:T(8,128)} %broadcast_select_fusion), channel_id=1, source_target_pairs={{0,2},{1,0},{2,3},{3,1},{4,6},{5,4},{6,7},{7,5},{8,10},{9,8},{10,1... | collective-permute-start | bytes 3145736 | tf_op jit(solution)/shard_map/ppermute | solution.py:35
  51.3 1.2 %copy-done.14 = bf16[2,256,1024]{2,1,0:T(8,128)(2,1)S(1)} copy-done((bf16[2,256,1024]{2,1,0:T(8,128)(2,1)S(1)}, bf16[2,256,1024]{2,1,0:T(8,128)(2,1)}, u32[]{:S(2)}) %copy-start.14) | copy-done | bytes 1048600
  52.5 1.2 %copy-done.17 = bf16[2,256,1024]{2,1,0:T(8,128)(2,1)S(1)} copy-done((bf16[2,256,1024]{2,1,0:T(8,128)(2,1)S(1)}, bf16[2,256,1024]{2,1,0:T(8,128)(2,1)}, u32[]{:S(2)}) %copy-start.17) | copy-done | bytes 1048600
  53.7 0.6 product.11
  54.4 2.3 %collective-permute-start.3 = (f32[256,256]{1,0:T(8,128)S(1)}, f32[256,256]{1,0:T(8,128)S(1)}, u32[]{:S(2)}, u32[]{:S(2)}) collective-permute-start(f32[256,256]{1,0:T(8,128)S(1)} %product.11), channel_id=1, source_target_pairs={{0,4},{1,5},{2,6},{3,7},{4,0},{5,1},{6,2},{7,3},{8,12},{9,13},{10,... | collective-permute-start | bytes 786440 | tf_op jit(solution)/shard_map/ppermute | solution.py:35
  56.6 1.2 %copy-done.8 = bf16[2,256,1024]{2,1,0:T(8,128)(2,1)S(1)} copy-done((bf16[2,256,1024]{2,1,0:T(8,128)(2,1)S(1)}, bf16[2,256,1024]{2,1,0:T(8,128)(2,1)}, u32[]{:S(2)}) %copy-start.8) | copy-done | bytes 1048600
  57.9 1.2 %copy-done.11 = bf16[2,256,1024]{2,1,0:T(8,128)(2,1)S(1)} copy-done((bf16[2,256,1024]{2,1,0:T(8,128)(2,1)S(1)}, bf16[2,256,1024]{2,1,0:T(8,128)(2,1)}, u32[]{:S(2)}) %copy-start.11) | copy-done | bytes 1048600
  59.1 0.6 product.13
  59.7 0.1 collective-permute-start.4
  59.9 1.2 %copy-done.18 = bf16[2,256,1024]{2,1,0:T(8,128)(2,1)S(1)} copy-done((bf16[2,256,1024]{2,1,0:T(8,128)(2,1)S(1)}, bf16[2,256,1024]{2,1,0:T(8,128)(2,1)}, u32[]{:S(2)}) %copy-start.18) | copy-done | bytes 1048600
  61.1 0.6 product.10
  61.7 0.0 copy-start.19
  61.8 0.0 copy-start.20
  61.8 0.6 product.12
  62.4 0.0 collective-permute-done.3
  62.5 0.0 collective-permute-done.4
  62.5 0.9 pad_maximum_fusion
  63.4 6.8 %all-to-all-start.1 = ((f32[16,32,256]{2,1,0:T(8,128)}), f32[16,32,256]{2,1,0:T(8,128)S(1)}, u32[]{:S(2)}, u32[]{:S(2)}) async-start(f32[16,32,256]{2,1,0:T(8,128)} %pad_maximum_fusion), calls=%async_computation.1 | async-start | bytes 1048576 | tf_op jit(solution)/shard_map/all_to_all | solution.py:146
  70.1 2.6 %collective-permute-done.5.slab = f32[1024,256]{1,0:T(8,128)} collective-permute-done((f32[1024,256]{1,0:T(8,128)}, f32[1024,256]{1,0:T(8,128)}, u32[]{:S(2)}, u32[]{:S(2)}) %collective-permute-start.5) | collective-permute-done | bytes 1048608 | tf_op jit(solution)/shard_map/ppermute | solution.py:35
  72.8 1.2 %copy-done.5 = bf16[2,256,1024]{2,1,0:T(8,128)(2,1)S(1)} copy-done((bf16[2,256,1024]{2,1,0:T(8,128)(2,1)S(1)}, bf16[2,256,1024]{2,1,0:T(8,128)(2,1)}, u32[]{:S(2)}) %copy-start.5) | copy-done | bytes 1048600
  74.0 1.9 %product.15 = f32[256,256]{1,0:T(8,128)S(1)} custom-call(f32[1024,256]{1,0:T(8,128)} %collective-permute-done.5.slab, bf16[2,256,1024]{2,1,0:T(8,128)(2,1)S(1)} %copy-done.3, bf16[2,256,1024]{2,1,0:T(8,128)(2,1)S(1)} %copy-done.5), custom_call_target="tpu_custom_call" | custom-call | flops 402653184 | bytes 2097152 | tf_op jit(solution)/shard_map/product/pallas_call | solution.py:109
  75.9 3.8 %collective-permute-start.6 = (f32[256,256]{1,0:T(8,128)S(1)}, f32[256,256]{1,0:T(8,128)S(1)}, u32[]{:S(2)}, u32[]{:S(2)}) collective-permute-start(f32[256,256]{1,0:T(8,128)S(1)} %product.15), channel_id=1, source_target_pairs={{0,4},{1,5},{2,6},{3,7},{4,0},{5,1},{6,2},{7,3},{8,12},{9,13},{10,... | collective-permute-start | bytes 786440 | tf_op jit(solution)/shard_map/ppermute | solution.py:35
  79.7 1.2 %copy-done.6 = bf16[2,256,1024]{2,1,0:T(8,128)(2,1)S(1)} copy-done((bf16[2,256,1024]{2,1,0:T(8,128)(2,1)S(1)}, bf16[2,256,1024]{2,1,0:T(8,128)(2,1)}, u32[]{:S(2)}) %copy-start.6) | copy-done | bytes 1048600
  80.9 1.9 %product.14 = f32[256,256]{1,0:T(8,128)S(1)} custom-call(f32[1024,256]{1,0:T(8,128)} %collective-permute-done.5.slab, bf16[2,256,1024]{2,1,0:T(8,128)(2,1)S(1)} %copy-done.3, bf16[2,256,1024]{2,1,0:T(8,128)(2,1)S(1)} %copy-done.6), custom_call_target="tpu_custom_call" | custom-call | flops 402653184 | bytes 2097152 | tf_op jit(solution)/shard_map/product/pallas_call | solution.py:109
  82.8 0.0 collective-permute-done.6
  82.8 0.7 add.76
  83.5 0.0 all-to-all-done.1
  83.5 6.8 %all-to-all-start.2 = ((f32[16,16,256]{2,1,0:T(8,128)}), f32[16,16,256]{2,1,0:T(8,128)S(1)}, u32[]{:S(2)}, u32[]{:S(2)}) async-start(f32[16,16,256]{2,1,0:T(8,128)} %bitcast.10), calls=%async_computation.2 | async-start | bytes 524288 | tf_op jit(solution)/shard_map/all_to_all | solution.py:146
  90.4 0.1 and_convert_fusion
  90.5 8.3 %all-to-all-done.2 = f32[16,16,256]{2,1,0:T(8,128)S(1)} async-done(((f32[16,16,256]{2,1,0:T(8,128)}), f32[16,16,256]{2,1,0:T(8,128)S(1)}, u32[]{:S(2)}, u32[]{:S(2)}) %all-to-all-start.2) | async-done | bytes 262176 | tf_op jit(solution)/shard_map/all_to_all | solution.py:146
  98.8 4.8 %collective-permute-start.7 = (f32[4,8,256]{2,1,0:T(8,128)S(1)}, f32[4,8,256]{2,1,0:T(8,128)S(1)}, u32[]{:S(2)}, u32[]{:S(2)}) collective-permute-start(f32[4,8,256]{2,1,0:T(8,128)S(1)} %dynamic-slice_bitcast_fusion), channel_id=1, source_target_pairs={{0,8},{1,9},{2,10},{3,11},{4,12},{5,13},{6,14},{7,15},{8,0},{9,1},... | collective-permute-start | bytes 98312 | tf_op jit(solution)/shard_map/ppermute | solution.py:35
  103.7 1.9 %collective-permute-done.7 = f32[4,8,256]{2,1,0:T(8,128)S(1)} collective-permute-done((f32[4,8,256]{2,1,0:T(8,128)S(1)}, f32[4,8,256]{2,1,0:T(8,128)S(1)}, u32[]{:S(2)}, u32[]{:S(2)}) %collective-permute-start.7) | collective-permute-done | bytes 32800 | tf_op jit(solution)/shard_map/ppermute | solution.py:35
  105.7 2.5 %collective-permute-start.8 = (f32[4,4,256]{2,1,0:T(4,128)S(1)}, f32[4,4,256]{2,1,0:T(4,128)S(1)}, u32[]{:S(2)}, u32[]{:S(2)}) collective-permute-start(f32[4,4,256]{2,1,0:T(4,128)S(1)} %bitcast.37), channel_id=1, source_target_pairs={{0,4},{1,5},{2,6},{3,7},{4,0},{5,1},{6,2},{7,3},{8,12},{9,13},{10,... | collective-permute-start | bytes 49160 | tf_op jit(solution)/shard_map/ppermute | solution.py:35
  108.1 0.8 collective-permute-done.8
  109.0 0.6 gather_fusion
  109.6 0.7 multiply_bitcast_fusion
  (35 shorter events, 0.3 us)
Async XLA Ops:
  0.0 45.9 %collective-permute-start = (f32[1024,256]{1,0:T(8,128)}, f32[1024,256]{1,0:T(8,128)S(1)}, u32[]{:S(2)}, u32[]{:S(2)}) collective-permute-start(f32[1024,256]{1,0:T(8,128)} %bitcast.28), channel_id=1, source_target_pairs={{0,1},{1,0},{2,3},{3,2},{4,5},{5,4},{6,7},{7,6},{8,9},{9,8},{10,11... | collective-permute-start | bytes 3145736 | tf_op jit(solution)/shard_map/ppermute | solution.py:35
  2.5 44.7 %collective-permute-start.1 = (f32[1024,256]{1,0:T(8,128)}, f32[1024,256]{1,0:T(8,128)S(1)}, u32[]{:S(2)}, u32[]{:S(2)}) collective-permute-start(f32[1024,256]{1,0:T(8,128)} %bitcast.29), channel_id=1, source_target_pairs={{0,2},{1,3},{2,0},{3,1},{4,6},{5,7},{6,4},{7,5},{8,10},{9,11},{10,... | collective-permute-start | bytes 3145736 | tf_op jit(solution)/shard_map/ppermute | solution.py:35
  6.2 3.4 %copy-start = (f32[512,4,1024]{2,1,0:T(4,128)S(1)}, f32[512,4,1024]{2,1,0:T(4,128)}, u32[]{:S(2)}) copy-start(f32[512,4,1024]{2,1,0:T(4,128)} %param.4) | copy-start | bytes 25165828
  9.6 7.4 %copy-start.1 = (f32[1,1024,256]{2,1,0:T(8,128)S(1)}, f32[1,1024,256]{2,1,0:T(8,128)}, u32[]{:S(2)}) copy-start(f32[1,1024,256]{2,1,0:T(8,128)} %param.5) | copy-start | bytes 3145732
  16.9 2.7 %copy-start.2 = (bf16[2,256,1024]{2,1,0:T(8,128)(2,1)}, bf16[2,256,1024]{2,1,0:T(8,128)(2,1)S(1)}, u32[]{:S(2)}) copy-start(bf16[2,256,1024]{2,1,0:T(8,128)(2,1)S(1)} %get-tuple-element.25.high) | copy-start | bytes 3145732
  16.9 3.2 %copy-start.4 = (bf16[2,256,1024]{2,1,0:T(8,128)(2,1)}, bf16[2,256,1024]{2,1,0:T(8,128)(2,1)S(1)}, u32[]{:S(2)}) copy-start(bf16[2,256,1024]{2,1,0:T(8,128)(2,1)S(1)} %get-tuple-element.26.low) | copy-start | bytes 3145732
  16.9 4.0 %copy-start.7 = (bf16[2,256,1024]{2,1,0:T(8,128)(2,1)}, bf16[2,256,1024]{2,1,0:T(8,128)(2,1)S(1)}, u32[]{:S(2)}) copy-start(bf16[2,256,1024]{2,1,0:T(8,128)(2,1)S(1)} %get-tuple-element.23.high) | copy-start | bytes 3145732
  17.0 3.9 %copy-start.10 = (bf16[2,256,1024]{2,1,0:T(8,128)(2,1)}, bf16[2,256,1024]{2,1,0:T(8,128)(2,1)S(1)}, u32[]{:S(2)}) copy-start(bf16[2,256,1024]{2,1,0:T(8,128)(2,1)S(1)} %get-tuple-element.24.low) | copy-start | bytes 3145732
  17.0 3.9 %copy-start.13 = (bf16[2,256,1024]{2,1,0:T(8,128)(2,1)}, bf16[2,256,1024]{2,1,0:T(8,128)(2,1)S(1)}, u32[]{:S(2)}) copy-start(bf16[2,256,1024]{2,1,0:T(8,128)(2,1)S(1)} %get-tuple-element.20.high) | copy-start | bytes 3145732
  17.0 3.9 %copy-start.16 = (bf16[2,256,1024]{2,1,0:T(8,128)(2,1)}, bf16[2,256,1024]{2,1,0:T(8,128)(2,1)S(1)}, u32[]{:S(2)}) copy-start(bf16[2,256,1024]{2,1,0:T(8,128)(2,1)S(1)} %get-tuple-element.21.low) | copy-start | bytes 3145732
  17.7 2.5 %collective-permute-start.2 = (f32[256,256]{1,0:T(8,128)S(1)}, f32[256,256]{1,0:T(8,128)S(1)}, u32[]{:S(2)}, u32[]{:S(2)}) collective-permute-start(f32[256,256]{1,0:T(8,128)S(1)} %product.9), channel_id=1, source_target_pairs={{0,4},{1,5},{2,6},{3,7},{4,0},{5,1},{6,2},{7,3},{8,12},{9,13},{10,... | collective-permute-start | bytes 786440 | tf_op jit(solution)/shard_map/ppermute | solution.py:35
  20.9 14.9 %all-to-all-start = ((f32[16,16,256]{2,1,0:T(8,128)}), f32[16,16,256]{2,1,0:T(8,128)S(1)}, u32[]{:S(2)}, u32[]{:S(2)}) async-start(f32[16,16,256]{2,1,0:T(8,128)} %bitcast.7), calls=%async_computation | async-start | bytes 524288 | tf_op jit(solution)/shard_map/all_to_all | solution.py:146
  35.8 24.0 %copy-start.15 = (bf16[2,256,1024]{2,1,0:T(8,128)(2,1)S(1)}, bf16[2,256,1024]{2,1,0:T(8,128)(2,1)}, u32[]{:S(2)}) copy-start(bf16[2,256,1024]{2,1,0:T(8,128)(2,1)} %copy-done.13) | copy-start | bytes 3145732
  35.8 25.9 %copy-start.9 = (bf16[2,256,1024]{2,1,0:T(8,128)(2,1)S(1)}, bf16[2,256,1024]{2,1,0:T(8,128)(2,1)}, u32[]{:S(2)}) copy-start(bf16[2,256,1024]{2,1,0:T(8,128)(2,1)} %copy-done.7) | copy-start | bytes 3145732
  35.9 25.9 %copy-start.12 = (bf16[2,256,1024]{2,1,0:T(8,128)(2,1)S(1)}, bf16[2,256,1024]{2,1,0:T(8,128)(2,1)}, u32[]{:S(2)}) copy-start(bf16[2,256,1024]{2,1,0:T(8,128)(2,1)} %copy-done.10) | copy-start | bytes 3145732
  48.3 24.5 %collective-permute-start.5 = (f32[1024,256]{1,0:T(8,128)}, f32[1024,256]{1,0:T(8,128)}, u32[]{:S(2)}, u32[]{:S(2)}) collective-permute-start(f32[1024,256]{1,0:T(8,128)} %broadcast_select_fusion), channel_id=1, source_target_pairs={{0,2},{1,0},{2,3},{3,1},{4,6},{5,4},{6,7},{7,5},{8,10},{9,8},{10,1... | collective-permute-start | bytes 3145736 | tf_op jit(solution)/shard_map/ppermute | solution.py:35
  51.3 1.2 %copy-start.14 = (bf16[2,256,1024]{2,1,0:T(8,128)(2,1)S(1)}, bf16[2,256,1024]{2,1,0:T(8,128)(2,1)}, u32[]{:S(2)}) copy-start(bf16[2,256,1024]{2,1,0:T(8,128)(2,1)} %copy-done.13) | copy-start | bytes 3145732
  52.5 1.2 %copy-start.17 = (bf16[2,256,1024]{2,1,0:T(8,128)(2,1)S(1)}, bf16[2,256,1024]{2,1,0:T(8,128)(2,1)}, u32[]{:S(2)}) copy-start(bf16[2,256,1024]{2,1,0:T(8,128)(2,1)} %copy-done.16) | copy-start | bytes 3145732
  53.7 19.1 %copy-start.3 = (bf16[2,256,1024]{2,1,0:T(8,128)(2,1)S(1)}, bf16[2,256,1024]{2,1,0:T(8,128)(2,1)}, u32[]{:S(2)}) copy-start(bf16[2,256,1024]{2,1,0:T(8,128)(2,1)} %copy-done.2) | copy-start | bytes 3145732
  54.4 8.1 %collective-permute-start.3 = (f32[256,256]{1,0:T(8,128)S(1)}, f32[256,256]{1,0:T(8,128)S(1)}, u32[]{:S(2)}, u32[]{:S(2)}) collective-permute-start(f32[256,256]{1,0:T(8,128)S(1)} %product.11), channel_id=1, source_target_pairs={{0,4},{1,5},{2,6},{3,7},{4,0},{5,1},{6,2},{7,3},{8,12},{9,13},{10,... | collective-permute-start | bytes 786440 | tf_op jit(solution)/shard_map/ppermute | solution.py:35
  56.6 1.2 %copy-start.8 = (bf16[2,256,1024]{2,1,0:T(8,128)(2,1)S(1)}, bf16[2,256,1024]{2,1,0:T(8,128)(2,1)}, u32[]{:S(2)}) copy-start(bf16[2,256,1024]{2,1,0:T(8,128)(2,1)} %copy-done.7) | copy-start | bytes 3145732
  57.9 1.2 %copy-start.11 = (bf16[2,256,1024]{2,1,0:T(8,128)(2,1)S(1)}, bf16[2,256,1024]{2,1,0:T(8,128)(2,1)}, u32[]{:S(2)}) copy-start(bf16[2,256,1024]{2,1,0:T(8,128)(2,1)} %copy-done.10) | copy-start | bytes 3145732
  59.7 2.7 %collective-permute-start.4 = (f32[256,256]{1,0:T(8,128)S(1)}, f32[256,256]{1,0:T(8,128)S(1)}, u32[]{:S(2)}, u32[]{:S(2)}) collective-permute-start(f32[256,256]{1,0:T(8,128)S(1)} %product.13), channel_id=1, source_target_pairs={{0,4},{1,5},{2,6},{3,7},{4,0},{5,1},{6,2},{7,3},{8,12},{9,13},{10,... | collective-permute-start | bytes 786440 | tf_op jit(solution)/shard_map/ppermute | solution.py:35
  59.8 1.2 %copy-start.18 = (bf16[2,256,1024]{2,1,0:T(8,128)(2,1)S(1)}, bf16[2,256,1024]{2,1,0:T(8,128)(2,1)}, u32[]{:S(2)}) copy-start(bf16[2,256,1024]{2,1,0:T(8,128)(2,1)} %copy-done.16) | copy-start | bytes 3145732
  61.7 28.6 %copy-start.19 = (s32[4]{0:T(128)S(1)}, s32[4]{0:T(128)}, u32[]{:S(2)}) copy-start(s32[4]{0:T(128)} %param.6) | copy-start | bytes 52
  61.8 41.9 %copy-start.20 = (s32[4]{0:T(128)S(1)}, s32[4]{0:T(128)}, u32[]{:S(2)}) copy-start(s32[4]{0:T(128)} %param.7) | copy-start | bytes 52
  63.4 20.1 %all-to-all-start.1 = ((f32[16,32,256]{2,1,0:T(8,128)}), f32[16,32,256]{2,1,0:T(8,128)S(1)}, u32[]{:S(2)}, u32[]{:S(2)}) async-start(f32[16,32,256]{2,1,0:T(8,128)} %pad_maximum_fusion), calls=%async_computation.1 | async-start | bytes 1048576 | tf_op jit(solution)/shard_map/all_to_all | solution.py:146
  72.8 1.2 %copy-start.5 = (bf16[2,256,1024]{2,1,0:T(8,128)(2,1)S(1)}, bf16[2,256,1024]{2,1,0:T(8,128)(2,1)}, u32[]{:S(2)}) copy-start(bf16[2,256,1024]{2,1,0:T(8,128)(2,1)} %copy-done.4) | copy-start | bytes 3145732
  75.9 6.9 %collective-permute-start.6 = (f32[256,256]{1,0:T(8,128)S(1)}, f32[256,256]{1,0:T(8,128)S(1)}, u32[]{:S(2)}, u32[]{:S(2)}) collective-permute-start(f32[256,256]{1,0:T(8,128)S(1)} %product.15), channel_id=1, source_target_pairs={{0,4},{1,5},{2,6},{3,7},{4,0},{5,1},{6,2},{7,3},{8,12},{9,13},{10,... | collective-permute-start | bytes 786440 | tf_op jit(solution)/shard_map/ppermute | solution.py:35
  79.7 1.2 %copy-start.6 = (bf16[2,256,1024]{2,1,0:T(8,128)(2,1)S(1)}, bf16[2,256,1024]{2,1,0:T(8,128)(2,1)}, u32[]{:S(2)}) copy-start(bf16[2,256,1024]{2,1,0:T(8,128)(2,1)} %copy-done.4) | copy-start | bytes 3145732
  83.5 15.3 %all-to-all-start.2 = ((f32[16,16,256]{2,1,0:T(8,128)}), f32[16,16,256]{2,1,0:T(8,128)S(1)}, u32[]{:S(2)}, u32[]{:S(2)}) async-start(f32[16,16,256]{2,1,0:T(8,128)} %bitcast.10), calls=%async_computation.2 | async-start | bytes 524288 | tf_op jit(solution)/shard_map/all_to_all | solution.py:146
  98.8 6.8 %collective-permute-start.7 = (f32[4,8,256]{2,1,0:T(8,128)S(1)}, f32[4,8,256]{2,1,0:T(8,128)S(1)}, u32[]{:S(2)}, u32[]{:S(2)}) collective-permute-start(f32[4,8,256]{2,1,0:T(8,128)S(1)} %dynamic-slice_bitcast_fusion), channel_id=1, source_target_pairs={{0,8},{1,9},{2,10},{3,11},{4,12},{5,13},{6,14},{7,15},{8,0},{9,1},... | collective-permute-start | bytes 98312 | tf_op jit(solution)/shard_map/ppermute | solution.py:35
  105.7 3.3 %collective-permute-start.8 = (f32[4,4,256]{2,1,0:T(4,128)S(1)}, f32[4,4,256]{2,1,0:T(4,128)S(1)}, u32[]{:S(2)}, u32[]{:S(2)}) collective-permute-start(f32[4,4,256]{2,1,0:T(4,128)S(1)} %bitcast.37), channel_id=1, source_target_pairs={{0,4},{1,5},{2,6},{3,7},{4,0},{5,1},{6,2},{7,3},{8,12},{9,13},{10,... | collective-permute-start | bytes 49160 | tf_op jit(solution)/shard_map/ppermute | solution.py:35

commit v3 on v2

v3 whole, which is shorter than its diff:
```python
import functools

import jax
import jax.numpy as jnp
from jax import lax
from jax.experimental import pallas as pl
from jax.experimental.pallas import tpu as pltpu
from jax.sharding import PartitionSpec as P


BLOCK = 256
IRREPS = 4
LANES = 128
NY, NX, NZ, NC, NG = 4, 4, 2, 2, 4
AXES = ("blk", "grp")


def blk_index(y, x, z, c):
    return ((y * NX + x) * NZ + z) * NC + c


def every_device():
    for y in range(NY):
        for x in range(NX):
            for z in range(NZ):
                for c in range(NC):
                    for g in range(NG):
                        yield y, x, z, c, g


def permute(value, target):
    pairs = []
    for place in every_device():
        there = target(*place)
        if there is None:
            continue
        pairs.append((blk_index(*place[:4]) * NG + place[4], blk_index(*there[:4]) * NG + there[4]))
    return lax.ppermute(value, AXES, pairs)


def plane_groups():
    return [[blk_index(y, x, z, c) for y in range(NY) for x in range(NX)] for z in range(NZ) for c in range(NC)]


def plane_sum(chip):
    spread = lax.all_to_all(chip, "blk", 0, 0, tiled=True, axis_index_groups=plane_groups())
    return jnp.sum(spread, axis=0)


def pair_swap(y, x, z, c, g):
    return y, x, z, c, g ^ 1


def middle_swap(y, x, z, c, g):
    return (y, x, z, c, 3 - g) if g in (1, 2) else None


def outward(y, x, z, c, g):
    return (y, x, z, c, {1: 0, 2: 3}[g]) if g in (1, 2) else None


def split_kernel(rows, slot_width, scalars, source, *outputs):
    tiles = slot_width // LANES
    group, position = scalars[2 * IRREPS], scalars[2 * IRREPS + 1]
    lane = lax.broadcasted_iota(jnp.int32, (rows, LANES), 1)
    for slot in range(IRREPS):
        irrep = jnp.int32(0)
        for h in range(IRREPS):
            irrep = jnp.where(scalars[h] == (group ^ slot), h, irrep)
        size = scalars[IRREPS + irrep]
        high, low = outputs[2 * slot], outputs[2 * slot + 1]
        for tile in range(tiles):
            first = position * slot_width + tile * LANES
            limit = jnp.where(first // BLOCK < size, size - first % BLOCK, 0)
            value = source[pl.ds(tile * IRREPS + irrep, rows, stride=tiles * IRREPS), :]
            value = jnp.where(lane < limit, value, 0.0)
            rounded = value.astype(jnp.bfloat16)
            place = slice(tile * LANES, (tile + 1) * LANES)
            high[:, place] = rounded
            low[:, place] = (value - rounded.astype(jnp.float32)).astype(jnp.bfloat16)


def split_rows(amplitudes, scalars):
    pairs, _, slot_width = amplitudes.shape
    rows = 64
    view = amplitudes.reshape(pairs, IRREPS, slot_width // LANES, LANES).transpose(0, 2, 1, 3).reshape(-1, LANES)
    return pl.pallas_call(
        functools.partial(split_kernel, rows, slot_width),
        out_shape=[jax.ShapeDtypeStruct((pairs, slot_width), jnp.bfloat16)] * (2 * IRREPS),
        grid_spec=pltpu.PrefetchScalarGridSpec(
            num_scalar_prefetch=1,
            grid=(pairs // rows,),
            in_specs=[pl.BlockSpec((rows * IRREPS * slot_width // LANES, LANES), lambda i, scalars: (i, 0))],
            out_specs=[pl.BlockSpec((rows, slot_width), lambda i, scalars: (i, 0))] * (2 * IRREPS),
        ),
        compiler_params=pltpu.CompilerParams(vmem_limit_bytes=16 << 20),
        cost_estimate=pl.CostEstimate(flops=0, bytes_accessed=8 * pairs * IRREPS * slot_width, transcendentals=0),
        name="split_rows",
    )(scalars, view)


def product_kernel(alternatives, parts, scalars, *refs):
    slabs, (high, low, out, high_here, low_here, sems) = refs[: alternatives * parts], refs[alternatives * parts :]
    depth = slabs[0].shape[0]
    copies = []
    for part in range(parts):
        place = pl.ds(part * depth, depth)
        for k, (there, here) in enumerate(((high, high_here), (low, low_here))):
            copies.append(pltpu.make_async_copy(there.at[:, place], here.at[:, place], sems.at[part, k]))
            copies[-1].start()
    group = scalars[2 * IRREPS]
    ends = (group == 0) | (group == NG - 1)
    dot = functools.partial(jnp.dot, preferred_element_type=jnp.float32)
    total = None
    for part in range(parts):
        if alternatives == 1:
            value = slabs[part][...]
        else:
            value = jnp.where(ends, slabs[part][...], slabs[parts + part][...])
        rounded = value.astype(jnp.bfloat16)
        rest = (value - rounded.astype(jnp.float32)).astype(jnp.bfloat16)
        copies[2 * part].wait()
        copies[2 * part + 1].wait()
        place = slice(part * depth, (part + 1) * depth)
        high_part, low_part = high_here[:, place], low_here[:, place]
        term = dot(high_part, rounded) + (dot(high_part, rest) + dot(low_part, rounded))
        total = term if total is None else total + term
    out[...] = total.T


def product(scalars, choices, high, low):
    parts = len(choices[0])
    _, columns = choices[0][0].shape
    pairs, slots = high.shape
    vmem = pl.BlockSpec(memory_space=pltpu.VMEM)
    return pl.pallas_call(
        functools.partial(product_kernel, len(choices), parts),
        out_shape=jax.ShapeDtypeStruct((columns, pairs), jnp.float32),
        in_specs=[pl.BlockSpec(memory_space=pltpu.SMEM)]
        + [vmem] * (len(choices) * parts)
        + [pl.BlockSpec(memory_space=pl.ANY)] * 2,
        out_specs=vmem,
        scratch_shapes=[pltpu.VMEM((pairs, slots), jnp.bfloat16)] * 2 + [pltpu.SemaphoreType.DMA((parts, 2))],
        compiler_params=pltpu.CompilerParams(vmem_limit_bytes=16 << 20),
        cost_estimate=pl.CostEstimate(
            flops=6 * slots * columns * pairs, bytes_accessed=4 * slots * (columns + pairs), transcendentals=0
        ),
        name="product",
    )(scalars, *[piece for choice in choices for piece in choice], high, low)


def finish_kernel(column_width, scalars, *refs):
    parts, out = refs[:-1], refs[-1]
    group, position = scalars[2 * IRREPS], scalars[2 * IRREPS + 1]
    column = position * column_width + lax.broadcasted_iota(jnp.int32, out.shape[1:], 0)
    for irrep in range(IRREPS):
        slot = scalars[irrep] ^ group
        size = scalars[IRREPS + irrep]
        total = parts[0][slot]
        for part in parts[1:]:
            total = total + part[slot]
        valid = (column // BLOCK < size) & (column % BLOCK < size)
        out[irrep] = jnp.where(valid, total, 0.0)


def finish(scalars, parts):
    vmem = pl.BlockSpec(memory_space=pltpu.VMEM)
    return pl.pallas_call(
        functools.partial(finish_kernel, parts[0].shape[1]),
        out_shape=jax.ShapeDtypeStruct(parts[0].shape, jnp.float32),
        in_specs=[pl.BlockSpec(memory_space=pltpu.SMEM)] + [vmem] * len(parts),
        out_specs=vmem,
        compiler_params=pltpu.CompilerParams(vmem_limit_bytes=4 << 20),
        name="finish",
    )(scalars, *parts)


def local(amplitudes, integrals, irrep_sizes, owner_map):
    pairs = amplitudes.shape[0]
    rows, columns = integrals.shape[1:]
    column_width = columns // lax.axis_size("blk")
    position = lax.axis_index("blk")
    group = lax.axis_index("grp")
    core = position % NC
    z_part = (position // NC) % NZ

    own = integrals[0]
    halves = [own[: rows // 2], own[rows // 2 :]]
    near, middle = [], []
    for piece in halves:
        near.append(permute(piece, pair_swap))
        middle.append(permute(piece, middle_swap))
    crossed = [permute(piece, middle_swap) for piece in near]
    passed = [permute(piece, outward) for piece in middle]
    far = [permute(piece, outward) for piece in crossed]

    scalars = jnp.concatenate([owner_map, irrep_sizes, jnp.stack([group, position])])
    split = split_rows(amplitudes, scalars)

    def columns_of(slot, *choices):
        result = product(scalars, choices, split[2 * slot], split[2 * slot + 1])
        return result.reshape(NY * NX, columns // (NY * NX), pairs)

    first = plane_sum(jnp.concatenate([columns_of(0, [own]), columns_of(1, near)], axis=1))
    second = plane_sum(columns_of(2, passed, crossed))
    third = plane_sum(columns_of(3, far, middle))
    total = jnp.concatenate([first, second, third], axis=0).reshape(IRREPS, NZ * NC, column_width, pairs)

    def share(flip):
        here = (z_part * NC + core) ^ flip
        return lax.dynamic_index_in_dim(total, here, 1, keepdims=False)

    parts = [share(0)]
    for flip in (3, 2, 1):
        parts.append(permute(share(flip), lambda y, x, z, c, g: (y, x, z ^ (flip >> 1), c ^ (flip & 1), g)))
    return jnp.transpose(finish(scalars, parts), (2, 0, 1))


def solution(mesh):
    in_specs = (P("grp", None, "blk"), P("grp", "blk", None), P(), P())
    out_specs = P("grp", None, "blk")
    return jax.shard_map(local, mesh=mesh, in_specs=in_specs, out_specs=out_specs, check_vma=False)
```

time: 111 us -> 131 us (1.18)
  waiting for transfers between devices: 33.6 us -> 52.2 us
  Pallas kernels: 15 us -> 23.4 us
  local copies, waits for them, and re-layouts: 13.4 us -> 7.03 us
    ppermute x9 -> x13, waiting for transfers between devices: 17.1 us -> 44.6 us  [permute(): return lax.ppermute(value, AXES, pairs)]
    all_to_all x3, waiting for transfers between devices: 16.4 us -> 7.59 us  [plane_sum(): lax.all_to_all(chip, 'blk', 0, 0, tiled=True, axis_index_groups=plane_gro...]
    pallas_call x8 -> x5, Pallas kernels: 7.62 us -> 16.2 us  [the longest x4 15.1 us: product(): pl.pallas_call(functools.partial(product_kernel, len(choices), parts), ou...]
    unnamed x42 -> x12, local copies, waits for them, and re-layouts: 12 us -> 4.62 us
    slice x0 -> x1, local copies, waits for them, and re-layouts: none -> 2.34 us  [local(): halves = [own[:rows // 2], own[rows // 2:]]]
    add x5 -> x0, other arithmetic: 1.55 us -> none  [the longest x4 1.55 us: on_chip(): chip = product(slab, high, low, 1) + sent]
    ppermute x9 -> x13, starting transfers between devices: 23.3 us -> 23.7 us  [permute(): return lax.ppermute(value, AXES, pairs)]
  transfers between devices with their start and end apart: 12 -> 16, of which waited for: 8 -> 7; matrix products, arithmetic and copies ran while one was open for 3% -> 2% of each run, Pallas kernels for 14% -> 17%
where the time goes in v3:
time: 131 us; the launch traced here: 130 us
  waiting for transfers between devices  52.2 us (40%)
  starting transfers between devices  44 us (34%)
  Pallas kernels  23.4 us (18%)
  local copies, waits for them, and re-layouts  7.03 us (5%)
  other arithmetic  3.22 us (2%)
    ppermute x13, waiting for transfers between devices, permute(): return lax.ppermute(value, AXES, pairs)  44.6 us
    ppermute x13, starting transfers between devices, permute(): return lax.ppermute(value, AXES, pairs)  23.7 us
    all_to_all x3, starting transfers between devices, plane_sum(): lax.all_to_all(chip, 'blk', 0, 0, tiled=True, axis_index_groups=plane_gro...  20.4 us
    pallas_call x4, Pallas kernels, product(): pl.pallas_call(functools.partial(product_kernel, len(choices), parts), ou...  15.1 us
    all_to_all x3, waiting for transfers between devices, plane_sum(): lax.all_to_all(chip, 'blk', 0, 0, tiled=True, axis_index_groups=plane_gro...  7.59 us
    pallas_call x1, Pallas kernels, split_rows(): pl.pallas_call(functools.partial(split_kernel, rows, slot_width), out_sha...  7.17 us
    unnamed x12, local copies, waits for them, and re-layouts  4.62 us
  transfers between devices with their start and end apart: 16, of which 7 were waited for; matrix products, arithmetic and copies ran while one was open for 2% of the time, Pallas kernels for 17%

profile of v3, /device:TPU:1, one launch (start us, length us, event | category | flops | bytes accessed | tf_op | source)
XLA Modules:
  0.0 130.2 jit_solution(11927906924993166185)
XLA Ops:
  0.0 0.0 copy-start.1
  0.0 2.3 %slice_bitcast_fusion = (f32[512,256]{1,0:T(8,128)}, f32[512,256]{1,0:T(8,128)}) fusion(f32[1,1024,256]{2,1,0:T(8,128)} %param.5), kind=kLoop, calls=%fused_computation.1 | loop fusion | bytes 2097152 | tf_op jit(solution)/shard_map/slice | solution.py:188
  2.3 2.5 %collective-permute-start = (f32[512,256]{1,0:T(8,128)}, f32[512,256]{1,0:T(8,128)}, u32[]{:S(2)}, u32[]{:S(2)}) collective-permute-start(f32[512,256]{1,0:T(8,128)} %get-tuple-element.22), channel_id=1, source_target_pairs={{0,1},{1,0},{2,3},{3,2},{4,5},{5,4},{6,7},{7,6},{8,9},{9,8},{10,11... | collective-permute-start | bytes 1572872 | tf_op jit(solution)/shard_map/ppermute | solution.py:38
  4.8 0.0 collective-permute-start.1
  4.8 1.4 %collective-permute-start.2 = (f32[512,256]{1,0:T(8,128)}, f32[512,256]{1,0:T(8,128)}, u32[]{:S(2)}, u32[]{:S(2)}) collective-permute-start(f32[512,256]{1,0:T(8,128)} %get-tuple-element.22), channel_id=1, source_target_pairs={{1,2},{2,1},{5,6},{6,5},{9,10},{10,9},{13,14},{14,13},{17,18},{18,... | collective-permute-start | bytes 1572872 | tf_op jit(solution)/shard_map/ppermute | solution.py:38
  6.3 1.5 %collective-permute-start.4 = (f32[512,256]{1,0:T(8,128)}, f32[512,256]{1,0:T(8,128)}, u32[]{:S(2)}, u32[]{:S(2)}) collective-permute-start(f32[512,256]{1,0:T(8,128)} %get-tuple-element.21), channel_id=1, source_target_pairs={{1,2},{2,1},{5,6},{6,5},{9,10},{10,9},{13,14},{14,13},{17,18},{18,... | collective-permute-start | bytes 1572872 | tf_op jit(solution)/shard_map/ppermute | solution.py:38
  7.7 0.7 pad_add_fusion.scalars
  8.5 0.0 copy-start
  8.5 3.4 %copy-done = f32[512,4,1024]{2,1,0:T(4,128)S(1)} copy-done((f32[512,4,1024]{2,1,0:T(4,128)S(1)}, f32[512,4,1024]{2,1,0:T(4,128)}, u32[]{:S(2)}) %copy-start) | copy-done | bytes 8388632
  11.9 7.2 %split_rows.1 = (bf16[512,1024]{1,0:T(8,128)(2,1)S(1)}, bf16[512,1024]{1,0:T(8,128)(2,1)S(1)}, bf16[512,1024]{1,0:T(8,128)(2,1)S(1)}, bf16[512,1024]{1,0:T(8,128...) custom-call(s32[10]{0:T(128)S(1)} %pad_add_fusion.scalars, ...), custom_call_target="tpu_custom_call" | custom-call | bytes 16777216 | tf_op jit(solution)/shard_map/split_rows/pallas_call | solution.py:87
  19.0 0.0 copy-start.2
  19.0 0.0 copy-start.4
  19.1 0.0 copy-done.1
  19.1 2.0 %product.4 = f32[256,512]{1,0:T(8,128)S(1)} custom-call(s32[10]{0:T(128)S(1)} %pad_add_fusion.scalars, f32[1024,256]{1,0:T(8,128)S(1)} %bitcast.26, bf16[512,1024]{1,0:T(8,128)(2,1)S(1)} %get-tuple-element.13.refs_1_, bf16[512,1024]{1,0:T(8,128)(2,1)S(1)} %get-tuple-element.14.refs_2_), custom_call_target="tpu_custom_call" | custom-call | flops 805306368 | bytes 3145728 | tf_op jit(solution)/shard_map/product/pallas_call | solution.py:136
  21.0 0.0 collective-permute-done.refs_0_
  21.0 5.9 %collective-permute-done.1.refs_1_ = f32[512,256]{1,0:T(8,128)} collective-permute-done((f32[512,256]{1,0:T(8,128)}, f32[512,256]{1,0:T(8,128)}, u32[]{:S(2)}, u32[]{:S(2)}) %collective-permute-start.1) | collective-permute-done | bytes 524320 | tf_op jit(solution)/shard_map/ppermute | solution.py:38
  27.0 0.0 copy-done.2
  27.0 0.0 copy-done.4
  27.0 0.0 copy-start.3
  27.0 3.7 %product.5 = f32[256,512]{1,0:T(8,128)S(1)} custom-call(s32[10]{0:T(128)S(1)} %pad_add_fusion.scalars, f32[512,256]{1,0:T(8,128)} %collective-permute-done.refs_0_, f32[512,256]{1,0:T(8,128)} %collective-permute-done.1.refs_1_, bf16[512,1024]{1,0:T(8,128)(2,1)S(1)} %get-tuple-element.15.refs_2_, bf16[512,1024]{1,0:T(8,128)(2,1)S(1)} %get-tuple-element.16.refs_3_), custom_call_target="tpu_custom_call" | custom-call | flops 805306368 | bytes 3145728 | tf_op jit(solution)/shard_map/product/pallas_call | solution.py:136
  30.7 1.1 pad_maximum_fusion
  31.8 7.7 %all-to-all-start = ((f32[16,32,512]{2,1,0:T(8,128)}), f32[16,32,512]{2,1,0:T(8,128)}, u32[]{:S(2)}, u32[]{:S(2)}) async-start(f32[16,32,512]{2,1,0:T(8,128)} %pad_maximum_fusion), calls=%async_computation | async-start | bytes 2097152 | tf_op jit(solution)/shard_map/all_to_all | solution.py:46
  39.5 1.5 %collective-permute-start.6 = (f32[512,256]{1,0:T(8,128)}, f32[512,256]{1,0:T(8,128)}, u32[]{:S(2)}, u32[]{:S(2)}) collective-permute-start(f32[512,256]{1,0:T(8,128)} %collective-permute-done.refs_0_), channel_id=1, source_target_pairs={{1,2},{2,1},{5,6},{6,5},{9,10},{10,9},{13,14},{14,13},{17,18},{18,... | collective-permute-start | bytes 1572872 | tf_op jit(solution)/shard_map/ppermute | solution.py:38
  41.0 1.5 %collective-permute-start.7 = (f32[512,256]{1,0:T(8,128)}, f32[512,256]{1,0:T(8,128)}, u32[]{:S(2)}, u32[]{:S(2)}) collective-permute-start(f32[512,256]{1,0:T(8,128)} %collective-permute-done.1.refs_1_), channel_id=1, source_target_pairs={{1,2},{2,1},{5,6},{6,5},{9,10},{10,9},{13,14},{14,13},{17,18},{18,... | collective-permute-start | bytes 1572872 | tf_op jit(solution)/shard_map/ppermute | solution.py:38
  42.5 0.0 collective-permute-done.2.refs_2_
  42.5 1.3 collective-permute-start.3
  43.8 0.0 collective-permute-done.4.refs_3_
  43.8 1.3 collective-permute-start.5
  45.1 0.0 collective-permute-done.6.refs_2_
  45.1 1.3 collective-permute-start.8
  46.4 0.0 collective-permute-done.7.refs_3_
  46.4 1.3 collective-permute-start.9
  47.7 10.8 %collective-permute-done.3.refs_0_ = f32[512,256]{1,0:T(8,128)S(1)} collective-permute-done((f32[512,256]{1,0:T(8,128)}, f32[512,256]{1,0:T(8,128)S(1)}, u32[]{:S(2)}, u32[]{:S(2)}) %collective-permute-start.3) | collective-permute-done | bytes 524320 | tf_op jit(solution)/shard_map/ppermute | solution.py:38
  58.5 11.2 %collective-permute-done.5.refs_1_ = f32[512,256]{1,0:T(8,128)S(1)} collective-permute-done((f32[512,256]{1,0:T(8,128)}, f32[512,256]{1,0:T(8,128)S(1)}, u32[]{:S(2)}, u32[]{:S(2)}) %collective-permute-start.5) | collective-permute-done | bytes 524320 | tf_op jit(solution)/shard_map/ppermute | solution.py:38
  69.8 0.0 copy-done.3
  69.8 0.0 copy-start.5
  69.8 1.2 copy-done.5
  71.0 4.5 %product.6 = f32[256,512]{1,0:T(8,128)} custom-call(s32[10]{0:T(128)S(1)} %pad_add_fusion.scalars, f32[512,256]{1,0:T(8,128)S(1)} %collective-permute-done.3.refs_0_, f32[512,256]{1,0:T(8,128)S(1)} %collective-permute-done.5.refs_1_, f32[512,256]{1,0:T(8,128)} %collective-permute-done.6.refs_2_, f32[512,256]{1,0:T(8,128)} %collective-permute-done.7.refs_3_, ...), custom_call_target="tpu_custom_call" | custom-call | flops 805306368 | bytes 3145728 | tf_op jit(solution)/shard_map/product/pallas_call | solution.py:136
  75.5 0.0 all-to-all-done
  75.5 6.3 %all-to-all-start.1 = ((f32[16,16,512]{2,1,0:T(8,128)}), f32[16,16,512]{2,1,0:T(8,128)S(1)}, u32[]{:S(2)}, u32[]{:S(2)}) async-start(f32[16,16,512]{2,1,0:T(8,128)} %bitcast.10), calls=%async_computation.1 | async-start | bytes 1048576 | tf_op jit(solution)/shard_map/all_to_all | solution.py:46
  81.9 0.0 collective-permute-done.8.refs_0_
  81.9 10.4 %collective-permute-done.9.refs_1_ = f32[512,256]{1,0:T(8,128)} collective-permute-done((f32[512,256]{1,0:T(8,128)}, f32[512,256]{1,0:T(8,128)}, u32[]{:S(2)}, u32[]{:S(2)}) %collective-permute-start.9) | collective-permute-done | bytes 524320 | tf_op jit(solution)/shard_map/ppermute | solution.py:38
  92.3 4.8 %product.7 = f32[256,512]{1,0:T(8,128)} custom-call(s32[10]{0:T(128)S(1)} %pad_add_fusion.scalars, f32[512,256]{1,0:T(8,128)} %collective-permute-done.8.refs_0_, f32[512,256]{1,0:T(8,128)} %collective-permute-done.9.refs_1_, f32[512,256]{1,0:T(8,128)} %collective-permute-done.2.refs_2_, f32[512,256]{1,0:T(8,128)} %collective-permute-done.4.refs_3_, ...), custom_call_target="tpu_custom_call" | custom-call | flops 805306368 | bytes 3145728 | tf_op jit(solution)/shard_map/product/pallas_call | solution.py:136
  97.2 0.0 all-to-all-done.1
  97.2 6.3 %all-to-all-start.2 = ((f32[16,16,512]{2,1,0:T(8,128)}), f32[16,16,512]{2,1,0:T(8,128)S(1)}, u32[]{:S(2)}, u32[]{:S(2)}) async-start(f32[16,16,512]{2,1,0:T(8,128)} %bitcast.11), calls=%async_computation.2 | async-start | bytes 1048576 | tf_op jit(solution)/shard_map/all_to_all | solution.py:46
  103.6 1.3 %reduce_sum.27 = f32[32,512]{1,0:T(8,128)S(1)} reduce(f32[16,32,512]{2,1,0:T(8,128)} %all-to-all-done, f32[]{:T(128)} %constant.46.clone.1), dimensions={0}, to_apply=%region_0.1 | reduce | flops 245760 | bytes 1114116 | tf_op jit(solution)/shard_map/reduce_sum | solution.py:47
  104.9 7.6 %all-to-all-done.2 = f32[16,16,512]{2,1,0:T(8,128)S(1)} async-done(((f32[16,16,512]{2,1,0:T(8,128)}), f32[16,16,512]{2,1,0:T(8,128)S(1)}, u32[]{:S(2)}, u32[]{:S(2)}) %all-to-all-start.2) | async-done | bytes 524320 | tf_op jit(solution)/shard_map/all_to_all | solution.py:46
  112.6 9.7 %collective-permute-start.10 = (f32[4,4,512]{2,1,0:T(4,128)S(1)}, f32[4,4,512]{2,1,0:T(4,128)S(1)}, u32[]{:S(2)}, u32[]{:S(2)}) collective-permute-start(f32[4,4,512]{2,1,0:T(4,128)S(1)} %get-tuple-element.25), channel_id=1, source_target_pairs={{0,12},{1,13},{2,14},{3,15},{4,8},{5,9},{6,10},{7,11},{8,4},{9,5},... | collective-permute-start | bytes 98312 | tf_op jit(solution)/shard_map/ppermute | solution.py:38
  122.3 0.0 collective-permute-start.11
  122.3 0.5 collective-permute-start.12
  122.8 1.1 collective-permute-done.10.refs_1_
  123.9 5.1 %collective-permute-done.11.refs_2_ = f32[4,4,512]{2,1,0:T(4,128)S(1)} collective-permute-done((f32[4,4,512]{2,1,0:T(4,128)S(1)}, f32[4,4,512]{2,1,0:T(4,128)S(1)}, u32[]{:S(2)}, u32[]{:S(2)}) %collective-permute-start.11) | collective-permute-done | bytes 32800 | tf_op jit(solution)/shard_map/ppermute | solution.py:38
  129.0 0.0 collective-permute-done.12.refs_3_
  129.0 1.2 finish.1
  (5 shorter events, 0.1 us)
Async XLA Ops:
  0.0 19.1 %copy-start.1 = (f32[1,1024,256]{2,1,0:T(8,128)S(1)}, f32[1,1024,256]{2,1,0:T(8,128)}, u32[]{:S(2)}) copy-start(f32[1,1024,256]{2,1,0:T(8,128)} %param.5) | copy-start | bytes 3145732
  2.3 18.7 %collective-permute-start = (f32[512,256]{1,0:T(8,128)}, f32[512,256]{1,0:T(8,128)}, u32[]{:S(2)}, u32[]{:S(2)}) collective-permute-start(f32[512,256]{1,0:T(8,128)} %get-tuple-element.22), channel_id=1, source_target_pairs={{0,1},{1,0},{2,3},{3,2},{4,5},{5,4},{6,7},{7,6},{8,9},{9,8},{10,11... | collective-permute-start | bytes 1572872 | tf_op jit(solution)/shard_map/ppermute | solution.py:38
  4.8 22.2 %collective-permute-start.1 = (f32[512,256]{1,0:T(8,128)}, f32[512,256]{1,0:T(8,128)}, u32[]{:S(2)}, u32[]{:S(2)}) collective-permute-start(f32[512,256]{1,0:T(8,128)} %get-tuple-element.21), channel_id=1, source_target_pairs={{0,1},{1,0},{2,3},{3,2},{4,5},{5,4},{6,7},{7,6},{8,9},{9,8},{10,11... | collective-permute-start | bytes 1572872 | tf_op jit(solution)/shard_map/ppermute | solution.py:38
  4.8 37.7 %collective-permute-start.2 = (f32[512,256]{1,0:T(8,128)}, f32[512,256]{1,0:T(8,128)}, u32[]{:S(2)}, u32[]{:S(2)}) collective-permute-start(f32[512,256]{1,0:T(8,128)} %get-tuple-element.22), channel_id=1, source_target_pairs={{1,2},{2,1},{5,6},{6,5},{9,10},{10,9},{13,14},{14,13},{17,18},{18,... | collective-permute-start | bytes 1572872 | tf_op jit(solution)/shard_map/ppermute | solution.py:38
  6.3 37.5 %collective-permute-start.4 = (f32[512,256]{1,0:T(8,128)}, f32[512,256]{1,0:T(8,128)}, u32[]{:S(2)}, u32[]{:S(2)}) collective-permute-start(f32[512,256]{1,0:T(8,128)} %get-tuple-element.21), channel_id=1, source_target_pairs={{1,2},{2,1},{5,6},{6,5},{9,10},{10,9},{13,14},{14,13},{17,18},{18,... | collective-permute-start | bytes 1572872 | tf_op jit(solution)/shard_map/ppermute | solution.py:38
  8.5 3.4 %copy-start = (f32[512,4,1024]{2,1,0:T(4,128)S(1)}, f32[512,4,1024]{2,1,0:T(4,128)}, u32[]{:S(2)}) copy-start(f32[512,4,1024]{2,1,0:T(4,128)} %param.4) | copy-start | bytes 25165828
  19.0 7.9 %copy-start.2 = (bf16[512,1024]{1,0:T(8,128)(2,1)}, bf16[512,1024]{1,0:T(8,128)(2,1)S(1)}, u32[]{:S(2)}) copy-start(bf16[512,1024]{1,0:T(8,128)(2,1)S(1)} %get-tuple-element.17.refs_4_) | copy-start | bytes 3145732
  19.0 7.9 %copy-start.4 = (bf16[512,1024]{1,0:T(8,128)(2,1)}, bf16[512,1024]{1,0:T(8,128)(2,1)S(1)}, u32[]{:S(2)}) copy-start(bf16[512,1024]{1,0:T(8,128)(2,1)S(1)} %get-tuple-element.18.refs_5_) | copy-start | bytes 3145732
  27.0 42.8 %copy-start.3 = (bf16[512,1024]{1,0:T(8,128)(2,1)S(1)}, bf16[512,1024]{1,0:T(8,128)(2,1)}, u32[]{:S(2)}) copy-start(bf16[512,1024]{1,0:T(8,128)(2,1)} %copy-done.2) | copy-start | bytes 3145732
  31.8 43.7 %all-to-all-start = ((f32[16,32,512]{2,1,0:T(8,128)}), f32[16,32,512]{2,1,0:T(8,128)}, u32[]{:S(2)}, u32[]{:S(2)}) async-start(f32[16,32,512]{2,1,0:T(8,128)} %pad_maximum_fusion), calls=%async_computation | async-start | bytes 2097152 | tf_op jit(solution)/shard_map/all_to_all | solution.py:46
  39.5 5.6 %collective-permute-start.6 = (f32[512,256]{1,0:T(8,128)}, f32[512,256]{1,0:T(8,128)}, u32[]{:S(2)}, u32[]{:S(2)}) collective-permute-start(f32[512,256]{1,0:T(8,128)} %collective-permute-done.refs_0_), channel_id=1, source_target_pairs={{1,2},{2,1},{5,6},{6,5},{9,10},{10,9},{13,14},{14,13},{17,18},{18,... | collective-permute-start | bytes 1572872 | tf_op jit(solution)/shard_map/ppermute | solution.py:38
  41.0 5.4 %collective-permute-start.7 = (f32[512,256]{1,0:T(8,128)}, f32[512,256]{1,0:T(8,128)}, u32[]{:S(2)}, u32[]{:S(2)}) collective-permute-start(f32[512,256]{1,0:T(8,128)} %collective-permute-done.1.refs_1_), channel_id=1, source_target_pairs={{1,2},{2,1},{5,6},{6,5},{9,10},{10,9},{13,14},{14,13},{17,18},{18,... | collective-permute-start | bytes 1572872 | tf_op jit(solution)/shard_map/ppermute | solution.py:38
  42.5 16.0 %collective-permute-start.3 = (f32[512,256]{1,0:T(8,128)}, f32[512,256]{1,0:T(8,128)S(1)}, u32[]{:S(2)}, u32[]{:S(2)}) collective-permute-start(f32[512,256]{1,0:T(8,128)} %collective-permute-done.2.refs_2_), channel_id=1, source_target_pairs={{1,0},{2,3},{5,4},{6,7},{9,8},{10,11},{13,12},{14,15},{17,16},{18,... | collective-permute-start | bytes 1572872 | tf_op jit(solution)/shard_map/ppermute | solution.py:38
  43.8 26.0 %collective-permute-start.5 = (f32[512,256]{1,0:T(8,128)}, f32[512,256]{1,0:T(8,128)S(1)}, u32[]{:S(2)}, u32[]{:S(2)}) collective-permute-start(f32[512,256]{1,0:T(8,128)} %collective-permute-done.4.refs_3_), channel_id=1, source_target_pairs={{1,0},{2,3},{5,4},{6,7},{9,8},{10,11},{13,12},{14,15},{17,16},{18,... | collective-permute-start | bytes 1572872 | tf_op jit(solution)/shard_map/ppermute | solution.py:38
  45.1 36.8 %collective-permute-start.8 = (f32[512,256]{1,0:T(8,128)}, f32[512,256]{1,0:T(8,128)}, u32[]{:S(2)}, u32[]{:S(2)}) collective-permute-start(f32[512,256]{1,0:T(8,128)} %collective-permute-done.6.refs_2_), channel_id=1, source_target_pairs={{1,0},{2,3},{5,4},{6,7},{9,8},{10,11},{13,12},{14,15},{17,16},{18,... | collective-permute-start | bytes 1572872 | tf_op jit(solution)/shard_map/ppermute | solution.py:38
  46.4 45.9 %collective-permute-start.9 = (f32[512,256]{1,0:T(8,128)}, f32[512,256]{1,0:T(8,128)}, u32[]{:S(2)}, u32[]{:S(2)}) collective-permute-start(f32[512,256]{1,0:T(8,128)} %collective-permute-done.7.refs_3_), channel_id=1, source_target_pairs={{1,0},{2,3},{5,4},{6,7},{9,8},{10,11},{13,12},{14,15},{17,16},{18,... | collective-permute-start | bytes 1572872 | tf_op jit(solution)/shard_map/ppermute | solution.py:38
  69.8 1.2 copy-start.5
  75.5 21.6 %all-to-all-start.1 = ((f32[16,16,512]{2,1,0:T(8,128)}), f32[16,16,512]{2,1,0:T(8,128)S(1)}, u32[]{:S(2)}, u32[]{:S(2)}) async-start(f32[16,16,512]{2,1,0:T(8,128)} %bitcast.10), calls=%async_computation.1 | async-start | bytes 1048576 | tf_op jit(solution)/shard_map/all_to_all | solution.py:46
  97.2 15.3 %all-to-all-start.2 = ((f32[16,16,512]{2,1,0:T(8,128)}), f32[16,16,512]{2,1,0:T(8,128)S(1)}, u32[]{:S(2)}, u32[]{:S(2)}) async-start(f32[16,16,512]{2,1,0:T(8,128)} %bitcast.11), calls=%async_computation.2 | async-start | bytes 1048576 | tf_op jit(solution)/shard_map/all_to_all | solution.py:46
  112.6 11.3 %collective-permute-start.10 = (f32[4,4,512]{2,1,0:T(4,128)S(1)}, f32[4,4,512]{2,1,0:T(4,128)S(1)}, u32[]{:S(2)}, u32[]{:S(2)}) collective-permute-start(f32[4,4,512]{2,1,0:T(4,128)S(1)} %get-tuple-element.25), channel_id=1, source_target_pairs={{0,12},{1,13},{2,14},{3,15},{4,8},{5,9},{6,10},{7,11},{8,4},{9,5},... | collective-permute-start | bytes 98312 | tf_op jit(solution)/shard_map/ppermute | solution.py:38
  122.3 6.7 %collective-permute-start.11 = (f32[4,4,512]{2,1,0:T(4,128)S(1)}, f32[4,4,512]{2,1,0:T(4,128)S(1)}, u32[]{:S(2)}, u32[]{:S(2)}) collective-permute-start(f32[4,4,512]{2,1,0:T(4,128)S(1)} %get-tuple-element.24), channel_id=1, source_target_pairs={{0,8},{1,9},{2,10},{3,11},{4,12},{5,13},{6,14},{7,15},{8,0},{9,1},... | collective-permute-start | bytes 98312 | tf_op jit(solution)/shard_map/ppermute | solution.py:38
  122.3 6.7 %collective-permute-start.12 = (f32[4,4,512]{2,1,0:T(4,128)S(1)}, f32[4,4,512]{2,1,0:T(4,128)S(1)}, u32[]{:S(2)}, u32[]{:S(2)}) collective-permute-start(f32[4,4,512]{2,1,0:T(4,128)S(1)} %get-tuple-element.23), channel_id=1, source_target_pairs={{0,4},{1,5},{2,6},{3,7},{4,0},{5,1},{6,2},{7,3},{8,12},{9,13},{10,... | collective-permute-start | bytes 98312 | tf_op jit(solution)/shard_map/ppermute | solution.py:38

commit v4 on v3

--- a/solution.py
+++ b/solution.py
@@ -53,6 +53,10 @@
 
 def middle_swap(y, x, z, c, g):
     return (y, x, z, c, 3 - g) if g in (1, 2) else None
+
+
+def inward(y, x, z, c, g):
+    return (y, x, z, c, {0: 1, 3: 2}[g]) if g in (0, 3) else None
 
 
 def outward(y, x, z, c, g):
@@ -76,6 +80,8 @@
             value = jnp.where(lane < limit, value, 0.0)
             rounded = value.astype(jnp.bfloat16)
             place = slice(tile * LANES, (tile + 1) * LANES)
+            if slot == IRREPS - 1 and tile >= tiles // 2:
+                outputs[-1][:, (tile - tiles // 2) * LANES : (tile + 1 - tiles // 2) * LANES] = value
             high[:, place] = rounded
             low[:, place] = (value - rounded.astype(jnp.float32)).astype(jnp.bfloat16)
 
@@ -86,67 +92,143 @@
     view = amplitudes.reshape(pairs, IRREPS, slot_width // LANES, LANES).transpose(0, 2, 1, 3).reshape(-1, LANES)
     return pl.pallas_call(
         functools.partial(split_kernel, rows, slot_width),
-        out_shape=[jax.ShapeDtypeStruct((pairs, slot_width), jnp.bfloat16)] * (2 * IRREPS),
+        out_shape=[pltpu.HBM((pairs, slot_width), jnp.bfloat16)] * (2 * IRREPS)
+        + [pltpu.HBM((pairs, slot_width // 2), jnp.float32)],
         grid_spec=pltpu.PrefetchScalarGridSpec(
             num_scalar_prefetch=1,
             grid=(pairs // rows,),
             in_specs=[pl.BlockSpec((rows * IRREPS * slot_width // LANES, LANES), lambda i, scalars: (i, 0))],
-            out_specs=[pl.BlockSpec((rows, slot_width), lambda i, scalars: (i, 0))] * (2 * IRREPS),
+            out_specs=[pl.BlockSpec((rows, slot_width), lambda i, scalars: (i, 0))] * (2 * IRREPS)
+            + [pl.BlockSpec((rows, slot_width // 2), lambda i, scalars: (i, 0))],
         ),
         compiler_params=pltpu.CompilerParams(vmem_limit_bytes=16 << 20),
         cost_estimate=pl.CostEstimate(flops=0, bytes_accessed=8 * pairs * IRREPS * slot_width, transcendentals=0),
         name="split_rows",
-    )(scalars, view)
-
-
-def product_kernel(alternatives, parts, scalars, *refs):
-    slabs, (high, low, out, high_here, low_here, sems) = refs[: alternatives * parts], refs[alternatives * parts :]
-    depth = slabs[0].shape[0]
-    copies = []
-    for part in range(parts):
-        place = pl.ds(part * depth, depth)
-        for k, (there, here) in enumerate(((high, high_here), (low, low_here))):
-            copies.append(pltpu.make_async_copy(there.at[:, place], here.at[:, place], sems.at[part, k]))
-            copies[-1].start()
+    )(scalars, *in_hbm([view]))
+
+
+PARTS = 2
+
+
+def halves_of(value):
+    rounded = value.astype(jnp.bfloat16)
+    return rounded, (value - rounded.astype(jnp.float32)).astype(jnp.bfloat16)
+
+
+def split_dot(left, right):
+    dot = functools.partial(jnp.dot, preferred_element_type=jnp.float32)
+    return dot(left[0], right[0]) + (dot(left[0], right[1]) + dot(left[1], right[0]))
+
+
+def in_hbm(values):
+    return [pltpu.with_memory_space_constraint(value, pltpu.HBM) for value in values]
+
+
+def product_kernel(kind, scalars, *refs):
+    slabs, (high, low, out, high_here, low_here, slab_here, total, sems) = refs[:-8], refs[-8:]
+    depth = high.shape[1] // PARTS
+    places = [pl.ds(part * depth, depth) for part in range(PARTS)]
     group = scalars[2 * IRREPS]
     ends = (group == 0) | (group == NG - 1)
-    dot = functools.partial(jnp.dot, preferred_element_type=jnp.float32)
-    total = None
-    for part in range(parts):
-        if alternatives == 1:
-            value = slabs[part][...]
-        else:
-            value = jnp.where(ends, slabs[part][...], slabs[parts + part][...])
-        rounded = value.astype(jnp.bfloat16)
-        rest = (value - rounded.astype(jnp.float32)).astype(jnp.bfloat16)
-        copies[2 * part].wait()
-        copies[2 * part + 1].wait()
-        place = slice(part * depth, (part + 1) * depth)
-        high_part, low_part = high_here[:, place], low_here[:, place]
-        term = dot(high_part, rounded) + (dot(high_part, rest) + dot(low_part, rounded))
-        total = term if total is None else total + term
-    out[...] = total.T
-
-
-def product(scalars, choices, high, low):
-    parts = len(choices[0])
-    _, columns = choices[0][0].shape
+    inner = jnp.logical_not(ends)
+
+    def copies_of(part, slab):
+        place = places[part]
+        return [
+            pltpu.make_async_copy(slab.at[place, :], slab_here.at[place, :], sems.at[part, 0]),
+            pltpu.make_async_copy(high.at[:, place], high_here.at[:, place], sems.at[part, 1]),
+            pltpu.make_async_copy(low.at[:, place], low_here.at[:, place], sems.at[part, 2]),
+        ]
+
+    def start(part, slab):
+        for copy in copies_of(part, slab):
+            copy.start()
+
+    def add(part, first):
+        for copy in copies_of(part, slabs[-1]):
+            copy.wait()
+        right = halves_of(slab_here[places[part], :])
+        term = split_dot((high_here[:, places[part]], low_here[:, places[part]]), right)
+        total[...] = term if first else total[...] + term
+
+    if kind == "one":
+        start(0, slabs[0])
+        start(1, slabs[0])
+    else:
+
+        @pl.when(ends)
+        def _():
+            start(0, slabs[0])
+            if kind == "two":
+                start(1, slabs[0])
+
+        @pl.when(inner)
+        def _():
+            start(0, slabs[1])
+            start(1, slabs[1])
+
+    add(0, True)
+    if kind == "last":
+        pl.when(inner)(lambda: add(1, False))
+    else:
+        add(1, False)
+    out[...] = total[...].T
+
+
+def product(kind, scalars, slabs, high, low):
+    columns = slabs[0].shape[1]
     pairs, slots = high.shape
-    vmem = pl.BlockSpec(memory_space=pltpu.VMEM)
     return pl.pallas_call(
-        functools.partial(product_kernel, len(choices), parts),
+        functools.partial(product_kernel, kind),
         out_shape=jax.ShapeDtypeStruct((columns, pairs), jnp.float32),
-        in_specs=[pl.BlockSpec(memory_space=pltpu.SMEM)]
-        + [vmem] * (len(choices) * parts)
-        + [pl.BlockSpec(memory_space=pl.ANY)] * 2,
-        out_specs=vmem,
-        scratch_shapes=[pltpu.VMEM((pairs, slots), jnp.bfloat16)] * 2 + [pltpu.SemaphoreType.DMA((parts, 2))],
-        compiler_params=pltpu.CompilerParams(vmem_limit_bytes=16 << 20),
+        in_specs=[pl.BlockSpec(memory_space=pltpu.SMEM)] + [pl.BlockSpec(memory_space=pl.ANY)] * (len(slabs) + 2),
+        out_specs=pl.BlockSpec(memory_space=pltpu.VMEM),
+        scratch_shapes=[pltpu.VMEM((pairs, slots), jnp.bfloat16)] * 2
+        + [
+            pltpu.VMEM((slots, columns), jnp.float32),
+            pltpu.VMEM((pairs, columns), jnp.float32),
+            pltpu.SemaphoreType.DMA((PARTS, 3)),
+        ],
+        compiler_params=pltpu.CompilerParams(vmem_limit_bytes=12 << 20),
         cost_estimate=pl.CostEstimate(
             flops=6 * slots * columns * pairs, bytes_accessed=4 * slots * (columns + pairs), transcendentals=0
         ),
         name="product",
-    )(scalars, *[piece for choice in choices for piece in choice], high, low)
+    )(scalars, *in_hbm([*slabs, high, low]))
+
+
+def guest_kernel(slab, rows, out, slab_here, rows_here, sems):
+    depth = rows.shape[1]
+    copies = [
+        pltpu.make_async_copy(slab.at[pl.ds(depth, depth), :], slab_here, sems.at[0]),
+        pltpu.make_async_copy(rows, rows_here, sems.at[1]),
+    ]
+    for copy in copies:
+        copy.start()
+    for copy in copies:
+        copy.wait()
+    out[...] = split_dot(halves_of(rows_here[...]), halves_of(slab_here[...])).T
+
+
+def guest_product(slab, rows):
+    columns = slab.shape[1]
+    pairs, depth = rows.shape
+    return pl.pallas_call(
+        guest_kernel,
+        out_shape=jax.ShapeDtypeStruct((columns, pairs), jnp.float32),
+        in_specs=[pl.BlockSpec(memory_space=pl.ANY)] * 2,
+        out_specs=pl.BlockSpec(memory_space=pltpu.VMEM),
+        scratch_shapes=[
+            pltpu.VMEM((depth, columns), jnp.float32),
+            pltpu.VMEM((pairs, depth), jnp.float32),
+            pltpu.SemaphoreType.DMA((2,)),
+        ],
+        compiler_params=pltpu.CompilerParams(vmem_limit_bytes=12 << 20),
+        cost_estimate=pl.CostEstimate(
+            flops=6 * depth * columns * pairs, bytes_accessed=4 * depth * (columns + pairs), transcendentals=0
+        ),
+        name="guest_product",
+    )(*in_hbm([slab, rows]))
 
 
 def finish_kernel(column_width, scalars, *refs):
@@ -185,25 +267,27 @@
     z_part = (position // NC) % NZ
 
     own = integrals[0]
-    halves = [own[: rows // 2], own[rows // 2 :]]
-    near, middle = [], []
-    for piece in halves:
-        near.append(permute(piece, pair_swap))
-        middle.append(permute(piece, middle_swap))
-    crossed = [permute(piece, middle_swap) for piece in near]
-    passed = [permute(piece, outward) for piece in middle]
-    far = [permute(piece, outward) for piece in crossed]
-
+    near = permute(own, pair_swap)
+    middle = permute(own, middle_swap)
     scalars = jnp.concatenate([owner_map, irrep_sizes, jnp.stack([group, position])])
-    split = split_rows(amplitudes, scalars)
-
-    def columns_of(slot, *choices):
-        result = product(scalars, choices, split[2 * slot], split[2 * slot + 1])
+    *split, moved = split_rows(amplitudes, scalars)
+    guests = permute(moved, inward)
+    crossed = permute(near, middle_swap)
+    passed = permute(middle, outward)
+    far = permute(crossed[: rows // 2], outward)
+
+    def by_plane(result):
         return result.reshape(NY * NX, columns // (NY * NX), pairs)
 
-    first = plane_sum(jnp.concatenate([columns_of(0, [own]), columns_of(1, near)], axis=1))
-    second = plane_sum(columns_of(2, passed, crossed))
-    third = plane_sum(columns_of(3, far, middle))
+    def columns_of(kind, slot, *slabs):
+        return by_plane(product(kind, scalars, slabs, split[2 * slot], split[2 * slot + 1]))
+
+    first = plane_sum(jnp.concatenate([columns_of("one", 0, own), columns_of("one", 1, near)], axis=1))
+    guest = by_plane(guest_product(crossed, guests))
+    second = plane_sum(jnp.concatenate([columns_of("two", 2, passed, crossed), guest], axis=1))
+    second, handed = jnp.split(second, 2)
+    third = plane_sum(columns_of("last", 3, far, middle))
+    third = third + permute(handed, outward)
     total = jnp.concatenate([first, second, third], axis=0).reshape(IRREPS, NZ * NC, column_width, pairs)
 
     def share(flip):

time: 131 us -> 117 us (0.89)
  waiting for transfers between devices: 52.2 us -> 31.9 us
  Pallas kernels: 23.4 us -> 31.4 us
  local copies, waits for them, and re-layouts: 7.03 us -> 2.88 us
  starting transfers between devices: 44 us -> 46.5 us
    ppermute x13 -> x10, waiting for transfers between devices: 44.6 us -> 24.3 us  [permute(): return lax.ppermute(value, AXES, pairs)]
    pallas_call x1, Pallas kernels: 7.17 us -> 12.8 us  [split_rows(): pl.pallas_call(functools.partial(split_kernel, rows, slot_width), out_sha...]
    pallas_call x4 -> x5, Pallas kernels: 15.1 us -> 17.4 us  [the longest x4 15.4 us: product(): pl.pallas_call(functools.partial(product_kernel, kind), out_shape=jax.Sha...]
    slice x1, local copies, waits for them, and re-layouts: 2.34 us -> 0.04 us  [local(): far = permute(crossed[:rows // 2], outward)]
    ppermute x13 -> x10, starting transfers between devices: 23.7 us -> 25.9 us  [permute(): return lax.ppermute(value, AXES, pairs)]
    unnamed x12 -> x8, local copies, waits for them, and re-layouts: 4.62 us -> 2.77 us
  transfers between devices with their start and end apart: 16 -> 13, of which waited for: 7 -> 8; matrix products, arithmetic and copies ran while one was open for 2% -> 3% of each run, Pallas kernels for 17% -> 26%
where the time goes in v4:
time: 117 us; the launch traced here: 116 us
  starting transfers between devices  46.5 us (40%)
  waiting for transfers between devices  31.9 us (27%)
  Pallas kernels  31.4 us (27%)
  other arithmetic  3.19 us (3%)
  local copies, waits for them, and re-layouts  2.88 us (2%)
    ppermute x10, starting transfers between devices, permute(): return lax.ppermute(value, AXES, pairs)  25.9 us
    ppermute x10, waiting for transfers between devices, permute(): return lax.ppermute(value, AXES, pairs)  24.3 us
    all_to_all x3, starting transfers between devices, plane_sum(): lax.all_to_all(chip, 'blk', 0, 0, tiled=True, axis_index_groups=plane_gro...  20.7 us
    pallas_call x4, Pallas kernels, product(): pl.pallas_call(functools.partial(product_kernel, kind), out_shape=jax.Sha...  15.4 us
    pallas_call x1, Pallas kernels, split_rows(): pl.pallas_call(functools.partial(split_kernel, rows, slot_width), out_sha...  12.8 us
    all_to_all x3, waiting for transfers between devices, plane_sum(): lax.all_to_all(chip, 'blk', 0, 0, tiled=True, axis_index_groups=plane_gro...  7.68 us
    unnamed x8, local copies, waits for them, and re-layouts  2.77 us
  transfers between devices with their start and end apart: 13, of which 8 were waited for; matrix products, arithmetic and copies ran while one was open for 3% of the time, Pallas kernels for 26%

profile of v4, /device:TPU:1, one launch (start us, length us, event | category | flops | bytes accessed | tf_op | source)
XLA Modules:
  0.0 116.2 jit_solution(6188482402725898781)
XLA Ops:
  0.0 2.5 %collective-permute-start = (f32[1024,256]{1,0:T(8,128)}, f32[1024,256]{1,0:T(8,128)}, u32[]{:S(2)}, u32[]{:S(2)}) collective-permute-start(f32[1024,256]{1,0:T(8,128)} %bitcast.27), channel_id=1, source_target_pairs={{0,1},{1,0},{2,3},{3,2},{4,5},{5,4},{6,7},{7,6},{8,9},{9,8},{10,11... | collective-permute-start | bytes 3145736 | tf_op jit(solution)/shard_map/ppermute | solution.py:38
  2.5 1.6 %collective-permute-start.1 = (f32[1024,256]{1,0:T(8,128)}, f32[1024,256]{1,0:T(8,128)}, u32[]{:S(2)}, u32[]{:S(2)}) collective-permute-start(f32[1024,256]{1,0:T(8,128)} %bitcast.28), channel_id=1, source_target_pairs={{1,2},{2,1},{5,6},{6,5},{9,10},{10,9},{13,14},{14,13},{17,18},{18,... | collective-permute-start | bytes 3145736 | tf_op jit(solution)/shard_map/ppermute | solution.py:38
  4.1 0.7 pad_add_fusion.scalars
  4.8 12.8 %split_rows.1 = (bf16[512,1024]{1,0:T(8,128)(2,1)}, bf16[512,1024]{1,0:T(8,128)(2,1)}, bf16[512,1024]{1,0:T(8,128)(2,1)}, bf16[512,1024]{1,0:T(8,128)(2,1)}, bf1...) custom-call(s32[10]{0:T(128)S(1)} %pad_add_fusion.scalars, ...), custom_call_target="tpu_custom_call" | custom-call | bytes 16777216 | tf_op jit(solution)/shard_map/split_rows/pallas_call | solution.py:93
  17.6 5.5 %collective-permute-start.4 = (f32[512,512]{1,0:T(8,128)}, f32[512,512]{1,0:T(8,128)S(1)}, u32[]{:S(2)}, u32[]{:S(2)}) collective-permute-start(f32[512,512]{1,0:T(8,128)} %get-tuple-element.20), channel_id=1, source_target_pairs={{0,1},{3,2},{4,5},{7,6},{8,9},{11,10},{12,13},{15,14},{16,17},{19,... | collective-permute-start | bytes 3145736 | tf_op jit(solution)/shard_map/ppermute | solution.py:38
  23.1 1.5 %collective-permute-done.refs_0_ = f32[1024,256]{1,0:T(8,128)} collective-permute-done((f32[1024,256]{1,0:T(8,128)}, f32[1024,256]{1,0:T(8,128)}, u32[]{:S(2)}, u32[]{:S(2)}) %collective-permute-start) | collective-permute-done | bytes 1048608 | tf_op jit(solution)/shard_map/ppermute | solution.py:38
  24.6 0.7 collective-permute-start.3
  25.3 0.0 collective-permute-done.1.refs_1_
  25.4 1.3 %collective-permute-start.2 = (f32[1024,256]{1,0:T(8,128)}, f32[1024,256]{1,0:T(8,128)}, u32[]{:S(2)}, u32[]{:S(2)}) collective-permute-start(f32[1024,256]{1,0:T(8,128)} %collective-permute-done.1.refs_1_), channel_id=1, source_target_pairs={{1,0},{2,3},{5,4},{6,7},{9,8},{10,11},{13,12},{14,15},{17,16},{18,... | collective-permute-start | bytes 3145736 | tf_op jit(solution)/shard_map/ppermute | solution.py:38
  26.6 3.9 %product.4 = f32[256,512]{1,0:T(8,128)S(1)} custom-call(s32[10]{0:T(128)S(1)} %pad_add_fusion.scalars, f32[1024,256]{1,0:T(8,128)} %bitcast.29, bf16[512,1024]{1,0:T(8,128)(2,1)} %get-tuple-element.14.refs_1_, bf16[512,1024]{1,0:T(8,128)(2,1)} %get-tuple-element.15.refs_2_), custom_call_target="tpu_custom_call" | custom-call | flops 805306368 | bytes 3145728 | tf_op jit(solution)/shard_map/product/pallas_call | solution.py:181
  30.6 3.9 %product.5 = f32[256,512]{1,0:T(8,128)S(1)} custom-call(s32[10]{0:T(128)S(1)} %pad_add_fusion.scalars, f32[1024,256]{1,0:T(8,128)} %collective-permute-done.refs_0_, bf16[512,1024]{1,0:T(8,128)(2,1)} %get-tuple-element.16.refs_1_, bf16[512,1024]{1,0:T(8,128)(2,1)} %get-tuple-element.17.refs_2_), custom_call_target="tpu_custom_call" | custom-call | flops 805306368 | bytes 3145728 | tf_op jit(solution)/shard_map/product/pallas_call | solution.py:181
  34.6 1.2 pad_maximum_fusion
  35.7 7.7 %all-to-all-start = ((f32[16,32,512]{2,1,0:T(8,128)}), f32[16,32,512]{2,1,0:T(8,128)S(1)}, u32[]{:S(2)}, u32[]{:S(2)}) async-start(f32[16,32,512]{2,1,0:T(8,128)} %pad_maximum_fusion), calls=%async_computation | async-start | bytes 2097152 | tf_op jit(solution)/shard_map/all_to_all | solution.py:46
  43.4 3.7 %collective-permute-done.4.rows = f32[512,512]{1,0:T(8,128)S(1)} collective-permute-done((f32[512,512]{1,0:T(8,128)}, f32[512,512]{1,0:T(8,128)S(1)}, u32[]{:S(2)}, u32[]{:S(2)}) %collective-permute-start.4) | collective-permute-done | bytes 1048608 | tf_op jit(solution)/shard_map/ppermute | solution.py:38
  47.1 0.0 copy-start.2
  47.1 0.0 collective-permute-done.3.refs_1_.slab
  47.1 1.0 copy-done.2
  48.1 0.0 copy-start
  48.1 1.0 copy-done
  49.1 2.1 %guest_product.1 = f32[256,512]{1,0:T(8,128)S(1)} custom-call(f32[1024,256]{1,0:T(8,128)} %copy-done, f32[512,512]{1,0:T(8,128)} %copy-done.2), custom_call_target="tpu_custom_call" | custom-call | flops 402653184 | bytes 1572864 | tf_op jit(solution)/shard_map/guest_product/pallas_call | solution.py:216
  51.1 0.0 copy-start.1
  51.1 2.1 %collective-permute-done.2.refs_0_ = f32[1024,256]{1,0:T(8,128)} collective-permute-done((f32[1024,256]{1,0:T(8,128)}, f32[1024,256]{1,0:T(8,128)}, u32[]{:S(2)}, u32[]{:S(2)}) %collective-permute-start.2) | collective-permute-done | bytes 1048608 | tf_op jit(solution)/shard_map/ppermute | solution.py:38
  53.2 3.9 %product.6 = f32[256,512]{1,0:T(8,128)S(1)} custom-call(s32[10]{0:T(128)S(1)} %pad_add_fusion.scalars, f32[1024,256]{1,0:T(8,128)} %collective-permute-done.2.refs_0_, f32[1024,256]{1,0:T(8,128)} %copy-done, bf16[512,1024]{1,0:T(8,128)(2,1)} %get-tuple-element.18.refs_2_, bf16[512,1024]{1,0:T(8,128)(2,1)} %get-tuple-element.19.refs_3_), custom_call_target="tpu_custom_call" | custom-call | flops 805306368 | bytes 3145728 | tf_op jit(solution)/shard_map/product/pallas_call | solution.py:181
  57.2 1.1 pad_maximum_fusion.1
  58.3 0.2 all-to-all-done
  58.5 6.5 %all-to-all-start.1 = ((f32[16,32,512]{2,1,0:T(8,128)}), f32[16,32,512]{2,1,0:T(8,128)S(1)}, u32[]{:S(2)}, u32[]{:S(2)}) async-start(f32[16,32,512]{2,1,0:T(8,128)} %pad_maximum_fusion.1), calls=%async_computation.1 | async-start | bytes 2097152 | tf_op jit(solution)/shard_map/all_to_all | solution.py:46
  65.0 0.0 copy-done.1
  65.1 1.3 %collective-permute-start.5 = (f32[512,256]{1,0:T(8,128)S(1)}, f32[512,256]{1,0:T(8,128)S(1)}, u32[]{:S(2)}, u32[]{:S(2)}) collective-permute-start(f32[512,256]{1,0:T(8,128)S(1)} %slice.4), channel_id=1, source_target_pairs={{1,0},{2,3},{5,4},{6,7},{9,8},{10,11},{13,12},{14,15},{17,16},{18,... | collective-permute-start | bytes 1572872 | tf_op jit(solution)/shard_map/ppermute | solution.py:38
  66.4 10.5 %collective-permute-done.5.refs_0_ = f32[512,256]{1,0:T(8,128)S(1)} collective-permute-done((f32[512,256]{1,0:T(8,128)S(1)}, f32[512,256]{1,0:T(8,128)S(1)}, u32[]{:S(2)}, u32[]{:S(2)}) %collective-permute-start.5) | collective-permute-done | bytes 524320 | tf_op jit(solution)/shard_map/ppermute | solution.py:38
  76.9 0.0 copy-start.3
  76.9 0.8 copy-done.3
  77.7 3.5 %product.7 = f32[256,512]{1,0:T(8,128)} custom-call(s32[10]{0:T(128)S(1)} %pad_add_fusion.scalars, f32[512,256]{1,0:T(8,128)} %copy-done.3, f32[1024,256]{1,0:T(8,128)} %collective-permute-done.1.refs_1_, bf16[512,1024]{1,0:T(8,128)(2,1)} %get-tuple-element.21.refs_2_, bf16[512,1024]{1,0:T(8,128)(2,1)} %get-tuple-element.22.refs_3_), custom_call_target="tpu_custom_call" | custom-call | flops 805306368 | bytes 3145728 | tf_op jit(solution)/shard_map/product/pallas_call | solution.py:181
  81.2 0.0 all-to-all-done.1
  81.2 6.4 %all-to-all-start.2 = ((f32[16,16,512]{2,1,0:T(8,128)}), f32[16,16,512]{2,1,0:T(8,128)S(1)}, u32[]{:S(2)}, u32[]{:S(2)}) async-start(f32[16,16,512]{2,1,0:T(8,128)} %bitcast.10), calls=%async_computation.2 | async-start | bytes 1048576 | tf_op jit(solution)/shard_map/all_to_all | solution.py:46
  87.7 0.1 reduce_sum.28
  87.8 1.3 %collective-permute-start.6 = (f32[16,512]{1,0:T(8,128)S(1)}, f32[16,512]{1,0:T(8,128)S(1)}, u32[]{:S(2)}, u32[]{:S(2)}) collective-permute-start(f32[16,512]{1,0:T(8,128)S(1)} %get-tuple-element.28), channel_id=1, source_target_pairs={{1,0},{2,3},{5,4},{6,7},{9,8},{10,11},{13,12},{14,15},{17,16},{18,... | collective-permute-start | bytes 98312 | tf_op jit(solution)/shard_map/ppermute | solution.py:38
  89.1 0.1 reduce_sum.27
  89.2 7.5 %all-to-all-done.2 = f32[16,16,512]{2,1,0:T(8,128)S(1)} async-done(((f32[16,16,512]{2,1,0:T(8,128)}), f32[16,16,512]{2,1,0:T(8,128)S(1)}, u32[]{:S(2)}, u32[]{:S(2)}) %all-to-all-start.2) | async-done | bytes 524320 | tf_op jit(solution)/shard_map/all_to_all | solution.py:46
  96.7 0.0 collective-permute-done.6
  96.8 11.2 %collective-permute-start.7 = (f32[4,4,512]{2,1,0:T(4,128)S(1)}, f32[4,4,512]{2,1,0:T(4,128)S(1)}, u32[]{:S(2)}, u32[]{:S(2)}) collective-permute-start(f32[4,4,512]{2,1,0:T(4,128)S(1)} %get-tuple-element.25), channel_id=1, source_target_pairs={{0,12},{1,13},{2,14},{3,15},{4,8},{5,9},{6,10},{7,11},{8,4},{9,5},... | collective-permute-start | bytes 98312 | tf_op jit(solution)/shard_map/ppermute | solution.py:38
  108.0 0.3 collective-permute-start.8
  108.3 0.2 collective-permute-start.9
  108.5 2.1 %collective-permute-done.7.refs_1_ = f32[4,4,512]{2,1,0:T(4,128)S(1)} collective-permute-done((f32[4,4,512]{2,1,0:T(4,128)S(1)}, f32[4,4,512]{2,1,0:T(4,128)S(1)}, u32[]{:S(2)}, u32[]{:S(2)}) %collective-permute-start.7) | collective-permute-done | bytes 32800 | tf_op jit(solution)/shard_map/ppermute | solution.py:38
  110.6 4.4 %collective-permute-done.8.refs_2_ = f32[4,4,512]{2,1,0:T(4,128)S(1)} collective-permute-done((f32[4,4,512]{2,1,0:T(4,128)S(1)}, f32[4,4,512]{2,1,0:T(4,128)S(1)}, u32[]{:S(2)}, u32[]{:S(2)}) %collective-permute-start.8) | collective-permute-done | bytes 32800 | tf_op jit(solution)/shard_map/ppermute | solution.py:38
  115.0 0.0 collective-permute-done.9.refs_3_
  115.0 1.2 %finish.1 = f32[4,4,512]{2,1,0:T(4,128)} custom-call(s32[10]{0:T(128)S(1)} %pad_add_fusion.scalars, f32[4,4,512]{2,1,0:T(4,128)S(1)} %get-tuple-element.26.refs_0_, f32[4,4,512]{2,1,0:T(4,128)S(1)} %collective-permute-done.7.refs_1_, f32[4,4,512]{2,1,0:T(4,128)S(1)} %collective-permute-done.8.refs_2_, f32[4,4,512]{2,1,0:T(4,128)S(1)} %collective-permute-done.9.refs_3_), custom_call_target="tpu_custom_call" | custom-call | tf_op jit(solution)/shard_map/finish/pallas_call | solution.py:250
  (7 shorter events, 0.2 us)
Async XLA Ops:
  0.0 24.6 %collective-permute-start = (f32[1024,256]{1,0:T(8,128)}, f32[1024,256]{1,0:T(8,128)}, u32[]{:S(2)}, u32[]{:S(2)}) collective-permute-start(f32[1024,256]{1,0:T(8,128)} %bitcast.27), channel_id=1, source_target_pairs={{0,1},{1,0},{2,3},{3,2},{4,5},{5,4},{6,7},{7,6},{8,9},{9,8},{10,11... | collective-permute-start | bytes 3145736 | tf_op jit(solution)/shard_map/ppermute | solution.py:38
  2.5 22.9 %collective-permute-start.1 = (f32[1024,256]{1,0:T(8,128)}, f32[1024,256]{1,0:T(8,128)}, u32[]{:S(2)}, u32[]{:S(2)}) collective-permute-start(f32[1024,256]{1,0:T(8,128)} %bitcast.28), channel_id=1, source_target_pairs={{1,2},{2,1},{5,6},{6,5},{9,10},{10,9},{13,14},{14,13},{17,18},{18,... | collective-permute-start | bytes 3145736 | tf_op jit(solution)/shard_map/ppermute | solution.py:38
  17.6 29.5 %collective-permute-start.4 = (f32[512,512]{1,0:T(8,128)}, f32[512,512]{1,0:T(8,128)S(1)}, u32[]{:S(2)}, u32[]{:S(2)}) collective-permute-start(f32[512,512]{1,0:T(8,128)} %get-tuple-element.20), channel_id=1, source_target_pairs={{0,1},{3,2},{4,5},{7,6},{8,9},{11,10},{12,13},{15,14},{16,17},{19,... | collective-permute-start | bytes 3145736 | tf_op jit(solution)/shard_map/ppermute | solution.py:38
  24.6 22.5 %collective-permute-start.3 = (f32[1024,256]{1,0:T(8,128)}, f32[1024,256]{1,0:T(8,128)S(1)}, u32[]{:S(2)}, u32[]{:S(2)}) collective-permute-start(f32[1024,256]{1,0:T(8,128)} %collective-permute-done.refs_0_), channel_id=1, source_target_pairs={{1,2},{2,1},{5,6},{6,5},{9,10},{10,9},{13,14},{14,13},{17,18},{18,... | collective-permute-start | bytes 3145736 | tf_op jit(solution)/shard_map/ppermute | solution.py:38
  25.4 27.9 %collective-permute-start.2 = (f32[1024,256]{1,0:T(8,128)}, f32[1024,256]{1,0:T(8,128)}, u32[]{:S(2)}, u32[]{:S(2)}) collective-permute-start(f32[1024,256]{1,0:T(8,128)} %collective-permute-done.1.refs_1_), channel_id=1, source_target_pairs={{1,0},{2,3},{5,4},{6,7},{9,8},{10,11},{13,12},{14,15},{17,16},{18,... | collective-permute-start | bytes 3145736 | tf_op jit(solution)/shard_map/ppermute | solution.py:38
  35.7 22.8 %all-to-all-start = ((f32[16,32,512]{2,1,0:T(8,128)}), f32[16,32,512]{2,1,0:T(8,128)S(1)}, u32[]{:S(2)}, u32[]{:S(2)}) async-start(f32[16,32,512]{2,1,0:T(8,128)} %pad_maximum_fusion), calls=%async_computation | async-start | bytes 2097152 | tf_op jit(solution)/shard_map/all_to_all | solution.py:46
  47.1 1.0 copy-start.2
  48.1 1.0 copy-start
  51.1 13.9 %copy-start.1 = (f32[1024,256]{1,0:T(8,128)S(1)}, f32[1024,256]{1,0:T(8,128)}, u32[]{:S(2)}) copy-start(f32[1024,256]{1,0:T(8,128)} %copy-done) | copy-start | bytes 3145732
  58.5 22.7 %all-to-all-start.1 = ((f32[16,32,512]{2,1,0:T(8,128)}), f32[16,32,512]{2,1,0:T(8,128)S(1)}, u32[]{:S(2)}, u32[]{:S(2)}) async-start(f32[16,32,512]{2,1,0:T(8,128)} %pad_maximum_fusion.1), calls=%async_computation.1 | async-start | bytes 2097152 | tf_op jit(solution)/shard_map/all_to_all | solution.py:46
  65.1 11.8 %collective-permute-start.5 = (f32[512,256]{1,0:T(8,128)S(1)}, f32[512,256]{1,0:T(8,128)S(1)}, u32[]{:S(2)}, u32[]{:S(2)}) collective-permute-start(f32[512,256]{1,0:T(8,128)S(1)} %slice.4), channel_id=1, source_target_pairs={{1,0},{2,3},{5,4},{6,7},{9,8},{10,11},{13,12},{14,15},{17,16},{18,... | collective-permute-start | bytes 1572872 | tf_op jit(solution)/shard_map/ppermute | solution.py:38
  76.9 0.8 copy-start.3
  81.2 15.4 %all-to-all-start.2 = ((f32[16,16,512]{2,1,0:T(8,128)}), f32[16,16,512]{2,1,0:T(8,128)S(1)}, u32[]{:S(2)}, u32[]{:S(2)}) async-start(f32[16,16,512]{2,1,0:T(8,128)} %bitcast.10), calls=%async_computation.2 | async-start | bytes 1048576 | tf_op jit(solution)/shard_map/all_to_all | solution.py:46
  87.8 8.9 %collective-permute-start.6 = (f32[16,512]{1,0:T(8,128)S(1)}, f32[16,512]{1,0:T(8,128)S(1)}, u32[]{:S(2)}, u32[]{:S(2)}) collective-permute-start(f32[16,512]{1,0:T(8,128)S(1)} %get-tuple-element.28), channel_id=1, source_target_pairs={{1,0},{2,3},{5,4},{6,7},{9,8},{10,11},{13,12},{14,15},{17,16},{18,... | collective-permute-start | bytes 98312 | tf_op jit(solution)/shard_map/ppermute | solution.py:38
  96.8 13.8 %collective-permute-start.7 = (f32[4,4,512]{2,1,0:T(4,128)S(1)}, f32[4,4,512]{2,1,0:T(4,128)S(1)}, u32[]{:S(2)}, u32[]{:S(2)}) collective-permute-start(f32[4,4,512]{2,1,0:T(4,128)S(1)} %get-tuple-element.25), channel_id=1, source_target_pairs={{0,12},{1,13},{2,14},{3,15},{4,8},{5,9},{6,10},{7,11},{8,4},{9,5},... | collective-permute-start | bytes 98312 | tf_op jit(solution)/shard_map/ppermute | solution.py:38
  108.0 7.0 %collective-permute-start.8 = (f32[4,4,512]{2,1,0:T(4,128)S(1)}, f32[4,4,512]{2,1,0:T(4,128)S(1)}, u32[]{:S(2)}, u32[]{:S(2)}) collective-permute-start(f32[4,4,512]{2,1,0:T(4,128)S(1)} %get-tuple-element.24), channel_id=1, source_target_pairs={{0,8},{1,9},{2,10},{3,11},{4,12},{5,13},{6,14},{7,15},{8,0},{9,1},... | collective-permute-start | bytes 98312 | tf_op jit(solution)/shard_map/ppermute | solution.py:38
  108.3 6.7 %collective-permute-start.9 = (f32[4,4,512]{2,1,0:T(4,128)S(1)}, f32[4,4,512]{2,1,0:T(4,128)S(1)}, u32[]{:S(2)}, u32[]{:S(2)}) collective-permute-start(f32[4,4,512]{2,1,0:T(4,128)S(1)} %get-tuple-element.23), channel_id=1, source_target_pairs={{0,4},{1,5},{2,6},{3,7},{4,0},{5,1},{6,2},{7,3},{8,12},{9,13},{10,... | collective-permute-start | bytes 98312 | tf_op jit(solution)/shard_map/ppermute | solution.py:38

commit v5 on v3

v5 whole, which is shorter than its diff:
```python
import functools

import jax
import jax.numpy as jnp
from jax import lax
from jax.experimental import pallas as pl
from jax.experimental.pallas import tpu as pltpu
from jax.sharding import PartitionSpec as P


BLOCK = 256
IRREPS = 4
LANES = 128
NY, NX, NZ, NC, NG = 4, 4, 2, 2, 4
AXES = ("blk", "grp")


def blk_index(y, x, z, c):
    return ((y * NX + x) * NZ + z) * NC + c


def every_device():
    for y in range(NY):
        for x in range(NX):
            for z in range(NZ):
                for c in range(NC):
                    for g in range(NG):
                        yield y, x, z, c, g


def permute(value, target):
    pairs = []
    for place in every_device():
        there = target(*place)
        if there is None:
            continue
        pairs.append((blk_index(*place[:4]) * NG + place[4], blk_index(*there[:4]) * NG + there[4]))
    return lax.ppermute(value, AXES, pairs)


def plane_groups():
    return [[blk_index(y, x, z, c) for y in range(NY) for x in range(NX)] for z in range(NZ) for c in range(NC)]


def plane_sum(chip):
    spread = lax.all_to_all(chip, "blk", 0, 0, tiled=True, axis_index_groups=plane_groups())
    return jnp.sum(spread, axis=0)


def pair_swap(y, x, z, c, g):
    return y, x, z, c, g ^ 1


def middle_swap(y, x, z, c, g):
    return (y, x, z, c, 3 - g) if g in (1, 2) else None


def inward(y, x, z, c, g):
    return (y, x, z, c, {0: 1, 3: 2}[g]) if g in (0, 3) else None


def outward(y, x, z, c, g):
    return (y, x, z, c, {1: 0, 2: 3}[g]) if g in (1, 2) else None


def split_kernel(rows, slot_width, scalars, source, *outputs):
    tiles = slot_width // LANES
    group, position = scalars[2 * IRREPS], scalars[2 * IRREPS + 1]
    lane = lax.broadcasted_iota(jnp.int32, (rows, LANES), 1)
    for slot in range(IRREPS):
        irrep = jnp.int32(0)
        for h in range(IRREPS):
            irrep = jnp.where(scalars[h] == (group ^ slot), h, irrep)
        size = scalars[IRREPS + irrep]
        high, low = outputs[2 * slot], outputs[2 * slot + 1]
        for tile in range(tiles):
            first = position * slot_width + tile * LANES
            limit = jnp.where(first // BLOCK < size, size - first % BLOCK, 0)
            value = source[pl.ds(tile * IRREPS + irrep, rows, stride=tiles * IRREPS), :]
            value = jnp.where(lane < limit, value, 0.0)
            rounded = value.astype(jnp.bfloat16)
            place = slice(tile * LANES, (tile + 1) * LANES)
            if slot == IRREPS - 1 and tile >= tiles // 2:
                outputs[-1][:, (tile - tiles // 2) * LANES : (tile + 1 - tiles // 2) * LANES] = value
            high[:, place] = rounded
            low[:, place] = (value - rounded.astype(jnp.float32)).astype(jnp.bfloat16)


def split_rows(amplitudes, scalars):
    pairs, _, slot_width = amplitudes.shape
    rows = 64
    view = amplitudes.reshape(pairs, IRREPS, slot_width // LANES, LANES).transpose(0, 2, 1, 3).reshape(-1, LANES)
    return pl.pallas_call(
        functools.partial(split_kernel, rows, slot_width),
        out_shape=[pltpu.HBM((pairs, slot_width), jnp.bfloat16)] * (2 * IRREPS)
        + [pltpu.HBM((pairs, slot_width // 2), jnp.float32)],
        grid_spec=pltpu.PrefetchScalarGridSpec(
            num_scalar_prefetch=1,
            grid=(pairs // rows,),
            in_specs=[pl.BlockSpec((rows * IRREPS * slot_width // LANES, LANES), lambda i, scalars: (i, 0))],
            out_specs=[pl.BlockSpec((rows, slot_width), lambda i, scalars: (i, 0))] * (2 * IRREPS)
            + [pl.BlockSpec((rows, slot_width // 2), lambda i, scalars: (i, 0))],
        ),
        compiler_params=pltpu.CompilerParams(vmem_limit_bytes=16 << 20),
        cost_estimate=pl.CostEstimate(flops=0, bytes_accessed=8 * pairs * IRREPS * slot_width, transcendentals=0),
        name="split_rows",
    )(scalars, *in_hbm([view]))


PARTS = 4


def halves_of(value):
    rounded = value.astype(jnp.bfloat16)
    return rounded, (value - rounded.astype(jnp.float32)).astype(jnp.bfloat16)


def split_dot(left, right):
    dot = functools.partial(jnp.dot, preferred_element_type=jnp.float32)
    return dot(left[0], right[0]) + (dot(left[0], right[1]) + dot(left[1], right[0]))


def in_hbm(values):
    return [pltpu.with_memory_space_constraint(value, pltpu.HBM) for value in values]


def part_copies(part, sources, here, sems):
    slab, high, low = sources
    slab_here, high_here, low_here = here
    depth = high.shape[1] // PARTS
    place = pl.ds(part * depth, depth)
    return [
        pltpu.make_async_copy(slab.at[place, :], slab_here.at[place, :], sems.at[part, 0]),
        pltpu.make_async_copy(high.at[:, place], high_here.at[:, place], sems.at[part, 1]),
        pltpu.make_async_copy(low.at[:, place], low_here.at[:, place], sems.at[part, 2]),
    ]


def start_parts(parts, sources, here, sems):
    for part in parts:
        for copy in part_copies(part, sources, here, sems):
            copy.start()


def add_parts(parts, sources, here, sems, total):
    slab_here, high_here, low_here = here
    depth = high_here.shape[1] // PARTS
    for part in parts:
        for copy in part_copies(part, sources, here, sems):
            copy.wait()
        place = pl.ds(part * depth, depth)
        term = split_dot((high_here[:, place], low_here[:, place]), halves_of(slab_here[place, :]))
        total[...] = term if part == 0 else total[...] + term


def is_end(scalars):
    group = scalars[2 * IRREPS]
    return (group == 0) | (group == NG - 1)


def put_halves(scalars, total, kept, sent, index):
    groups, width, half = kept.shape[0], kept.shape[1] // 2, kept.shape[2]
    core = scalars[2 * IRREPS + 1] % NC
    for out, which in ((sent, 1 - core), (kept, core)):
        rows = total[pl.ds(pl.multiple_of(which * half, half), half), :]
        out[:, index * width : (index + 1) * width, :] = rows.T.reshape(groups, width, half)


def first_kernel(scalars, own, near, high_0, low_0, high_1, low_1, kept, sent, slabs, highs, lows, total, sems):
    sources = ((own, high_0, low_0), (near, high_1, low_1))
    here = [(slabs.at[k], highs.at[k], lows.at[k]) for k in range(2)]
    for k in range(2):
        start_parts(range(PARTS), sources[k], here[k], sems.at[k])
    for k in range(2):
        add_parts(range(PARTS), sources[k], here[k], sems.at[k], total)
        put_halves(scalars, total, kept, sent, k)


def second_kernel(
    scalars, passed, crossed, guests, high, low, kept, sent, slab, high_here, low_here, guest_slab, rows, total, sems, guest_sems
):
    depth = rows.shape[1]
    here = (slab, high_here, low_here)
    ends = is_end(scalars)
    pl.when(ends)(lambda: start_parts(range(PARTS), (passed, high, low), here, sems))
    pl.when(jnp.logical_not(ends))(lambda: start_parts(range(PARTS), (crossed, high, low), here, sems))
    guest_copies = [
        pltpu.make_async_copy(crossed.at[pl.ds(depth, depth), :], guest_slab, guest_sems.at[0]),
        pltpu.make_async_copy(guests, rows, guest_sems.at[1]),
    ]
    for copy in guest_copies:
        copy.start()
    add_parts(range(PARTS), (crossed, high, low), here, sems, total)
    put_halves(scalars, total, kept, sent, 0)
    for copy in guest_copies:
        copy.wait()
    total[...] = split_dot(halves_of(rows[...]), halves_of(guest_slab[...]))
    put_halves(scalars, total, kept, sent, 1)


def last_kernel(scalars, far, middle, high, low, out, slab, high_here, low_here, total, sems):
    here = (slab, high_here, low_here)
    ends = is_end(scalars)
    inner = jnp.logical_not(ends)
    front, back = range(PARTS // 2), range(PARTS // 2, PARTS)
    pl.when(ends)(lambda: start_parts(front, (far, high, low), here, sems))
    pl.when(inner)(lambda: start_parts(range(PARTS), (middle, high, low), here, sems))
    add_parts(front, (middle, high, low), here, sems, total)
    pl.when(inner)(lambda: add_parts(back, (middle, high, low), here, sems, total))
    out[...] = total[...].T.reshape(out.shape)


def call_product(kernel, scalars, slabs, split, out_shapes, scratch, terms):
    count = len(out_shapes)
    vmem = pl.BlockSpec(memory_space=pltpu.VMEM)
    return pl.pallas_call(
        kernel,
        out_shape=[jax.ShapeDtypeStruct(shape, jnp.float32) for shape in out_shapes],
        in_specs=[pl.BlockSpec(memory_space=pltpu.SMEM)] + [pl.BlockSpec(memory_space=pl.ANY)] * (len(slabs) + len(split)),
        out_specs=[vmem] * count,
        scratch_shapes=scratch,
        compiler_params=pltpu.CompilerParams(vmem_limit_bytes=16 << 20),
        cost_estimate=pl.CostEstimate(flops=6 * terms, bytes_accessed=6 << 20, transcendentals=0),
    )(scalars, *slabs, *in_hbm(split))


def finish_kernel(column_width, scalars, *refs):
    parts, out = refs[:-1], refs[-1]
    half = parts[0].shape[2]
    group, position = scalars[2 * IRREPS], scalars[2 * IRREPS + 1]
    core = position % NC
    column = position * column_width + lax.broadcasted_iota(jnp.int32, parts[0].shape[1:], 0)
    for irrep in range(IRREPS):
        slot = scalars[irrep] ^ group
        size = scalars[IRREPS + irrep]
        valid = (column // BLOCK < size) & (column % BLOCK < size)
        mine = parts[0][slot] + parts[2][slot]
        other = parts[1][slot] + parts[3][slot]
        for k in range(NC):
            both = (parts[0][IRREPS + k] + parts[2][IRREPS + k]) + (parts[1][IRREPS + k] + parts[3][IRREPS + k])
            value = jnp.where(core == k, mine, other) + jnp.where(slot == IRREPS - 1, both, 0.0)
            out[irrep, :, k * half : (k + 1) * half] = jnp.where(valid, value, 0.0)


def finish(scalars, parts):
    _, column_width, half = parts[0].shape
    vmem = pl.BlockSpec(memory_space=pltpu.VMEM)
    return pl.pallas_call(
        functools.partial(finish_kernel, column_width),
        out_shape=jax.ShapeDtypeStruct((IRREPS, column_width, NC * half), jnp.float32),
        in_specs=[pl.BlockSpec(memory_space=pltpu.SMEM)] + [vmem] * len(parts),
        out_specs=vmem,
        compiler_params=pltpu.CompilerParams(vmem_limit_bytes=4 << 20),
        name="finish",
    )(scalars, *parts)


def local(amplitudes, integrals, irrep_sizes, owner_map):
    pairs, _, slots = amplitudes.shape
    rows, columns = integrals.shape[1:]
    column_width = columns // lax.axis_size("blk")
    plane = NY * NX
    width = columns // plane
    half = pairs // NC
    position = lax.axis_index("blk")
    group = lax.axis_index("grp")
    core = position % NC
    z_part = (position // NC) % NZ

    own = integrals[0]
    near = permute(own, pair_swap)
    middle = permute(own, middle_swap)
    scalars = jnp.concatenate([owner_map, irrep_sizes, jnp.stack([group, position])])
    *split, moved = split_rows(amplitudes, scalars)
    guests = permute(moved, inward)
    crossed = permute(near, middle_swap)
    passed = permute(middle, outward)
    far = permute(crossed[: rows // 2], outward)

    matrix = pltpu.VMEM((pairs, slots), jnp.bfloat16)
    slab = pltpu.VMEM((rows, columns), jnp.float32)
    total = pltpu.VMEM((pairs, columns), jnp.float32)
    sems = pltpu.SemaphoreType.DMA((PARTS, 3))
    terms = pairs * columns * slots
    joint = [(plane, 2 * width, half)] * 2

    def chip_sum(kept, sent):
        return kept + permute(sent, lambda y, x, z, c, g: (y, x, z, 1 - c, g))

    scratch = [
        pltpu.VMEM((2, rows, columns), jnp.float32),
        pltpu.VMEM((2, pairs, slots), jnp.bfloat16),
        pltpu.VMEM((2, pairs, slots), jnp.bfloat16),
        total,
        pltpu.SemaphoreType.DMA((2, PARTS, 3)),
    ]
    result = call_product(first_kernel, scalars, [own, near], split[:4], joint, scratch, 2 * terms)
    first_chip = chip_sum(*result)
    first = plane_sum(first_chip)
    scratch = [
        slab,
        matrix,
        matrix,
        pltpu.VMEM((rows // 2, columns), jnp.float32),
        pltpu.VMEM((pairs, slots // 2), jnp.float32),
        total,
        sems,
        pltpu.SemaphoreType.DMA((2,)),
    ]
    result = call_product(second_kernel, scalars, [passed, crossed, guests], split[4:6], joint, scratch, 2 * terms)
    second_chip = chip_sum(*result)
    second = plane_sum(second_chip)
    scratch = [slab, matrix, matrix, total, sems]
    (result,) = call_product(last_kernel, scalars, [far, middle], split[6:], [(plane, width, pairs)], scratch, terms)
    third = plane_sum(result)
    third = third.reshape(width, NC, half).swapaxes(0, 1)
    handed = permute(second[width:], outward)
    units = jnp.concatenate([first.reshape(2, width, half), second[None, :width], handed[None], third], axis=0)
    units = units.reshape(-1, NZ * NC, column_width, half)

    def share(flip):
        here = (z_part * NC + core) ^ flip
        return lax.dynamic_index_in_dim(units, here, 1, keepdims=False)

    parts = [share(0)] + [None] * 3
    for flip in (3, 2, 1):
        parts[flip] = permute(share(flip), lambda y, x, z, c, g: (y, x, z ^ (flip >> 1), c ^ (flip & 1), g))
    return jnp.transpose(finish(scalars, parts), (2, 0, 1))


def solution(mesh):
    in_specs = (P("grp", None, "blk"), P("grp", "blk", None), P(), P())
    out_specs = P("grp", None, "blk")
    return jax.shard_map(local, mesh=mesh, in_specs=in_specs, out_specs=out_specs, check_vma=False)
```

time: 131 us -> 125 us (0.954)
  Pallas kernels: 23.4 us -> 28.7 us
  starting transfers between devices: 44 us -> 39.8 us
  local copies, waits for them, and re-layouts: 7.03 us -> 2.97 us
  waiting for transfers between devices: 52.2 us -> 48.5 us
    ppermute x13 -> x12, waiting for transfers between devices: 44.6 us -> 31.8 us  [permute(): return lax.ppermute(value, AXES, pairs)]
    all_to_all x3, waiting for transfers between devices: 7.59 us -> 16.7 us  [plane_sum(): lax.all_to_all(chip, 'blk', 0, 0, tiled=True, axis_index_groups=plane_gro...]
    all_to_all x3, starting transfers between devices: 20.4 us -> 14.6 us  [plane_sum(): lax.all_to_all(chip, 'blk', 0, 0, tiled=True, axis_index_groups=plane_gro...]
    pallas_call x1, Pallas kernels: 7.17 us -> 12.6 us  [split_rows(): pl.pallas_call(functools.partial(split_kernel, rows, slot_width), out_sha...]
    unnamed x12 -> x7, local copies, waits for them, and re-layouts: 4.62 us -> 0.99 us
    add x0 -> x2, other arithmetic: none -> 2.81 us  [chip_sum(): return kept + permute(sent, lambda y, x, z, c, g: (y, x, z, 1 - c, g))]
    ppermute x13 -> x12, starting transfers between devices: 23.7 us -> 25.3 us  [permute(): return lax.ppermute(value, AXES, pairs)]
    pallas_call x5 -> x4, Pallas kernels: 16.2 us -> 16.1 us  [the longest x3 14.9 us: call_product(): pl.pallas_call(kernel, out_shape=[jax.ShapeDtypeStruct(shape, jnp.float32...]
  transfers between devices with their start and end apart: 16 -> 15, of which waited for: 7 -> 9; matrix products, arithmetic and copies ran while one was open for 2% -> 5% of each run, Pallas kernels for 17% -> 22%
where the time goes in v5:
time: 125 us; the launch traced here: 124 us
  waiting for transfers between devices  48.5 us (39%)
  starting transfers between devices  39.8 us (32%)
  Pallas kernels  28.7 us (23%)
  other arithmetic  3.66 us (3%)
  local copies, waits for them, and re-layouts  2.97 us (2%)
    ppermute x12, waiting for transfers between devices, permute(): return lax.ppermute(value, AXES, pairs)  31.8 us
    ppermute x12, starting transfers between devices, permute(): return lax.ppermute(value, AXES, pairs)  25.3 us
    all_to_all x3, waiting for transfers between devices, plane_sum(): lax.all_to_all(chip, 'blk', 0, 0, tiled=True, axis_index_groups=plane_gro...  16.7 us
    pallas_call x3, Pallas kernels, call_product(): pl.pallas_call(kernel, out_shape=[jax.ShapeDtypeStruct(shape, jnp.float32...  14.9 us
    all_to_all x3, starting transfers between devices, plane_sum(): lax.all_to_all(chip, 'blk', 0, 0, tiled=True, axis_index_groups=plane_gro...  14.6 us
    pallas_call x1, Pallas kernels, split_rows(): pl.pallas_call(functools.partial(split_kernel, rows, slot_width), out_sha...  12.6 us
    add x2, other arithmetic, chip_sum(): return kept + permute(sent, lambda y, x, z, c, g: (y, x, z, 1 - c, g))  2.81 us
  transfers between devices with their start and end apart: 15, of which 9 were waited for; matrix products, arithmetic and copies ran while one was open for 5% of the time, Pallas kernels for 22%

profile of v5, /device:TPU:1, one launch (start us, length us, event | category | flops | bytes accessed | tf_op | source)
XLA Modules:
  0.0 124.0 jit_solution(12725607616572106758)
XLA Ops:
  0.0 0.0 copy-start
  0.0 0.8 collective-permute-start.2
  0.9 5.4 %collective-permute-start = (f32[1024,256]{1,0:T(8,128)}, f32[1024,256]{1,0:T(8,128)S(1)}, u32[]{:S(2)}, u32[]{:S(2)}) collective-permute-start(f32[1024,256]{1,0:T(8,128)} %bitcast.21), channel_id=1, source_target_pairs={{0,1},{1,0},{2,3},{3,2},{4,5},{5,4},{6,7},{7,6},{8,9},{9,8},{10,11... | collective-permute-start | bytes 3145736 | tf_op jit(solution)/shard_map/ppermute | solution.py:38
  6.2 0.7 pad_add_fusion.scalars
  7.0 12.6 %split_rows.1 = (bf16[512,1024]{1,0:T(8,128)(2,1)}, bf16[512,1024]{1,0:T(8,128)(2,1)}, bf16[512,1024]{1,0:T(8,128)(2,1)}, bf16[512,1024]{1,0:T(8,128)(2,1)}, bf1...) custom-call(s32[10]{0:T(128)S(1)} %pad_add_fusion.scalars, ...), custom_call_target="tpu_custom_call" | custom-call | bytes 16777216 | tf_op jit(solution)/shard_map/split_rows/pallas_call | solution.py:93
  19.6 2.0 %collective-permute-start.5 = (f32[512,512]{1,0:T(8,128)}, f32[512,512]{1,0:T(8,128)S(1)}, u32[]{:S(2)}, u32[]{:S(2)}) collective-permute-start(f32[512,512]{1,0:T(8,128)} %get-tuple-element.24), channel_id=1, source_target_pairs={{0,1},{3,2},{4,5},{7,6},{8,9},{11,10},{12,13},{15,14},{16,17},{19,... | collective-permute-start | bytes 3145736 | tf_op jit(solution)/shard_map/ppermute | solution.py:38
  21.6 0.0 collective-permute-done.2.middle
  21.6 1.3 %collective-permute-start.3 = (f32[1024,256]{1,0:T(8,128)S(1)}, f32[1024,256]{1,0:T(8,128)S(1)}, u32[]{:S(2)}, u32[]{:S(2)}) collective-permute-start(f32[1024,256]{1,0:T(8,128)S(1)} %collective-permute-done.2.middle), channel_id=1, source_target_pairs={{1,0},{2,3},{5,4},{6,7},{9,8},{10,11},{13,12},{14,15},{17,16},{18,... | collective-permute-start | bytes 3145736 | tf_op jit(solution)/shard_map/ppermute | solution.py:38
  22.9 6.1 %collective-permute-done.near = f32[1024,256]{1,0:T(8,128)S(1)} collective-permute-done((f32[1024,256]{1,0:T(8,128)}, f32[1024,256]{1,0:T(8,128)S(1)}, u32[]{:S(2)}, u32[]{:S(2)}) %collective-permute-start) | collective-permute-done | bytes 1048608 | tf_op jit(solution)/shard_map/ppermute | solution.py:38
  29.0 0.7 collective-permute-start.4
  29.7 0.0 copy-done
  29.7 6.0 %shard_map.46 = (f32[16,32,256]{2,1,0:T(8,128)S(1)}, f32[16,32,256]{2,1,0:T(8,128)S(1)}) custom-call(s32[10]{0:T(128)S(1)} %pad_add_fusion.scalars, f32[1024,256]{1,0:T(8,128)S(1)} %bitcast.22, f32[1024,256]{1,0:T(8,128)S(1)} %collective-permute-done.near, bf16[512,1024]{1,0:T(8,128)(2,1)} %get-tuple-element.18.high_0, ...), custom_call_target="tpu_custom_call" | custom-call | flops 1610612736 | bytes 6291456 | tf_op jit(solution)/shard_map/pallas_call | solution.py:216
  35.8 2.4 %collective-permute-start.1 = (f32[16,32,256]{2,1,0:T(8,128)S(1)}, f32[16,32,256]{2,1,0:T(8,128)S(1)}, u32[]{:S(2)}, u32[]{:S(2)}) collective-permute-start(f32[16,32,256]{2,1,0:T(8,128)S(1)} %get-tuple-element.23), channel_id=1, source_target_pairs={{0,4},{1,5},{2,6},{3,7},{4,0},{5,1},{6,2},{7,3},{8,12},{9,13},{10,... | collective-permute-start | bytes 1572872 | tf_op jit(solution)/shard_map/ppermute | solution.py:38
  38.1 12.4 %collective-permute-done.5.guests = f32[512,512]{1,0:T(8,128)S(1)} collective-permute-done((f32[512,512]{1,0:T(8,128)}, f32[512,512]{1,0:T(8,128)S(1)}, u32[]{:S(2)}, u32[]{:S(2)}) %collective-permute-start.5) | collective-permute-done | bytes 1048608 | tf_op jit(solution)/shard_map/ppermute | solution.py:38
  50.6 2.0 %collective-permute-done.3.passed = f32[1024,256]{1,0:T(8,128)S(1)} collective-permute-done((f32[1024,256]{1,0:T(8,128)S(1)}, f32[1024,256]{1,0:T(8,128)S(1)}, u32[]{:S(2)}, u32[]{:S(2)}) %collective-permute-start.3) | collective-permute-done | bytes 1048608 | tf_op jit(solution)/shard_map/ppermute | solution.py:38
  52.5 0.0 collective-permute-done.4.crossed
  52.5 5.1 %shard_map.47 = (f32[16,32,256]{2,1,0:T(8,128)S(1)}, f32[16,32,256]{2,1,0:T(8,128)S(1)}) custom-call(s32[10]{0:T(128)S(1)} %pad_add_fusion.scalars, f32[1024,256]{1,0:T(8,128)S(1)} %collective-permute-done.3.passed, f32[1024,256]{1,0:T(8,128)S(1)} %collective-permute-done.4.crossed, f32[512,512]{1,0:T(8,128)S(1)} %collective-permute-done.5.guests, ...), custom_call_target="tpu_custom_call" | custom-call | flops 1610612736 | bytes 6291456 | tf_op jit(solution)/shard_map/pallas_call | solution.py:216
  57.7 0.0 copy-start.1
  57.7 1.0 copy-done.1
  58.6 1.9 %collective-permute-start.6 = (f32[16,32,256]{2,1,0:T(8,128)S(1)}, f32[16,32,256]{2,1,0:T(8,128)}, u32[]{:S(2)}, u32[]{:S(2)}) collective-permute-start(f32[16,32,256]{2,1,0:T(8,128)S(1)} %get-tuple-element.28), channel_id=1, source_target_pairs={{0,4},{1,5},{2,6},{3,7},{4,0},{5,1},{6,2},{7,3},{8,12},{9,13},{10,... | collective-permute-start | bytes 1572872 | tf_op jit(solution)/shard_map/ppermute | solution.py:38
  60.5 0.0 collective-permute-done.1
  60.6 0.9 add.33
  61.4 6.8 %all-to-all-start = ((f32[16,32,256]{2,1,0:T(8,128)}), f32[16,32,256]{2,1,0:T(8,128)S(1)}, u32[]{:S(2)}, u32[]{:S(2)}) async-start(f32[16,32,256]{2,1,0:T(8,128)} %add.33), calls=%async_computation | async-start | bytes 1048576 | tf_op jit(solution)/shard_map/all_to_all | solution.py:46
  68.2 1.9 %slice.14 = f32[512,256]{1,0:T(8,128)} slice(f32[1024,256]{1,0:T(8,128)} %copy-done.1), slice={[0:512], [0:256]} | slice | bytes 1048576 | tf_op jit(solution)/shard_map/slice | solution.py:278
  70.1 1.3 %collective-permute-start.8 = (f32[512,256]{1,0:T(8,128)}, f32[512,256]{1,0:T(8,128)S(1)}, u32[]{:S(2)}, u32[]{:S(2)}) collective-permute-start(f32[512,256]{1,0:T(8,128)} %slice.14), channel_id=1, source_target_pairs={{1,0},{2,3},{5,4},{6,7},{9,8},{10,11},{13,12},{14,15},{17,16},{18,... | collective-permute-start | bytes 1572872 | tf_op jit(solution)/shard_map/ppermute | solution.py:38
  71.4 0.0 collective-permute-done.6
  71.4 1.9 %add.34 = f32[16,32,256]{2,1,0:T(8,128)} add(f32[16,32,256]{2,1,0:T(8,128)S(1)} %get-tuple-element.27, f32[16,32,256]{2,1,0:T(8,128)} %collective-permute-done.6) | non-fusion elementwise | flops 131072 | bytes 1572864 | tf_op jit(solution)/shard_map/add | solution.py:288
  73.3 5.9 %all-to-all-done = f32[16,32,256]{2,1,0:T(8,128)S(1)} async-done(((f32[16,32,256]{2,1,0:T(8,128)}), f32[16,32,256]{2,1,0:T(8,128)S(1)}, u32[]{:S(2)}, u32[]{:S(2)}) %all-to-all-start) | async-done | bytes 524320 | tf_op jit(solution)/shard_map/all_to_all | solution.py:46
  79.2 3.6 %all-to-all-start.1 = ((f32[16,32,256]{2,1,0:T(8,128)}), f32[16,32,256]{2,1,0:T(8,128)S(1)}, u32[]{:S(2)}, u32[]{:S(2)}) async-start(f32[16,32,256]{2,1,0:T(8,128)} %add.34), calls=%async_computation.1 | async-start | bytes 1048576 | tf_op jit(solution)/shard_map/all_to_all | solution.py:46
  82.8 4.2 %collective-permute-done.8.far = f32[512,256]{1,0:T(8,128)S(1)} collective-permute-done((f32[512,256]{1,0:T(8,128)}, f32[512,256]{1,0:T(8,128)S(1)}, u32[]{:S(2)}, u32[]{:S(2)}) %collective-permute-start.8) | collective-permute-done | bytes 524320 | tf_op jit(solution)/shard_map/ppermute | solution.py:38
  87.0 3.8 %shard_map.48 = f32[16,16,512]{2,1,0:T(8,128)} custom-call(s32[10]{0:T(128)S(1)} %pad_add_fusion.scalars, f32[512,256]{1,0:T(8,128)S(1)} %collective-permute-done.8.far, f32[1024,256]{1,0:T(8,128)S(1)} %collective-permute-done.2.middle, bf16[512,1024]{1,0:T(8,128)(2,1)} %get-tuple-element.29.high, bf16[512,1024]{1,0:T(8,128)(2,1)} %get-tuple-element.30.low), custom_call_target="tpu_custom_call" | custom-call | flops 805306368 | bytes 6291456 | tf_op jit(solution)/shard_map/pallas_call | solution.py:216
  90.9 2.2 %all-to-all-done.1 = f32[16,32,256]{2,1,0:T(8,128)S(1)} async-done(((f32[16,32,256]{2,1,0:T(8,128)}), f32[16,32,256]{2,1,0:T(8,128)S(1)}, u32[]{:S(2)}, u32[]{:S(2)}) %all-to-all-start.1) | async-done | bytes 524320 | tf_op jit(solution)/shard_map/all_to_all | solution.py:46
  93.0 4.2 %all-to-all-start.2 = ((f32[16,16,512]{2,1,0:T(8,128)}), f32[16,16,512]{2,1,0:T(8,128)S(1)}, u32[]{:S(2)}, u32[]{:S(2)}) async-start(f32[16,16,512]{2,1,0:T(8,128)} %shard_map.48), calls=%async_computation.2 | async-start | bytes 1048576 | tf_op jit(solution)/shard_map/all_to_all | solution.py:46
  97.5 1.3 %collective-permute-start.7 = (f32[16,256]{1,0:T(8,128)S(1)}, f32[16,256]{1,0:T(8,128)S(1)}, u32[]{:S(2)}, u32[]{:S(2)}) collective-permute-start(f32[16,256]{1,0:T(8,128)S(1)} %get-tuple-element.35), channel_id=1, source_target_pairs={{1,0},{2,3},{5,4},{6,7},{9,8},{10,11},{13,12},{14,15},{17,16},{18,... | collective-permute-start | bytes 49160 | tf_op jit(solution)/shard_map/ppermute | solution.py:38
  98.8 8.6 %all-to-all-done.2 = f32[16,16,512]{2,1,0:T(8,128)S(1)} async-done(((f32[16,16,512]{2,1,0:T(8,128)}), f32[16,16,512]{2,1,0:T(8,128)S(1)}, u32[]{:S(2)}, u32[]{:S(2)}) %all-to-all-start.2) | async-done | bytes 524320 | tf_op jit(solution)/shard_map/all_to_all | solution.py:46
  107.4 0.0 collective-permute-done.7
  107.5 2.5 %collective-permute-start.9 = (f32[6,4,256]{2,1,0:T(4,128)S(1)}, f32[6,4,256]{2,1,0:T(4,128)S(1)}, u32[]{:S(2)}, u32[]{:S(2)}) collective-permute-start(f32[6,4,256]{2,1,0:T(4,128)S(1)} %get-tuple-element.33), channel_id=1, source_target_pairs={{0,4},{1,5},{2,6},{3,7},{4,0},{5,1},{6,2},{7,3},{8,12},{9,13},{10,... | collective-permute-start | bytes 73736 | tf_op jit(solution)/shard_map/ppermute | solution.py:38
  110.0 5.6 %collective-permute-start.10 = (f32[6,4,256]{2,1,0:T(4,128)S(1)}, f32[6,4,256]{2,1,0:T(4,128)S(1)}, u32[]{:S(2)}, u32[]{:S(2)}) collective-permute-start(f32[6,4,256]{2,1,0:T(4,128)S(1)} %get-tuple-element.32), channel_id=1, source_target_pairs={{0,8},{1,9},{2,10},{3,11},{4,12},{5,13},{6,14},{7,15},{8,0},{9,1},... | collective-permute-start | bytes 73736 | tf_op jit(solution)/shard_map/ppermute | solution.py:38
  115.6 0.1 collective-permute-start.11
  115.7 0.0 collective-permute-done.9.refs_1_
  115.7 1.1 collective-permute-done.10.refs_2_
  116.9 5.9 %collective-permute-done.11.refs_3_ = f32[6,4,256]{2,1,0:T(4,128)S(1)} collective-permute-done((f32[6,4,256]{2,1,0:T(4,128)S(1)}, f32[6,4,256]{2,1,0:T(4,128)S(1)}, u32[]{:S(2)}, u32[]{:S(2)}) %collective-permute-start.11) | collective-permute-done | bytes 24608 | tf_op jit(solution)/shard_map/ppermute | solution.py:38
  122.8 1.2 finish.1
  (13 shorter events, 0.2 us)
Async XLA Ops:
  0.0 29.7 %copy-start = (f32[1,1024,256]{2,1,0:T(8,128)S(1)}, f32[1,1024,256]{2,1,0:T(8,128)}, u32[]{:S(2)}) copy-start(f32[1,1024,256]{2,1,0:T(8,128)} %param.5) | copy-start | bytes 3145732
  0.0 21.6 %collective-permute-start.2 = (f32[1024,256]{1,0:T(8,128)}, f32[1024,256]{1,0:T(8,128)S(1)}, u32[]{:S(2)}, u32[]{:S(2)}) collective-permute-start(f32[1024,256]{1,0:T(8,128)} %bitcast.20), channel_id=1, source_target_pairs={{1,2},{2,1},{5,6},{6,5},{9,10},{10,9},{13,14},{14,13},{17,18},{18,... | collective-permute-start | bytes 3145736 | tf_op jit(solution)/shard_map/ppermute | solution.py:38
  0.9 28.2 %collective-permute-start = (f32[1024,256]{1,0:T(8,128)}, f32[1024,256]{1,0:T(8,128)S(1)}, u32[]{:S(2)}, u32[]{:S(2)}) collective-permute-start(f32[1024,256]{1,0:T(8,128)} %bitcast.21), channel_id=1, source_target_pairs={{0,1},{1,0},{2,3},{3,2},{4,5},{5,4},{6,7},{7,6},{8,9},{9,8},{10,11... | collective-permute-start | bytes 3145736 | tf_op jit(solution)/shard_map/ppermute | solution.py:38
  19.6 31.0 %collective-permute-start.5 = (f32[512,512]{1,0:T(8,128)}, f32[512,512]{1,0:T(8,128)S(1)}, u32[]{:S(2)}, u32[]{:S(2)}) collective-permute-start(f32[512,512]{1,0:T(8,128)} %get-tuple-element.24), channel_id=1, source_target_pairs={{0,1},{3,2},{4,5},{7,6},{8,9},{11,10},{12,13},{15,14},{16,17},{19,... | collective-permute-start | bytes 3145736 | tf_op jit(solution)/shard_map/ppermute | solution.py:38
  21.6 30.9 %collective-permute-start.3 = (f32[1024,256]{1,0:T(8,128)S(1)}, f32[1024,256]{1,0:T(8,128)S(1)}, u32[]{:S(2)}, u32[]{:S(2)}) collective-permute-start(f32[1024,256]{1,0:T(8,128)S(1)} %collective-permute-done.2.middle), channel_id=1, source_target_pairs={{1,0},{2,3},{5,4},{6,7},{9,8},{10,11},{13,12},{14,15},{17,16},{18,... | collective-permute-start | bytes 3145736 | tf_op jit(solution)/shard_map/ppermute | solution.py:38
  29.0 23.5 %collective-permute-start.4 = (f32[1024,256]{1,0:T(8,128)S(1)}, f32[1024,256]{1,0:T(8,128)S(1)}, u32[]{:S(2)}, u32[]{:S(2)}) collective-permute-start(f32[1024,256]{1,0:T(8,128)S(1)} %collective-permute-done.near), channel_id=1, source_target_pairs={{1,2},{2,1},{5,6},{6,5},{9,10},{10,9},{13,14},{14,13},{17,18},{18,... | collective-permute-start | bytes 3145736 | tf_op jit(solution)/shard_map/ppermute | solution.py:38
  35.8 24.8 %collective-permute-start.1 = (f32[16,32,256]{2,1,0:T(8,128)S(1)}, f32[16,32,256]{2,1,0:T(8,128)S(1)}, u32[]{:S(2)}, u32[]{:S(2)}) collective-permute-start(f32[16,32,256]{2,1,0:T(8,128)S(1)} %get-tuple-element.23), channel_id=1, source_target_pairs={{0,4},{1,5},{2,6},{3,7},{4,0},{5,1},{6,2},{7,3},{8,12},{9,13},{10,... | collective-permute-start | bytes 1572872 | tf_op jit(solution)/shard_map/ppermute | solution.py:38
  57.7 1.0 copy-start.1
  58.6 12.7 %collective-permute-start.6 = (f32[16,32,256]{2,1,0:T(8,128)S(1)}, f32[16,32,256]{2,1,0:T(8,128)}, u32[]{:S(2)}, u32[]{:S(2)}) collective-permute-start(f32[16,32,256]{2,1,0:T(8,128)S(1)} %get-tuple-element.28), channel_id=1, source_target_pairs={{0,4},{1,5},{2,6},{3,7},{4,0},{5,1},{6,2},{7,3},{8,12},{9,13},{10,... | collective-permute-start | bytes 1572872 | tf_op jit(solution)/shard_map/ppermute | solution.py:38
  61.4 17.8 %all-to-all-start = ((f32[16,32,256]{2,1,0:T(8,128)}), f32[16,32,256]{2,1,0:T(8,128)S(1)}, u32[]{:S(2)}, u32[]{:S(2)}) async-start(f32[16,32,256]{2,1,0:T(8,128)} %add.33), calls=%async_computation | async-start | bytes 1048576 | tf_op jit(solution)/shard_map/all_to_all | solution.py:46
  70.1 16.9 %collective-permute-start.8 = (f32[512,256]{1,0:T(8,128)}, f32[512,256]{1,0:T(8,128)S(1)}, u32[]{:S(2)}, u32[]{:S(2)}) collective-permute-start(f32[512,256]{1,0:T(8,128)} %slice.14), channel_id=1, source_target_pairs={{1,0},{2,3},{5,4},{6,7},{9,8},{10,11},{13,12},{14,15},{17,16},{18,... | collective-permute-start | bytes 1572872 | tf_op jit(solution)/shard_map/ppermute | solution.py:38
  79.2 13.8 %all-to-all-start.1 = ((f32[16,32,256]{2,1,0:T(8,128)}), f32[16,32,256]{2,1,0:T(8,128)S(1)}, u32[]{:S(2)}, u32[]{:S(2)}) async-start(f32[16,32,256]{2,1,0:T(8,128)} %add.34), calls=%async_computation.1 | async-start | bytes 1048576 | tf_op jit(solution)/shard_map/all_to_all | solution.py:46
  93.0 14.4 %all-to-all-start.2 = ((f32[16,16,512]{2,1,0:T(8,128)}), f32[16,16,512]{2,1,0:T(8,128)S(1)}, u32[]{:S(2)}, u32[]{:S(2)}) async-start(f32[16,16,512]{2,1,0:T(8,128)} %shard_map.48), calls=%async_computation.2 | async-start | bytes 1048576 | tf_op jit(solution)/shard_map/all_to_all | solution.py:46
  97.5 10.0 %collective-permute-start.7 = (f32[16,256]{1,0:T(8,128)S(1)}, f32[16,256]{1,0:T(8,128)S(1)}, u32[]{:S(2)}, u32[]{:S(2)}) collective-permute-start(f32[16,256]{1,0:T(8,128)S(1)} %get-tuple-element.35), channel_id=1, source_target_pairs={{1,0},{2,3},{5,4},{6,7},{9,8},{10,11},{13,12},{14,15},{17,16},{18,... | collective-permute-start | bytes 49160 | tf_op jit(solution)/shard_map/ppermute | solution.py:38
  107.5 8.2 %collective-permute-start.9 = (f32[6,4,256]{2,1,0:T(4,128)S(1)}, f32[6,4,256]{2,1,0:T(4,128)S(1)}, u32[]{:S(2)}, u32[]{:S(2)}) collective-permute-start(f32[6,4,256]{2,1,0:T(4,128)S(1)} %get-tuple-element.33), channel_id=1, source_target_pairs={{0,4},{1,5},{2,6},{3,7},{4,0},{5,1},{6,2},{7,3},{8,12},{9,13},{10,... | collective-permute-start | bytes 73736 | tf_op jit(solution)/shard_map/ppermute | solution.py:38
  110.0 6.9 %collective-permute-start.10 = (f32[6,4,256]{2,1,0:T(4,128)S(1)}, f32[6,4,256]{2,1,0:T(4,128)S(1)}, u32[]{:S(2)}, u32[]{:S(2)}) collective-permute-start(f32[6,4,256]{2,1,0:T(4,128)S(1)} %get-tuple-element.32), channel_id=1, source_target_pairs={{0,8},{1,9},{2,10},{3,11},{4,12},{5,13},{6,14},{7,15},{8,0},{9,1},... | collective-permute-start | bytes 73736 | tf_op jit(solution)/shard_map/ppermute | solution.py:38
  115.6 7.2 %collective-permute-start.11 = (f32[6,4,256]{2,1,0:T(4,128)S(1)}, f32[6,4,256]{2,1,0:T(4,128)S(1)}, u32[]{:S(2)}, u32[]{:S(2)}) collective-permute-start(f32[6,4,256]{2,1,0:T(4,128)S(1)} %get-tuple-element.31), channel_id=1, source_target_pairs={{0,12},{1,13},{2,14},{3,15},{4,8},{5,9},{6,10},{7,11},{8,4},{9,5},... | collective-permute-start | bytes 73736 | tf_op jit(solution)/shard_map/ppermute | solution.py:38

commit v6 on v5

--- a/solution.py
+++ b/solution.py
@@ -45,6 +45,20 @@
 def plane_sum(chip):
     spread = lax.all_to_all(chip, "blk", 0, 0, tiled=True, axis_index_groups=plane_groups())
     return jnp.sum(spread, axis=0)
+
+
+def staged_sum(chip, position):
+    y, x = position // (NX * NZ * NC), (position // (NZ * NC)) % NX
+
+    def stage(value, place, count, target):
+        def block(step):
+            return lax.dynamic_index_in_dim(value, (place + step) % count, 0, keepdims=False)
+
+        arrived = [permute(block(step), functools.partial(target, step)) for step in (2, 1, 3)]
+        return block(0) + ((arrived[1] + arrived[2]) + arrived[0])
+
+    rows = stage(chip.reshape(NY, NX, *chip.shape[1:]), y, NY, lambda k, y, x, z, c, g: ((y + k) % NY, x, z, c, g))
+    return stage(rows, x, NX, lambda k, y, x, z, c, g: (y, (x + k) % NX, z, c, g))
 
 
 def pair_swap(y, x, z, c, g):
@@ -125,12 +139,15 @@
 
 
 def part_copies(part, sources, here, sems):
-    slab, high, low = sources
+    slabs, high, low = sources
     slab_here, high_here, low_here = here
     depth = high.shape[1] // PARTS
     place = pl.ds(part * depth, depth)
+    pieces, first = slabs[0].shape[0] // depth, part * depth
+    slab = slabs[min(part // pieces, len(slabs) - 1)]
+    there = pl.ds(first % slabs[0].shape[0], depth)
     return [
-        pltpu.make_async_copy(slab.at[place, :], slab_here.at[place, :], sems.at[part, 0]),
+        pltpu.make_async_copy(slab.at[there, :], slab_here.at[place, :], sems.at[part, 0]),
         pltpu.make_async_copy(high.at[:, place], high_here.at[:, place], sems.at[part, 1]),
         pltpu.make_async_copy(low.at[:, place], low_here.at[:, place], sems.at[part, 2]),
     ]
@@ -166,8 +183,8 @@
         out[:, index * width : (index + 1) * width, :] = rows.T.reshape(groups, width, half)
 
 
-def first_kernel(scalars, own, near, high_0, low_0, high_1, low_1, kept, sent, slabs, highs, lows, total, sems):
-    sources = ((own, high_0, low_0), (near, high_1, low_1))
+def first_kernel(scalars, own, near_a, near_b, high_0, low_0, high_1, low_1, kept, sent, slabs, highs, lows, total, sems):
+    sources = (((own,), high_0, low_0), ((near_a, near_b), high_1, low_1))
     here = [(slabs.at[k], highs.at[k], lows.at[k]) for k in range(2)]
     for k in range(2):
         start_parts(range(PARTS), sources[k], here[k], sems.at[k])
@@ -176,38 +193,63 @@
         put_halves(scalars, total, kept, sent, k)
 
 
+def guest_kernel(slab, rows, out, slab_here, rows_here, sems):
+    copies = [
+        pltpu.make_async_copy(slab, slab_here, sems.at[0]),
+        pltpu.make_async_copy(rows, rows_here, sems.at[1]),
+    ]
+    for copy in copies:
+        copy.start()
+    for copy in copies:
+        copy.wait()
+    out[...] = split_dot(halves_of(rows_here[...]), halves_of(slab_here[...]))
+
+
 def second_kernel(
-    scalars, passed, crossed, guests, high, low, kept, sent, slab, high_here, low_here, guest_slab, rows, total, sems, guest_sems
+    scalars, passed_a, passed_b, crossed_a, crossed_b, guest, high, low, kept, sent, slab, high_here, low_here, total, sems, guest_sem
 ):
-    depth = rows.shape[1]
     here = (slab, high_here, low_here)
     ends = is_end(scalars)
-    pl.when(ends)(lambda: start_parts(range(PARTS), (passed, high, low), here, sems))
-    pl.when(jnp.logical_not(ends))(lambda: start_parts(range(PARTS), (crossed, high, low), here, sems))
-    guest_copies = [
-        pltpu.make_async_copy(crossed.at[pl.ds(depth, depth), :], guest_slab, guest_sems.at[0]),
-        pltpu.make_async_copy(guests, rows, guest_sems.at[1]),
-    ]
-    for copy in guest_copies:
-        copy.start()
-    add_parts(range(PARTS), (crossed, high, low), here, sems, total)
-    put_halves(scalars, total, kept, sent, 0)
-    for copy in guest_copies:
-        copy.wait()
-    total[...] = split_dot(halves_of(rows[...]), halves_of(guest_slab[...]))
-    put_halves(scalars, total, kept, sent, 1)
-
-
-def last_kernel(scalars, far, middle, high, low, out, slab, high_here, low_here, total, sems):
+    crossed = ((crossed_a, crossed_b), high, low)
+    pl.when(ends)(lambda: start_parts(range(PARTS), ((passed_a, passed_b), high, low), here, sems))
+    pl.when(jnp.logical_not(ends))(lambda: start_parts(range(PARTS), crossed, here, sems))
+    guest_copy = pltpu.make_async_copy(guest, total.at[1], guest_sem)
+    guest_copy.start()
+    add_parts(range(PARTS), crossed, here, sems, total.at[0])
+    put_halves(scalars, total.at[0], kept, sent, 0)
+    guest_copy.wait()
+    put_halves(scalars, total.at[1], kept, sent, 1)
+
+
+def last_kernel(scalars, far, middle_a, middle_b, high, low, out, slab, high_here, low_here, total, sems):
     here = (slab, high_here, low_here)
     ends = is_end(scalars)
     inner = jnp.logical_not(ends)
     front, back = range(PARTS // 2), range(PARTS // 2, PARTS)
-    pl.when(ends)(lambda: start_parts(front, (far, high, low), here, sems))
-    pl.when(inner)(lambda: start_parts(range(PARTS), (middle, high, low), here, sems))
-    add_parts(front, (middle, high, low), here, sems, total)
-    pl.when(inner)(lambda: add_parts(back, (middle, high, low), here, sems, total))
+    middle = ((middle_a, middle_b), high, low)
+    pl.when(ends)(lambda: start_parts(front, ((far,), high, low), here, sems))
+    pl.when(inner)(lambda: start_parts(range(PARTS), middle, here, sems))
+    add_parts(front, middle, here, sems, total)
+    pl.when(inner)(lambda: add_parts(back, middle, here, sems, total))
     out[...] = total[...].T.reshape(out.shape)
+
+
+def guest_product(slab, rows):
+    pairs, columns = rows.shape[0], slab.shape[1]
+    return pl.pallas_call(
+        guest_kernel,
+        out_shape=jax.ShapeDtypeStruct((pairs, columns), jnp.float32),
+        in_specs=[pl.BlockSpec(memory_space=pl.ANY)] * 2,
+        out_specs=pl.BlockSpec(memory_space=pltpu.VMEM),
+        scratch_shapes=[
+            pltpu.VMEM(slab.shape, jnp.float32),
+            pltpu.VMEM(rows.shape, jnp.float32),
+            pltpu.SemaphoreType.DMA((2,)),
+        ],
+        compiler_params=pltpu.CompilerParams(vmem_limit_bytes=12 << 20),
+        cost_estimate=pl.CostEstimate(flops=6 * pairs * rows.shape[1] * columns, bytes_accessed=2 << 20, transcendentals=0),
+        name="guest_product",
+    )(slab, rows)
 
 
 def call_product(kernel, scalars, slabs, split, out_shapes, scratch, terms):
@@ -268,14 +310,20 @@
     z_part = (position // NC) % NZ
 
     own = integrals[0]
-    near = permute(own, pair_swap)
-    middle = permute(own, middle_swap)
+    own_a = own[: rows // 2]
+    near_a = permute(own_a, pair_swap)
+    middle_a = permute(own_a, middle_swap)
+    own_b = lax.optimization_barrier(own)[rows // 2 :]
+    near_b = permute(own_b, pair_swap)
+    middle_b = permute(own_b, middle_swap)
     scalars = jnp.concatenate([owner_map, irrep_sizes, jnp.stack([group, position])])
     *split, moved = split_rows(amplitudes, scalars)
+    passed_a = permute(middle_a, outward)
+    crossed_a = permute(near_a, middle_swap)
+    passed_b = permute(middle_b, outward)
+    crossed_b = permute(near_b, middle_swap)
     guests = permute(moved, inward)
-    crossed = permute(near, middle_swap)
-    passed = permute(middle, outward)
-    far = permute(crossed[: rows // 2], outward)
+    far = permute(crossed_a, outward)
 
     matrix = pltpu.VMEM((pairs, slots), jnp.bfloat16)
     slab = pltpu.VMEM((rows, columns), jnp.float32)
@@ -294,25 +342,18 @@
         total,
         pltpu.SemaphoreType.DMA((2, PARTS, 3)),
     ]
-    result = call_product(first_kernel, scalars, [own, near], split[:4], joint, scratch, 2 * terms)
+    result = call_product(first_kernel, scalars, [own, near_a, near_b], split[:4], joint, scratch, 2 * terms)
     first_chip = chip_sum(*result)
     first = plane_sum(first_chip)
-    scratch = [
-        slab,
-        matrix,
-        matrix,
-        pltpu.VMEM((rows // 2, columns), jnp.float32),
-        pltpu.VMEM((pairs, slots // 2), jnp.float32),
-        total,
-        sems,
-        pltpu.SemaphoreType.DMA((2,)),
-    ]
-    result = call_product(second_kernel, scalars, [passed, crossed, guests], split[4:6], joint, scratch, 2 * terms)
-    second_chip = chip_sum(*result)
-    second = plane_sum(second_chip)
+    guest = guest_product(crossed_b, guests)
+    scratch = [slab, matrix, matrix, pltpu.VMEM((2, pairs, columns), jnp.float32), sems, pltpu.SemaphoreType.DMA]
+    slabs = [passed_a, passed_b, crossed_a, crossed_b, guest]
+    result = call_product(second_kernel, scalars, slabs, split[4:6], joint, scratch, terms)
+    second = staged_sum(chip_sum(*result), position)
     scratch = [slab, matrix, matrix, total, sems]
-    (result,) = call_product(last_kernel, scalars, [far, middle], split[6:], [(plane, width, pairs)], scratch, terms)
-    third = plane_sum(result)
+    slabs = [far, middle_a, middle_b]
+    (result,) = call_product(last_kernel, scalars, slabs, split[6:], [(plane, width, pairs)], scratch, terms)
+    third = staged_sum(result, position)
     third = third.reshape(width, NC, half).swapaxes(0, 1)
     handed = permute(second[width:], outward)
     units = jnp.concatenate([first.reshape(2, width, half), second[None, :width], handed[None], third], axis=0)

time: 125 us -> 126 us (level)
  starting transfers between devices: 39.8 us -> 57.3 us
  waiting for transfers between devices: 48.5 us -> 31.4 us
    ppermute x12 -> x28, starting transfers between devices: 25.3 us -> 50.5 us  [permute(): return lax.ppermute(value, AXES, pairs)]
    all_to_all x3 -> x1, waiting for transfers between devices: 16.7 us -> 0.01 us  [plane_sum(): lax.all_to_all(chip, 'blk', 0, 0, tiled=True, axis_index_groups=plane_gro...]
    all_to_all x3 -> x1, starting transfers between devices: 14.6 us -> 6.81 us  [plane_sum(): lax.all_to_all(chip, 'blk', 0, 0, tiled=True, axis_index_groups=plane_gro...]
    slice x1 -> x2, local copies, waits for them, and re-layouts: 1.88 us -> 3.81 us  [the longest x1 1.96 us: local(): own_a = own[:rows // 2]]
    pallas_call x3, Pallas kernels: 14.9 us -> 13.4 us  [call_product(): pl.pallas_call(kernel, out_shape=[jax.ShapeDtypeStruct(shape, jnp.float32...]
    ppermute x12 -> x28, waiting for transfers between devices: 31.8 us -> 31.4 us  [permute(): return lax.ppermute(value, AXES, pairs)]
  transfers between devices with their start and end apart: 15 -> 29, of which waited for: 9 -> 7; matrix products, arithmetic and copies ran while one was open for 5% -> 5% of each run, Pallas kernels for 22% -> 21%
where the time goes in v6:
time: 126 us; the launch traced here: 125 us
  starting transfers between devices  57.3 us (45%)
  waiting for transfers between devices  31.4 us (25%)
  Pallas kernels  28 us (22%)
  local copies, waits for them, and re-layouts  4.05 us (3%)
  other arithmetic  3.96 us (3%)
    ppermute x28, starting transfers between devices, permute(): return lax.ppermute(value, AXES, pairs)  50.5 us
    ppermute x28, waiting for transfers between devices, permute(): return lax.ppermute(value, AXES, pairs)  31.4 us
    pallas_call x3, Pallas kernels, call_product(): pl.pallas_call(kernel, out_shape=[jax.ShapeDtypeStruct(shape, jnp.float32...  13.4 us
    pallas_call x1, Pallas kernels, split_rows(): pl.pallas_call(functools.partial(split_kernel, rows, slot_width), out_sha...  12.7 us
    all_to_all x1, starting transfers between devices, plane_sum(): lax.all_to_all(chip, 'blk', 0, 0, tiled=True, axis_index_groups=plane_gro...  6.81 us
  transfers between devices with their start and end apart: 29, of which 7 were waited for; matrix products, arithmetic and copies ran while one was open for 5% of the time, Pallas kernels for 21%

profile of v6, /device:TPU:1, one launch (start us, length us, event | category | flops | bytes accessed | tf_op | source)
XLA Modules:
  0.0 125.3 jit_solution(7304208223665830653)
XLA Ops:
  0.0 2.0 %slice_bitcast_fusion = f32[512,256]{1,0:T(8,128)} fusion(f32[1,1024,256]{2,1,0:T(8,128)} %param.5), kind=kLoop, calls=%fused_computation | loop fusion | bytes 1048576 | tf_op jit(solution)/shard_map/slice | solution.py:313
  2.0 2.5 %collective-permute-start = (f32[512,256]{1,0:T(8,128)}, f32[512,256]{1,0:T(8,128)}, u32[]{:S(2)}, u32[]{:S(2)}) collective-permute-start(f32[512,256]{1,0:T(8,128)} %slice_bitcast_fusion), channel_id=1, source_target_pairs={{0,1},{1,0},{2,3},{3,2},{4,5},{5,4},{6,7},{7,6},{8,9},{9,8},{10,11... | collective-permute-start | bytes 1572872 | tf_op jit(solution)/shard_map/ppermute | solution.py:38
  4.4 1.9 %slice.20 = f32[512,256]{1,0:T(8,128)} slice(f32[1024,256]{1,0:T(8,128)} %bitcast.56), slice={[512:1024], [0:256]} | slice | bytes 1048576 | tf_op jit(solution)/shard_map/slice | solution.py:316
  6.3 0.0 collective-permute-start.1
  6.3 0.7 collective-permute-start.3
  7.0 0.7 collective-permute-start.5
  7.7 0.8 pad_add_fusion.scalars
  8.4 12.7 %split_rows.1 = (bf16[512,1024]{1,0:T(8,128)(2,1)}, bf16[512,1024]{1,0:T(8,128)(2,1)}, bf16[512,1024]{1,0:T(8,128)(2,1)}, bf16[512,1024]{1,0:T(8,128)(2,1)}, bf1...) custom-call(s32[10]{0:T(128)S(1)} %pad_add_fusion.scalars, ...), custom_call_target="tpu_custom_call" | custom-call | bytes 16777216 | tf_op jit(solution)/shard_map/split_rows/pallas_call | solution.py:107
  21.1 7.7 %collective-permute-start.9 = (f32[512,512]{1,0:T(8,128)}, f32[512,512]{1,0:T(8,128)S(1)}, u32[]{:S(2)}, u32[]{:S(2)}) collective-permute-start(f32[512,512]{1,0:T(8,128)} %get-tuple-element.24), channel_id=1, source_target_pairs={{0,1},{3,2},{4,5},{7,6},{8,9},{11,10},{12,13},{15,14},{16,17},{19,... | collective-permute-start | bytes 3145736 | tf_op jit(solution)/shard_map/ppermute | solution.py:38
  28.8 0.0 collective-permute-done.near_a
  28.8 0.0 collective-permute-done.1.near_b
  28.8 6.0 %shard_map.46 = (f32[16,32,256]{2,1,0:T(8,128)S(1)}, f32[16,32,256]{2,1,0:T(8,128)S(1)}) custom-call(s32[10]{0:T(128)S(1)} %pad_add_fusion.scalars, f32[1024,256]{1,0:T(8,128)S(1)} %bitcast.57, f32[512,256]{1,0:T(8,128)} %collective-permute-done.near_a, f32[512,256]{1,0:T(8,128)} %collective-permute-done.1.near_b, ...), custom_call_target="tpu_custom_call" | custom-call | flops 1610612736 | bytes 6291456 | tf_op jit(solution)/shard_map/pallas_call | solution.py:258
  34.8 1.8 %collective-permute-start.2 = (f32[16,32,256]{2,1,0:T(8,128)S(1)}, f32[16,32,256]{2,1,0:T(8,128)S(1)}, u32[]{:S(2)}, u32[]{:S(2)}) collective-permute-start(f32[16,32,256]{2,1,0:T(8,128)S(1)} %get-tuple-element.23), channel_id=1, source_target_pairs={{0,4},{1,5},{2,6},{3,7},{4,0},{5,1},{6,2},{7,3},{8,12},{9,13},{10,... | collective-permute-start | bytes 1572872 | tf_op jit(solution)/shard_map/ppermute | solution.py:38
  36.6 0.7 collective-permute-start.8
  37.3 0.0 collective-permute-done.3.middle_a
  37.3 1.3 %collective-permute-start.4 = (f32[512,256]{1,0:T(8,128)S(1)}, f32[512,256]{1,0:T(8,128)}, u32[]{:S(2)}, u32[]{:S(2)}) collective-permute-start(f32[512,256]{1,0:T(8,128)S(1)} %collective-permute-done.3.middle_a), channel_id=1, source_target_pairs={{1,0},{2,3},{5,4},{6,7},{9,8},{10,11},{13,12},{14,15},{17,16},{18,... | collective-permute-start | bytes 1572872 | tf_op jit(solution)/shard_map/ppermute | solution.py:38
  38.6 0.0 collective-permute-done.5.middle_b
  38.7 1.3 %collective-permute-start.6 = (f32[512,256]{1,0:T(8,128)S(1)}, f32[512,256]{1,0:T(8,128)}, u32[]{:S(2)}, u32[]{:S(2)}) collective-permute-start(f32[512,256]{1,0:T(8,128)S(1)} %collective-permute-done.5.middle_b), channel_id=1, source_target_pairs={{1,0},{2,3},{5,4},{6,7},{9,8},{10,11},{13,12},{14,15},{17,16},{18,... | collective-permute-start | bytes 1572872 | tf_op jit(solution)/shard_map/ppermute | solution.py:38
  40.0 0.0 collective-permute-done.2
  40.0 0.7 collective-permute-start.7
  40.7 0.9 add.167
  41.5 6.8 %all-to-all-start = ((f32[16,32,256]{2,1,0:T(8,128)}), f32[16,32,256]{2,1,0:T(8,128)}, u32[]{:S(2)}, u32[]{:S(2)}) async-start(f32[16,32,256]{2,1,0:T(8,128)} %add.167), calls=%async_computation | async-start | bytes 1048576 | tf_op jit(solution)/shard_map/all_to_all | solution.py:46
  48.4 0.0 collective-permute-done.8.slab.crossed_b
  48.4 1.7 %collective-permute-done.9.rows = f32[512,512]{1,0:T(8,128)S(1)} collective-permute-done((f32[512,512]{1,0:T(8,128)}, f32[512,512]{1,0:T(8,128)S(1)}, u32[]{:S(2)}, u32[]{:S(2)}) %collective-permute-start.9) | collective-permute-done | bytes 1048608 | tf_op jit(solution)/shard_map/ppermute | solution.py:38
  50.1 0.7 guest_product.1.guest
  50.8 2.7 %collective-permute-done.4.passed_a = f32[512,256]{1,0:T(8,128)} collective-permute-done((f32[512,256]{1,0:T(8,128)S(1)}, f32[512,256]{1,0:T(8,128)}, u32[]{:S(2)}, u32[]{:S(2)}) %collective-permute-start.4) | collective-permute-done | bytes 524320 | tf_op jit(solution)/shard_map/ppermute | solution.py:38
  53.5 11.2 %collective-permute-done.6.passed_b = f32[512,256]{1,0:T(8,128)} collective-permute-done((f32[512,256]{1,0:T(8,128)S(1)}, f32[512,256]{1,0:T(8,128)}, u32[]{:S(2)}, u32[]{:S(2)}) %collective-permute-start.6) | collective-permute-done | bytes 524320 | tf_op jit(solution)/shard_map/ppermute | solution.py:38
  64.7 0.0 collective-permute-done.7.crossed_a
  64.7 4.2 %shard_map.47 = (f32[16,32,256]{2,1,0:T(8,128)S(1)}, f32[16,32,256]{2,1,0:T(8,128)S(1)}) custom-call(s32[10]{0:T(128)S(1)} %pad_add_fusion.scalars, f32[512,256]{1,0:T(8,128)} %collective-permute-done.4.passed_a, f32[512,256]{1,0:T(8,128)} %collective-permute-done.6.passed_b, f32[512,256]{1,0:T(8,128)S(1)} %collective-permute-done.7.crossed_a, ...), custom_call_target="tpu_custom_call" | custom-call | flops 805306368 | bytes 6291456 | tf_op jit(solution)/shard_map/pallas_call | solution.py:258
  68.9 1.0 collective-permute-start.10
  69.9 1.3 %collective-permute-start.18 = (f32[512,256]{1,0:T(8,128)S(1)}, f32[512,256]{1,0:T(8,128)S(1)}, u32[]{:S(2)}, u32[]{:S(2)}) collective-permute-start(f32[512,256]{1,0:T(8,128)S(1)} %collective-permute-done.7.crossed_a), channel_id=1, source_target_pairs={{1,0},{2,3},{5,4},{6,7},{9,8},{10,11},{13,12},{14,15},{17,16},{18,... | collective-permute-start | bytes 1572872 | tf_op jit(solution)/shard_map/ppermute | solution.py:38
  71.4 0.0 all-to-all-done
  71.4 1.1 reduce_sum.9
  72.6 0.0 collective-permute-done.10
  72.6 1.1 add.168
  73.8 3.0 %collective-permute-start.13 = (f32[4,32,256]{2,1,0:T(8,128)S(1)}, f32[4,32,256]{2,1,0:T(8,128)S(1)}, u32[]{:S(2)}, u32[]{:S(2)}) collective-permute-start(f32[4,32,256]{2,1,0:T(8,128)S(1)} %get-tuple-element.35), channel_id=1, source_target_pairs={{0,128},{1,129},{2,130},{3,131},{4,132},{5,133},{6,134},{7,135},{8... | collective-permute-start | bytes 393224 | tf_op jit(solution)/shard_map/ppermute | solution.py:38
  76.8 0.4 collective-permute-start.11
  77.2 2.3 %collective-permute-start.12 = (f32[4,32,256]{2,1,0:T(8,128)S(1)}, f32[4,32,256]{2,1,0:T(8,128)S(1)}, u32[]{:S(2)}, u32[]{:S(2)}) collective-permute-start(f32[4,32,256]{2,1,0:T(8,128)S(1)} %get-tuple-element.34), channel_id=1, source_target_pairs={{0,192},{1,193},{2,194},{3,195},{4,196},{5,197},{6,198},{7,199},{8... | collective-permute-start | bytes 393224 | tf_op jit(solution)/shard_map/ppermute | solution.py:38
  79.4 5.8 %collective-permute-done.18.far = f32[512,256]{1,0:T(8,128)S(1)} collective-permute-done((f32[512,256]{1,0:T(8,128)S(1)}, f32[512,256]{1,0:T(8,128)S(1)}, u32[]{:S(2)}, u32[]{:S(2)}) %collective-permute-start.18) | collective-permute-done | bytes 524320 | tf_op jit(solution)/shard_map/ppermute | solution.py:38
  85.2 3.2 %shard_map.48 = f32[16,16,512]{2,1,0:T(8,128)S(1)} custom-call(s32[10]{0:T(128)S(1)} %pad_add_fusion.scalars, f32[512,256]{1,0:T(8,128)S(1)} %collective-permute-done.18.far, f32[512,256]{1,0:T(8,128)S(1)} %collective-permute-done.3.middle_a, f32[512,256]{1,0:T(8,128)S(1)} %collective-permute-done.5.middle_b, bf16[512,1024]{1,0:T(8,128)(2,1)} %get-tuple-element.29.high, ...), custom_call_target="tpu_custom_call" | custom-call | flops 805306368 | bytes 6291456 | tf_op jit(solution)/shard_map/pallas_call | solution.py:258
  88.5 3.0 %collective-permute-start.21 = (f32[4,16,512]{2,1,0:T(8,128)S(1)}, f32[4,16,512]{2,1,0:T(8,128)S(1)}, u32[]{:S(2)}, u32[]{:S(2)}) collective-permute-start(f32[4,16,512]{2,1,0:T(8,128)S(1)} %get-tuple-element.32), channel_id=1, source_target_pairs={{0,128},{1,129},{2,130},{3,131},{4,132},{5,133},{6,134},{7,135},{8... | collective-permute-start | bytes 393224 | tf_op jit(solution)/shard_map/ppermute | solution.py:38
  91.5 0.4 collective-permute-start.19
  91.9 0.0 collective-permute-done.13
  91.9 2.3 %collective-permute-start.20 = (f32[4,16,512]{2,1,0:T(8,128)S(1)}, f32[4,16,512]{2,1,0:T(8,128)S(1)}, u32[]{:S(2)}, u32[]{:S(2)}) collective-permute-start(f32[4,16,512]{2,1,0:T(8,128)S(1)} %get-tuple-element.31), channel_id=1, source_target_pairs={{0,192},{1,193},{2,194},{3,195},{4,196},{5,197},{6,198},{7,199},{8... | collective-permute-start | bytes 393224 | tf_op jit(solution)/shard_map/ppermute | solution.py:38
  94.2 2.8 %collective-permute-start.16 = (f32[32,256]{1,0:T(8,128)S(1)}, f32[32,256]{1,0:T(8,128)S(1)}, u32[]{:S(2)}, u32[]{:S(2)}) collective-permute-start(f32[32,256]{1,0:T(8,128)S(1)} %get-tuple-element.41), channel_id=1, source_target_pairs={{0,32},{1,33},{2,34},{3,35},{4,36},{5,37},{6,38},{7,39},{8,40},{9,... | collective-permute-start | bytes 98312 | tf_op jit(solution)/shard_map/ppermute | solution.py:38
  97.1 0.3 collective-permute-start.14
  97.4 0.0 collective-permute-done.21
  97.4 2.4 %collective-permute-start.15 = (f32[32,256]{1,0:T(8,128)S(1)}, f32[32,256]{1,0:T(8,128)S(1)}, u32[]{:S(2)}, u32[]{:S(2)}) collective-permute-start(f32[32,256]{1,0:T(8,128)S(1)} %get-tuple-element.40), channel_id=1, source_target_pairs={{0,48},{1,49},{2,50},{3,51},{4,52},{5,53},{6,54},{7,55},{8,56},{9,... | collective-permute-start | bytes 98312 | tf_op jit(solution)/shard_map/ppermute | solution.py:38
  99.8 0.8 collective-permute-start.24
  100.6 0.3 collective-permute-start.22
  100.9 0.0 collective-permute-done.16
  100.9 2.4 %collective-permute-start.23 = (f32[16,512]{1,0:T(8,128)S(1)}, f32[16,512]{1,0:T(8,128)S(1)}, u32[]{:S(2)}, u32[]{:S(2)}) collective-permute-start(f32[16,512]{1,0:T(8,128)S(1)} %get-tuple-element.37), channel_id=1, source_target_pairs={{0,48},{1,49},{2,50},{3,51},{4,52},{5,53},{6,54},{7,55},{8,56},{9,... | collective-permute-start | bytes 98312 | tf_op jit(solution)/shard_map/ppermute | solution.py:38
  103.3 0.0 collective-permute-done.14
  103.3 0.0 collective-permute-done.15
  103.3 1.3 %collective-permute-start.17 = (f32[16,256]{1,0:T(8,128)S(1)}, f32[16,256]{1,0:T(8,128)S(1)}, u32[]{:S(2)}, u32[]{:S(2)}) collective-permute-start(f32[16,256]{1,0:T(8,128)S(1)} %get-tuple-element.47), channel_id=1, source_target_pairs={{1,0},{2,3},{5,4},{6,7},{9,8},{10,11},{13,12},{14,15},{17,16},{18,... | collective-permute-start | bytes 49160 | tf_op jit(solution)/shard_map/ppermute | solution.py:38
  104.6 0.0 collective-permute-done.24
  104.7 3.1 %collective-permute-done.17 = f32[16,256]{1,0:T(8,128)S(1)} collective-permute-done((f32[16,256]{1,0:T(8,128)S(1)}, f32[16,256]{1,0:T(8,128)S(1)}, u32[]{:S(2)}, u32[]{:S(2)}) %collective-permute-start.17) | collective-permute-done | bytes 16416 | tf_op jit(solution)/shard_map/ppermute | solution.py:38
  107.9 3.8 %collective-permute-start.25 = (f32[6,4,256]{2,1,0:T(4,128)S(1)}, f32[6,4,256]{2,1,0:T(4,128)S(1)}, u32[]{:S(2)}, u32[]{:S(2)}) collective-permute-start(f32[6,4,256]{2,1,0:T(4,128)S(1)} %get-tuple-element.45), channel_id=1, source_target_pairs={{0,4},{1,5},{2,6},{3,7},{4,0},{5,1},{6,2},{7,3},{8,12},{9,13},{10,... | collective-permute-start | bytes 73736 | tf_op jit(solution)/shard_map/ppermute | solution.py:38
  111.7 5.3 %collective-permute-start.26 = (f32[6,4,256]{2,1,0:T(4,128)S(1)}, f32[6,4,256]{2,1,0:T(4,128)S(1)}, u32[]{:S(2)}, u32[]{:S(2)}) collective-permute-start(f32[6,4,256]{2,1,0:T(4,128)S(1)} %get-tuple-element.44), channel_id=1, source_target_pairs={{0,8},{1,9},{2,10},{3,11},{4,12},{5,13},{6,14},{7,15},{8,0},{9,1},... | collective-permute-start | bytes 73736 | tf_op jit(solution)/shard_map/ppermute | solution.py:38
  117.0 0.3 collective-permute-start.27
  117.3 0.0 collective-permute-done.25.refs_1_
  117.3 0.9 collective-permute-done.26.refs_2_
  118.2 5.9 %collective-permute-done.27.refs_3_ = f32[6,4,256]{2,1,0:T(4,128)S(1)} collective-permute-done((f32[6,4,256]{2,1,0:T(4,128)S(1)}, f32[6,4,256]{2,1,0:T(4,128)S(1)}, u32[]{:S(2)}, u32[]{:S(2)}) %collective-permute-start.27) | collective-permute-done | bytes 24608 | tf_op jit(solution)/shard_map/ppermute | solution.py:38
  124.1 1.2 finish.1
  (26 shorter events, 0.4 us)
Async XLA Ops:
  0.0 28.8 %copy-start = (f32[1,1024,256]{2,1,0:T(8,128)S(1)}, f32[1,1024,256]{2,1,0:T(8,128)}, u32[]{:S(2)}) copy-start(f32[1,1024,256]{2,1,0:T(8,128)} %param.5) | copy-start | bytes 3145732
  2.0 26.8 %collective-permute-start = (f32[512,256]{1,0:T(8,128)}, f32[512,256]{1,0:T(8,128)}, u32[]{:S(2)}, u32[]{:S(2)}) collective-permute-start(f32[512,256]{1,0:T(8,128)} %slice_bitcast_fusion), channel_id=1, source_target_pairs={{0,1},{1,0},{2,3},{3,2},{4,5},{5,4},{6,7},{7,6},{8,9},{9,8},{10,11... | collective-permute-start | bytes 1572872 | tf_op jit(solution)/shard_map/ppermute | solution.py:38
  6.3 22.5 %collective-permute-start.1 = (f32[512,256]{1,0:T(8,128)}, f32[512,256]{1,0:T(8,128)}, u32[]{:S(2)}, u32[]{:S(2)}) collective-permute-start(f32[512,256]{1,0:T(8,128)} %slice.20), channel_id=1, source_target_pairs={{0,1},{1,0},{2,3},{3,2},{4,5},{5,4},{6,7},{7,6},{8,9},{9,8},{10,11... | collective-permute-start | bytes 1572872 | tf_op jit(solution)/shard_map/ppermute | solution.py:38
  6.3 31.1 %collective-permute-start.3 = (f32[512,256]{1,0:T(8,128)}, f32[512,256]{1,0:T(8,128)S(1)}, u32[]{:S(2)}, u32[]{:S(2)}) collective-permute-start(f32[512,256]{1,0:T(8,128)} %slice_bitcast_fusion), channel_id=1, source_target_pairs={{1,2},{2,1},{5,6},{6,5},{9,10},{10,9},{13,14},{14,13},{17,18},{18,... | collective-permute-start | bytes 1572872 | tf_op jit(solution)/shard_map/ppermute | solution.py:38
  7.0 31.7 %collective-permute-start.5 = (f32[512,256]{1,0:T(8,128)}, f32[512,256]{1,0:T(8,128)S(1)}, u32[]{:S(2)}, u32[]{:S(2)}) collective-permute-start(f32[512,256]{1,0:T(8,128)} %slice.20), channel_id=1, source_target_pairs={{1,2},{2,1},{5,6},{6,5},{9,10},{10,9},{13,14},{14,13},{17,18},{18,... | collective-permute-start | bytes 1572872 | tf_op jit(solution)/shard_map/ppermute | solution.py:38
  21.1 29.0 %collective-permute-start.9 = (f32[512,512]{1,0:T(8,128)}, f32[512,512]{1,0:T(8,128)S(1)}, u32[]{:S(2)}, u32[]{:S(2)}) collective-permute-start(f32[512,512]{1,0:T(8,128)} %get-tuple-element.24), channel_id=1, source_target_pairs={{0,1},{3,2},{4,5},{7,6},{8,9},{11,10},{12,13},{15,14},{16,17},{19,... | collective-permute-start | bytes 3145736 | tf_op jit(solution)/shard_map/ppermute | solution.py:38
  34.8 5.1 %collective-permute-start.2 = (f32[16,32,256]{2,1,0:T(8,128)S(1)}, f32[16,32,256]{2,1,0:T(8,128)S(1)}, u32[]{:S(2)}, u32[]{:S(2)}) collective-permute-start(f32[16,32,256]{2,1,0:T(8,128)S(1)} %get-tuple-element.23), channel_id=1, source_target_pairs={{0,4},{1,5},{2,6},{3,7},{4,0},{5,1},{6,2},{7,3},{8,12},{9,13},{10,... | collective-permute-start | bytes 1572872 | tf_op jit(solution)/shard_map/ppermute | solution.py:38
  36.6 11.7 %collective-permute-start.8 = (f32[512,256]{1,0:T(8,128)}, f32[512,256]{1,0:T(8,128)S(1)}, u32[]{:S(2)}, u32[]{:S(2)}) collective-permute-start(f32[512,256]{1,0:T(8,128)} %collective-permute-done.1.near_b), channel_id=1, source_target_pairs={{1,2},{2,1},{5,6},{6,5},{9,10},{10,9},{13,14},{14,13},{17,18},{18,... | collective-permute-start | bytes 1572872 | tf_op jit(solution)/shard_map/ppermute | solution.py:38
  37.3 16.2 %collective-permute-start.4 = (f32[512,256]{1,0:T(8,128)S(1)}, f32[512,256]{1,0:T(8,128)}, u32[]{:S(2)}, u32[]{:S(2)}) collective-permute-start(f32[512,256]{1,0:T(8,128)S(1)} %collective-permute-done.3.middle_a), channel_id=1, source_target_pairs={{1,0},{2,3},{5,4},{6,7},{9,8},{10,11},{13,12},{14,15},{17,16},{18,... | collective-permute-start | bytes 1572872 | tf_op jit(solution)/shard_map/ppermute | solution.py:38
  38.7 26.1 %collective-permute-start.6 = (f32[512,256]{1,0:T(8,128)S(1)}, f32[512,256]{1,0:T(8,128)}, u32[]{:S(2)}, u32[]{:S(2)}) collective-permute-start(f32[512,256]{1,0:T(8,128)S(1)} %collective-permute-done.5.middle_b), channel_id=1, source_target_pairs={{1,0},{2,3},{5,4},{6,7},{9,8},{10,11},{13,12},{14,15},{17,16},{18,... | collective-permute-start | bytes 1572872 | tf_op jit(solution)/shard_map/ppermute | solution.py:38
  40.0 24.8 %collective-permute-start.7 = (f32[512,256]{1,0:T(8,128)}, f32[512,256]{1,0:T(8,128)S(1)}, u32[]{:S(2)}, u32[]{:S(2)}) collective-permute-start(f32[512,256]{1,0:T(8,128)} %collective-permute-done.near_a), channel_id=1, source_target_pairs={{1,2},{2,1},{5,6},{6,5},{9,10},{10,9},{13,14},{14,13},{17,18},{18,... | collective-permute-start | bytes 1572872 | tf_op jit(solution)/shard_map/ppermute | solution.py:38
  41.5 29.9 %all-to-all-start = ((f32[16,32,256]{2,1,0:T(8,128)}), f32[16,32,256]{2,1,0:T(8,128)}, u32[]{:S(2)}, u32[]{:S(2)}) async-start(f32[16,32,256]{2,1,0:T(8,128)} %add.167), calls=%async_computation | async-start | bytes 1048576 | tf_op jit(solution)/shard_map/all_to_all | solution.py:46
  68.9 3.6 %collective-permute-start.10 = (f32[16,32,256]{2,1,0:T(8,128)S(1)}, f32[16,32,256]{2,1,0:T(8,128)}, u32[]{:S(2)}, u32[]{:S(2)}) collective-permute-start(f32[16,32,256]{2,1,0:T(8,128)S(1)} %get-tuple-element.28), channel_id=1, source_target_pairs={{0,4},{1,5},{2,6},{3,7},{4,0},{5,1},{6,2},{7,3},{8,12},{9,13},{10,... | collective-permute-start | bytes 1572872 | tf_op jit(solution)/shard_map/ppermute | solution.py:38
  69.9 15.3 %collective-permute-start.18 = (f32[512,256]{1,0:T(8,128)S(1)}, f32[512,256]{1,0:T(8,128)S(1)}, u32[]{:S(2)}, u32[]{:S(2)}) collective-permute-start(f32[512,256]{1,0:T(8,128)S(1)} %collective-permute-done.7.crossed_a), channel_id=1, source_target_pairs={{1,0},{2,3},{5,4},{6,7},{9,8},{10,11},{13,12},{14,15},{17,16},{18,... | collective-permute-start | bytes 1572872 | tf_op jit(solution)/shard_map/ppermute | solution.py:38
  73.8 18.1 %collective-permute-start.13 = (f32[4,32,256]{2,1,0:T(8,128)S(1)}, f32[4,32,256]{2,1,0:T(8,128)S(1)}, u32[]{:S(2)}, u32[]{:S(2)}) collective-permute-start(f32[4,32,256]{2,1,0:T(8,128)S(1)} %get-tuple-element.35), channel_id=1, source_target_pairs={{0,128},{1,129},{2,130},{3,131},{4,132},{5,133},{6,134},{7,135},{8... | collective-permute-start | bytes 393224 | tf_op jit(solution)/shard_map/ppermute | solution.py:38
  76.8 17.4 %collective-permute-start.11 = (f32[4,32,256]{2,1,0:T(8,128)S(1)}, f32[4,32,256]{2,1,0:T(8,128)S(1)}, u32[]{:S(2)}, u32[]{:S(2)}) collective-permute-start(f32[4,32,256]{2,1,0:T(8,128)S(1)} %get-tuple-element.36), channel_id=1, source_target_pairs={{0,64},{1,65},{2,66},{3,67},{4,68},{5,69},{6,70},{7,71},{8,72},{9,... | collective-permute-start | bytes 393224 | tf_op jit(solution)/shard_map/ppermute | solution.py:38
  77.2 17.0 %collective-permute-start.12 = (f32[4,32,256]{2,1,0:T(8,128)S(1)}, f32[4,32,256]{2,1,0:T(8,128)S(1)}, u32[]{:S(2)}, u32[]{:S(2)}) collective-permute-start(f32[4,32,256]{2,1,0:T(8,128)S(1)} %get-tuple-element.34), channel_id=1, source_target_pairs={{0,192},{1,193},{2,194},{3,195},{4,196},{5,197},{6,198},{7,199},{8... | collective-permute-start | bytes 393224 | tf_op jit(solution)/shard_map/ppermute | solution.py:38
  88.5 8.9 %collective-permute-start.21 = (f32[4,16,512]{2,1,0:T(8,128)S(1)}, f32[4,16,512]{2,1,0:T(8,128)S(1)}, u32[]{:S(2)}, u32[]{:S(2)}) collective-permute-start(f32[4,16,512]{2,1,0:T(8,128)S(1)} %get-tuple-element.32), channel_id=1, source_target_pairs={{0,128},{1,129},{2,130},{3,131},{4,132},{5,133},{6,134},{7,135},{8... | collective-permute-start | bytes 393224 | tf_op jit(solution)/shard_map/ppermute | solution.py:38
  91.5 8.3 %collective-permute-start.19 = (f32[4,16,512]{2,1,0:T(8,128)S(1)}, f32[4,16,512]{2,1,0:T(8,128)S(1)}, u32[]{:S(2)}, u32[]{:S(2)}) collective-permute-start(f32[4,16,512]{2,1,0:T(8,128)S(1)} %get-tuple-element.33), channel_id=1, source_target_pairs={{0,64},{1,65},{2,66},{3,67},{4,68},{5,69},{6,70},{7,71},{8,72},{9,... | collective-permute-start | bytes 393224 | tf_op jit(solution)/shard_map/ppermute | solution.py:38
  91.9 7.9 %collective-permute-start.20 = (f32[4,16,512]{2,1,0:T(8,128)S(1)}, f32[4,16,512]{2,1,0:T(8,128)S(1)}, u32[]{:S(2)}, u32[]{:S(2)}) collective-permute-start(f32[4,16,512]{2,1,0:T(8,128)S(1)} %get-tuple-element.31), channel_id=1, source_target_pairs={{0,192},{1,193},{2,194},{3,195},{4,196},{5,197},{6,198},{7,199},{8... | collective-permute-start | bytes 393224 | tf_op jit(solution)/shard_map/ppermute | solution.py:38
  94.2 6.7 %collective-permute-start.16 = (f32[32,256]{1,0:T(8,128)S(1)}, f32[32,256]{1,0:T(8,128)S(1)}, u32[]{:S(2)}, u32[]{:S(2)}) collective-permute-start(f32[32,256]{1,0:T(8,128)S(1)} %get-tuple-element.41), channel_id=1, source_target_pairs={{0,32},{1,33},{2,34},{3,35},{4,36},{5,37},{6,38},{7,39},{8,40},{9,... | collective-permute-start | bytes 98312 | tf_op jit(solution)/shard_map/ppermute | solution.py:38
  97.1 6.2 %collective-permute-start.14 = (f32[32,256]{1,0:T(8,128)S(1)}, f32[32,256]{1,0:T(8,128)S(1)}, u32[]{:S(2)}, u32[]{:S(2)}) collective-permute-start(f32[32,256]{1,0:T(8,128)S(1)} %get-tuple-element.42), channel_id=1, source_target_pairs={{0,16},{1,17},{2,18},{3,19},{4,20},{5,21},{6,22},{7,23},{8,24},{9,... | collective-permute-start | bytes 98312 | tf_op jit(solution)/shard_map/ppermute | solution.py:38
  97.4 5.9 %collective-permute-start.15 = (f32[32,256]{1,0:T(8,128)S(1)}, f32[32,256]{1,0:T(8,128)S(1)}, u32[]{:S(2)}, u32[]{:S(2)}) collective-permute-start(f32[32,256]{1,0:T(8,128)S(1)} %get-tuple-element.40), channel_id=1, source_target_pairs={{0,48},{1,49},{2,50},{3,51},{4,52},{5,53},{6,54},{7,55},{8,56},{9,... | collective-permute-start | bytes 98312 | tf_op jit(solution)/shard_map/ppermute | solution.py:38
  99.8 4.8 %collective-permute-start.24 = (f32[16,512]{1,0:T(8,128)S(1)}, f32[16,512]{1,0:T(8,128)S(1)}, u32[]{:S(2)}, u32[]{:S(2)}) collective-permute-start(f32[16,512]{1,0:T(8,128)S(1)} %get-tuple-element.38), channel_id=1, source_target_pairs={{0,32},{1,33},{2,34},{3,35},{4,36},{5,37},{6,38},{7,39},{8,40},{9,... | collective-permute-start | bytes 98312 | tf_op jit(solution)/shard_map/ppermute | solution.py:38
  100.6 4.0 %collective-permute-start.22 = (f32[16,512]{1,0:T(8,128)S(1)}, f32[16,512]{1,0:T(8,128)S(1)}, u32[]{:S(2)}, u32[]{:S(2)}) collective-permute-start(f32[16,512]{1,0:T(8,128)S(1)} %get-tuple-element.39), channel_id=1, source_target_pairs={{0,16},{1,17},{2,18},{3,19},{4,20},{5,21},{6,22},{7,23},{8,24},{9,... | collective-permute-start | bytes 98312 | tf_op jit(solution)/shard_map/ppermute | solution.py:38
  100.9 3.7 %collective-permute-start.23 = (f32[16,512]{1,0:T(8,128)S(1)}, f32[16,512]{1,0:T(8,128)S(1)}, u32[]{:S(2)}, u32[]{:S(2)}) collective-permute-start(f32[16,512]{1,0:T(8,128)S(1)} %get-tuple-element.37), channel_id=1, source_target_pairs={{0,48},{1,49},{2,50},{3,51},{4,52},{5,53},{6,54},{7,55},{8,56},{9,... | collective-permute-start | bytes 98312 | tf_op jit(solution)/shard_map/ppermute | solution.py:38
  103.3 4.5 %collective-permute-start.17 = (f32[16,256]{1,0:T(8,128)S(1)}, f32[16,256]{1,0:T(8,128)S(1)}, u32[]{:S(2)}, u32[]{:S(2)}) collective-permute-start(f32[16,256]{1,0:T(8,128)S(1)} %get-tuple-element.47), channel_id=1, source_target_pairs={{1,0},{2,3},{5,4},{6,7},{9,8},{10,11},{13,12},{14,15},{17,16},{18,... | collective-permute-start | bytes 49160 | tf_op jit(solution)/shard_map/ppermute | solution.py:38
  107.9 9.4 %collective-permute-start.25 = (f32[6,4,256]{2,1,0:T(4,128)S(1)}, f32[6,4,256]{2,1,0:T(4,128)S(1)}, u32[]{:S(2)}, u32[]{:S(2)}) collective-permute-start(f32[6,4,256]{2,1,0:T(4,128)S(1)} %get-tuple-element.45), channel_id=1, source_target_pairs={{0,4},{1,5},{2,6},{3,7},{4,0},{5,1},{6,2},{7,3},{8,12},{9,13},{10,... | collective-permute-start | bytes 73736 | tf_op jit(solution)/shard_map/ppermute | solution.py:38
  111.7 6.6 %collective-permute-start.26 = (f32[6,4,256]{2,1,0:T(4,128)S(1)}, f32[6,4,256]{2,1,0:T(4,128)S(1)}, u32[]{:S(2)}, u32[]{:S(2)}) collective-permute-start(f32[6,4,256]{2,1,0:T(4,128)S(1)} %get-tuple-element.44), channel_id=1, source_target_pairs={{0,8},{1,9},{2,10},{3,11},{4,12},{5,13},{6,14},{7,15},{8,0},{9,1},... | collective-permute-start | bytes 73736 | tf_op jit(solution)/shard_map/ppermute | solution.py:38
  117.0 7.2 %collective-permute-start.27 = (f32[6,4,256]{2,1,0:T(4,128)S(1)}, f32[6,4,256]{2,1,0:T(4,128)S(1)}, u32[]{:S(2)}, u32[]{:S(2)}) collective-permute-start(f32[6,4,256]{2,1,0:T(4,128)S(1)} %get-tuple-element.43), channel_id=1, source_target_pairs={{0,12},{1,13},{2,14},{3,15},{4,8},{5,9},{6,10},{7,11},{8,4},{9,5},... | collective-permute-start | bytes 73736 | tf_op jit(solution)/shard_map/ppermute | solution.py:38

commit v7 on v5

--- a/solution.py
+++ b/solution.py
@@ -11,6 +11,7 @@
 BLOCK = 256
 IRREPS = 4
 LANES = 128
+PARTS = 4
 NY, NX, NZ, NC, NG = 4, 4, 2, 2, 4
 AXES = ("blk", "grp")
 
@@ -45,6 +46,20 @@
 def plane_sum(chip):
     spread = lax.all_to_all(chip, "blk", 0, 0, tiled=True, axis_index_groups=plane_groups())
     return jnp.sum(spread, axis=0)
+
+
+def staged_sum(chip, position):
+    y, x = position // (NX * NZ * NC), (position // (NZ * NC)) % NX
+
+    def stage(value, place, count, target):
+        def block(step):
+            return lax.dynamic_index_in_dim(value, (place + step) % count, 0, keepdims=False)
+
+        arrived = [permute(block(step), functools.partial(target, step)) for step in (2, 1, 3)]
+        return block(0) + ((arrived[1] + arrived[2]) + arrived[0])
+
+    rows = stage(chip.reshape(NY, NX, *chip.shape[1:]), y, NY, lambda k, y, x, z, c, g: ((y + k) % NY, x, z, c, g))
+    return stage(rows, x, NX, lambda k, y, x, z, c, g: (y, (x + k) % NX, z, c, g))
 
 
 def pair_swap(y, x, z, c, g):
@@ -80,8 +95,9 @@
             value = jnp.where(lane < limit, value, 0.0)
             rounded = value.astype(jnp.bfloat16)
             place = slice(tile * LANES, (tile + 1) * LANES)
-            if slot == IRREPS - 1 and tile >= tiles // 2:
-                outputs[-1][:, (tile - tiles // 2) * LANES : (tile + 1 - tiles // 2) * LANES] = value
+            kept = tiles // PARTS
+            if slot == IRREPS - 1 and tile >= kept:
+                outputs[-1][:, (tile - kept) * LANES : (tile + 1 - kept) * LANES] = value
             high[:, place] = rounded
             low[:, place] = (value - rounded.astype(jnp.float32)).astype(jnp.bfloat16)
 
@@ -89,25 +105,23 @@
 def split_rows(amplitudes, scalars):
     pairs, _, slot_width = amplitudes.shape
     rows = 64
+    guest_width = slot_width - slot_width // PARTS
     view = amplitudes.reshape(pairs, IRREPS, slot_width // LANES, LANES).transpose(0, 2, 1, 3).reshape(-1, LANES)
     return pl.pallas_call(
         functools.partial(split_kernel, rows, slot_width),
         out_shape=[pltpu.HBM((pairs, slot_width), jnp.bfloat16)] * (2 * IRREPS)
-        + [pltpu.HBM((pairs, slot_width // 2), jnp.float32)],
+        + [pltpu.HBM((pairs, guest_width), jnp.float32)],
         grid_spec=pltpu.PrefetchScalarGridSpec(
             num_scalar_prefetch=1,
             grid=(pairs // rows,),
             in_specs=[pl.BlockSpec((rows * IRREPS * slot_width // LANES, LANES), lambda i, scalars: (i, 0))],
             out_specs=[pl.BlockSpec((rows, slot_width), lambda i, scalars: (i, 0))] * (2 * IRREPS)
-            + [pl.BlockSpec((rows, slot_width // 2), lambda i, scalars: (i, 0))],
+            + [pl.BlockSpec((rows, guest_width), lambda i, scalars: (i, 0))],
         ),
         compiler_params=pltpu.CompilerParams(vmem_limit_bytes=16 << 20),
         cost_estimate=pl.CostEstimate(flops=0, bytes_accessed=8 * pairs * IRREPS * slot_width, transcendentals=0),
         name="split_rows",
     )(scalars, *in_hbm([view]))
-
-
-PARTS = 4
 
 
 def halves_of(value):
@@ -159,7 +173,8 @@
 
 
 def put_halves(scalars, total, kept, sent, index):
-    groups, width, half = kept.shape[0], kept.shape[1] // 2, kept.shape[2]
+    groups, _, half = kept.shape
+    width = total.shape[1] // groups
     core = scalars[2 * IRREPS + 1] % NC
     for out, which in ((sent, 1 - core), (kept, core)):
         rows = total[pl.ds(pl.multiple_of(which * half, half), half), :]
@@ -176,52 +191,86 @@
         put_halves(scalars, total, kept, sent, k)
 
 
+def guest_kernel(scalars, crossed, guests, kept, sent, slab, rows, total, sems):
+    depth = rows.shape[1]
+    copies = [
+        pltpu.make_async_copy(crossed.at[pl.ds(crossed.shape[0] - depth, depth), :], slab, sems.at[0]),
+        pltpu.make_async_copy(guests, rows, sems.at[1]),
+    ]
+    for copy in copies:
+        copy.start()
+    for copy in copies:
+        copy.wait()
+    total[...] = split_dot(halves_of(rows[...]), halves_of(slab[...]))
+    put_halves(scalars, total, kept, sent, 0)
+
+
 def second_kernel(
-    scalars, passed, crossed, guests, high, low, kept, sent, slab, high_here, low_here, guest_slab, rows, total, sems, guest_sems
+    scalars, passed, crossed, high, low, high_last, low_last, kept, sent, high_out, low_out, slab, high_here, low_here, total, sems, last_sems
 ):
-    depth = rows.shape[1]
     here = (slab, high_here, low_here)
     ends = is_end(scalars)
     pl.when(ends)(lambda: start_parts(range(PARTS), (passed, high, low), here, sems))
     pl.when(jnp.logical_not(ends))(lambda: start_parts(range(PARTS), (crossed, high, low), here, sems))
-    guest_copies = [
-        pltpu.make_async_copy(crossed.at[pl.ds(depth, depth), :], guest_slab, guest_sems.at[0]),
-        pltpu.make_async_copy(guests, rows, guest_sems.at[1]),
+    copies = [
+        pltpu.make_async_copy(high_last, high_out, last_sems.at[0]),
+        pltpu.make_async_copy(low_last, low_out, last_sems.at[1]),
     ]
-    for copy in guest_copies:
+    for copy in copies:
         copy.start()
     add_parts(range(PARTS), (crossed, high, low), here, sems, total)
     put_halves(scalars, total, kept, sent, 0)
-    for copy in guest_copies:
+    for copy in copies:
         copy.wait()
-    total[...] = split_dot(halves_of(rows[...]), halves_of(guest_slab[...]))
-    put_halves(scalars, total, kept, sent, 1)
-
-
-def last_kernel(scalars, far, middle, high, low, out, slab, high_here, low_here, total, sems):
-    here = (slab, high_here, low_here)
+
+
+def last_kernel(scalars, far, middle, high, low, kept, got, out, slab, total, sems):
     ends = is_end(scalars)
     inner = jnp.logical_not(ends)
-    front, back = range(PARTS // 2), range(PARTS // 2, PARTS)
-    pl.when(ends)(lambda: start_parts(front, (far, high, low), here, sems))
-    pl.when(inner)(lambda: start_parts(range(PARTS), (middle, high, low), here, sems))
-    add_parts(front, (middle, high, low), here, sems, total)
-    pl.when(inner)(lambda: add_parts(back, (middle, high, low), here, sems, total))
-    out[...] = total[...].T.reshape(out.shape)
-
-
-def call_product(kernel, scalars, slabs, split, out_shapes, scratch, terms):
-    count = len(out_shapes)
+    depth = far.shape[0]
+    pairs = high.shape[0]
+
+    def copy_of(source, part):
+        place = pl.ds(part * depth, depth)
+        return pltpu.make_async_copy(source.at[place, :], slab.at[place, :], sems.at[part])
+
+    def add(part):
+        copy_of(middle, part).wait()
+        place = slice(part * depth, (part + 1) * depth)
+        term = split_dot((high[:, place], low[:, place]), halves_of(slab[place, :]))
+        total[...] = term if part == 0 else total[...] + term
+
+    pl.when(ends)(lambda: copy_of(far, 0).start())
+
+    @pl.when(inner)
+    def _():
+        for part in range(PARTS):
+            copy_of(middle, part).start()
+
+    out[:, :, pairs:] = kept[...] + got[...]
+    add(0)
+
+    @pl.when(inner)
+    def _():
+        for part in range(1, PARTS):
+            add(part)
+
+    out[:, :, :pairs] = total[...].T.reshape(out.shape[0], out.shape[1], pairs)
+
+
+def call_product(kernel, scalars, moved, fixed, resident, out_shapes, scratch, terms):
     vmem = pl.BlockSpec(memory_space=pltpu.VMEM)
     return pl.pallas_call(
         kernel,
-        out_shape=[jax.ShapeDtypeStruct(shape, jnp.float32) for shape in out_shapes],
-        in_specs=[pl.BlockSpec(memory_space=pltpu.SMEM)] + [pl.BlockSpec(memory_space=pl.ANY)] * (len(slabs) + len(split)),
-        out_specs=[vmem] * count,
+        out_shape=out_shapes,
+        in_specs=[pl.BlockSpec(memory_space=pltpu.SMEM)]
+        + [pl.BlockSpec(memory_space=pl.ANY)] * (len(moved) + len(fixed))
+        + [vmem] * len(resident),
+        out_specs=[vmem] * len(out_shapes),
         scratch_shapes=scratch,
         compiler_params=pltpu.CompilerParams(vmem_limit_bytes=16 << 20),
         cost_estimate=pl.CostEstimate(flops=6 * terms, bytes_accessed=6 << 20, transcendentals=0),
-    )(scalars, *slabs, *in_hbm(split))
+    )(scalars, *moved, *in_hbm(fixed), *resident)
 
 
 def finish_kernel(column_width, scalars, *refs):
@@ -273,19 +322,23 @@
     scalars = jnp.concatenate([owner_map, irrep_sizes, jnp.stack([group, position])])
     *split, moved = split_rows(amplitudes, scalars)
     guests = permute(moved, inward)
+    passed = permute(middle, outward)
     crossed = permute(near, middle_swap)
-    passed = permute(middle, outward)
-    far = permute(crossed[: rows // 2], outward)
+    far = permute(crossed[: rows // PARTS], outward)
 
     matrix = pltpu.VMEM((pairs, slots), jnp.bfloat16)
     slab = pltpu.VMEM((rows, columns), jnp.float32)
     total = pltpu.VMEM((pairs, columns), jnp.float32)
     sems = pltpu.SemaphoreType.DMA((PARTS, 3))
+    two_sems = pltpu.SemaphoreType.DMA((2,))
     terms = pairs * columns * slots
-    joint = [(plane, 2 * width, half)] * 2
-
-    def chip_sum(kept, sent):
-        return kept + permute(sent, lambda y, x, z, c, g: (y, x, z, 1 - c, g))
+    guest_width = moved.shape[1]
+
+    def of(*shape):
+        return jax.ShapeDtypeStruct(shape, jnp.float32)
+
+    def other_core(value):
+        return permute(value, lambda y, x, z, c, g: (y, x, z, 1 - c, g))
 
     scratch = [
         pltpu.VMEM((2, rows, columns), jnp.float32),
@@ -294,28 +347,37 @@
         total,
         pltpu.SemaphoreType.DMA((2, PARTS, 3)),
     ]
-    result = call_product(first_kernel, scalars, [own, near], split[:4], joint, scratch, 2 * terms)
-    first_chip = chip_sum(*result)
+    outs = [of(plane, 2 * width, half)] * 2
+    kept, sent = call_product(first_kernel, scalars, [own, near], split[:4], [], outs, scratch, 2 * terms)
+    first_chip = kept + other_core(sent)
     first = plane_sum(first_chip)
-    scratch = [
-        slab,
-        matrix,
-        matrix,
-        pltpu.VMEM((rows // 2, columns), jnp.float32),
-        pltpu.VMEM((pairs, slots // 2), jnp.float32),
-        total,
-        sems,
-        pltpu.SemaphoreType.DMA((2,)),
-    ]
-    result = call_product(second_kernel, scalars, [passed, crossed, guests], split[4:6], joint, scratch, 2 * terms)
-    second_chip = chip_sum(*result)
-    second = plane_sum(second_chip)
-    scratch = [slab, matrix, matrix, total, sems]
-    (result,) = call_product(last_kernel, scalars, [far, middle], split[6:], [(plane, width, pairs)], scratch, terms)
-    third = plane_sum(result)
-    third = third.reshape(width, NC, half).swapaxes(0, 1)
-    handed = permute(second[width:], outward)
-    units = jnp.concatenate([first.reshape(2, width, half), second[None, :width], handed[None], third], axis=0)
+
+    scratch = [pltpu.VMEM((guest_width, columns), jnp.float32), pltpu.VMEM((pairs, guest_width), jnp.float32), total, two_sems]
+    outs = [of(plane, width, half)] * 2
+    kept, sent = call_product(
+        guest_kernel, scalars, [crossed, guests], [], [], outs, scratch, pairs * columns * guest_width
+    )
+    guest = staged_sum(kept + other_core(sent), position)
+    handed = permute(guest, outward)
+
+    scratch = [slab, matrix, matrix, total, sems, two_sems]
+    outs = [of(plane, width, half)] * 2 + [jax.ShapeDtypeStruct((pairs, slots), jnp.bfloat16)] * 2
+    kept, sent, *resident = call_product(second_kernel, scalars, [passed, crossed], split[4:], [], outs, scratch, terms)
+    got = other_core(sent)
+    scratch = [slab, total, pltpu.SemaphoreType.DMA((PARTS,))]
+    (result,) = call_product(
+        last_kernel,
+        scalars,
+        [far, middle],
+        [],
+        [*resident, kept, got],
+        [of(plane, width, pairs + half)],
+        scratch,
+        terms,
+    )
+    late = plane_sum(result)
+    late = late.reshape(width, NC + 1, half).swapaxes(0, 1)
+    units = jnp.concatenate([first.reshape(2, width, half), late[NC:], handed[None], late[:NC]], axis=0)
     units = units.reshape(-1, NZ * NC, column_width, half)
 
     def share(flip):

time: 125 us -> 121 us (0.968)
  waiting for transfers between devices: 48.5 us -> 34.6 us
  starting transfers between devices: 39.8 us -> 49.5 us
    all_to_all x3 -> x2, waiting for transfers between devices: 16.7 us -> 0.01 us  [plane_sum(): lax.all_to_all(chip, 'blk', 0, 0, tiled=True, axis_index_groups=plane_gro...]
    ppermute x12 -> x19, starting transfers between devices: 25.3 us -> 38.5 us  [permute(): return lax.ppermute(value, AXES, pairs)]
    all_to_all x3 -> x2, starting transfers between devices: 14.6 us -> 11 us  [plane_sum(): lax.all_to_all(chip, 'blk', 0, 0, tiled=True, axis_index_groups=plane_gro...]
    ppermute x12 -> x19, waiting for transfers between devices: 31.8 us -> 34.6 us  [permute(): return lax.ppermute(value, AXES, pairs)]
    add x2 -> x4, other arithmetic: 2.81 us -> 1.96 us  [the longest x1 1.07 us: local(): guest = staged_sum(kept + other_core(sent), position)]
    pallas_call x3 -> x4, Pallas kernels: 14.9 us -> 15.3 us  [call_product(): pl.pallas_call(kernel, out_shape=out_shapes, in_specs=[pl.BlockSpec(memor...]
  transfers between devices with their start and end apart: 15 -> 21, of which waited for: 9 -> 8; matrix products, arithmetic and copies ran while one was open for 5% -> 4% of each run, Pallas kernels for 22% -> 23%
where the time goes in v7:
time: 121 us; the launch traced here: 120 us
  starting transfers between devices  49.5 us (41%)
  waiting for transfers between devices  34.6 us (29%)
  Pallas kernels  29.3 us (24%)
  other arithmetic  3.83 us (3%)
  local copies, waits for them, and re-layouts  2.62 us (2%)
    ppermute x19, starting transfers between devices, permute(): return lax.ppermute(value, AXES, pairs)  38.5 us
    ppermute x19, waiting for transfers between devices, permute(): return lax.ppermute(value, AXES, pairs)  34.6 us
    pallas_call x4, Pallas kernels, call_product(): pl.pallas_call(kernel, out_shape=out_shapes, in_specs=[pl.BlockSpec(memor...  15.3 us
    pallas_call x1, Pallas kernels, split_rows(): pl.pallas_call(functools.partial(split_kernel, rows, slot_width), out_sha...  12.8 us
    all_to_all x2, starting transfers between devices, plane_sum(): lax.all_to_all(chip, 'blk', 0, 0, tiled=True, axis_index_groups=plane_gro...  11 us
  transfers between devices with their start and end apart: 21, of which 8 were waited for; matrix products, arithmetic and copies ran while one was open for 4% of the time, Pallas kernels for 23%

profile of v7, /device:TPU:1, one launch (start us, length us, event | category | flops | bytes accessed | tf_op | source)
XLA Modules:
  0.0 120.3 jit_solution(8974584355192204546)
XLA Ops:
  0.0 2.5 %collective-permute-start = (f32[1024,256]{1,0:T(8,128)}, f32[1024,256]{1,0:T(8,128)}, u32[]{:S(2)}, u32[]{:S(2)}) collective-permute-start(f32[1024,256]{1,0:T(8,128)} %bitcast.36), channel_id=1, source_target_pairs={{0,1},{1,0},{2,3},{3,2},{4,5},{5,4},{6,7},{7,6},{8,9},{9,8},{10,11... | collective-permute-start | bytes 3145736 | tf_op jit(solution)/shard_map/ppermute | solution.py:39
  2.5 1.6 %collective-permute-start.4 = (f32[1024,256]{1,0:T(8,128)}, f32[1024,256]{1,0:T(8,128)}, u32[]{:S(2)}, u32[]{:S(2)}) collective-permute-start(f32[1024,256]{1,0:T(8,128)} %bitcast.37), channel_id=1, source_target_pairs={{1,2},{2,1},{5,6},{6,5},{9,10},{10,9},{13,14},{14,13},{17,18},{18,... | collective-permute-start | bytes 3145736 | tf_op jit(solution)/shard_map/ppermute | solution.py:39
  4.1 0.7 pad_add_fusion.scalars
  4.8 0.0 copy-start
  4.8 12.8 %split_rows.1 = (bf16[512,1024]{1,0:T(8,128)(2,1)}, bf16[512,1024]{1,0:T(8,128)(2,1)}, bf16[512,1024]{1,0:T(8,128)(2,1)}, bf16[512,1024]{1,0:T(8,128)(2,1)}, bf1...) custom-call(s32[10]{0:T(128)S(1)} %pad_add_fusion.scalars, ...), custom_call_target="tpu_custom_call" | custom-call | bytes 16777216 | tf_op jit(solution)/shard_map/split_rows/pallas_call | solution.py:110
  17.7 5.6 %collective-permute-start.7 = (f32[512,768]{1,0:T(8,128)}, f32[512,768]{1,0:T(8,128)S(1)}, u32[]{:S(2)}, u32[]{:S(2)}) collective-permute-start(f32[512,768]{1,0:T(8,128)} %get-tuple-element.36), channel_id=1, source_target_pairs={{0,1},{3,2},{4,5},{7,6},{8,9},{11,10},{12,13},{15,14},{16,17},{19,... | collective-permute-start | bytes 4718600 | tf_op jit(solution)/shard_map/ppermute | solution.py:39
  23.2 1.4 %collective-permute-done.near = f32[1024,256]{1,0:T(8,128)} collective-permute-done((f32[1024,256]{1,0:T(8,128)}, f32[1024,256]{1,0:T(8,128)}, u32[]{:S(2)}, u32[]{:S(2)}) %collective-permute-start) | collective-permute-done | bytes 1048608 | tf_op jit(solution)/shard_map/ppermute | solution.py:39
  24.6 0.7 collective-permute-start.2
  25.3 0.0 collective-permute-done.4.middle
  25.4 1.3 %collective-permute-start.5 = (f32[1024,256]{1,0:T(8,128)}, f32[1024,256]{1,0:T(8,128)}, u32[]{:S(2)}, u32[]{:S(2)}) collective-permute-start(f32[1024,256]{1,0:T(8,128)} %collective-permute-done.4.middle), channel_id=1, source_target_pairs={{1,0},{2,3},{5,4},{6,7},{9,8},{10,11},{13,12},{14,15},{17,16},{18,... | collective-permute-start | bytes 3145736 | tf_op jit(solution)/shard_map/ppermute | solution.py:39
  26.6 0.0 copy-done
  26.7 6.0 %shard_map.46 = (f32[16,32,256]{2,1,0:T(8,128)S(1)}, f32[16,32,256]{2,1,0:T(8,128)S(1)}) custom-call(s32[10]{0:T(128)S(1)} %pad_add_fusion.scalars, f32[1024,256]{1,0:T(8,128)S(1)} %bitcast.38, f32[1024,256]{1,0:T(8,128)} %collective-permute-done.near, bf16[512,1024]{1,0:T(8,128)(2,1)} %get-tuple-element.22.high_0, ...), custom_call_target="tpu_custom_call" | custom-call | flops 1610612736 | bytes 6291456 | tf_op jit(solution)/shard_map/pallas_call | solution.py:263
  32.7 2.7 %collective-permute-start.1 = (f32[16,32,256]{2,1,0:T(8,128)S(1)}, f32[16,32,256]{2,1,0:T(8,128)S(1)}, u32[]{:S(2)}, u32[]{:S(2)}) collective-permute-start(f32[16,32,256]{2,1,0:T(8,128)S(1)} %get-tuple-element.27), channel_id=1, source_target_pairs={{0,4},{1,5},{2,6},{3,7},{4,0},{5,1},{6,2},{7,3},{8,12},{9,13},{10,... | collective-permute-start | bytes 1572872 | tf_op jit(solution)/shard_map/ppermute | solution.py:39
  35.4 1.5 %collective-permute-done.1 = f32[16,32,256]{2,1,0:T(8,128)S(1)} collective-permute-done((f32[16,32,256]{2,1,0:T(8,128)S(1)}, f32[16,32,256]{2,1,0:T(8,128)S(1)}, u32[]{:S(2)}, u32[]{:S(2)}) %collective-permute-start.1) | collective-permute-done | bytes 524320 | tf_op jit(solution)/shard_map/ppermute | solution.py:39
  37.0 0.9 add.124
  37.8 6.8 %all-to-all-start = ((f32[16,32,256]{2,1,0:T(8,128)}), f32[16,32,256]{2,1,0:T(8,128)}, u32[]{:S(2)}, u32[]{:S(2)}) async-start(f32[16,32,256]{2,1,0:T(8,128)} %add.124), calls=%async_computation | async-start | bytes 1048576 | tf_op jit(solution)/shard_map/all_to_all | solution.py:47
  44.6 13.7 %collective-permute-done.7.guests = f32[512,768]{1,0:T(8,128)S(1)} collective-permute-done((f32[512,768]{1,0:T(8,128)}, f32[512,768]{1,0:T(8,128)S(1)}, u32[]{:S(2)}, u32[]{:S(2)}) %collective-permute-start.7) | collective-permute-done | bytes 1572896 | tf_op jit(solution)/shard_map/ppermute | solution.py:39
  58.3 0.0 collective-permute-done.2.crossed
  58.3 2.4 %shard_map.49 = (f32[16,16,256]{2,1,0:T(8,128)S(1)}, f32[16,16,256]{2,1,0:T(8,128)}) custom-call(s32[10]{0:T(128)S(1)} %pad_add_fusion.scalars, f32[1024,256]{1,0:T(8,128)S(1)} %collective-permute-done.2.crossed, f32[512,768]{1,0:T(8,128)S(1)} %collective-permute-done.7.guests), custom_call_target="tpu_custom_call" | custom-call | flops 603979776 | bytes 6291456 | tf_op jit(solution)/shard_map/pallas_call | solution.py:263
  60.7 0.0 copy-start.3
  60.7 1.6 %collective-permute-start.8 = (f32[16,16,256]{2,1,0:T(8,128)}, f32[16,16,256]{2,1,0:T(8,128)}, u32[]{:S(2)}, u32[]{:S(2)}) collective-permute-start(f32[16,16,256]{2,1,0:T(8,128)} %get-tuple-element.38), channel_id=1, source_target_pairs={{0,4},{1,5},{2,6},{3,7},{4,0},{5,1},{6,2},{7,3},{8,12},{9,13},{10,... | collective-permute-start | bytes 786440 | tf_op jit(solution)/shard_map/ppermute | solution.py:39
  62.3 0.7 slice.12
  63.1 1.3 %collective-permute-start.3 = (f32[256,256]{1,0:T(8,128)}, f32[256,256]{1,0:T(8,128)S(1)}, u32[]{:S(2)}, u32[]{:S(2)}) collective-permute-start(f32[256,256]{1,0:T(8,128)} %slice.12), channel_id=1, source_target_pairs={{1,0},{2,3},{5,4},{6,7},{9,8},{10,11},{13,12},{14,15},{17,16},{18,... | collective-permute-start | bytes 786440 | tf_op jit(solution)/shard_map/ppermute | solution.py:39
  64.4 0.0 collective-permute-done.5.passed
  64.4 0.0 copy-done.3
  64.4 4.7 %shard_map.47 = (f32[16,16,256]{2,1,0:T(8,128)S(1)}, f32[16,16,256]{2,1,0:T(8,128)}, bf16[512,1024]{1,0:T(8,128)(2,1)S(1)}, bf16[512,1024]{1,0:T(8,128)(2,1)S(1)}) custom-call(s32[10]{0:T(128)S(1)} %pad_add_fusion.scalars, f32[1024,256]{1,0:T(8,128)} %collective-permute-done.5.passed, f32[1024,256]{1,0:T(8,128)S(1)} %collective-permute-done.2.crossed, ...), custom_call_target="tpu_custom_call" | custom-call | flops 805306368 | bytes 6291456 | tf_op jit(solution)/shard_map/pallas_call | solution.py:263
  69.1 0.0 copy-start.1
  69.1 0.7 copy-done.1
  69.8 0.0 collective-permute-start.6
  69.8 0.0 collective-permute-done.8
  69.8 1.1 add.125
  70.9 3.0 %collective-permute-start.11 = (f32[4,16,256]{2,1,0:T(8,128)S(1)}, f32[4,16,256]{2,1,0:T(8,128)S(1)}, u32[]{:S(2)}, u32[]{:S(2)}) collective-permute-start(f32[4,16,256]{2,1,0:T(8,128)S(1)} %get-tuple-element.40), channel_id=1, source_target_pairs={{0,128},{1,129},{2,130},{3,131},{4,132},{5,133},{6,134},{7,135},{8... | collective-permute-start | bytes 196616 | tf_op jit(solution)/shard_map/ppermute | solution.py:39
  73.9 0.4 collective-permute-start.9
  74.3 2.3 %collective-permute-start.10 = (f32[4,16,256]{2,1,0:T(8,128)S(1)}, f32[4,16,256]{2,1,0:T(8,128)S(1)}, u32[]{:S(2)}, u32[]{:S(2)}) collective-permute-start(f32[4,16,256]{2,1,0:T(8,128)S(1)} %get-tuple-element.39), channel_id=1, source_target_pairs={{0,192},{1,193},{2,194},{3,195},{4,196},{5,197},{6,198},{7,199},{8... | collective-permute-start | bytes 196616 | tf_op jit(solution)/shard_map/ppermute | solution.py:39
  76.6 0.0 collective-permute-done.3.far
  76.6 0.0 collective-permute-done.6.got
  76.6 0.0 copy-start.2
  76.6 0.9 copy-done.2
  77.5 2.3 %shard_map.48 = f32[16,16,768]{2,1,0:T(8,128)} custom-call(s32[10]{0:T(128)S(1)} %pad_add_fusion.scalars, f32[256,256]{1,0:T(8,128)S(1)} %collective-permute-done.3.far, f32[1024,256]{1,0:T(8,128)} %collective-permute-done.4.middle, bf16[512,1024]{1,0:T(8,128)(2,1)S(1)} %get-tuple-element.32.high, bf16[512,1024]{1,0:T(8,128)(2,1)S(1)} %get-tuple-element.33.low, ...), custom_call_target="tpu_custom_call" | custom-call | flops 805306368 | bytes 6291456 | tf_op jit(solution)/shard_map/pallas_call | solution.py:263
  79.8 0.0 all-to-all-done
  79.8 4.2 %all-to-all-start.1 = ((f32[16,16,768]{2,1,0:T(8,128)}), f32[16,16,768]{2,1,0:T(8,128)S(1)}, u32[]{:S(2)}, u32[]{:S(2)}) async-start(f32[16,16,768]{2,1,0:T(8,128)} %shard_map.48), calls=%async_computation.1 | async-start | bytes 1572864 | tf_op jit(solution)/shard_map/all_to_all | solution.py:47
  84.1 0.0 collective-permute-done.11
  84.1 0.0 collective-permute-done.9
  84.1 0.0 collective-permute-done.10
  84.2 2.8 %collective-permute-start.14 = (f32[16,256]{1,0:T(8,128)S(1)}, f32[16,256]{1,0:T(8,128)S(1)}, u32[]{:S(2)}, u32[]{:S(2)}) collective-permute-start(f32[16,256]{1,0:T(8,128)S(1)} %get-tuple-element.47), channel_id=1, source_target_pairs={{0,32},{1,33},{2,34},{3,35},{4,36},{5,37},{6,38},{7,39},{8,40},{9,... | collective-permute-start | bytes 49160 | tf_op jit(solution)/shard_map/ppermute | solution.py:39
  87.0 0.3 collective-permute-start.12
  87.3 2.4 %collective-permute-start.13 = (f32[16,256]{1,0:T(8,128)S(1)}, f32[16,256]{1,0:T(8,128)S(1)}, u32[]{:S(2)}, u32[]{:S(2)}) collective-permute-start(f32[16,256]{1,0:T(8,128)S(1)} %get-tuple-element.46), channel_id=1, source_target_pairs={{0,48},{1,49},{2,50},{3,51},{4,52},{5,53},{6,54},{7,55},{8,56},{9,... | collective-permute-start | bytes 49160 | tf_op jit(solution)/shard_map/ppermute | solution.py:39
  89.7 1.1 reduce_sum.18
  90.8 4.3 %collective-permute-done.14 = f32[16,256]{1,0:T(8,128)S(1)} collective-permute-done((f32[16,256]{1,0:T(8,128)S(1)}, f32[16,256]{1,0:T(8,128)S(1)}, u32[]{:S(2)}, u32[]{:S(2)}) %collective-permute-start.14) | collective-permute-done | bytes 16416 | tf_op jit(solution)/shard_map/ppermute | solution.py:39
  95.1 0.9 collective-permute-done.12
  95.9 0.0 collective-permute-done.13
  96.0 1.3 %collective-permute-start.15 = (f32[16,256]{1,0:T(8,128)S(1)}, f32[16,256]{1,0:T(8,128)S(1)}, u32[]{:S(2)}, u32[]{:S(2)}) collective-permute-start(f32[16,256]{1,0:T(8,128)S(1)} %bitcast_add_fusion.1), channel_id=1, source_target_pairs={{1,0},{2,3},{5,4},{6,7},{9,8},{10,11},{13,12},{14,15},{17,16},{18,... | collective-permute-start | bytes 49160 | tf_op jit(solution)/shard_map/ppermute | solution.py:39
  97.3 5.8 %collective-permute-done.15 = f32[16,256]{1,0:T(8,128)S(1)} collective-permute-done((f32[16,256]{1,0:T(8,128)S(1)}, f32[16,256]{1,0:T(8,128)S(1)}, u32[]{:S(2)}, u32[]{:S(2)}) %collective-permute-start.15) | collective-permute-done | bytes 16416 | tf_op jit(solution)/shard_map/ppermute | solution.py:39
  103.1 0.0 all-to-all-done.1
  103.3 2.6 %collective-permute-start.16 = (f32[6,4,256]{2,1,0:T(4,128)S(1)}, f32[6,4,256]{2,1,0:T(4,128)S(1)}, u32[]{:S(2)}, u32[]{:S(2)}) collective-permute-start(f32[6,4,256]{2,1,0:T(4,128)S(1)} %get-tuple-element.44), channel_id=1, source_target_pairs={{0,4},{1,5},{2,6},{3,7},{4,0},{5,1},{6,2},{7,3},{8,12},{9,13},{10,... | collective-permute-start | bytes 73736 | tf_op jit(solution)/shard_map/ppermute | solution.py:39
  105.9 6.0 %collective-permute-start.17 = (f32[6,4,256]{2,1,0:T(4,128)S(1)}, f32[6,4,256]{2,1,0:T(4,128)S(1)}, u32[]{:S(2)}, u32[]{:S(2)}) collective-permute-start(f32[6,4,256]{2,1,0:T(4,128)S(1)} %get-tuple-element.43), channel_id=1, source_target_pairs={{0,8},{1,9},{2,10},{3,11},{4,12},{5,13},{6,14},{7,15},{8,0},{9,1},... | collective-permute-start | bytes 73736 | tf_op jit(solution)/shard_map/ppermute | solution.py:39
  111.9 0.1 collective-permute-start.18
  112.0 0.0 collective-permute-done.16.refs_1_
  112.0 1.1 collective-permute-done.17.refs_2_
  113.2 5.9 %collective-permute-done.18.refs_3_ = f32[6,4,256]{2,1,0:T(4,128)S(1)} collective-permute-done((f32[6,4,256]{2,1,0:T(4,128)S(1)}, f32[6,4,256]{2,1,0:T(4,128)S(1)}, u32[]{:S(2)}, u32[]{:S(2)}) %collective-permute-start.18) | collective-permute-done | bytes 24608 | tf_op jit(solution)/shard_map/ppermute | solution.py:39
  119.1 1.2 finish.1
  (16 shorter events, 0.3 us)
Async XLA Ops:
  0.0 24.6 %collective-permute-start = (f32[1024,256]{1,0:T(8,128)}, f32[1024,256]{1,0:T(8,128)}, u32[]{:S(2)}, u32[]{:S(2)}) collective-permute-start(f32[1024,256]{1,0:T(8,128)} %bitcast.36), channel_id=1, source_target_pairs={{0,1},{1,0},{2,3},{3,2},{4,5},{5,4},{6,7},{7,6},{8,9},{9,8},{10,11... | collective-permute-start | bytes 3145736 | tf_op jit(solution)/shard_map/ppermute | solution.py:39
  2.5 22.9 %collective-permute-start.4 = (f32[1024,256]{1,0:T(8,128)}, f32[1024,256]{1,0:T(8,128)}, u32[]{:S(2)}, u32[]{:S(2)}) collective-permute-start(f32[1024,256]{1,0:T(8,128)} %bitcast.37), channel_id=1, source_target_pairs={{1,2},{2,1},{5,6},{6,5},{9,10},{10,9},{13,14},{14,13},{17,18},{18,... | collective-permute-start | bytes 3145736 | tf_op jit(solution)/shard_map/ppermute | solution.py:39
  4.8 21.8 %copy-start = (f32[1,1024,256]{2,1,0:T(8,128)S(1)}, f32[1,1024,256]{2,1,0:T(8,128)}, u32[]{:S(2)}) copy-start(f32[1,1024,256]{2,1,0:T(8,128)} %param.5) | copy-start | bytes 3145732
  17.7 40.7 %collective-permute-start.7 = (f32[512,768]{1,0:T(8,128)}, f32[512,768]{1,0:T(8,128)S(1)}, u32[]{:S(2)}, u32[]{:S(2)}) collective-permute-start(f32[512,768]{1,0:T(8,128)} %get-tuple-element.36), channel_id=1, source_target_pairs={{0,1},{3,2},{4,5},{7,6},{8,9},{11,10},{12,13},{15,14},{16,17},{19,... | collective-permute-start | bytes 4718600 | tf_op jit(solution)/shard_map/ppermute | solution.py:39
  24.6 33.7 %collective-permute-start.2 = (f32[1024,256]{1,0:T(8,128)}, f32[1024,256]{1,0:T(8,128)S(1)}, u32[]{:S(2)}, u32[]{:S(2)}) collective-permute-start(f32[1024,256]{1,0:T(8,128)} %collective-permute-done.near), channel_id=1, source_target_pairs={{1,2},{2,1},{5,6},{6,5},{9,10},{10,9},{13,14},{14,13},{17,18},{18,... | collective-permute-start | bytes 3145736 | tf_op jit(solution)/shard_map/ppermute | solution.py:39
  25.4 39.0 %collective-permute-start.5 = (f32[1024,256]{1,0:T(8,128)}, f32[1024,256]{1,0:T(8,128)}, u32[]{:S(2)}, u32[]{:S(2)}) collective-permute-start(f32[1024,256]{1,0:T(8,128)} %collective-permute-done.4.middle), channel_id=1, source_target_pairs={{1,0},{2,3},{5,4},{6,7},{9,8},{10,11},{13,12},{14,15},{17,16},{18,... | collective-permute-start | bytes 3145736 | tf_op jit(solution)/shard_map/ppermute | solution.py:39
  32.7 4.3 %collective-permute-start.1 = (f32[16,32,256]{2,1,0:T(8,128)S(1)}, f32[16,32,256]{2,1,0:T(8,128)S(1)}, u32[]{:S(2)}, u32[]{:S(2)}) collective-permute-start(f32[16,32,256]{2,1,0:T(8,128)S(1)} %get-tuple-element.27), channel_id=1, source_target_pairs={{0,4},{1,5},{2,6},{3,7},{4,0},{5,1},{6,2},{7,3},{8,12},{9,13},{10,... | collective-permute-start | bytes 1572872 | tf_op jit(solution)/shard_map/ppermute | solution.py:39
  37.8 42.0 %all-to-all-start = ((f32[16,32,256]{2,1,0:T(8,128)}), f32[16,32,256]{2,1,0:T(8,128)}, u32[]{:S(2)}, u32[]{:S(2)}) async-start(f32[16,32,256]{2,1,0:T(8,128)} %add.124), calls=%async_computation | async-start | bytes 1048576 | tf_op jit(solution)/shard_map/all_to_all | solution.py:47
  60.7 3.7 %copy-start.3 = (f32[16,16,256]{2,1,0:T(8,128)}, f32[16,16,256]{2,1,0:T(8,128)S(1)}, u32[]{:S(2)}) copy-start(f32[16,16,256]{2,1,0:T(8,128)S(1)} %get-tuple-element.37) | copy-start | bytes 786436
  60.7 9.1 %collective-permute-start.8 = (f32[16,16,256]{2,1,0:T(8,128)}, f32[16,16,256]{2,1,0:T(8,128)}, u32[]{:S(2)}, u32[]{:S(2)}) collective-permute-start(f32[16,16,256]{2,1,0:T(8,128)} %get-tuple-element.38), channel_id=1, source_target_pairs={{0,4},{1,5},{2,6},{3,7},{4,0},{5,1},{6,2},{7,3},{8,12},{9,13},{10,... | collective-permute-start | bytes 786440 | tf_op jit(solution)/shard_map/ppermute | solution.py:39
  63.1 13.5 %collective-permute-start.3 = (f32[256,256]{1,0:T(8,128)}, f32[256,256]{1,0:T(8,128)S(1)}, u32[]{:S(2)}, u32[]{:S(2)}) collective-permute-start(f32[256,256]{1,0:T(8,128)} %slice.12), channel_id=1, source_target_pairs={{1,0},{2,3},{5,4},{6,7},{9,8},{10,11},{13,12},{14,15},{17,16},{18,... | collective-permute-start | bytes 786440 | tf_op jit(solution)/shard_map/ppermute | solution.py:39
  69.1 0.7 copy-start.1
  69.8 6.8 %collective-permute-start.6 = (f32[16,16,256]{2,1,0:T(8,128)}, f32[16,16,256]{2,1,0:T(8,128)S(1)}, u32[]{:S(2)}, u32[]{:S(2)}) collective-permute-start(f32[16,16,256]{2,1,0:T(8,128)} %get-tuple-element.35), channel_id=1, source_target_pairs={{0,4},{1,5},{2,6},{3,7},{4,0},{5,1},{6,2},{7,3},{8,12},{9,13},{10,... | collective-permute-start | bytes 786440 | tf_op jit(solution)/shard_map/ppermute | solution.py:39
  70.9 13.2 %collective-permute-start.11 = (f32[4,16,256]{2,1,0:T(8,128)S(1)}, f32[4,16,256]{2,1,0:T(8,128)S(1)}, u32[]{:S(2)}, u32[]{:S(2)}) collective-permute-start(f32[4,16,256]{2,1,0:T(8,128)S(1)} %get-tuple-element.40), channel_id=1, source_target_pairs={{0,128},{1,129},{2,130},{3,131},{4,132},{5,133},{6,134},{7,135},{8... | collective-permute-start | bytes 196616 | tf_op jit(solution)/shard_map/ppermute | solution.py:39
  73.9 10.2 %collective-permute-start.9 = (f32[4,16,256]{2,1,0:T(8,128)S(1)}, f32[4,16,256]{2,1,0:T(8,128)S(1)}, u32[]{:S(2)}, u32[]{:S(2)}) collective-permute-start(f32[4,16,256]{2,1,0:T(8,128)S(1)} %get-tuple-element.41), channel_id=1, source_target_pairs={{0,64},{1,65},{2,66},{3,67},{4,68},{5,69},{6,70},{7,71},{8,72},{9,... | collective-permute-start | bytes 196616 | tf_op jit(solution)/shard_map/ppermute | solution.py:39
  74.3 9.8 %collective-permute-start.10 = (f32[4,16,256]{2,1,0:T(8,128)S(1)}, f32[4,16,256]{2,1,0:T(8,128)S(1)}, u32[]{:S(2)}, u32[]{:S(2)}) collective-permute-start(f32[4,16,256]{2,1,0:T(8,128)S(1)} %get-tuple-element.39), channel_id=1, source_target_pairs={{0,192},{1,193},{2,194},{3,195},{4,196},{5,197},{6,198},{7,199},{8... | collective-permute-start | bytes 196616 | tf_op jit(solution)/shard_map/ppermute | solution.py:39
  76.6 1.0 copy-start.2
  79.8 23.2 %all-to-all-start.1 = ((f32[16,16,768]{2,1,0:T(8,128)}), f32[16,16,768]{2,1,0:T(8,128)S(1)}, u32[]{:S(2)}, u32[]{:S(2)}) async-start(f32[16,16,768]{2,1,0:T(8,128)} %shard_map.48), calls=%async_computation.1 | async-start | bytes 1572864 | tf_op jit(solution)/shard_map/all_to_all | solution.py:47
  84.2 10.9 %collective-permute-start.14 = (f32[16,256]{1,0:T(8,128)S(1)}, f32[16,256]{1,0:T(8,128)S(1)}, u32[]{:S(2)}, u32[]{:S(2)}) collective-permute-start(f32[16,256]{1,0:T(8,128)S(1)} %get-tuple-element.47), channel_id=1, source_target_pairs={{0,32},{1,33},{2,34},{3,35},{4,36},{5,37},{6,38},{7,39},{8,40},{9,... | collective-permute-start | bytes 49160 | tf_op jit(solution)/shard_map/ppermute | solution.py:39
  87.0 8.9 %collective-permute-start.12 = (f32[16,256]{1,0:T(8,128)S(1)}, f32[16,256]{1,0:T(8,128)S(1)}, u32[]{:S(2)}, u32[]{:S(2)}) collective-permute-start(f32[16,256]{1,0:T(8,128)S(1)} %get-tuple-element.48), channel_id=1, source_target_pairs={{0,16},{1,17},{2,18},{3,19},{4,20},{5,21},{6,22},{7,23},{8,24},{9,... | collective-permute-start | bytes 49160 | tf_op jit(solution)/shard_map/ppermute | solution.py:39
  87.3 8.6 %collective-permute-start.13 = (f32[16,256]{1,0:T(8,128)S(1)}, f32[16,256]{1,0:T(8,128)S(1)}, u32[]{:S(2)}, u32[]{:S(2)}) collective-permute-start(f32[16,256]{1,0:T(8,128)S(1)} %get-tuple-element.46), channel_id=1, source_target_pairs={{0,48},{1,49},{2,50},{3,51},{4,52},{5,53},{6,54},{7,55},{8,56},{9,... | collective-permute-start | bytes 49160 | tf_op jit(solution)/shard_map/ppermute | solution.py:39
  96.0 7.1 %collective-permute-start.15 = (f32[16,256]{1,0:T(8,128)S(1)}, f32[16,256]{1,0:T(8,128)S(1)}, u32[]{:S(2)}, u32[]{:S(2)}) collective-permute-start(f32[16,256]{1,0:T(8,128)S(1)} %bitcast_add_fusion.1), channel_id=1, source_target_pairs={{1,0},{2,3},{5,4},{6,7},{9,8},{10,11},{13,12},{14,15},{17,16},{18,... | collective-permute-start | bytes 49160 | tf_op jit(solution)/shard_map/ppermute | solution.py:39
  103.3 8.7 %collective-permute-start.16 = (f32[6,4,256]{2,1,0:T(4,128)S(1)}, f32[6,4,256]{2,1,0:T(4,128)S(1)}, u32[]{:S(2)}, u32[]{:S(2)}) collective-permute-start(f32[6,4,256]{2,1,0:T(4,128)S(1)} %get-tuple-element.44), channel_id=1, source_target_pairs={{0,4},{1,5},{2,6},{3,7},{4,0},{5,1},{6,2},{7,3},{8,12},{9,13},{10,... | collective-permute-start | bytes 73736 | tf_op jit(solution)/shard_map/ppermute | solution.py:39
  105.9 7.2 %collective-permute-start.17 = (f32[6,4,256]{2,1,0:T(4,128)S(1)}, f32[6,4,256]{2,1,0:T(4,128)S(1)}, u32[]{:S(2)}, u32[]{:S(2)}) collective-permute-start(f32[6,4,256]{2,1,0:T(4,128)S(1)} %get-tuple-element.43), channel_id=1, source_target_pairs={{0,8},{1,9},{2,10},{3,11},{4,12},{5,13},{6,14},{7,15},{8,0},{9,1},... | collective-permute-start | bytes 73736 | tf_op jit(solution)/shard_map/ppermute | solution.py:39
  111.9 7.2 %collective-permute-start.18 = (f32[6,4,256]{2,1,0:T(4,128)S(1)}, f32[6,4,256]{2,1,0:T(4,128)S(1)}, u32[]{:S(2)}, u32[]{:S(2)}) collective-permute-start(f32[6,4,256]{2,1,0:T(4,128)S(1)} %get-tuple-element.42), channel_id=1, source_target_pairs={{0,12},{1,13},{2,14},{3,15},{4,8},{5,9},{6,10},{7,11},{8,4},{9,5},... | collective-permute-start | bytes 73736 | tf_op jit(solution)/shard_map/ppermute | solution.py:39

commit v8 on v7

--- a/solution.py
+++ b/solution.py
@@ -12,6 +12,7 @@
 IRREPS = 4
 LANES = 128
 PARTS = 4
+FAR = 2
 NY, NX, NZ, NC, NG = 4, 4, 2, 2, 4
 AXES = ("blk", "grp")
 
@@ -46,20 +47,6 @@
 def plane_sum(chip):
     spread = lax.all_to_all(chip, "blk", 0, 0, tiled=True, axis_index_groups=plane_groups())
     return jnp.sum(spread, axis=0)
-
-
-def staged_sum(chip, position):
-    y, x = position // (NX * NZ * NC), (position // (NZ * NC)) % NX
-
-    def stage(value, place, count, target):
-        def block(step):
-            return lax.dynamic_index_in_dim(value, (place + step) % count, 0, keepdims=False)
-
-        arrived = [permute(block(step), functools.partial(target, step)) for step in (2, 1, 3)]
-        return block(0) + ((arrived[1] + arrived[2]) + arrived[0])
-
-    rows = stage(chip.reshape(NY, NX, *chip.shape[1:]), y, NY, lambda k, y, x, z, c, g: ((y + k) % NY, x, z, c, g))
-    return stage(rows, x, NX, lambda k, y, x, z, c, g: (y, (x + k) % NX, z, c, g))
 
 
 def pair_swap(y, x, z, c, g):
@@ -95,7 +82,7 @@
             value = jnp.where(lane < limit, value, 0.0)
             rounded = value.astype(jnp.bfloat16)
             place = slice(tile * LANES, (tile + 1) * LANES)
-            kept = tiles // PARTS
+            kept = tiles // FAR
             if slot == IRREPS - 1 and tile >= kept:
                 outputs[-1][:, (tile - kept) * LANES : (tile + 1 - kept) * LANES] = value
             high[:, place] = rounded
@@ -105,7 +92,7 @@
 def split_rows(amplitudes, scalars):
     pairs, _, slot_width = amplitudes.shape
     rows = 64
-    guest_width = slot_width - slot_width // PARTS
+    guest_width = slot_width - slot_width // FAR
     view = amplitudes.reshape(pairs, IRREPS, slot_width // LANES, LANES).transpose(0, 2, 1, 3).reshape(-1, LANES)
     return pl.pallas_call(
         functools.partial(split_kernel, rows, slot_width),
@@ -191,7 +178,7 @@
         put_halves(scalars, total, kept, sent, k)
 
 
-def guest_kernel(scalars, crossed, guests, kept, sent, slab, rows, total, sems):
+def guest_kernel(scalars, crossed, guests, out, slab, rows, sems):
     depth = rows.shape[1]
     copies = [
         pltpu.make_async_copy(crossed.at[pl.ds(crossed.shape[0] - depth, depth), :], slab, sems.at[0]),
@@ -201,8 +188,7 @@
         copy.start()
     for copy in copies:
         copy.wait()
-    total[...] = split_dot(halves_of(rows[...]), halves_of(slab[...]))
-    put_halves(scalars, total, kept, sent, 0)
+    out[...] = split_dot(halves_of(rows[...]), halves_of(slab[...])).T.reshape(out.shape)
 
 
 def second_kernel(
@@ -244,7 +230,7 @@
 
     @pl.when(inner)
     def _():
-        for part in range(PARTS):
+        for part in range(FAR):
             copy_of(middle, part).start()
 
     out[:, :, pairs:] = kept[...] + got[...]
@@ -252,7 +238,7 @@
 
     @pl.when(inner)
     def _():
-        for part in range(1, PARTS):
+        for part in range(1, FAR):
             add(part)
 
     out[:, :, :pairs] = total[...].T.reshape(out.shape[0], out.shape[1], pairs)
@@ -279,6 +265,7 @@
     group, position = scalars[2 * IRREPS], scalars[2 * IRREPS + 1]
     core = position % NC
     column = position * column_width + lax.broadcasted_iota(jnp.int32, parts[0].shape[1:], 0)
+    last = IRREPS - 1
     for irrep in range(IRREPS):
         slot = scalars[irrep] ^ group
         size = scalars[IRREPS + irrep]
@@ -286,8 +273,8 @@
         mine = parts[0][slot] + parts[2][slot]
         other = parts[1][slot] + parts[3][slot]
         for k in range(NC):
-            both = (parts[0][IRREPS + k] + parts[2][IRREPS + k]) + (parts[1][IRREPS + k] + parts[3][IRREPS + k])
-            value = jnp.where(core == k, mine, other) + jnp.where(slot == IRREPS - 1, both, 0.0)
+            whole = (parts[0][last + k] + parts[2][last + k]) + (parts[1][last + k] + parts[3][last + k])
+            value = jnp.where(slot == last, whole, jnp.where(core == k, mine, other))
             out[irrep, :, k * half : (k + 1) * half] = jnp.where(valid, value, 0.0)
 
 
@@ -324,7 +311,7 @@
     guests = permute(moved, inward)
     passed = permute(middle, outward)
     crossed = permute(near, middle_swap)
-    far = permute(crossed[: rows // PARTS], outward)
+    far = permute(crossed[: rows // FAR], outward)
 
     matrix = pltpu.VMEM((pairs, slots), jnp.bfloat16)
     slab = pltpu.VMEM((rows, columns), jnp.float32)
@@ -352,19 +339,19 @@
     first_chip = kept + other_core(sent)
     first = plane_sum(first_chip)
 
-    scratch = [pltpu.VMEM((guest_width, columns), jnp.float32), pltpu.VMEM((pairs, guest_width), jnp.float32), total, two_sems]
-    outs = [of(plane, width, half)] * 2
-    kept, sent = call_product(
+    scratch = [pltpu.VMEM((guest_width, columns), jnp.float32), pltpu.VMEM((pairs, guest_width), jnp.float32), two_sems]
+    outs = [of(plane, width, pairs)]
+    (guest,) = call_product(
         guest_kernel, scalars, [crossed, guests], [], [], outs, scratch, pairs * columns * guest_width
     )
-    guest = staged_sum(kept + other_core(sent), position)
+    guest = plane_sum(guest)
     handed = permute(guest, outward)
 
     scratch = [slab, matrix, matrix, total, sems, two_sems]
     outs = [of(plane, width, half)] * 2 + [jax.ShapeDtypeStruct((pairs, slots), jnp.bfloat16)] * 2
     kept, sent, *resident = call_product(second_kernel, scalars, [passed, crossed], split[4:], [], outs, scratch, terms)
     got = other_core(sent)
-    scratch = [slab, total, pltpu.SemaphoreType.DMA((PARTS,))]
+    scratch = [slab, total, pltpu.SemaphoreType.DMA((FAR,))]
     (result,) = call_product(
         last_kernel,
         scalars,
@@ -376,8 +363,8 @@
         terms,
     )
     late = plane_sum(result)
-    late = late.reshape(width, NC + 1, half).swapaxes(0, 1)
-    units = jnp.concatenate([first.reshape(2, width, half), late[NC:], handed[None], late[:NC]], axis=0)
+    third = (late[:, :pairs] + handed).reshape(width, NC, half).swapaxes(0, 1)
+    units = jnp.concatenate([first.reshape(2, width, half), late[None, :, pairs:], third], axis=0)
     units = units.reshape(-1, NZ * NC, column_width, half)
 
     def share(flip):

time: 121 us -> 116 us (0.959)
  starting transfers between devices: 49.5 us -> 44.5 us
  local copies, waits for them, and re-layouts: 2.62 us -> 0.94 us
    all_to_all x2 -> x3, waiting for transfers between devices: 0.01 us -> 13.5 us  [plane_sum(): lax.all_to_all(chip, 'blk', 0, 0, tiled=True, axis_index_groups=plane_gro...]
    ppermute x19 -> x12, waiting for transfers between devices: 34.6 us -> 21.3 us  [permute(): return lax.ppermute(value, AXES, pairs)]
    ppermute x19 -> x12, starting transfers between devices: 38.5 us -> 26.7 us  [permute(): return lax.ppermute(value, AXES, pairs)]
    all_to_all x2 -> x3, starting transfers between devices: 11 us -> 17.8 us  [plane_sum(): lax.all_to_all(chip, 'blk', 0, 0, tiled=True, axis_index_groups=plane_gro...]
    unnamed x11 -> x4, local copies, waits for them, and re-layouts: 1.68 us -> 0.02 us
    pallas_call x4, Pallas kernels: 15.3 us -> 16.5 us  [call_product(): pl.pallas_call(kernel, out_shape=out_shapes, in_specs=[pl.BlockSpec(memor...]
  transfers between devices with their start and end apart: 21 -> 15, of which waited for: 8 -> 10; matrix products, arithmetic and copies ran while one was open for 4% -> 4% of each run, Pallas kernels for 23% -> 26%
where the time goes in v8:
time: 116 us; the launch traced here: 115 us
  starting transfers between devices  44.5 us (38%)
  waiting for transfers between devices  34.8 us (30%)
  Pallas kernels  30.5 us (26%)
  other arithmetic  3.86 us (3%)
    ppermute x12, starting transfers between devices, permute(): return lax.ppermute(value, AXES, pairs)  26.7 us
    ppermute x12, waiting for transfers between devices, permute(): return lax.ppermute(value, AXES, pairs)  21.3 us
    all_to_all x3, starting transfers between devices, plane_sum(): lax.all_to_all(chip, 'blk', 0, 0, tiled=True, axis_index_groups=plane_gro...  17.8 us
    pallas_call x4, Pallas kernels, call_product(): pl.pallas_call(kernel, out_shape=out_shapes, in_specs=[pl.BlockSpec(memor...  16.5 us
    all_to_all x3, waiting for transfers between devices, plane_sum(): lax.all_to_all(chip, 'blk', 0, 0, tiled=True, axis_index_groups=plane_gro...  13.5 us
    pallas_call x1, Pallas kernels, split_rows(): pl.pallas_call(functools.partial(split_kernel, rows, slot_width), out_sha...  12.7 us
  transfers between devices with their start and end apart: 15, of which 10 were waited for; matrix products, arithmetic and copies ran while one was open for 4% of the time, Pallas kernels for 26%

profile of v8, /device:TPU:1, one launch (start us, length us, event | category | flops | bytes accessed | tf_op | source)
XLA Modules:
  0.0 114.8 jit_solution(7906811791857006249)
XLA Ops:
  0.0 0.0 copy-start
  0.0 2.5 %collective-permute-start = (f32[1024,256]{1,0:T(8,128)}, f32[1024,256]{1,0:T(8,128)}, u32[]{:S(2)}, u32[]{:S(2)}) collective-permute-start(f32[1024,256]{1,0:T(8,128)} %bitcast.20), channel_id=1, source_target_pairs={{0,1},{1,0},{2,3},{3,2},{4,5},{5,4},{6,7},{7,6},{8,9},{9,8},{10,11... | collective-permute-start | bytes 3145736 | tf_op jit(solution)/shard_map/ppermute | solution.py:40
  2.5 0.7 collective-permute-start.4
  3.2 0.8 pad_add_fusion.scalars
  3.9 12.7 %split_rows.1 = (bf16[512,1024]{1,0:T(8,128)(2,1)}, bf16[512,1024]{1,0:T(8,128)(2,1)}, bf16[512,1024]{1,0:T(8,128)(2,1)}, bf16[512,1024]{1,0:T(8,128)(2,1)}, bf1...) custom-call(s32[10]{0:T(128)S(1)} %pad_add_fusion.scalars, ...), custom_call_target="tpu_custom_call" | custom-call | bytes 16777216 | tf_op jit(solution)/shard_map/split_rows/pallas_call | solution.py:97
  16.7 7.4 %collective-permute-start.7 = (f32[512,512]{1,0:T(8,128)}, f32[512,512]{1,0:T(8,128)}, u32[]{:S(2)}, u32[]{:S(2)}) collective-permute-start(f32[512,512]{1,0:T(8,128)} %get-tuple-element.34), channel_id=1, source_target_pairs={{0,1},{3,2},{4,5},{7,6},{8,9},{11,10},{12,13},{15,14},{16,17},{19,... | collective-permute-start | bytes 3145736 | tf_op jit(solution)/shard_map/ppermute | solution.py:40
  24.0 0.6 collective-permute-done.near
  24.6 0.7 collective-permute-start.2
  25.3 0.0 copy-done
  25.4 6.0 %shard_map.46 = (f32[16,32,256]{2,1,0:T(8,128)S(1)}, f32[16,32,256]{2,1,0:T(8,128)S(1)}) custom-call(s32[10]{0:T(128)S(1)} %pad_add_fusion.scalars, f32[1024,256]{1,0:T(8,128)S(1)} %bitcast.22, f32[1024,256]{1,0:T(8,128)} %collective-permute-done.near, bf16[512,1024]{1,0:T(8,128)(2,1)} %get-tuple-element.20.high_0, ...), custom_call_target="tpu_custom_call" | custom-call | flops 1610612736 | bytes 6291456 | tf_op jit(solution)/shard_map/pallas_call | solution.py:249
  31.4 2.7 %collective-permute-start.1 = (f32[16,32,256]{2,1,0:T(8,128)S(1)}, f32[16,32,256]{2,1,0:T(8,128)S(1)}, u32[]{:S(2)}, u32[]{:S(2)}) collective-permute-start(f32[16,32,256]{2,1,0:T(8,128)S(1)} %get-tuple-element.25), channel_id=1, source_target_pairs={{0,4},{1,5},{2,6},{3,7},{4,0},{5,1},{6,2},{7,3},{8,12},{9,13},{10,... | collective-permute-start | bytes 1572872 | tf_op jit(solution)/shard_map/ppermute | solution.py:40
  34.1 0.0 collective-permute-done.4.middle
  34.1 1.3 %collective-permute-start.5 = (f32[1024,256]{1,0:T(8,128)S(1)}, f32[1024,256]{1,0:T(8,128)S(1)}, u32[]{:S(2)}, u32[]{:S(2)}) collective-permute-start(f32[1024,256]{1,0:T(8,128)S(1)} %collective-permute-done.4.middle), channel_id=1, source_target_pairs={{1,0},{2,3},{5,4},{6,7},{9,8},{10,11},{13,12},{14,15},{17,16},{18,... | collective-permute-start | bytes 3145736 | tf_op jit(solution)/shard_map/ppermute | solution.py:40
  35.4 0.2 collective-permute-done.1
  35.6 0.9 add.33
  36.5 6.8 %all-to-all-start = ((f32[16,32,256]{2,1,0:T(8,128)}), f32[16,32,256]{2,1,0:T(8,128)}, u32[]{:S(2)}, u32[]{:S(2)}) async-start(f32[16,32,256]{2,1,0:T(8,128)} %add.33), calls=%async_computation | async-start | bytes 1048576 | tf_op jit(solution)/shard_map/all_to_all | solution.py:48
  43.4 0.0 collective-permute-done.2.crossed
  43.4 0.8 slice.12
  44.2 1.3 %collective-permute-start.3 = (f32[512,256]{1,0:T(8,128)}, f32[512,256]{1,0:T(8,128)}, u32[]{:S(2)}, u32[]{:S(2)}) collective-permute-start(f32[512,256]{1,0:T(8,128)} %slice.12), channel_id=1, source_target_pairs={{1,0},{2,3},{5,4},{6,7},{9,8},{10,11},{13,12},{14,15},{17,16},{18,... | collective-permute-start | bytes 1572872 | tf_op jit(solution)/shard_map/ppermute | solution.py:40
  45.5 1.6 %collective-permute-done.7.guests = f32[512,512]{1,0:T(8,128)} collective-permute-done((f32[512,512]{1,0:T(8,128)}, f32[512,512]{1,0:T(8,128)}, u32[]{:S(2)}, u32[]{:S(2)}) %collective-permute-start.7) | collective-permute-done | bytes 1048608 | tf_op jit(solution)/shard_map/ppermute | solution.py:40
  47.1 3.3 %shard_map.49 = f32[16,16,512]{2,1,0:T(8,128)} custom-call(s32[10]{0:T(128)S(1)} %pad_add_fusion.scalars, f32[1024,256]{1,0:T(8,128)S(1)} %collective-permute-done.2.crossed, f32[512,512]{1,0:T(8,128)} %collective-permute-done.7.guests), custom_call_target="tpu_custom_call" | custom-call | flops 402653184 | bytes 6291456 | tf_op jit(solution)/shard_map/pallas_call | solution.py:249
  50.4 3.7 %all-to-all-done = f32[16,32,256]{2,1,0:T(8,128)} async-done(((f32[16,32,256]{2,1,0:T(8,128)}), f32[16,32,256]{2,1,0:T(8,128)}, u32[]{:S(2)}, u32[]{:S(2)}) %all-to-all-start) | async-done | bytes 524320 | tf_op jit(solution)/shard_map/all_to_all | solution.py:48
  54.1 4.2 %all-to-all-start.2 = ((f32[16,16,512]{2,1,0:T(8,128)}), f32[16,16,512]{2,1,0:T(8,128)}, u32[]{:S(2)}, u32[]{:S(2)}) async-start(f32[16,16,512]{2,1,0:T(8,128)} %shard_map.49), calls=%async_computation.2 | async-start | bytes 1048576 | tf_op jit(solution)/shard_map/all_to_all | solution.py:48
  58.4 5.8 %collective-permute-done.5.passed = f32[1024,256]{1,0:T(8,128)S(1)} collective-permute-done((f32[1024,256]{1,0:T(8,128)S(1)}, f32[1024,256]{1,0:T(8,128)S(1)}, u32[]{:S(2)}, u32[]{:S(2)}) %collective-permute-start.5) | collective-permute-done | bytes 1048608 | tf_op jit(solution)/shard_map/ppermute | solution.py:40
  64.2 3.9 %shard_map.47 = (f32[16,16,256]{2,1,0:T(8,128)S(1)}, f32[16,16,256]{2,1,0:T(8,128)S(1)}, bf16[512,1024]{1,0:T(8,128)(2,1)S(1)}, bf16[512,1024]{1,0:T(8,128)(2,1)S(1)}) custom-call(s32[10]{0:T(128)S(1)} %pad_add_fusion.scalars, f32[1024,256]{1,0:T(8,128)S(1)} %collective-permute-done.5.passed, f32[1024,256]{1,0:T(8,128)S(1)} %collective-permute-done.2.crossed, ...), custom_call_target="tpu_custom_call" | custom-call | flops 805306368 | bytes 6291456 | tf_op jit(solution)/shard_map/pallas_call | solution.py:249
  68.1 0.9 collective-permute-start.6
  69.0 1.2 %collective-permute-done.6.got = f32[16,16,256]{2,1,0:T(8,128)S(1)} collective-permute-done((f32[16,16,256]{2,1,0:T(8,128)S(1)}, f32[16,16,256]{2,1,0:T(8,128)S(1)}, u32[]{:S(2)}, u32[]{:S(2)}) %collective-permute-start.6) | collective-permute-done | bytes 262176 | tf_op jit(solution)/shard_map/ppermute | solution.py:40
  70.2 5.3 %collective-permute-done.3.far = f32[512,256]{1,0:T(8,128)} collective-permute-done((f32[512,256]{1,0:T(8,128)}, f32[512,256]{1,0:T(8,128)}, u32[]{:S(2)}, u32[]{:S(2)}) %collective-permute-start.3) | collective-permute-done | bytes 524320 | tf_op jit(solution)/shard_map/ppermute | solution.py:40
  75.5 3.3 %shard_map.48 = f32[16,16,768]{2,1,0:T(8,128)} custom-call(s32[10]{0:T(128)S(1)} %pad_add_fusion.scalars, f32[512,256]{1,0:T(8,128)} %collective-permute-done.3.far, f32[1024,256]{1,0:T(8,128)S(1)} %collective-permute-done.4.middle, bf16[512,1024]{1,0:T(8,128)(2,1)S(1)} %get-tuple-element.30.high, bf16[512,1024]{1,0:T(8,128)(2,1)S(1)} %get-tuple-element.31.low, ...), custom_call_target="tpu_custom_call" | custom-call | flops 805306368 | bytes 6291456 | tf_op jit(solution)/shard_map/pallas_call | solution.py:249
  78.8 0.0 all-to-all-done.2
  78.8 6.8 %all-to-all-start.1 = ((f32[16,16,768]{2,1,0:T(8,128)}), f32[16,16,768]{2,1,0:T(8,128)S(1)}, u32[]{:S(2)}, u32[]{:S(2)}) async-start(f32[16,16,768]{2,1,0:T(8,128)} %shard_map.48), calls=%async_computation.1 | async-start | bytes 1572864 | tf_op jit(solution)/shard_map/all_to_all | solution.py:48
  85.7 1.1 reduce_sum.27
  86.8 1.1 reduce_sum.29
  87.9 1.3 %collective-permute-start.8 = (f32[16,512]{1,0:T(8,128)S(1)}, f32[16,512]{1,0:T(8,128)S(1)}, u32[]{:S(2)}, u32[]{:S(2)}) collective-permute-start(f32[16,512]{1,0:T(8,128)S(1)} %reduce_sum.29), channel_id=1, source_target_pairs={{1,0},{2,3},{5,4},{6,7},{9,8},{10,11},{13,12},{14,15},{17,16},{18,... | collective-permute-start | bytes 98312 | tf_op jit(solution)/shard_map/ppermute | solution.py:40
  89.2 9.7 %all-to-all-done.1 = f32[16,16,768]{2,1,0:T(8,128)S(1)} async-done(((f32[16,16,768]{2,1,0:T(8,128)}), f32[16,16,768]{2,1,0:T(8,128)S(1)}, u32[]{:S(2)}, u32[]{:S(2)}) %all-to-all-start.1) | async-done | bytes 786464 | tf_op jit(solution)/shard_map/all_to_all | solution.py:48
  99.0 0.0 collective-permute-done.8
  99.1 2.2 %collective-permute-start.9 = (f32[5,4,256]{2,1,0:T(4,128)S(1)}, f32[5,4,256]{2,1,0:T(4,128)S(1)}, u32[]{:S(2)}, u32[]{:S(2)}) collective-permute-start(f32[5,4,256]{2,1,0:T(4,128)S(1)} %get-tuple-element.37), channel_id=1, source_target_pairs={{0,4},{1,5},{2,6},{3,7},{4,0},{5,1},{6,2},{7,3},{8,12},{9,13},{10,... | collective-permute-start | bytes 61448 | tf_op jit(solution)/shard_map/ppermute | solution.py:40
  101.4 5.1 %collective-permute-start.10 = (f32[5,4,256]{2,1,0:T(4,128)S(1)}, f32[5,4,256]{2,1,0:T(4,128)S(1)}, u32[]{:S(2)}, u32[]{:S(2)}) collective-permute-start(f32[5,4,256]{2,1,0:T(4,128)S(1)} %get-tuple-element.36), channel_id=1, source_target_pairs={{0,8},{1,9},{2,10},{3,11},{4,12},{5,13},{6,14},{7,15},{8,0},{9,1},... | collective-permute-start | bytes 61448 | tf_op jit(solution)/shard_map/ppermute | solution.py:40
  106.5 0.5 collective-permute-start.11
  107.0 0.0 collective-permute-done.9.refs_1_
  107.0 0.9 collective-permute-done.10.refs_2_
  107.9 5.7 %collective-permute-done.11.refs_3_ = f32[5,4,256]{2,1,0:T(4,128)S(1)} collective-permute-done((f32[5,4,256]{2,1,0:T(4,128)S(1)}, f32[5,4,256]{2,1,0:T(4,128)S(1)}, u32[]{:S(2)}, u32[]{:S(2)}) %collective-permute-start.11) | collective-permute-done | bytes 20512 | tf_op jit(solution)/shard_map/ppermute | solution.py:40
  113.6 1.2 %finish.1 = f32[4,4,512]{2,1,0:T(4,128)} custom-call(s32[10]{0:T(128)S(1)} %pad_add_fusion.scalars, f32[5,4,256]{2,1,0:T(4,128)S(1)} %get-tuple-element.38.refs_0_, f32[5,4,256]{2,1,0:T(4,128)S(1)} %collective-permute-done.9.refs_1_, f32[5,4,256]{2,1,0:T(4,128)S(1)} %collective-permute-done.10.refs_2_, f32[5,4,256]{2,1,0:T(4,128)S(1)} %collective-permute-done.11.refs_3_), custom_call_target="tpu_custom_call" | custom-call | tf_op jit(solution)/shard_map/finish/pallas_call | solution.py:284
  (10 shorter events, 0.2 us)
Async XLA Ops:
  0.0 25.3 %copy-start = (f32[1,1024,256]{2,1,0:T(8,128)S(1)}, f32[1,1024,256]{2,1,0:T(8,128)}, u32[]{:S(2)}) copy-start(f32[1,1024,256]{2,1,0:T(8,128)} %param.5) | copy-start | bytes 3145732
  0.0 24.6 %collective-permute-start = (f32[1024,256]{1,0:T(8,128)}, f32[1024,256]{1,0:T(8,128)}, u32[]{:S(2)}, u32[]{:S(2)}) collective-permute-start(f32[1024,256]{1,0:T(8,128)} %bitcast.20), channel_id=1, source_target_pairs={{0,1},{1,0},{2,3},{3,2},{4,5},{5,4},{6,7},{7,6},{8,9},{9,8},{10,11... | collective-permute-start | bytes 3145736 | tf_op jit(solution)/shard_map/ppermute | solution.py:40
  2.5 31.7 %collective-permute-start.4 = (f32[1024,256]{1,0:T(8,128)}, f32[1024,256]{1,0:T(8,128)S(1)}, u32[]{:S(2)}, u32[]{:S(2)}) collective-permute-start(f32[1024,256]{1,0:T(8,128)} %bitcast.21), channel_id=1, source_target_pairs={{1,2},{2,1},{5,6},{6,5},{9,10},{10,9},{13,14},{14,13},{17,18},{18,... | collective-permute-start | bytes 3145736 | tf_op jit(solution)/shard_map/ppermute | solution.py:40
  16.7 30.4 %collective-permute-start.7 = (f32[512,512]{1,0:T(8,128)}, f32[512,512]{1,0:T(8,128)}, u32[]{:S(2)}, u32[]{:S(2)}) collective-permute-start(f32[512,512]{1,0:T(8,128)} %get-tuple-element.34), channel_id=1, source_target_pairs={{0,1},{3,2},{4,5},{7,6},{8,9},{11,10},{12,13},{15,14},{16,17},{19,... | collective-permute-start | bytes 3145736 | tf_op jit(solution)/shard_map/ppermute | solution.py:40
  24.6 18.7 %collective-permute-start.2 = (f32[1024,256]{1,0:T(8,128)}, f32[1024,256]{1,0:T(8,128)S(1)}, u32[]{:S(2)}, u32[]{:S(2)}) collective-permute-start(f32[1024,256]{1,0:T(8,128)} %collective-permute-done.near), channel_id=1, source_target_pairs={{1,2},{2,1},{5,6},{6,5},{9,10},{10,9},{13,14},{14,13},{17,18},{18,... | collective-permute-start | bytes 3145736 | tf_op jit(solution)/shard_map/ppermute | solution.py:40
  31.4 4.3 %collective-permute-start.1 = (f32[16,32,256]{2,1,0:T(8,128)S(1)}, f32[16,32,256]{2,1,0:T(8,128)S(1)}, u32[]{:S(2)}, u32[]{:S(2)}) collective-permute-start(f32[16,32,256]{2,1,0:T(8,128)S(1)} %get-tuple-element.25), channel_id=1, source_target_pairs={{0,4},{1,5},{2,6},{3,7},{4,0},{5,1},{6,2},{7,3},{8,12},{9,13},{10,... | collective-permute-start | bytes 1572872 | tf_op jit(solution)/shard_map/ppermute | solution.py:40
  34.1 30.1 %collective-permute-start.5 = (f32[1024,256]{1,0:T(8,128)S(1)}, f32[1024,256]{1,0:T(8,128)S(1)}, u32[]{:S(2)}, u32[]{:S(2)}) collective-permute-start(f32[1024,256]{1,0:T(8,128)S(1)} %collective-permute-done.4.middle), channel_id=1, source_target_pairs={{1,0},{2,3},{5,4},{6,7},{9,8},{10,11},{13,12},{14,15},{17,16},{18,... | collective-permute-start | bytes 3145736 | tf_op jit(solution)/shard_map/ppermute | solution.py:40
  36.5 17.6 %all-to-all-start = ((f32[16,32,256]{2,1,0:T(8,128)}), f32[16,32,256]{2,1,0:T(8,128)}, u32[]{:S(2)}, u32[]{:S(2)}) async-start(f32[16,32,256]{2,1,0:T(8,128)} %add.33), calls=%async_computation | async-start | bytes 1048576 | tf_op jit(solution)/shard_map/all_to_all | solution.py:48
  44.2 31.3 %collective-permute-start.3 = (f32[512,256]{1,0:T(8,128)}, f32[512,256]{1,0:T(8,128)}, u32[]{:S(2)}, u32[]{:S(2)}) collective-permute-start(f32[512,256]{1,0:T(8,128)} %slice.12), channel_id=1, source_target_pairs={{1,0},{2,3},{5,4},{6,7},{9,8},{10,11},{13,12},{14,15},{17,16},{18,... | collective-permute-start | bytes 1572872 | tf_op jit(solution)/shard_map/ppermute | solution.py:40
  54.1 24.7 %all-to-all-start.2 = ((f32[16,16,512]{2,1,0:T(8,128)}), f32[16,16,512]{2,1,0:T(8,128)}, u32[]{:S(2)}, u32[]{:S(2)}) async-start(f32[16,16,512]{2,1,0:T(8,128)} %shard_map.49), calls=%async_computation.2 | async-start | bytes 1048576 | tf_op jit(solution)/shard_map/all_to_all | solution.py:48
  68.1 2.1 %collective-permute-start.6 = (f32[16,16,256]{2,1,0:T(8,128)S(1)}, f32[16,16,256]{2,1,0:T(8,128)S(1)}, u32[]{:S(2)}, u32[]{:S(2)}) collective-permute-start(f32[16,16,256]{2,1,0:T(8,128)S(1)} %get-tuple-element.33), channel_id=1, source_target_pairs={{0,4},{1,5},{2,6},{3,7},{4,0},{5,1},{6,2},{7,3},{8,12},{9,13},{10,... | collective-permute-start | bytes 786440 | tf_op jit(solution)/shard_map/ppermute | solution.py:40
  78.8 20.1 %all-to-all-start.1 = ((f32[16,16,768]{2,1,0:T(8,128)}), f32[16,16,768]{2,1,0:T(8,128)S(1)}, u32[]{:S(2)}, u32[]{:S(2)}) async-start(f32[16,16,768]{2,1,0:T(8,128)} %shard_map.48), calls=%async_computation.1 | async-start | bytes 1572864 | tf_op jit(solution)/shard_map/all_to_all | solution.py:48
  87.9 11.1 %collective-permute-start.8 = (f32[16,512]{1,0:T(8,128)S(1)}, f32[16,512]{1,0:T(8,128)S(1)}, u32[]{:S(2)}, u32[]{:S(2)}) collective-permute-start(f32[16,512]{1,0:T(8,128)S(1)} %reduce_sum.29), channel_id=1, source_target_pairs={{1,0},{2,3},{5,4},{6,7},{9,8},{10,11},{13,12},{14,15},{17,16},{18,... | collective-permute-start | bytes 98312 | tf_op jit(solution)/shard_map/ppermute | solution.py:40
  99.1 7.9 %collective-permute-start.9 = (f32[5,4,256]{2,1,0:T(4,128)S(1)}, f32[5,4,256]{2,1,0:T(4,128)S(1)}, u32[]{:S(2)}, u32[]{:S(2)}) collective-permute-start(f32[5,4,256]{2,1,0:T(4,128)S(1)} %get-tuple-element.37), channel_id=1, source_target_pairs={{0,4},{1,5},{2,6},{3,7},{4,0},{5,1},{6,2},{7,3},{8,12},{9,13},{10,... | collective-permute-start | bytes 61448 | tf_op jit(solution)/shard_map/ppermute | solution.py:40
  101.4 6.5 %collective-permute-start.10 = (f32[5,4,256]{2,1,0:T(4,128)S(1)}, f32[5,4,256]{2,1,0:T(4,128)S(1)}, u32[]{:S(2)}, u32[]{:S(2)}) collective-permute-start(f32[5,4,256]{2,1,0:T(4,128)S(1)} %get-tuple-element.36), channel_id=1, source_target_pairs={{0,8},{1,9},{2,10},{3,11},{4,12},{5,13},{6,14},{7,15},{8,0},{9,1},... | collective-permute-start | bytes 61448 | tf_op jit(solution)/shard_map/ppermute | solution.py:40
  106.5 7.1 %collective-permute-start.11 = (f32[5,4,256]{2,1,0:T(4,128)S(1)}, f32[5,4,256]{2,1,0:T(4,128)S(1)}, u32[]{:S(2)}, u32[]{:S(2)}) collective-permute-start(f32[5,4,256]{2,1,0:T(4,128)S(1)} %get-tuple-element.35), channel_id=1, source_target_pairs={{0,12},{1,13},{2,14},{3,15},{4,8},{5,9},{6,10},{7,11},{8,4},{9,5},... | collective-permute-start | bytes 61448 | tf_op jit(solution)/shard_map/ppermute | solution.py:40

commit v9 on v5

--- a/solution.py
+++ b/solution.py
@@ -11,6 +11,7 @@
 BLOCK = 256
 IRREPS = 4
 LANES = 128
+PARTS = 4
 NY, NX, NZ, NC, NG = 4, 4, 2, 2, 4
 AXES = ("blk", "grp")
 
@@ -51,16 +52,15 @@
     return y, x, z, c, g ^ 1
 
 
-def middle_swap(y, x, z, c, g):
-    return (y, x, z, c, 3 - g) if g in (1, 2) else None
-
-
-def inward(y, x, z, c, g):
-    return (y, x, z, c, {0: 1, 3: 2}[g]) if g in (0, 3) else None
-
-
-def outward(y, x, z, c, g):
-    return (y, x, z, c, {1: 0, 2: 3}[g]) if g in (1, 2) else None
+def across(y, x, z, c, g):
+    return y, x, z, c, g ^ 2
+
+
+RELAY = {1: 0, 0: 2, 2: 3, 3: 1}
+
+
+def relay(y, x, z, c, g):
+    return y, x, z, c, RELAY[g]
 
 
 def split_kernel(rows, slot_width, scalars, source, *outputs):
@@ -80,8 +80,6 @@
             value = jnp.where(lane < limit, value, 0.0)
             rounded = value.astype(jnp.bfloat16)
             place = slice(tile * LANES, (tile + 1) * LANES)
-            if slot == IRREPS - 1 and tile >= tiles // 2:
-                outputs[-1][:, (tile - tiles // 2) * LANES : (tile + 1 - tiles // 2) * LANES] = value
             high[:, place] = rounded
             low[:, place] = (value - rounded.astype(jnp.float32)).astype(jnp.bfloat16)
 
@@ -92,22 +90,17 @@
     view = amplitudes.reshape(pairs, IRREPS, slot_width // LANES, LANES).transpose(0, 2, 1, 3).reshape(-1, LANES)
     return pl.pallas_call(
         functools.partial(split_kernel, rows, slot_width),
-        out_shape=[pltpu.HBM((pairs, slot_width), jnp.bfloat16)] * (2 * IRREPS)
-        + [pltpu.HBM((pairs, slot_width // 2), jnp.float32)],
+        out_shape=[pltpu.HBM((pairs, slot_width), jnp.bfloat16)] * (2 * IRREPS),
         grid_spec=pltpu.PrefetchScalarGridSpec(
             num_scalar_prefetch=1,
             grid=(pairs // rows,),
             in_specs=[pl.BlockSpec((rows * IRREPS * slot_width // LANES, LANES), lambda i, scalars: (i, 0))],
-            out_specs=[pl.BlockSpec((rows, slot_width), lambda i, scalars: (i, 0))] * (2 * IRREPS)
-            + [pl.BlockSpec((rows, slot_width // 2), lambda i, scalars: (i, 0))],
+            out_specs=[pl.BlockSpec((rows, slot_width), lambda i, scalars: (i, 0))] * (2 * IRREPS),
         ),
         compiler_params=pltpu.CompilerParams(vmem_limit_bytes=16 << 20),
         cost_estimate=pl.CostEstimate(flops=0, bytes_accessed=8 * pairs * IRREPS * slot_width, transcendentals=0),
         name="split_rows",
     )(scalars, *in_hbm([view]))
-
-
-PARTS = 4
 
 
 def halves_of(value):
@@ -153,21 +146,24 @@
         total[...] = term if part == 0 else total[...] + term
 
 
-def is_end(scalars):
-    group = scalars[2 * IRREPS]
-    return (group == 0) | (group == NG - 1)
-
-
 def put_halves(scalars, total, kept, sent, index):
-    groups, width, half = kept.shape[0], kept.shape[1] // 2, kept.shape[2]
+    groups, _, half = kept.shape
+    width = total.shape[1] // groups
     core = scalars[2 * IRREPS + 1] % NC
     for out, which in ((sent, 1 - core), (kept, core)):
         rows = total[pl.ds(pl.multiple_of(which * half, half), half), :]
         out[:, index * width : (index + 1) * width, :] = rows.T.reshape(groups, width, half)
 
 
-def first_kernel(scalars, own, near, high_0, low_0, high_1, low_1, kept, sent, slabs, highs, lows, total, sems):
-    sources = ((own, high_0, low_0), (near, high_1, low_1))
+def own_kernel(scalars, own, high, low, kept, sent, slab, high_here, low_here, total, sems):
+    here = (slab, high_here, low_here)
+    start_parts(range(PARTS), (own, high, low), here, sems)
+    add_parts(range(PARTS), (own, high, low), here, sems, total)
+    put_halves(scalars, total, kept, sent, 0)
+
+
+def pair_kernel(scalars, one, two, high_1, low_1, high_2, low_2, kept, sent, slabs, highs, lows, total, sems):
+    sources = ((one, high_1, low_1), (two, high_2, low_2))
     here = [(slabs.at[k], highs.at[k], lows.at[k]) for k in range(2)]
     for k in range(2):
         start_parts(range(PARTS), sources[k], here[k], sems.at[k])
@@ -176,52 +172,47 @@
         put_halves(scalars, total, kept, sent, k)
 
 
-def second_kernel(
-    scalars, passed, crossed, guests, high, low, kept, sent, slab, high_here, low_here, guest_slab, rows, total, sems, guest_sems
-):
-    depth = rows.shape[1]
-    here = (slab, high_here, low_here)
-    ends = is_end(scalars)
-    pl.when(ends)(lambda: start_parts(range(PARTS), (passed, high, low), here, sems))
-    pl.when(jnp.logical_not(ends))(lambda: start_parts(range(PARTS), (crossed, high, low), here, sems))
-    guest_copies = [
-        pltpu.make_async_copy(crossed.at[pl.ds(depth, depth), :], guest_slab, guest_sems.at[0]),
-        pltpu.make_async_copy(guests, rows, guest_sems.at[1]),
+def rows_kernel(scalars, high, low, high_out, low_out, sems):
+    depth = high.shape[0] // PARTS
+    copies = []
+    for part in range(PARTS):
+        place = pl.ds(part * depth, depth)
+        for k, (there, here) in enumerate(((high, high_out), (low, low_out))):
+            copies.append(pltpu.make_async_copy(there.at[place, :], here.at[place, :], sems.at[part, k]))
+            copies[-1].start()
+    for copy in copies:
+        copy.wait()
+
+
+def last_kernel(scalars, three, high, low, out, slab, total, sems):
+    depth = slab.shape[0] // PARTS
+    places = [slice(part * depth, (part + 1) * depth) for part in range(PARTS)]
+    copies = [
+        pltpu.make_async_copy(three.at[pl.ds(part * depth, depth), :], slab.at[pl.ds(part * depth, depth), :], sems.at[part])
+        for part in range(PARTS)
     ]
-    for copy in guest_copies:
+    for copy in copies:
         copy.start()
-    add_parts(range(PARTS), (crossed, high, low), here, sems, total)
-    put_halves(scalars, total, kept, sent, 0)
-    for copy in guest_copies:
-        copy.wait()
-    total[...] = split_dot(halves_of(rows[...]), halves_of(guest_slab[...]))
-    put_halves(scalars, total, kept, sent, 1)
-
-
-def last_kernel(scalars, far, middle, high, low, out, slab, high_here, low_here, total, sems):
-    here = (slab, high_here, low_here)
-    ends = is_end(scalars)
-    inner = jnp.logical_not(ends)
-    front, back = range(PARTS // 2), range(PARTS // 2, PARTS)
-    pl.when(ends)(lambda: start_parts(front, (far, high, low), here, sems))
-    pl.when(inner)(lambda: start_parts(range(PARTS), (middle, high, low), here, sems))
-    add_parts(front, (middle, high, low), here, sems, total)
-    pl.when(inner)(lambda: add_parts(back, (middle, high, low), here, sems, total))
+    for part, place in enumerate(places):
+        copies[part].wait()
+        term = split_dot((high[:, place], low[:, place]), halves_of(slab[place, :]))
+        total[...] = term if part == 0 else total[...] + term
     out[...] = total[...].T.reshape(out.shape)
 
 
-def call_product(kernel, scalars, slabs, split, out_shapes, scratch, terms):
-    count = len(out_shapes)
+def call_product(kernel, scalars, moved, fixed, resident, out_shapes, scratch, terms):
     vmem = pl.BlockSpec(memory_space=pltpu.VMEM)
     return pl.pallas_call(
         kernel,
-        out_shape=[jax.ShapeDtypeStruct(shape, jnp.float32) for shape in out_shapes],
-        in_specs=[pl.BlockSpec(memory_space=pltpu.SMEM)] + [pl.BlockSpec(memory_space=pl.ANY)] * (len(slabs) + len(split)),
-        out_specs=[vmem] * count,
+        out_shape=out_shapes,
+        in_specs=[pl.BlockSpec(memory_space=pltpu.SMEM)]
+        + [pl.BlockSpec(memory_space=pl.ANY)] * (len(moved) + len(fixed))
+        + [vmem] * len(resident),
+        out_specs=[vmem] * len(out_shapes),
         scratch_shapes=scratch,
         compiler_params=pltpu.CompilerParams(vmem_limit_bytes=16 << 20),
         cost_estimate=pl.CostEstimate(flops=6 * terms, bytes_accessed=6 << 20, transcendentals=0),
-    )(scalars, *slabs, *in_hbm(split))
+    )(scalars, *moved, *in_hbm(fixed), *resident)
 
 
 def finish_kernel(column_width, scalars, *refs):
@@ -230,6 +221,7 @@
     group, position = scalars[2 * IRREPS], scalars[2 * IRREPS + 1]
     core = position % NC
     column = position * column_width + lax.broadcasted_iota(jnp.int32, parts[0].shape[1:], 0)
+    last = IRREPS - 1
     for irrep in range(IRREPS):
         slot = scalars[irrep] ^ group
         size = scalars[IRREPS + irrep]
@@ -237,8 +229,8 @@
         mine = parts[0][slot] + parts[2][slot]
         other = parts[1][slot] + parts[3][slot]
         for k in range(NC):
-            both = (parts[0][IRREPS + k] + parts[2][IRREPS + k]) + (parts[1][IRREPS + k] + parts[3][IRREPS + k])
-            value = jnp.where(core == k, mine, other) + jnp.where(slot == IRREPS - 1, both, 0.0)
+            whole = (parts[0][last + k] + parts[2][last + k]) + (parts[1][last + k] + parts[3][last + k])
+            value = jnp.where(slot == last, whole, jnp.where(core == k, mine, other))
             out[irrep, :, k * half : (k + 1) * half] = jnp.where(valid, value, 0.0)
 
 
@@ -268,24 +260,28 @@
     z_part = (position // NC) % NZ
 
     own = integrals[0]
-    near = permute(own, pair_swap)
-    middle = permute(own, middle_swap)
+    one = permute(own, pair_swap)
+    two = permute(own, across)
+    three = permute(jnp.where((group == 0) | (group == NG - 1), one, two), relay)
     scalars = jnp.concatenate([owner_map, irrep_sizes, jnp.stack([group, position])])
-    *split, moved = split_rows(amplitudes, scalars)
-    guests = permute(moved, inward)
-    crossed = permute(near, middle_swap)
-    passed = permute(middle, outward)
-    far = permute(crossed[: rows // 2], outward)
+    split = split_rows(amplitudes, scalars)
 
     matrix = pltpu.VMEM((pairs, slots), jnp.bfloat16)
     slab = pltpu.VMEM((rows, columns), jnp.float32)
     total = pltpu.VMEM((pairs, columns), jnp.float32)
-    sems = pltpu.SemaphoreType.DMA((PARTS, 3))
     terms = pairs * columns * slots
-    joint = [(plane, 2 * width, half)] * 2
+
+    def of(*shape):
+        return jax.ShapeDtypeStruct(shape, jnp.float32)
 
     def chip_sum(kept, sent):
         return kept + permute(sent, lambda y, x, z, c, g: (y, x, z, 1 - c, g))
+
+    scratch = [slab, matrix, matrix, total, pltpu.SemaphoreType.DMA((PARTS, 3))]
+    outs = [of(plane, width, half)] * 2
+    result = call_product(own_kernel, scalars, [own], split[:2], [], outs, scratch, terms)
+    chip = chip_sum(*result)
+    first = plane_sum(chip)
 
     scratch = [
         pltpu.VMEM((2, rows, columns), jnp.float32),
@@ -294,28 +290,20 @@
         total,
         pltpu.SemaphoreType.DMA((2, PARTS, 3)),
     ]
-    result = call_product(first_kernel, scalars, [own, near], split[:4], joint, scratch, 2 * terms)
-    first_chip = chip_sum(*result)
-    first = plane_sum(first_chip)
-    scratch = [
-        slab,
-        matrix,
-        matrix,
-        pltpu.VMEM((rows // 2, columns), jnp.float32),
-        pltpu.VMEM((pairs, slots // 2), jnp.float32),
-        total,
-        sems,
-        pltpu.SemaphoreType.DMA((2,)),
-    ]
-    result = call_product(second_kernel, scalars, [passed, crossed, guests], split[4:6], joint, scratch, 2 * terms)
-    second_chip = chip_sum(*result)
-    second = plane_sum(second_chip)
-    scratch = [slab, matrix, matrix, total, sems]
-    (result,) = call_product(last_kernel, scalars, [far, middle], split[6:], [(plane, width, pairs)], scratch, terms)
+    outs = [of(plane, 2 * width, half)] * 2
+    kept, sent = call_product(pair_kernel, scalars, [one, two], split[2:6], [], outs, scratch, 2 * terms)
+    chip = chip_sum(kept, sent)
+    second = plane_sum(chip)
+
+    outs = [jax.ShapeDtypeStruct((pairs, slots), jnp.bfloat16)] * 2
+    scratch = [pltpu.SemaphoreType.DMA((PARTS, 2))]
+    resident = call_product(rows_kernel, scalars, [], split[6:], [], outs, scratch, 0)
+    scratch = [slab, total, pltpu.SemaphoreType.DMA((PARTS,))]
+    outs = [of(plane, width, pairs)]
+    (result,) = call_product(last_kernel, scalars, [three], [], resident, outs, scratch, terms)
     third = plane_sum(result)
     third = third.reshape(width, NC, half).swapaxes(0, 1)
-    handed = permute(second[width:], outward)
-    units = jnp.concatenate([first.reshape(2, width, half), second[None, :width], handed[None], third], axis=0)
+    units = jnp.concatenate([first[None], second.reshape(2, width, half), third], axis=0)
     units = units.reshape(-1, NZ * NC, column_width, half)
 
     def share(flip):

time: 125 us -> 127 us (1.016)
  waiting for transfers between devices: 48.5 us -> 56.8 us
  starting transfers between devices: 39.8 us -> 33.5 us
  local copies, waits for them, and re-layouts: 2.97 us -> 0.11 us
  Pallas kernels: 28.7 us -> 30.8 us
    ppermute x12 -> x8, starting transfers between devices: 25.3 us -> 19.6 us  [permute(): return lax.ppermute(value, AXES, pairs)]
    ppermute x12 -> x8, waiting for transfers between devices: 31.8 us -> 37.2 us  [permute(): return lax.ppermute(value, AXES, pairs)]
    all_to_all x3, waiting for transfers between devices: 16.7 us -> 19.6 us  [plane_sum(): lax.all_to_all(chip, 'blk', 0, 0, tiled=True, axis_index_groups=plane_gro...]
    pallas_call x3 -> x4, Pallas kernels: 14.9 us -> 17.2 us  [call_product(): pl.pallas_call(kernel, out_shape=out_shapes, in_specs=[pl.BlockSpec(memor...]
    slice x2 -> x0, local copies, waits for them, and re-layouts: 1.88 us -> none  [the longest x1 1.88 us: local(): far = permute(crossed[:rows // 2], outward)]
  transfers between devices with their start and end apart: 15 -> 11, of which waited for: 9 -> 8; matrix products, arithmetic and copies ran while one was open for 5% -> 3% of each run, Pallas kernels for 22% -> 24%
where the time goes in v9:
time: 127 us; the launch traced here: 126 us
  waiting for transfers between devices  56.8 us (45%)
  starting transfers between devices  33.5 us (26%)
  Pallas kernels  30.8 us (24%)
  other arithmetic  4.65 us (4%)
    ppermute x8, waiting for transfers between devices, permute(): return lax.ppermute(value, AXES, pairs)  37.2 us
    ppermute x8, starting transfers between devices, permute(): return lax.ppermute(value, AXES, pairs)  19.6 us
    all_to_all x3, waiting for transfers between devices, plane_sum(): lax.all_to_all(chip, 'blk', 0, 0, tiled=True, axis_index_groups=plane_gro...  19.6 us
    pallas_call x4, Pallas kernels, call_product(): pl.pallas_call(kernel, out_shape=out_shapes, in_specs=[pl.BlockSpec(memor...  17.2 us
    all_to_all x3, starting transfers between devices, plane_sum(): lax.all_to_all(chip, 'blk', 0, 0, tiled=True, axis_index_groups=plane_gro...  13.9 us
    pallas_call x1, Pallas kernels, split_rows(): pl.pallas_call(functools.partial(split_kernel, rows, slot_width), out_sha...  12.4 us
    add x2, other arithmetic, chip_sum(): return kept + permute(sent, lambda y, x, z, c, g: (y, x, z, 1 - c, g))  2.67 us
  transfers between devices with their start and end apart: 11, of which 8 were waited for; matrix products, arithmetic and copies ran while one was open for 3% of the time, Pallas kernels for 24%

profile of v9, /device:TPU:1, one launch (start us, length us, event | category | flops | bytes accessed | tf_op | source)
XLA Modules:
  0.0 126.1 jit_solution(17104580262571527085)
XLA Ops:
  0.0 2.5 %collective-permute-start.1 = (f32[1024,256]{1,0:T(8,128)}, f32[1024,256]{1,0:T(8,128)S(1)}, u32[]{:S(2)}, u32[]{:S(2)}) collective-permute-start(f32[1024,256]{1,0:T(8,128)} %bitcast.20), channel_id=1, source_target_pairs={{0,1},{1,0},{2,3},{3,2},{4,5},{5,4},{6,7},{7,6},{8,9},{9,8},{10,11... | collective-permute-start | bytes 3145736 | tf_op jit(solution)/shard_map/ppermute | solution.py:39
  2.5 3.0 %collective-permute-start.2 = (f32[1024,256]{1,0:T(8,128)}, f32[1024,256]{1,0:T(8,128)S(1)}, u32[]{:S(2)}, u32[]{:S(2)}) collective-permute-start(f32[1024,256]{1,0:T(8,128)} %bitcast.21), channel_id=1, source_target_pairs={{0,2},{1,3},{2,0},{3,1},{4,6},{5,7},{6,4},{7,5},{8,10},{9,11},{10,... | collective-permute-start | bytes 3145736 | tf_op jit(solution)/shard_map/ppermute | solution.py:39
  5.4 0.7 pad_add_fusion.scalars
  6.2 0.0 copy-start
  6.2 12.4 %split_rows.1 = (bf16[512,1024]{1,0:T(8,128)(2,1)}, bf16[512,1024]{1,0:T(8,128)(2,1)}, bf16[512,1024]{1,0:T(8,128)(2,1)}, bf16[512,1024]{1,0:T(8,128)(2,1)}, bf1...) custom-call(s32[10]{0:T(128)S(1)} %pad_add_fusion.scalars, ...), custom_call_target="tpu_custom_call" | custom-call | bytes 16777216 | tf_op jit(solution)/shard_map/split_rows/pallas_call | solution.py:91
  18.6 27.3 %collective-permute-done.1.one = f32[1024,256]{1,0:T(8,128)S(1)} collective-permute-done((f32[1024,256]{1,0:T(8,128)}, f32[1024,256]{1,0:T(8,128)S(1)}, u32[]{:S(2)}, u32[]{:S(2)}) %collective-permute-start.1) | collective-permute-done | bytes 1048608 | tf_op jit(solution)/shard_map/ppermute | solution.py:39
  45.9 1.2 collective-permute-done.2.two
  47.1 1.1 broadcast_select_fusion
  48.3 3.0 %collective-permute-start.4 = (f32[1024,256]{1,0:T(8,128)}, f32[1024,256]{1,0:T(8,128)}, u32[]{:S(2)}, u32[]{:S(2)}) collective-permute-start(f32[1024,256]{1,0:T(8,128)} %broadcast_select_fusion), channel_id=1, source_target_pairs={{0,2},{1,0},{2,3},{3,1},{4,6},{5,4},{6,7},{7,5},{8,10},{9,8},{10,1... | collective-permute-start | bytes 3145736 | tf_op jit(solution)/shard_map/ppermute | solution.py:39
  51.3 6.8 %shard_map.47 = (f32[16,32,256]{2,1,0:T(8,128)S(1)}, f32[16,32,256]{2,1,0:T(8,128)}) custom-call(s32[10]{0:T(128)S(1)} %pad_add_fusion.scalars, f32[1024,256]{1,0:T(8,128)S(1)} %collective-permute-done.1.one, f32[1024,256]{1,0:T(8,128)S(1)} %collective-permute-done.2.two, bf16[512,1024]{1,0:T(8,128)(2,1)} %get-tuple-element.23.high_1, ...), custom_call_target="tpu_custom_call" | custom-call | flops 1610612736 | bytes 6291456 | tf_op jit(solution)/shard_map/pallas_call | solution.py:205
  58.0 0.0 copy-start.1
  58.0 2.3 %collective-permute-start.3 = (f32[16,32,256]{2,1,0:T(8,128)}, f32[16,32,256]{2,1,0:T(8,128)S(1)}, u32[]{:S(2)}, u32[]{:S(2)}) collective-permute-start(f32[16,32,256]{2,1,0:T(8,128)} %get-tuple-element.28), channel_id=1, source_target_pairs={{0,4},{1,5},{2,6},{3,7},{4,0},{5,1},{6,2},{7,3},{8,12},{9,13},{10,... | collective-permute-start | bytes 1572872 | tf_op jit(solution)/shard_map/ppermute | solution.py:39
  60.3 0.0 copy-done
  60.3 3.9 %shard_map.46 = (f32[16,16,256]{2,1,0:T(8,128)S(1)}, f32[16,16,256]{2,1,0:T(8,128)S(1)}) custom-call(s32[10]{0:T(128)S(1)} %pad_add_fusion.scalars, f32[1024,256]{1,0:T(8,128)S(1)} %bitcast.22, bf16[512,1024]{1,0:T(8,128)(2,1)} %get-tuple-element.19.high, bf16[512,1024]{1,0:T(8,128)(2,1)} %get-tuple-element.20.low), custom_call_target="tpu_custom_call" | custom-call | flops 805306368 | bytes 6291456 | tf_op jit(solution)/shard_map/pallas_call | solution.py:205
  64.2 0.0 copy-done.1
  64.3 0.1 collective-permute-start
  64.4 1.5 %collective-permute-done = f32[16,16,256]{2,1,0:T(8,128)S(1)} collective-permute-done((f32[16,16,256]{2,1,0:T(8,128)S(1)}, f32[16,16,256]{2,1,0:T(8,128)S(1)}, u32[]{:S(2)}, u32[]{:S(2)}) %collective-permute-start) | collective-permute-done | bytes 262176 | tf_op jit(solution)/shard_map/ppermute | solution.py:39
  65.9 0.8 add.33
  66.6 6.8 %all-to-all-start = ((f32[16,16,256]{2,1,0:T(8,128)}), f32[16,16,256]{2,1,0:T(8,128)S(1)}, u32[]{:S(2)}, u32[]{:S(2)}) async-start(f32[16,16,256]{2,1,0:T(8,128)} %add.33), calls=%async_computation | async-start | bytes 524288 | tf_op jit(solution)/shard_map/all_to_all | solution.py:47
  73.4 0.0 collective-permute-done.3
  73.4 1.9 %add.34 = f32[16,32,256]{2,1,0:T(8,128)} add(f32[16,32,256]{2,1,0:T(8,128)} %copy-done.1, f32[16,32,256]{2,1,0:T(8,128)S(1)} %collective-permute-done.3) | non-fusion elementwise | flops 131072 | bytes 1572864 | tf_op jit(solution)/shard_map/add | solution.py:278
  75.3 6.4 %all-to-all-done = f32[16,16,256]{2,1,0:T(8,128)S(1)} async-done(((f32[16,16,256]{2,1,0:T(8,128)}), f32[16,16,256]{2,1,0:T(8,128)S(1)}, u32[]{:S(2)}, u32[]{:S(2)}) %all-to-all-start) | async-done | bytes 262176 | tf_op jit(solution)/shard_map/all_to_all | solution.py:47
  81.8 3.6 %all-to-all-start.1 = ((f32[16,32,256]{2,1,0:T(8,128)}), f32[16,32,256]{2,1,0:T(8,128)S(1)}, u32[]{:S(2)}, u32[]{:S(2)}) async-start(f32[16,32,256]{2,1,0:T(8,128)} %add.34), calls=%async_computation.1 | async-start | bytes 1048576 | tf_op jit(solution)/shard_map/all_to_all | solution.py:47
  85.3 2.1 %shard_map.48 = (bf16[512,1024]{1,0:T(8,128)(2,1)S(1)}, bf16[512,1024]{1,0:T(8,128)(2,1)S(1)}) custom-call(s32[10]{0:T(128)S(1)} %pad_add_fusion.scalars, bf16[512,1024]{1,0:T(8,128)(2,1)} %get-tuple-element.29.high, bf16[512,1024]{1,0:T(8,128)(2,1)} %get-tuple-element.30.low), custom_call_target="tpu_custom_call" | custom-call | bytes 6291456 | tf_op jit(solution)/shard_map/pallas_call | solution.py:205
  87.5 0.0 collective-permute-done.4.three
  87.5 4.4 %shard_map.49 = f32[16,16,512]{2,1,0:T(8,128)} custom-call(s32[10]{0:T(128)S(1)} %pad_add_fusion.scalars, f32[1024,256]{1,0:T(8,128)} %collective-permute-done.4.three, bf16[512,1024]{1,0:T(8,128)(2,1)S(1)} %get-tuple-element.31.high, bf16[512,1024]{1,0:T(8,128)(2,1)S(1)} %get-tuple-element.32.low), custom_call_target="tpu_custom_call" | custom-call | flops 805306368 | bytes 6291456 | tf_op jit(solution)/shard_map/pallas_call | solution.py:205
  91.9 3.8 %all-to-all-done.1 = f32[16,32,256]{2,1,0:T(8,128)S(1)} async-done(((f32[16,32,256]{2,1,0:T(8,128)}), f32[16,32,256]{2,1,0:T(8,128)S(1)}, u32[]{:S(2)}, u32[]{:S(2)}) %all-to-all-start.1) | async-done | bytes 524320 | tf_op jit(solution)/shard_map/all_to_all | solution.py:47
  95.7 3.6 %all-to-all-start.2 = ((f32[16,16,512]{2,1,0:T(8,128)}), f32[16,16,512]{2,1,0:T(8,128)S(1)}, u32[]{:S(2)}, u32[]{:S(2)}) async-start(f32[16,16,512]{2,1,0:T(8,128)} %shard_map.49), calls=%async_computation.2 | async-start | bytes 1048576 | tf_op jit(solution)/shard_map/all_to_all | solution.py:47
  99.5 9.4 %all-to-all-done.2 = f32[16,16,512]{2,1,0:T(8,128)S(1)} async-done(((f32[16,16,512]{2,1,0:T(8,128)}), f32[16,16,512]{2,1,0:T(8,128)S(1)}, u32[]{:S(2)}, u32[]{:S(2)}) %all-to-all-start.2) | async-done | bytes 524320 | tf_op jit(solution)/shard_map/all_to_all | solution.py:47
  109.0 3.0 %collective-permute-start.5 = (f32[5,4,256]{2,1,0:T(4,128)S(1)}, f32[5,4,256]{2,1,0:T(4,128)S(1)}, u32[]{:S(2)}, u32[]{:S(2)}) collective-permute-start(f32[5,4,256]{2,1,0:T(4,128)S(1)} %get-tuple-element.35), channel_id=1, source_target_pairs={{0,4},{1,5},{2,6},{3,7},{4,0},{5,1},{6,2},{7,3},{8,12},{9,13},{10,... | collective-permute-start | bytes 61448 | tf_op jit(solution)/shard_map/ppermute | solution.py:39
  112.0 5.7 %collective-permute-start.6 = (f32[5,4,256]{2,1,0:T(4,128)S(1)}, f32[5,4,256]{2,1,0:T(4,128)S(1)}, u32[]{:S(2)}, u32[]{:S(2)}) collective-permute-start(f32[5,4,256]{2,1,0:T(4,128)S(1)} %get-tuple-element.34), channel_id=1, source_target_pairs={{0,8},{1,9},{2,10},{3,11},{4,12},{5,13},{6,14},{7,15},{8,0},{9,1},... | collective-permute-start | bytes 61448 | tf_op jit(solution)/shard_map/ppermute | solution.py:39
  117.7 0.1 collective-permute-start.7
  117.8 0.0 collective-permute-done.5.refs_1_
  117.8 1.1 collective-permute-done.6.refs_2_
  118.9 6.1 %collective-permute-done.7.refs_3_ = f32[5,4,256]{2,1,0:T(4,128)S(1)} collective-permute-done((f32[5,4,256]{2,1,0:T(4,128)S(1)}, f32[5,4,256]{2,1,0:T(4,128)S(1)}, u32[]{:S(2)}, u32[]{:S(2)}) %collective-permute-start.7) | collective-permute-done | bytes 20512 | tf_op jit(solution)/shard_map/ppermute | solution.py:39
  124.9 1.2 finish.1
  (10 shorter events, 0.2 us)
Async XLA Ops:
  0.0 45.9 %collective-permute-start.1 = (f32[1024,256]{1,0:T(8,128)}, f32[1024,256]{1,0:T(8,128)S(1)}, u32[]{:S(2)}, u32[]{:S(2)}) collective-permute-start(f32[1024,256]{1,0:T(8,128)} %bitcast.20), channel_id=1, source_target_pairs={{0,1},{1,0},{2,3},{3,2},{4,5},{5,4},{6,7},{7,6},{8,9},{9,8},{10,11... | collective-permute-start | bytes 3145736 | tf_op jit(solution)/shard_map/ppermute | solution.py:39
  2.5 44.7 %collective-permute-start.2 = (f32[1024,256]{1,0:T(8,128)}, f32[1024,256]{1,0:T(8,128)S(1)}, u32[]{:S(2)}, u32[]{:S(2)}) collective-permute-start(f32[1024,256]{1,0:T(8,128)} %bitcast.21), channel_id=1, source_target_pairs={{0,2},{1,3},{2,0},{3,1},{4,6},{5,7},{6,4},{7,5},{8,10},{9,11},{10,... | collective-permute-start | bytes 3145736 | tf_op jit(solution)/shard_map/ppermute | solution.py:39
  6.2 54.1 %copy-start = (f32[1,1024,256]{2,1,0:T(8,128)S(1)}, f32[1,1024,256]{2,1,0:T(8,128)}, u32[]{:S(2)}) copy-start(f32[1,1024,256]{2,1,0:T(8,128)} %param.5) | copy-start | bytes 3145732
  48.3 39.2 %collective-permute-start.4 = (f32[1024,256]{1,0:T(8,128)}, f32[1024,256]{1,0:T(8,128)}, u32[]{:S(2)}, u32[]{:S(2)}) collective-permute-start(f32[1024,256]{1,0:T(8,128)} %broadcast_select_fusion), channel_id=1, source_target_pairs={{0,2},{1,0},{2,3},{3,1},{4,6},{5,4},{6,7},{7,5},{8,10},{9,8},{10,1... | collective-permute-start | bytes 3145736 | tf_op jit(solution)/shard_map/ppermute | solution.py:39
  58.0 6.2 %copy-start.1 = (f32[16,32,256]{2,1,0:T(8,128)}, f32[16,32,256]{2,1,0:T(8,128)S(1)}, u32[]{:S(2)}) copy-start(f32[16,32,256]{2,1,0:T(8,128)S(1)} %get-tuple-element.27) | copy-start | bytes 1572868
  58.0 15.4 %collective-permute-start.3 = (f32[16,32,256]{2,1,0:T(8,128)}, f32[16,32,256]{2,1,0:T(8,128)S(1)}, u32[]{:S(2)}, u32[]{:S(2)}) collective-permute-start(f32[16,32,256]{2,1,0:T(8,128)} %get-tuple-element.28), channel_id=1, source_target_pairs={{0,4},{1,5},{2,6},{3,7},{4,0},{5,1},{6,2},{7,3},{8,12},{9,13},{10,... | collective-permute-start | bytes 1572872 | tf_op jit(solution)/shard_map/ppermute | solution.py:39
  64.3 1.6 %collective-permute-start = (f32[16,16,256]{2,1,0:T(8,128)S(1)}, f32[16,16,256]{2,1,0:T(8,128)S(1)}, u32[]{:S(2)}, u32[]{:S(2)}) collective-permute-start(f32[16,16,256]{2,1,0:T(8,128)S(1)} %get-tuple-element.22), channel_id=1, source_target_pairs={{0,4},{1,5},{2,6},{3,7},{4,0},{5,1},{6,2},{7,3},{8,12},{9,13},{10,... | collective-permute-start | bytes 786440 | tf_op jit(solution)/shard_map/ppermute | solution.py:39
  66.6 15.1 %all-to-all-start = ((f32[16,16,256]{2,1,0:T(8,128)}), f32[16,16,256]{2,1,0:T(8,128)S(1)}, u32[]{:S(2)}, u32[]{:S(2)}) async-start(f32[16,16,256]{2,1,0:T(8,128)} %add.33), calls=%async_computation | async-start | bytes 524288 | tf_op jit(solution)/shard_map/all_to_all | solution.py:47
  81.8 13.9 %all-to-all-start.1 = ((f32[16,32,256]{2,1,0:T(8,128)}), f32[16,32,256]{2,1,0:T(8,128)S(1)}, u32[]{:S(2)}, u32[]{:S(2)}) async-start(f32[16,32,256]{2,1,0:T(8,128)} %add.34), calls=%async_computation.1 | async-start | bytes 1048576 | tf_op jit(solution)/shard_map/all_to_all | solution.py:47
  95.7 13.1 %all-to-all-start.2 = ((f32[16,16,512]{2,1,0:T(8,128)}), f32[16,16,512]{2,1,0:T(8,128)S(1)}, u32[]{:S(2)}, u32[]{:S(2)}) async-start(f32[16,16,512]{2,1,0:T(8,128)} %shard_map.49), calls=%async_computation.2 | async-start | bytes 1048576 | tf_op jit(solution)/shard_map/all_to_all | solution.py:47
  109.0 8.8 %collective-permute-start.5 = (f32[5,4,256]{2,1,0:T(4,128)S(1)}, f32[5,4,256]{2,1,0:T(4,128)S(1)}, u32[]{:S(2)}, u32[]{:S(2)}) collective-permute-start(f32[5,4,256]{2,1,0:T(4,128)S(1)} %get-tuple-element.35), channel_id=1, source_target_pairs={{0,4},{1,5},{2,6},{3,7},{4,0},{5,1},{6,2},{7,3},{8,12},{9,13},{10,... | collective-permute-start | bytes 61448 | tf_op jit(solution)/shard_map/ppermute | solution.py:39
  112.0 6.9 %collective-permute-start.6 = (f32[5,4,256]{2,1,0:T(4,128)S(1)}, f32[5,4,256]{2,1,0:T(4,128)S(1)}, u32[]{:S(2)}, u32[]{:S(2)}) collective-permute-start(f32[5,4,256]{2,1,0:T(4,128)S(1)} %get-tuple-element.34), channel_id=1, source_target_pairs={{0,8},{1,9},{2,10},{3,11},{4,12},{5,13},{6,14},{7,15},{8,0},{9,1},... | collective-permute-start | bytes 61448 | tf_op jit(solution)/shard_map/ppermute | solution.py:39
  117.7 7.2 %collective-permute-start.7 = (f32[5,4,256]{2,1,0:T(4,128)S(1)}, f32[5,4,256]{2,1,0:T(4,128)S(1)}, u32[]{:S(2)}, u32[]{:S(2)}) collective-permute-start(f32[5,4,256]{2,1,0:T(4,128)S(1)} %get-tuple-element.33), channel_id=1, source_target_pairs={{0,12},{1,13},{2,14},{3,15},{4,8},{5,9},{6,10},{7,11},{8,4},{9,5},... | collective-permute-start | bytes 61448 | tf_op jit(solution)/shard_map/ppermute | solution.py:39

commit v10 on v9

--- a/solution.py
+++ b/solution.py
@@ -162,42 +162,28 @@
     put_halves(scalars, total, kept, sent, 0)
 
 
-def pair_kernel(scalars, one, two, high_1, low_1, high_2, low_2, kept, sent, slabs, highs, lows, total, sems):
-    sources = ((one, high_1, low_1), (two, high_2, low_2))
-    here = [(slabs.at[k], highs.at[k], lows.at[k]) for k in range(2)]
-    for k in range(2):
-        start_parts(range(PARTS), sources[k], here[k], sems.at[k])
-    for k in range(2):
-        add_parts(range(PARTS), sources[k], here[k], sems.at[k], total)
+def pair_kernel(scalars, one, two, high_1, low_1, high_2, low_2, kept, sent, total):
+    for k, (slab, high, low) in enumerate(((one, high_1, low_1), (two, high_2, low_2))):
+        total[...] = split_dot((high[...], low[...]), halves_of(slab[...]))
         put_halves(scalars, total, kept, sent, k)
 
 
-def rows_kernel(scalars, high, low, high_out, low_out, sems):
-    depth = high.shape[0] // PARTS
+def rows_kernel(scalars, *refs):
+    count = (len(refs) - 1) // 2
+    there, here, sems = refs[:count], refs[count:-1], refs[-1]
+    depth = there[0].shape[0] // PARTS
     copies = []
-    for part in range(PARTS):
-        place = pl.ds(part * depth, depth)
-        for k, (there, here) in enumerate(((high, high_out), (low, low_out))):
-            copies.append(pltpu.make_async_copy(there.at[place, :], here.at[place, :], sems.at[part, k]))
+    for k in range(count):
+        for part in range(PARTS):
+            place = pl.ds(part * depth, depth)
+            copies.append(pltpu.make_async_copy(there[k].at[place, :], here[k].at[place, :], sems.at[k, part]))
             copies[-1].start()
     for copy in copies:
         copy.wait()
 
 
-def last_kernel(scalars, three, high, low, out, slab, total, sems):
-    depth = slab.shape[0] // PARTS
-    places = [slice(part * depth, (part + 1) * depth) for part in range(PARTS)]
-    copies = [
-        pltpu.make_async_copy(three.at[pl.ds(part * depth, depth), :], slab.at[pl.ds(part * depth, depth), :], sems.at[part])
-        for part in range(PARTS)
-    ]
-    for copy in copies:
-        copy.start()
-    for part, place in enumerate(places):
-        copies[part].wait()
-        term = split_dot((high[:, place], low[:, place]), halves_of(slab[place, :]))
-        total[...] = term if part == 0 else total[...] + term
-    out[...] = total[...].T.reshape(out.shape)
+def last_kernel(scalars, three, high, low, out):
+    out[...] = split_dot((high[...], low[...]), halves_of(three[...])).T.reshape(out.shape)
 
 
 def call_product(kernel, scalars, moved, fixed, resident, out_shapes, scratch, terms):
@@ -226,10 +212,9 @@
         slot = scalars[irrep] ^ group
         size = scalars[IRREPS + irrep]
         valid = (column // BLOCK < size) & (column % BLOCK < size)
-        mine = parts[0][slot] + parts[2][slot]
-        other = parts[1][slot] + parts[3][slot]
+        mine, other = parts[0][slot], parts[1][slot]
         for k in range(NC):
-            whole = (parts[0][last + k] + parts[2][last + k]) + (parts[1][last + k] + parts[3][last + k])
+            whole = parts[0][last + k] + parts[1][last + k]
             value = jnp.where(slot == last, whole, jnp.where(core == k, mine, other))
             out[irrep, :, k * half : (k + 1) * half] = jnp.where(valid, value, 0.0)
 
@@ -283,36 +268,31 @@
     chip = chip_sum(*result)
     first = plane_sum(chip)
 
-    scratch = [
-        pltpu.VMEM((2, rows, columns), jnp.float32),
-        pltpu.VMEM((2, pairs, slots), jnp.bfloat16),
-        pltpu.VMEM((2, pairs, slots), jnp.bfloat16),
-        total,
-        pltpu.SemaphoreType.DMA((2, PARTS, 3)),
-    ]
+    def brought(values):
+        outs = [jax.ShapeDtypeStruct((pairs, slots), jnp.bfloat16)] * len(values)
+        scratch = [pltpu.SemaphoreType.DMA((len(values), PARTS))]
+        return call_product(rows_kernel, scalars, [], values, [], outs, scratch, 0)
+
+    resident = brought(split[2:6])
     outs = [of(plane, 2 * width, half)] * 2
-    kept, sent = call_product(pair_kernel, scalars, [one, two], split[2:6], [], outs, scratch, 2 * terms)
+    kept, sent = call_product(pair_kernel, scalars, [], [], [one, two, *resident], outs, [total], 2 * terms)
     chip = chip_sum(kept, sent)
     second = plane_sum(chip)
 
-    outs = [jax.ShapeDtypeStruct((pairs, slots), jnp.bfloat16)] * 2
-    scratch = [pltpu.SemaphoreType.DMA((PARTS, 2))]
-    resident = call_product(rows_kernel, scalars, [], split[6:], [], outs, scratch, 0)
-    scratch = [slab, total, pltpu.SemaphoreType.DMA((PARTS,))]
+    resident = brought(split[6:])
     outs = [of(plane, width, pairs)]
-    (result,) = call_product(last_kernel, scalars, [three], [], resident, outs, scratch, terms)
+    (result,) = call_product(last_kernel, scalars, [], [], [three, *resident], outs, [], terms)
     third = plane_sum(result)
     third = third.reshape(width, NC, half).swapaxes(0, 1)
     units = jnp.concatenate([first[None], second.reshape(2, width, half), third], axis=0)
-    units = units.reshape(-1, NZ * NC, column_width, half)
-
-    def share(flip):
-        here = (z_part * NC + core) ^ flip
-        return lax.dynamic_index_in_dim(units, here, 1, keepdims=False)
-
-    parts = [share(0)] + [None] * 3
-    for flip in (3, 2, 1):
-        parts[flip] = permute(share(flip), lambda y, x, z, c, g: (y, x, z ^ (flip >> 1), c ^ (flip & 1), g))
+    units = units.reshape(-1, NZ, NC * column_width, half)
+    here = lax.dynamic_index_in_dim(units, z_part, 1, keepdims=False)
+    there = lax.dynamic_index_in_dim(units, 1 - z_part, 1, keepdims=False)
+    units = here + permute(there, lambda y, x, z, c, g: (y, x, 1 - z, c, g))
+    units = units.reshape(-1, NC, column_width, half)
+    here = lax.dynamic_index_in_dim(units, core, 1, keepdims=False)
+    there = lax.dynamic_index_in_dim(units, 1 - core, 1, keepdims=False)
+    parts = [here, permute(there, lambda y, x, z, c, g: (y, x, z, 1 - c, g))]
     return jnp.transpose(finish(scalars, parts), (2, 0, 1))
 
 

time: 127 us -> 120 us (0.945)
  waiting for transfers between devices: 56.8 us -> 52.9 us
  Pallas kernels: 30.8 us -> 28.4 us
    ppermute x8 -> x7, waiting for transfers between devices: 37.2 us -> 31.2 us  [permute(): return lax.ppermute(value, AXES, pairs)]
    pallas_call x4 -> x5, Pallas kernels: 17.2 us -> 14.8 us  [call_product(): pl.pallas_call(kernel, out_shape=out_shapes, in_specs=[pl.BlockSpec(memor...]
    all_to_all x3, waiting for transfers between devices: 19.6 us -> 21.7 us  [plane_sum(): lax.all_to_all(chip, 'blk', 0, 0, tiled=True, axis_index_groups=plane_gro...]
    ppermute x8 -> x7, starting transfers between devices: 19.6 us -> 18.9 us  [permute(): return lax.ppermute(value, AXES, pairs)]
  transfers between devices with their start and end apart: 11 -> 10, of which waited for: 8 -> 7; matrix products, arithmetic and copies ran while one was open for 3% -> 3% of each run, Pallas kernels for 24% -> 23%
where the time goes in v10:
time: 120 us; the launch traced here: 119 us
  waiting for transfers between devices  52.9 us (44%)
  starting transfers between devices  32.8 us (27%)
  Pallas kernels  28.4 us (24%)
  other arithmetic  4.66 us (4%)
    ppermute x7, waiting for transfers between devices, permute(): return lax.ppermute(value, AXES, pairs)  31.2 us
    all_to_all x3, waiting for transfers between devices, plane_sum(): lax.all_to_all(chip, 'blk', 0, 0, tiled=True, axis_index_groups=plane_gro...  21.7 us
    ppermute x7, starting transfers between devices, permute(): return lax.ppermute(value, AXES, pairs)  18.9 us
    pallas_call x5, Pallas kernels, call_product(): pl.pallas_call(kernel, out_shape=out_shapes, in_specs=[pl.BlockSpec(memor...  14.8 us
    all_to_all x3, starting transfers between devices, plane_sum(): lax.all_to_all(chip, 'blk', 0, 0, tiled=True, axis_index_groups=plane_gro...  13.9 us
    pallas_call x1, Pallas kernels, split_rows(): pl.pallas_call(functools.partial(split_kernel, rows, slot_width), out_sha...  12.4 us
    add x2, other arithmetic, chip_sum(): return kept + permute(sent, lambda y, x, z, c, g: (y, x, z, 1 - c, g))  2.69 us
  transfers between devices with their start and end apart: 10, of which 7 were waited for; matrix products, arithmetic and copies ran while one was open for 3% of the time, Pallas kernels for 23%

profile of v10, /device:TPU:1, one launch (start us, length us, event | category | flops | bytes accessed | tf_op | source)
XLA Modules:
  0.0 119.1 jit_solution(6590415740241691934)
XLA Ops:
  0.0 3.8 %collective-permute-start.2 = (f32[1024,256]{1,0:T(8,128)}, f32[1024,256]{1,0:T(8,128)S(1)}, u32[]{:S(2)}, u32[]{:S(2)}) collective-permute-start(f32[1024,256]{1,0:T(8,128)} %bitcast.23), channel_id=1, source_target_pairs={{0,2},{1,3},{2,0},{3,1},{4,6},{5,7},{6,4},{7,5},{8,10},{9,11},{10,... | collective-permute-start | bytes 3145736 | tf_op jit(solution)/shard_map/ppermute | solution.py:39
  3.8 1.6 %collective-permute-start.1 = (f32[1024,256]{1,0:T(8,128)}, f32[1024,256]{1,0:T(8,128)S(1)}, u32[]{:S(2)}, u32[]{:S(2)}) collective-permute-start(f32[1024,256]{1,0:T(8,128)} %bitcast.24), channel_id=1, source_target_pairs={{0,1},{1,0},{2,3},{3,2},{4,5},{5,4},{6,7},{7,6},{8,9},{9,8},{10,11... | collective-permute-start | bytes 3145736 | tf_op jit(solution)/shard_map/ppermute | solution.py:39
  5.4 0.7 pad_add_fusion.scalars
  6.2 12.4 %split_rows.1 = (bf16[512,1024]{1,0:T(8,128)(2,1)}, bf16[512,1024]{1,0:T(8,128)(2,1)}, bf16[512,1024]{1,0:T(8,128)(2,1)}, bf16[512,1024]{1,0:T(8,128)(2,1)}, bf1...) custom-call(s32[10]{0:T(128)S(1)} %pad_add_fusion.scalars, ...), custom_call_target="tpu_custom_call" | custom-call | bytes 16777216 | tf_op jit(solution)/shard_map/split_rows/pallas_call | solution.py:91
  18.6 0.0 copy-start
  18.6 2.8 %shard_map.47 = (bf16[512,1024]{1,0:T(8,128)(2,1)S(1)}, bf16[512,1024]{1,0:T(8,128)(2,1)S(1)}, bf16[512,1024]{1,0:T(8,128)(2,1)S(1)}, bf16[512,1024]{1,0:T(8,128)(2,1)S(1)}) custom-call(s32[10]{0:T(128)S(1)} %pad_add_fusion.scalars, bf16[512,1024]{1,0:T(8,128)(2,1)} %get-tuple-element.27.refs_0_, bf16[512,1024]{1,0:T(8,128)(2,1)} %get-tuple-element.28.refs_1_, ...), custom_call_target="tpu_custom_call" | custom-call | bytes 6291456 | tf_op jit(solution)/shard_map/pallas_call | solution.py:191
  21.4 27.4 %collective-permute-done.2.two = f32[1024,256]{1,0:T(8,128)S(1)} collective-permute-done((f32[1024,256]{1,0:T(8,128)}, f32[1024,256]{1,0:T(8,128)S(1)}, u32[]{:S(2)}, u32[]{:S(2)}) %collective-permute-start.2) | collective-permute-done | bytes 1048608 | tf_op jit(solution)/shard_map/ppermute | solution.py:39
  48.8 0.0 collective-permute-done.1.one
  48.8 1.1 broadcast_select_fusion
  49.9 2.2 %collective-permute-start.4 = (f32[1024,256]{1,0:T(8,128)}, f32[1024,256]{1,0:T(8,128)S(1)}, u32[]{:S(2)}, u32[]{:S(2)}) collective-permute-start(f32[1024,256]{1,0:T(8,128)} %broadcast_select_fusion), channel_id=1, source_target_pairs={{0,2},{1,0},{2,3},{3,1},{4,6},{5,4},{6,7},{7,5},{8,10},{9,8},{10,1... | collective-permute-start | bytes 3145736 | tf_op jit(solution)/shard_map/ppermute | solution.py:39
  52.1 3.5 %shard_map.48 = (f32[16,32,256]{2,1,0:T(8,128)S(1)}, f32[16,32,256]{2,1,0:T(8,128)}) custom-call(s32[10]{0:T(128)S(1)} %pad_add_fusion.scalars, f32[1024,256]{1,0:T(8,128)S(1)} %collective-permute-done.1.one, f32[1024,256]{1,0:T(8,128)S(1)} %collective-permute-done.2.two, bf16[512,1024]{1,0:T(8,128)(2,1)S(1)} %get-tuple-element.31.high_1, ...), custom_call_target="tpu_custom_call" | custom-call | flops 1610612736 | bytes 6291456 | tf_op jit(solution)/shard_map/pallas_call | solution.py:191
  55.7 0.0 copy-start.1
  55.7 1.5 %collective-permute-start.3 = (f32[16,32,256]{2,1,0:T(8,128)}, f32[16,32,256]{2,1,0:T(8,128)S(1)}, u32[]{:S(2)}, u32[]{:S(2)}) collective-permute-start(f32[16,32,256]{2,1,0:T(8,128)} %get-tuple-element.36), channel_id=1, source_target_pairs={{0,4},{1,5},{2,6},{3,7},{4,0},{5,1},{6,2},{7,3},{8,12},{9,13},{10,... | collective-permute-start | bytes 1572872 | tf_op jit(solution)/shard_map/ppermute | solution.py:39
  57.2 0.0 copy-done
  57.2 3.9 %shard_map.46 = (f32[16,16,256]{2,1,0:T(8,128)S(1)}, f32[16,16,256]{2,1,0:T(8,128)S(1)}) custom-call(s32[10]{0:T(128)S(1)} %pad_add_fusion.scalars, f32[1024,256]{1,0:T(8,128)S(1)} %bitcast.25, bf16[512,1024]{1,0:T(8,128)(2,1)} %get-tuple-element.23.high, bf16[512,1024]{1,0:T(8,128)(2,1)} %get-tuple-element.24.low), custom_call_target="tpu_custom_call" | custom-call | flops 805306368 | bytes 6291456 | tf_op jit(solution)/shard_map/pallas_call | solution.py:191
  61.1 0.0 copy-done.1
  61.1 0.1 collective-permute-start
  61.2 1.5 %collective-permute-done = f32[16,16,256]{2,1,0:T(8,128)S(1)} collective-permute-done((f32[16,16,256]{2,1,0:T(8,128)S(1)}, f32[16,16,256]{2,1,0:T(8,128)S(1)}, u32[]{:S(2)}, u32[]{:S(2)}) %collective-permute-start) | collective-permute-done | bytes 262176 | tf_op jit(solution)/shard_map/ppermute | solution.py:39
  62.8 0.8 add.33
  63.5 6.8 %all-to-all-start = ((f32[16,16,256]{2,1,0:T(8,128)}), f32[16,16,256]{2,1,0:T(8,128)S(1)}, u32[]{:S(2)}, u32[]{:S(2)}) async-start(f32[16,16,256]{2,1,0:T(8,128)} %add.33), calls=%async_computation | async-start | bytes 524288 | tf_op jit(solution)/shard_map/all_to_all | solution.py:47
  70.3 0.0 collective-permute-done.3
  70.3 1.9 %add.34 = f32[16,32,256]{2,1,0:T(8,128)} add(f32[16,32,256]{2,1,0:T(8,128)} %copy-done.1, f32[16,32,256]{2,1,0:T(8,128)S(1)} %collective-permute-done.3) | non-fusion elementwise | flops 131072 | bytes 1572864 | tf_op jit(solution)/shard_map/add | solution.py:263
  72.2 6.4 %all-to-all-done = f32[16,16,256]{2,1,0:T(8,128)S(1)} async-done(((f32[16,16,256]{2,1,0:T(8,128)}), f32[16,16,256]{2,1,0:T(8,128)S(1)}, u32[]{:S(2)}, u32[]{:S(2)}) %all-to-all-start) | async-done | bytes 262176 | tf_op jit(solution)/shard_map/all_to_all | solution.py:47
  78.7 3.6 %all-to-all-start.1 = ((f32[16,32,256]{2,1,0:T(8,128)}), f32[16,32,256]{2,1,0:T(8,128)S(1)}, u32[]{:S(2)}, u32[]{:S(2)}) async-start(f32[16,32,256]{2,1,0:T(8,128)} %add.34), calls=%async_computation.1 | async-start | bytes 1048576 | tf_op jit(solution)/shard_map/all_to_all | solution.py:47
  82.2 2.1 %shard_map.49 = (bf16[512,1024]{1,0:T(8,128)(2,1)S(1)}, bf16[512,1024]{1,0:T(8,128)(2,1)S(1)}) custom-call(s32[10]{0:T(128)S(1)} %pad_add_fusion.scalars, bf16[512,1024]{1,0:T(8,128)(2,1)} %get-tuple-element.37.refs_0_, bf16[512,1024]{1,0:T(8,128)(2,1)} %get-tuple-element.38.refs_1_), custom_call_target="tpu_custom_call" | custom-call | bytes 6291456 | tf_op jit(solution)/shard_map/pallas_call | solution.py:191
  84.4 0.0 collective-permute-done.4.three
  84.4 2.4 %shard_map.50 = f32[16,16,512]{2,1,0:T(8,128)} custom-call(s32[10]{0:T(128)S(1)} %pad_add_fusion.scalars, f32[1024,256]{1,0:T(8,128)S(1)} %collective-permute-done.4.three, bf16[512,1024]{1,0:T(8,128)(2,1)S(1)} %get-tuple-element.39.high, bf16[512,1024]{1,0:T(8,128)(2,1)S(1)} %get-tuple-element.40.low), custom_call_target="tpu_custom_call" | custom-call | flops 805306368 | bytes 6291456 | tf_op jit(solution)/shard_map/pallas_call | solution.py:191
  86.8 5.8 %all-to-all-done.1 = f32[16,32,256]{2,1,0:T(8,128)S(1)} async-done(((f32[16,32,256]{2,1,0:T(8,128)}), f32[16,32,256]{2,1,0:T(8,128)S(1)}, u32[]{:S(2)}, u32[]{:S(2)}) %all-to-all-start.1) | async-done | bytes 524320 | tf_op jit(solution)/shard_map/all_to_all | solution.py:47
  92.6 3.6 %all-to-all-start.2 = ((f32[16,16,512]{2,1,0:T(8,128)}), f32[16,16,512]{2,1,0:T(8,128)S(1)}, u32[]{:S(2)}, u32[]{:S(2)}) async-start(f32[16,16,512]{2,1,0:T(8,128)} %shard_map.50), calls=%async_computation.2 | async-start | bytes 1048576 | tf_op jit(solution)/shard_map/all_to_all | solution.py:47
  96.3 9.4 %all-to-all-done.2 = f32[16,16,512]{2,1,0:T(8,128)S(1)} async-done(((f32[16,16,512]{2,1,0:T(8,128)}), f32[16,16,512]{2,1,0:T(8,128)S(1)}, u32[]{:S(2)}, u32[]{:S(2)}) %all-to-all-start.2) | async-done | bytes 524320 | tf_op jit(solution)/shard_map/all_to_all | solution.py:47
  105.9 5.5 %collective-permute-start.5 = (f32[5,8,256]{2,1,0:T(8,128)S(1)}, f32[5,8,256]{2,1,0:T(8,128)S(1)}, u32[]{:S(2)}, u32[]{:S(2)}) collective-permute-start(f32[5,8,256]{2,1,0:T(8,128)S(1)} %dynamic-slice_bitcast_fusion), channel_id=1, source_target_pairs={{0,8},{1,9},{2,10},{3,11},{4,12},{5,13},{6,14},{7,15},{8,0},{9,1},... | collective-permute-start | bytes 122888 | tf_op jit(solution)/shard_map/ppermute | solution.py:39
  111.3 1.5 %collective-permute-done.5 = f32[5,8,256]{2,1,0:T(8,128)S(1)} collective-permute-done((f32[5,8,256]{2,1,0:T(8,128)S(1)}, f32[5,8,256]{2,1,0:T(8,128)S(1)}, u32[]{:S(2)}, u32[]{:S(2)}) %collective-permute-start.5) | collective-permute-done | bytes 40992 | tf_op jit(solution)/shard_map/ppermute | solution.py:39
  112.9 4.2 %collective-permute-start.6 = (f32[5,4,256]{2,1,0:T(4,128)S(1)}, f32[5,4,256]{2,1,0:T(4,128)S(1)}, u32[]{:S(2)}, u32[]{:S(2)}) collective-permute-start(f32[5,4,256]{2,1,0:T(4,128)S(1)} %get-tuple-element.41), channel_id=1, source_target_pairs={{0,4},{1,5},{2,6},{3,7},{4,0},{5,1},{6,2},{7,3},{8,12},{9,13},{10,... | collective-permute-start | bytes 61448 | tf_op jit(solution)/shard_map/ppermute | solution.py:39
  117.0 0.8 collective-permute-done.6.refs_1_
  117.9 1.2 finish.1
  (10 shorter events, 0.2 us)
Async XLA Ops:
  0.0 48.8 %collective-permute-start.2 = (f32[1024,256]{1,0:T(8,128)}, f32[1024,256]{1,0:T(8,128)S(1)}, u32[]{:S(2)}, u32[]{:S(2)}) collective-permute-start(f32[1024,256]{1,0:T(8,128)} %bitcast.23), channel_id=1, source_target_pairs={{0,2},{1,3},{2,0},{3,1},{4,6},{5,7},{6,4},{7,5},{8,10},{9,11},{10,... | collective-permute-start | bytes 3145736 | tf_op jit(solution)/shard_map/ppermute | solution.py:39
  3.8 45.0 %collective-permute-start.1 = (f32[1024,256]{1,0:T(8,128)}, f32[1024,256]{1,0:T(8,128)S(1)}, u32[]{:S(2)}, u32[]{:S(2)}) collective-permute-start(f32[1024,256]{1,0:T(8,128)} %bitcast.24), channel_id=1, source_target_pairs={{0,1},{1,0},{2,3},{3,2},{4,5},{5,4},{6,7},{7,6},{8,9},{9,8},{10,11... | collective-permute-start | bytes 3145736 | tf_op jit(solution)/shard_map/ppermute | solution.py:39
  18.6 38.6 %copy-start = (f32[1,1024,256]{2,1,0:T(8,128)S(1)}, f32[1,1024,256]{2,1,0:T(8,128)}, u32[]{:S(2)}) copy-start(f32[1,1024,256]{2,1,0:T(8,128)} %param.5) | copy-start | bytes 3145732
  49.9 34.5 %collective-permute-start.4 = (f32[1024,256]{1,0:T(8,128)}, f32[1024,256]{1,0:T(8,128)S(1)}, u32[]{:S(2)}, u32[]{:S(2)}) collective-permute-start(f32[1024,256]{1,0:T(8,128)} %broadcast_select_fusion), channel_id=1, source_target_pairs={{0,2},{1,0},{2,3},{3,1},{4,6},{5,4},{6,7},{7,5},{8,10},{9,8},{10,1... | collective-permute-start | bytes 3145736 | tf_op jit(solution)/shard_map/ppermute | solution.py:39
  55.7 5.5 %copy-start.1 = (f32[16,32,256]{2,1,0:T(8,128)}, f32[16,32,256]{2,1,0:T(8,128)S(1)}, u32[]{:S(2)}) copy-start(f32[16,32,256]{2,1,0:T(8,128)S(1)} %get-tuple-element.35) | copy-start | bytes 1572868
  55.7 14.6 %collective-permute-start.3 = (f32[16,32,256]{2,1,0:T(8,128)}, f32[16,32,256]{2,1,0:T(8,128)S(1)}, u32[]{:S(2)}, u32[]{:S(2)}) collective-permute-start(f32[16,32,256]{2,1,0:T(8,128)} %get-tuple-element.36), channel_id=1, source_target_pairs={{0,4},{1,5},{2,6},{3,7},{4,0},{5,1},{6,2},{7,3},{8,12},{9,13},{10,... | collective-permute-start | bytes 1572872 | tf_op jit(solution)/shard_map/ppermute | solution.py:39
  61.1 1.6 %collective-permute-start = (f32[16,16,256]{2,1,0:T(8,128)S(1)}, f32[16,16,256]{2,1,0:T(8,128)S(1)}, u32[]{:S(2)}, u32[]{:S(2)}) collective-permute-start(f32[16,16,256]{2,1,0:T(8,128)S(1)} %get-tuple-element.26), channel_id=1, source_target_pairs={{0,4},{1,5},{2,6},{3,7},{4,0},{5,1},{6,2},{7,3},{8,12},{9,13},{10,... | collective-permute-start | bytes 786440 | tf_op jit(solution)/shard_map/ppermute | solution.py:39
  63.5 15.1 %all-to-all-start = ((f32[16,16,256]{2,1,0:T(8,128)}), f32[16,16,256]{2,1,0:T(8,128)S(1)}, u32[]{:S(2)}, u32[]{:S(2)}) async-start(f32[16,16,256]{2,1,0:T(8,128)} %add.33), calls=%async_computation | async-start | bytes 524288 | tf_op jit(solution)/shard_map/all_to_all | solution.py:47
  78.7 13.9 %all-to-all-start.1 = ((f32[16,32,256]{2,1,0:T(8,128)}), f32[16,32,256]{2,1,0:T(8,128)S(1)}, u32[]{:S(2)}, u32[]{:S(2)}) async-start(f32[16,32,256]{2,1,0:T(8,128)} %add.34), calls=%async_computation.1 | async-start | bytes 1048576 | tf_op jit(solution)/shard_map/all_to_all | solution.py:47
  92.6 13.1 %all-to-all-start.2 = ((f32[16,16,512]{2,1,0:T(8,128)}), f32[16,16,512]{2,1,0:T(8,128)S(1)}, u32[]{:S(2)}, u32[]{:S(2)}) async-start(f32[16,16,512]{2,1,0:T(8,128)} %shard_map.50), calls=%async_computation.2 | async-start | bytes 1048576 | tf_op jit(solution)/shard_map/all_to_all | solution.py:47
  105.9 7.0 %collective-permute-start.5 = (f32[5,8,256]{2,1,0:T(8,128)S(1)}, f32[5,8,256]{2,1,0:T(8,128)S(1)}, u32[]{:S(2)}, u32[]{:S(2)}) collective-permute-start(f32[5,8,256]{2,1,0:T(8,128)S(1)} %dynamic-slice_bitcast_fusion), channel_id=1, source_target_pairs={{0,8},{1,9},{2,10},{3,11},{4,12},{5,13},{6,14},{7,15},{8,0},{9,1},... | collective-permute-start | bytes 122888 | tf_op jit(solution)/shard_map/ppermute | solution.py:39
  112.9 5.0 %collective-permute-start.6 = (f32[5,4,256]{2,1,0:T(4,128)S(1)}, f32[5,4,256]{2,1,0:T(4,128)S(1)}, u32[]{:S(2)}, u32[]{:S(2)}) collective-permute-start(f32[5,4,256]{2,1,0:T(4,128)S(1)} %get-tuple-element.41), channel_id=1, source_target_pairs={{0,4},{1,5},{2,6},{3,7},{4,0},{5,1},{6,2},{7,3},{8,12},{9,13},{10,... | collective-permute-start | bytes 61448 | tf_op jit(solution)/shard_map/ppermute | solution.py:39

commit v11 on v10

--- a/solution.py
+++ b/solution.py
@@ -45,6 +45,12 @@
 
 def plane_sum(chip):
     spread = lax.all_to_all(chip, "blk", 0, 0, tiled=True, axis_index_groups=plane_groups())
+    return jnp.sum(spread, axis=0)
+
+
+def box_sum(chip):
+    groups = [[blk_index(y, x, z, c) for y in range(NY) for x in range(NX) for z in range(NZ)] for c in range(NC)]
+    spread = lax.all_to_all(chip, "blk", 0, 0, tiled=True, axis_index_groups=groups)
     return jnp.sum(spread, axis=0)
 
 
@@ -282,13 +288,14 @@
     resident = brought(split[6:])
     outs = [of(plane, width, pairs)]
     (result,) = call_product(last_kernel, scalars, [], [], [three, *resident], outs, [], terms)
-    third = plane_sum(result)
-    third = third.reshape(width, NC, half).swapaxes(0, 1)
-    units = jnp.concatenate([first[None], second.reshape(2, width, half), third], axis=0)
-    units = units.reshape(-1, NZ, NC * column_width, half)
-    here = lax.dynamic_index_in_dim(units, z_part, 1, keepdims=False)
-    there = lax.dynamic_index_in_dim(units, 1 - z_part, 1, keepdims=False)
-    units = here + permute(there, lambda y, x, z, c, g: (y, x, 1 - z, c, g))
+    third = box_sum(result.reshape(plane * NZ, width // NZ, pairs))
+    third = third.reshape(width // NZ, NC, half).swapaxes(0, 1)
+    early = jnp.concatenate([first[None], second.reshape(2, width, half)], axis=0)
+    early = early.reshape(-1, NZ, NC * column_width, half)
+    here = lax.dynamic_index_in_dim(early, z_part, 1, keepdims=False)
+    there = lax.dynamic_index_in_dim(early, 1 - z_part, 1, keepdims=False)
+    early = here + permute(there, lambda y, x, z, c, g: (y, x, 1 - z, c, g))
+    units = jnp.concatenate([early, third], axis=0)
     units = units.reshape(-1, NC, column_width, half)
     here = lax.dynamic_index_in_dim(units, core, 1, keepdims=False)
     there = lax.dynamic_index_in_dim(units, 1 - core, 1, keepdims=False)

time: 120 us -> 126 us (1.050)
  the two profiles are of different devices: /device:TPU:1 before, /device:TPU:33 now
where the time goes in v11:
time: 126 us; the launch traced here: 125 us
  waiting for transfers between devices  59.9 us (48%)
  starting transfers between devices  31.9 us (25%)
  Pallas kernels  28.4 us (23%)
  other arithmetic  4.68 us (4%)
    ppermute x7, waiting for transfers between devices, permute(): return lax.ppermute(value, AXES, pairs)  43.8 us
    pallas_call x5, Pallas kernels, call_product(): pl.pallas_call(kernel, out_shape=out_shapes, in_specs=[pl.BlockSpec(memor...  14.8 us
    pallas_call x1, Pallas kernels, split_rows(): pl.pallas_call(functools.partial(split_kernel, rows, slot_width), out_sha...  12.4 us
    ppermute x7, starting transfers between devices, permute(): return lax.ppermute(value, AXES, pairs)  12.3 us
    all_to_all x2, waiting for transfers between devices, plane_sum(): lax.all_to_all(chip, 'blk', 0, 0, tiled=True, axis_index_groups=plane_gro...  12.2 us
    all_to_all x2, starting transfers between devices, plane_sum(): lax.all_to_all(chip, 'blk', 0, 0, tiled=True, axis_index_groups=plane_gro...  10.3 us
    all_to_all x1, starting transfers between devices, box_sum(): lax.all_to_all(chip, 'blk', 0, 0, tiled=True, axis_index_groups=groups)  9.22 us
    all_to_all x1, waiting for transfers between devices, box_sum(): lax.all_to_all(chip, 'blk', 0, 0, tiled=True, axis_index_groups=groups)  3.85 us
  transfers between devices with their start and end apart: 10, of which 7 were waited for; matrix products, arithmetic and copies ran while one was open for 3% of the time, Pallas kernels for 22%

profile of v11, /device:TPU:33, one launch (start us, length us, event | category | flops | bytes accessed | tf_op | source)
XLA Modules:
  0.0 125.1 jit_solution(6231927332129020483)
XLA Ops:
  0.0 3.0 %collective-permute-start.2 = (f32[1024,256]{1,0:T(8,128)}, f32[1024,256]{1,0:T(8,128)S(1)}, u32[]{:S(2)}, u32[]{:S(2)}) collective-permute-start(f32[1024,256]{1,0:T(8,128)} %bitcast.25), channel_id=1, source_target_pairs={{0,2},{1,3},{2,0},{3,1},{4,6},{5,7},{6,4},{7,5},{8,10},{9,11},{10,... | collective-permute-start | bytes 3145736 | tf_op jit(solution)/shard_map/ppermute | solution.py:39
  3.0 0.0 collective-permute-start.1
  3.0 0.7 pad_add_fusion.scalars
  3.7 12.4 %split_rows.1 = (bf16[512,1024]{1,0:T(8,128)(2,1)}, bf16[512,1024]{1,0:T(8,128)(2,1)}, bf16[512,1024]{1,0:T(8,128)(2,1)}, bf16[512,1024]{1,0:T(8,128)(2,1)}, bf1...) custom-call(s32[10]{0:T(128)S(1)} %pad_add_fusion.scalars, ...), custom_call_target="tpu_custom_call" | custom-call | bytes 16777216 | tf_op jit(solution)/shard_map/split_rows/pallas_call | solution.py:97
  16.2 0.0 copy-start
  16.2 2.8 %shard_map.47 = (bf16[512,1024]{1,0:T(8,128)(2,1)S(1)}, bf16[512,1024]{1,0:T(8,128)(2,1)S(1)}, bf16[512,1024]{1,0:T(8,128)(2,1)S(1)}, bf16[512,1024]{1,0:T(8,128)(2,1)S(1)}) custom-call(s32[10]{0:T(128)S(1)} %pad_add_fusion.scalars, bf16[512,1024]{1,0:T(8,128)(2,1)} %get-tuple-element.27.refs_0_, bf16[512,1024]{1,0:T(8,128)(2,1)} %get-tuple-element.28.refs_1_, ...), custom_call_target="tpu_custom_call" | custom-call | bytes 6291456 | tf_op jit(solution)/shard_map/pallas_call | solution.py:197
  19.0 29.2 %collective-permute-done.2.two = f32[1024,256]{1,0:T(8,128)S(1)} collective-permute-done((f32[1024,256]{1,0:T(8,128)}, f32[1024,256]{1,0:T(8,128)S(1)}, u32[]{:S(2)}, u32[]{:S(2)}) %collective-permute-start.2) | collective-permute-done | bytes 1048608 | tf_op jit(solution)/shard_map/ppermute | solution.py:39
  48.2 0.0 collective-permute-done.1.one
  48.2 1.1 broadcast_select_fusion
  49.3 0.0 collective-permute-start.5
  49.3 3.5 %shard_map.48 = (f32[16,32,256]{2,1,0:T(8,128)S(1)}, f32[16,32,256]{2,1,0:T(8,128)}) custom-call(s32[10]{0:T(128)S(1)} %pad_add_fusion.scalars, f32[1024,256]{1,0:T(8,128)S(1)} %collective-permute-done.1.one, f32[1024,256]{1,0:T(8,128)S(1)} %collective-permute-done.2.two, bf16[512,1024]{1,0:T(8,128)(2,1)S(1)} %get-tuple-element.31.high_1, ...), custom_call_target="tpu_custom_call" | custom-call | flops 1610612736 | bytes 6291456 | tf_op jit(solution)/shard_map/pallas_call | solution.py:197
  52.9 0.0 copy-start.1
  52.9 1.9 %collective-permute-start.3 = (f32[16,32,256]{2,1,0:T(8,128)}, f32[16,32,256]{2,1,0:T(8,128)S(1)}, u32[]{:S(2)}, u32[]{:S(2)}) collective-permute-start(f32[16,32,256]{2,1,0:T(8,128)} %get-tuple-element.36), channel_id=1, source_target_pairs={{0,4},{1,5},{2,6},{3,7},{4,0},{5,1},{6,2},{7,3},{8,12},{9,13},{10,... | collective-permute-start | bytes 1572872 | tf_op jit(solution)/shard_map/ppermute | solution.py:39
  54.8 0.0 copy-done
  54.8 3.9 %shard_map.46 = (f32[16,16,256]{2,1,0:T(8,128)S(1)}, f32[16,16,256]{2,1,0:T(8,128)S(1)}) custom-call(s32[10]{0:T(128)S(1)} %pad_add_fusion.scalars, f32[1024,256]{1,0:T(8,128)S(1)} %bitcast.27, bf16[512,1024]{1,0:T(8,128)(2,1)} %get-tuple-element.23.high, bf16[512,1024]{1,0:T(8,128)(2,1)} %get-tuple-element.24.low), custom_call_target="tpu_custom_call" | custom-call | flops 805306368 | bytes 6291456 | tf_op jit(solution)/shard_map/pallas_call | solution.py:197
  58.7 0.0 copy-done.1
  58.7 0.1 collective-permute-start
  58.8 1.5 %collective-permute-done = f32[16,16,256]{2,1,0:T(8,128)S(1)} collective-permute-done((f32[16,16,256]{2,1,0:T(8,128)S(1)}, f32[16,16,256]{2,1,0:T(8,128)S(1)}, u32[]{:S(2)}, u32[]{:S(2)}) %collective-permute-start) | collective-permute-done | bytes 262176 | tf_op jit(solution)/shard_map/ppermute | solution.py:39
  60.3 0.8 add.33
  61.1 6.8 %all-to-all-start = ((f32[16,16,256]{2,1,0:T(8,128)}), f32[16,16,256]{2,1,0:T(8,128)S(1)}, u32[]{:S(2)}, u32[]{:S(2)}) async-start(f32[16,16,256]{2,1,0:T(8,128)} %add.33), calls=%async_computation | async-start | bytes 524288 | tf_op jit(solution)/shard_map/all_to_all | solution.py:47
  67.8 0.0 collective-permute-done.3
  67.9 1.9 %add.34 = f32[16,32,256]{2,1,0:T(8,128)} add(f32[16,32,256]{2,1,0:T(8,128)} %copy-done.1, f32[16,32,256]{2,1,0:T(8,128)S(1)} %collective-permute-done.3) | non-fusion elementwise | flops 131072 | bytes 1572864 | tf_op jit(solution)/shard_map/add | solution.py:269
  69.8 6.4 %all-to-all-done = f32[16,16,256]{2,1,0:T(8,128)S(1)} async-done(((f32[16,16,256]{2,1,0:T(8,128)}), f32[16,16,256]{2,1,0:T(8,128)S(1)}, u32[]{:S(2)}, u32[]{:S(2)}) %all-to-all-start) | async-done | bytes 262176 | tf_op jit(solution)/shard_map/all_to_all | solution.py:47
  76.2 3.6 %all-to-all-start.1 = ((f32[16,32,256]{2,1,0:T(8,128)}), f32[16,32,256]{2,1,0:T(8,128)S(1)}, u32[]{:S(2)}, u32[]{:S(2)}) async-start(f32[16,32,256]{2,1,0:T(8,128)} %add.34), calls=%async_computation.1 | async-start | bytes 1048576 | tf_op jit(solution)/shard_map/all_to_all | solution.py:47
  79.8 2.1 %shard_map.49 = (bf16[512,1024]{1,0:T(8,128)(2,1)S(1)}, bf16[512,1024]{1,0:T(8,128)(2,1)S(1)}) custom-call(s32[10]{0:T(128)S(1)} %pad_add_fusion.scalars, bf16[512,1024]{1,0:T(8,128)(2,1)} %get-tuple-element.37.refs_0_, bf16[512,1024]{1,0:T(8,128)(2,1)} %get-tuple-element.38.refs_1_), custom_call_target="tpu_custom_call" | custom-call | bytes 6291456 | tf_op jit(solution)/shard_map/pallas_call | solution.py:197
  81.9 0.0 collective-permute-done.5.three
  81.9 2.4 %shard_map.50 = f32[16,16,512]{2,1,0:T(8,128)} custom-call(s32[10]{0:T(128)S(1)} %pad_add_fusion.scalars, f32[1024,256]{1,0:T(8,128)S(1)} %collective-permute-done.5.three, bf16[512,1024]{1,0:T(8,128)(2,1)S(1)} %get-tuple-element.39.high, bf16[512,1024]{1,0:T(8,128)(2,1)S(1)} %get-tuple-element.40.low), custom_call_target="tpu_custom_call" | custom-call | flops 805306368 | bytes 6291456 | tf_op jit(solution)/shard_map/pallas_call | solution.py:197
  84.3 5.8 %all-to-all-done.1 = f32[16,32,256]{2,1,0:T(8,128)S(1)} async-done(((f32[16,32,256]{2,1,0:T(8,128)}), f32[16,32,256]{2,1,0:T(8,128)S(1)}, u32[]{:S(2)}, u32[]{:S(2)}) %all-to-all-start.1) | async-done | bytes 524320 | tf_op jit(solution)/shard_map/all_to_all | solution.py:47
  90.2 9.2 %all-to-all-start.2 = ((f32[32,8,512]{2,1,0:T(8,128)}), f32[32,8,512]{2,1,0:T(8,128)S(1)}, u32[]{:S(2)}, u32[]{:S(2)}) async-start(f32[32,8,512]{2,1,0:T(8,128)} %bitcast.10), calls=%async_computation.2 | async-start | bytes 1048576 | tf_op jit(solution)/shard_map/all_to_all | solution.py:53
  99.5 5.2 %collective-permute-start.4 = (f32[3,8,256]{2,1,0:T(8,128)S(1)}, f32[3,8,256]{2,1,0:T(8,128)S(1)}, u32[]{:S(2)}, u32[]{:S(2)}) collective-permute-start(f32[3,8,256]{2,1,0:T(8,128)S(1)} %fusion.1), channel_id=1, source_target_pairs={{0,8},{1,9},{2,10},{3,11},{4,12},{5,13},{6,14},{7,15},{8,0},{9,1},... | collective-permute-start | bytes 73736 | tf_op jit(solution)/shard_map/ppermute | solution.py:39
  104.7 12.3 %collective-permute-done.4 = f32[3,8,256]{2,1,0:T(8,128)S(1)} collective-permute-done((f32[3,8,256]{2,1,0:T(8,128)S(1)}, f32[3,8,256]{2,1,0:T(8,128)S(1)}, u32[]{:S(2)}, u32[]{:S(2)}) %collective-permute-start.4) | collective-permute-done | bytes 24608 | tf_op jit(solution)/shard_map/ppermute | solution.py:39
  117.0 3.9 %all-to-all-done.2 = f32[32,8,512]{2,1,0:T(8,128)S(1)} async-done(((f32[32,8,512]{2,1,0:T(8,128)}), f32[32,8,512]{2,1,0:T(8,128)S(1)}, u32[]{:S(2)}, u32[]{:S(2)}) %all-to-all-start.2) | async-done | bytes 524320 | tf_op jit(solution)/shard_map/all_to_all | solution.py:53
  121.0 2.1 %collective-permute-start.6 = (f32[5,4,256]{2,1,0:T(4,128)S(1)}, f32[5,4,256]{2,1,0:T(4,128)S(1)}, u32[]{:S(2)}, u32[]{:S(2)}) collective-permute-start(f32[5,4,256]{2,1,0:T(4,128)S(1)} %get-tuple-element.41), channel_id=1, source_target_pairs={{0,4},{1,5},{2,6},{3,7},{4,0},{5,1},{6,2},{7,3},{8,12},{9,13},{10,... | collective-permute-start | bytes 61448 | tf_op jit(solution)/shard_map/ppermute | solution.py:39
  123.1 0.8 collective-permute-done.6.refs_1_
  123.9 1.2 finish.1
  (8 shorter events, 0.2 us)
Async XLA Ops:
  0.0 48.2 %collective-permute-start.2 = (f32[1024,256]{1,0:T(8,128)}, f32[1024,256]{1,0:T(8,128)S(1)}, u32[]{:S(2)}, u32[]{:S(2)}) collective-permute-start(f32[1024,256]{1,0:T(8,128)} %bitcast.25), channel_id=1, source_target_pairs={{0,2},{1,3},{2,0},{3,1},{4,6},{5,7},{6,4},{7,5},{8,10},{9,11},{10,... | collective-permute-start | bytes 3145736 | tf_op jit(solution)/shard_map/ppermute | solution.py:39
  3.0 45.2 %collective-permute-start.1 = (f32[1024,256]{1,0:T(8,128)}, f32[1024,256]{1,0:T(8,128)S(1)}, u32[]{:S(2)}, u32[]{:S(2)}) collective-permute-start(f32[1024,256]{1,0:T(8,128)} %bitcast.26), channel_id=1, source_target_pairs={{0,1},{1,0},{2,3},{3,2},{4,5},{5,4},{6,7},{7,6},{8,9},{9,8},{10,11... | collective-permute-start | bytes 3145736 | tf_op jit(solution)/shard_map/ppermute | solution.py:39
  16.2 38.6 %copy-start = (f32[1,1024,256]{2,1,0:T(8,128)S(1)}, f32[1,1024,256]{2,1,0:T(8,128)}, u32[]{:S(2)}) copy-start(f32[1,1024,256]{2,1,0:T(8,128)} %param.5) | copy-start | bytes 3145732
  49.3 32.6 %collective-permute-start.5 = (f32[1024,256]{1,0:T(8,128)}, f32[1024,256]{1,0:T(8,128)S(1)}, u32[]{:S(2)}, u32[]{:S(2)}) collective-permute-start(f32[1024,256]{1,0:T(8,128)} %broadcast_select_fusion), channel_id=1, source_target_pairs={{0,2},{1,0},{2,3},{3,1},{4,6},{5,4},{6,7},{7,5},{8,10},{9,8},{10,1... | collective-permute-start | bytes 3145736 | tf_op jit(solution)/shard_map/ppermute | solution.py:39
  52.9 5.8 %copy-start.1 = (f32[16,32,256]{2,1,0:T(8,128)}, f32[16,32,256]{2,1,0:T(8,128)S(1)}, u32[]{:S(2)}) copy-start(f32[16,32,256]{2,1,0:T(8,128)S(1)} %get-tuple-element.35) | copy-start | bytes 1572868
  52.9 15.0 %collective-permute-start.3 = (f32[16,32,256]{2,1,0:T(8,128)}, f32[16,32,256]{2,1,0:T(8,128)S(1)}, u32[]{:S(2)}, u32[]{:S(2)}) collective-permute-start(f32[16,32,256]{2,1,0:T(8,128)} %get-tuple-element.36), channel_id=1, source_target_pairs={{0,4},{1,5},{2,6},{3,7},{4,0},{5,1},{6,2},{7,3},{8,12},{9,13},{10,... | collective-permute-start | bytes 1572872 | tf_op jit(solution)/shard_map/ppermute | solution.py:39
  58.7 1.6 %collective-permute-start = (f32[16,16,256]{2,1,0:T(8,128)S(1)}, f32[16,16,256]{2,1,0:T(8,128)S(1)}, u32[]{:S(2)}, u32[]{:S(2)}) collective-permute-start(f32[16,16,256]{2,1,0:T(8,128)S(1)} %get-tuple-element.26), channel_id=1, source_target_pairs={{0,4},{1,5},{2,6},{3,7},{4,0},{5,1},{6,2},{7,3},{8,12},{9,13},{10,... | collective-permute-start | bytes 786440 | tf_op jit(solution)/shard_map/ppermute | solution.py:39
  61.1 15.1 %all-to-all-start = ((f32[16,16,256]{2,1,0:T(8,128)}), f32[16,16,256]{2,1,0:T(8,128)S(1)}, u32[]{:S(2)}, u32[]{:S(2)}) async-start(f32[16,16,256]{2,1,0:T(8,128)} %add.33), calls=%async_computation | async-start | bytes 524288 | tf_op jit(solution)/shard_map/all_to_all | solution.py:47
  76.2 13.9 %all-to-all-start.1 = ((f32[16,32,256]{2,1,0:T(8,128)}), f32[16,32,256]{2,1,0:T(8,128)S(1)}, u32[]{:S(2)}, u32[]{:S(2)}) async-start(f32[16,32,256]{2,1,0:T(8,128)} %add.34), calls=%async_computation.1 | async-start | bytes 1048576 | tf_op jit(solution)/shard_map/all_to_all | solution.py:47
  90.2 30.7 %all-to-all-start.2 = ((f32[32,8,512]{2,1,0:T(8,128)}), f32[32,8,512]{2,1,0:T(8,128)S(1)}, u32[]{:S(2)}, u32[]{:S(2)}) async-start(f32[32,8,512]{2,1,0:T(8,128)} %bitcast.10), calls=%async_computation.2 | async-start | bytes 1048576 | tf_op jit(solution)/shard_map/all_to_all | solution.py:53
  99.5 17.5 %collective-permute-start.4 = (f32[3,8,256]{2,1,0:T(8,128)S(1)}, f32[3,8,256]{2,1,0:T(8,128)S(1)}, u32[]{:S(2)}, u32[]{:S(2)}) collective-permute-start(f32[3,8,256]{2,1,0:T(8,128)S(1)} %fusion.1), channel_id=1, source_target_pairs={{0,8},{1,9},{2,10},{3,11},{4,12},{5,13},{6,14},{7,15},{8,0},{9,1},... | collective-permute-start | bytes 73736 | tf_op jit(solution)/shard_map/ppermute | solution.py:39
  121.0 2.9 %collective-permute-start.6 = (f32[5,4,256]{2,1,0:T(4,128)S(1)}, f32[5,4,256]{2,1,0:T(4,128)S(1)}, u32[]{:S(2)}, u32[]{:S(2)}) collective-permute-start(f32[5,4,256]{2,1,0:T(4,128)S(1)} %get-tuple-element.41), channel_id=1, source_target_pairs={{0,4},{1,5},{2,6},{3,7},{4,0},{5,1},{6,2},{7,3},{8,12},{9,13},{10,... | collective-permute-start | bytes 61448 | tf_op jit(solution)/shard_map/ppermute | solution.py:39
